TPU v7x, 32 devices: a whole 2x2x4 slice. The times are simulated.
32 devices in a mesh: dp: 8 (over z, y), tensor: 4 (over x, core).
Axes of the slice: x: 2, y: 2, z: 4, core: 2. Of those that a mesh axis runs over, the one named last changes fastest.
Arguments:
- inputs: bfloat16 [4096, 1280], P(('dp', 'tensor')), may hold values from -6 to 6
- weight_query: bfloat16 [1280, 1280], P('dp', 'tensor'), may hold values from -0.15625 to 0.15625
- weight_key: bfloat16 [1280, 1280], P('dp', 'tensor'), may hold values from -0.15625 to 0.15625
- weight_value: bfloat16 [1280, 1280], P('dp', 'tensor'), may hold values from -0.15625 to 0.15625
- weight_output: bfloat16 [1280, 1280], P('tensor', 'dp'), may hold values from -2 to 2
- weight_hidden: bfloat16 [1280, 1280], P('dp', 'tensor'), may hold values from -0.15625 to 0.15625
- weight_down: bfloat16 [1280, 1280], P('tensor', 'dp'), may hold values from -0.15625 to 0.15625
- bias_query: float32 [1280], replicated, may hold values from -6 to 6
- bias_value: float32 [1280], replicated, may hold values from -0.75 to 0.75
- bias_hidden: float32 [1280], replicated, may hold values from -6 to 6
- bias_output: float32 [1280], replicated, may hold values from -4 to 4
- bias_final: float32 [1280], replicated, may hold values from -4 to 4
- gain_attention: float32 [1280], replicated, may hold values from 0.25 to 1.75
- gain_mixer: float32 [1280], replicated, may hold values from 0.25 to 1.75
- query_scale: float32 [80], replicated, may hold values from 0 to 1.5
- lengths: int32 [8], P('dp'), may hold values from 128 to 512, as said below
- cotangent: bfloat16 [4096, 1280], P(('dp', 'tensor')), may hold values from -6 to 6
Outputs:
- output: bfloat16 [4096, 1280], P(('dp', 'tensor'))
- grad_inputs: bfloat16 [4096, 1280], P(('dp', 'tensor'))
- grad_weight_query: float32 [1280, 1280], P('dp', 'tensor')
- grad_weight_key: float32 [1280, 1280], P('dp', 'tensor')
- grad_weight_value: float32 [1280, 1280], P('dp', 'tensor')
- grad_weight_output: float32 [1280, 1280], P('tensor', 'dp')
- grad_weight_hidden: float32 [1280, 1280], P('dp', 'tensor')
- grad_weight_down: float32 [1280, 1280], P('tensor', 'dp')
- grad_bias_query: float32 [1280], replicated
- grad_bias_value: float32 [1280], replicated
- grad_bias_hidden: float32 [1280], replicated
- grad_bias_output: float32 [1280], replicated
- grad_bias_final: float32 [1280], replicated
- grad_gain_attention: float32 [1280], replicated
- grad_gain_mixer: float32 [1280], replicated
- grad_query_scale: float32 [80], replicated
Inputs may be any that keep to these rules, and one draw needn't show every extreme that they name: `lengths`: each series slot holds at least 128 live positions, then padding; in every draw some slot is live throughout.
All inputs are finite; a program needn't handle non-finite values.
Results may differ from a plain program's by a relative error of at most 0.017.
Values may be sent and summed in bfloat16 or wider, within the bound.
No kernel may reach another device: no remote copies, remote signals or barrier semaphores. Data moves between devices by JAX's collectives and lax.ppermute only.
A program may use at most 128 MiB of HBM per device.

v0:
```python
import jax
import jax.numpy as jnp
from jax import lax
from jax.experimental import pallas as pl
from jax.experimental.pallas import tpu as pltpu
from jax.sharding import PartitionSpec as P

EPSILON = 1e-06
SOFTPLUS_UNIT = 1.442695041
AXES = ("dp", "tensor")
F32 = jnp.float32
BF16 = jnp.bfloat16
LANES = 128
TENSOR_ORDER = (0, 2, 1, 3)
NN, NT, TN = ((1,), (0,)), ((1,), (1,)), ((0,), (0,))


def dot(left, right, dims=NN):
    return lax.dot_general(left, right, (dims, ((), ())), preferred_element_type=F32)


def shaped(shape, kind):
    return jax.ShapeDtypeStruct(shape, kind)


def call(name, kernel, outs, scalars, *arguments, flops=1e6, scratch=(), limit=12, remote=0):
    space = pl.BlockSpec(memory_space=pltpu.VMEM)
    apart = pl.BlockSpec(memory_space=pltpu.HBM)
    moved = sum(a.size * a.dtype.itemsize for a in (*arguments, *outs))
    return pl.pallas_call(
        kernel,
        name=name,
        out_shape=outs,
        in_specs=[pl.BlockSpec(memory_space=pltpu.SMEM)]
        + [space] * (len(arguments) - remote)
        + [apart] * remote,
        out_specs=[space] * len(outs),
        scratch_shapes=scratch,
        compiler_params=pltpu.CompilerParams(vmem_limit_bytes=limit << 20),
        cost_estimate=pl.CostEstimate(flops=int(flops), bytes_accessed=moved, transcendentals=0),
    )(scalars, *arguments)


def pack(first, second):
    main = first.shape[1] // LANES * LANES
    return jnp.concatenate([first[:, :main], second[:, :main], first[:, main:], second[:, main:]], axis=1)


def unpack(both):
    width = both.shape[1] // 2
    main = width // LANES * LANES
    edge = main * 2 + width - main
    first = jnp.concatenate([both[:, :main], both[:, 2 * main : edge]], axis=1)
    rest = both[:, 2 * main :].astype(F32)[:, width - main :].astype(both.dtype)
    second = jnp.concatenate([both[:, main : 2 * main], rest], axis=1)
    return first, second


def to_own(value, ring, pair, n_dp):
    width = value.shape[1]
    depth = width // n_dp
    value = swap_pairs(value, pair, depth)
    bit = 1
    while bit < n_dp // 2:
        moved = pltpu.roll(value, width - bit * 2 * depth, 1)
        value = jnp.where((ring & bit) != 0, moved, value)
        bit *= 2
    return value


def from_own(value, ring, pair, n_dp):
    width = value.shape[1]
    depth = width // n_dp
    bit = 1
    while bit < n_dp // 2:
        moved = pltpu.roll(value, bit * 2 * depth, 1)
        value = jnp.where((ring & bit) != 0, moved, value)
        bit *= 2
    return swap_pairs(value, pair, depth)


def swap_pairs(value, pair, depth):
    width = value.shape[1]
    lane = lax.broadcasted_iota(jnp.int32, value.shape, 1)
    low = lax.rem(lane, 2 * depth) < depth
    other = jnp.where(low, pltpu.roll(value, width - depth, 1), pltpu.roll(value, depth, 1))
    return jnp.where(pair != 0, other, value)


def row_mean(value):
    return jnp.sum(value, axis=1, keepdims=True) * (1.0 / value.shape[1])


def normalize(value):
    inverse = lax.rsqrt(row_mean(value * value) + EPSILON)
    return value * inverse, inverse


def norm_back(grad_normed, normed, inverse, gain):
    scaled = grad_normed * gain
    return inverse * (scaled - normed * row_mean(scaled * normed))


def load(sources, targets, sem):
    copies = [pltpu.make_async_copy(a, b, sem.at[k]) for k, (a, b) in enumerate(zip(sources, targets))]
    for copy in copies:
        copy.start()
    for copy in copies:
        copy.wait()


def pack_kernel(s, first, second, out, one, two, sem):
    load((first, second), (one, two), sem)
    out[...] = pack(one[...].astype(F32), two[...].astype(F32)).astype(BF16)


def row_of(ref):
    return jnp.concatenate([ref[k : k + 1] for k in range(ref.shape[0])], axis=1)


def prepare_kernel(n_dp, s, scale, *refs):
    sources, (h, x_own, grad, vectors, biases) = refs[:9], refs[9:14]
    x, cotangent, *given = refs[14:23]
    load(sources, refs[14:23], refs[23])
    ring, pair, place, length = s[0], s[1], s[2], s[3]
    value = to_own(x[...].astype(F32), ring, pair, n_dp)
    stacked = jnp.concatenate([row_of(given[k]) for k in (0, 1, 2, 3, 4, 5, 6, 6)], axis=0)
    width = biases.shape[1]
    mine = stacked[:, :width]
    for number in range(1, stacked.shape[1] // width):
        mine = jnp.where(place == number, stacked[:, number * width : (number + 1) * width], mine)
    biases[...] = mine
    biases[7:8] = scale[...]
    stacked = to_own(stacked, ring, pair, n_dp)
    normed, _ = normalize(value)
    h[...] = (normed * stacked[0:1]).astype(BF16)
    x_own[...] = value.astype(BF16)
    rows = value.shape[0]
    row = lax.broadcasted_iota(jnp.int32, value.shape, 0) + place * rows
    g = jnp.where(row < length, to_own(cotangent[...].astype(F32), ring, pair, n_dp), 0.0)
    grad[...] = g.astype(BF16)
    vectors[...] = stacked
    vectors[4:5] = jnp.sum(g, axis=0, keepdims=True)


def join(pieces, out):
    rows = pieces[0].shape[0]
    for number, piece in enumerate(pieces):
        out[pl.ds(number * rows, rows)] = piece[...]


def tiles(rows, body, size=128):
    def step(m, carry):
        body(pl.ds(pl.multiple_of(m * size, size), size), m)
        return carry

    lax.fori_loop(0, rows // size, step, 0)


def positions(shape, axis, place, local, offset=0):
    row = lax.broadcasted_iota(jnp.int32, shape, axis) + offset
    shift = local.bit_length() - 1
    block = row >> shift
    turned = ((block & 1) << 1) | (block >> 1)
    return ((place ^ turned) << shift) + (row & (local - 1))


def fetch(blocks, out, sem):
    depth = blocks[0].shape[0]
    n_ring = out.shape[0] // (2 * depth)
    copies = []

    def copy(source, row):
        copies.append(pltpu.make_async_copy(source, out.at[pl.ds(row, depth)], sem.at[len(copies)]))

    if n_ring == 0:
        copy(blocks[0], 0)
    else:
        for j in range(n_ring):
            copy(blocks[j], 2 * j * depth)
        j = 0
        for block in blocks[n_ring:]:
            for k in range(block.shape[0] // depth):
                copy(block.at[pl.ds(k * depth, depth)], (2 * j + 1) * depth)
                j += 1
    for one in copies:
        one.start()
    return copies


def stack_kernel(s, *refs):
    join(refs[:-1], refs[-1])


def of_head(value, number, head_size):
    lanes = lax.broadcasted_iota(jnp.int32, (1, value.shape[1]), 1) // head_size
    return jnp.where(lanes == number, value, jnp.zeros((), value.dtype))


def attend_kernel(n_blocks, head_size, s, p0, p1, p2, p3, biases, *refs):
    blocks, (q_raw, q_low, k_low, h, weight, turned, sem) = refs[:n_blocks], refs[n_blocks:]
    copies = fetch(blocks, weight, sem)
    join((p0, p1, p2, p3), h)
    for copy in copies:
        copy.wait()
    first, second = unpack(dot(h[...], weight[...]))
    first = first + biases[4:5]
    q_raw[...] = first
    q_low[...] = (first * biases[7:8]).astype(BF16)
    k_low[...] = second.astype(BF16)
    place, length = s[2], s[3]
    rows, local = q_low.shape[0], p0.shape[0]
    key_place = positions((rows, 1), 0, place, local)

    def head(number, carry):
        def part(at, m):
            score = dot(k_low[...], of_head(q_low[at], number, head_size), NT)
            query_place = positions((1, 128), 1, place, local, m * 128)
            last = jnp.minimum(query_place, length - 1)
            score = jnp.where(key_place <= last, score, -1e30)
            raised = jnp.exp(score - jnp.max(score, axis=0, keepdims=True))
            share = 1.0 / jnp.sum(raised, axis=0, keepdims=True)
            turned[number, :, at] = (raised * share).astype(BF16)

        tiles(rows, part)
        return carry

    lax.fori_loop(0, turned.shape[0], head, 0)


def mixed_heads(turned, value, head_size, dims):
    total = None
    for number in range(turned.shape[0]):
        term = dot(turned[number], of_head(value, number, head_size), dims)
        total = term if total is None else total + term
    return total


def split_weight(weight, one, two):
    def body(at, m):
        one[at], two[at] = unpack(weight[at])

    tiles(weight.shape[0], body)


def context_kernel(head_size, n_blocks, s, h, turned, biases, *refs):
    blocks, (v_low, context, far, near, w_value, w_output, weight, sem) = refs[:n_blocks], refs[n_blocks:]
    for copy in fetch(blocks, weight, sem):
        copy.wait()
    split_weight(weight, w_value, w_output)
    v_low[...] = (dot(h[...], w_value[...]) + biases[5:6]).astype(BF16)
    context[...] = mixed_heads(turned, v_low[...], head_size, TN).astype(BF16)
    split_product(context, w_output, far, near)


def split_product(left, right, far, near, extra=None, along=None):
    half, total = near.shape[0], None
    for start, out in ((half, far), (0, near)):
        at = pl.ds(start, half)
        value = dot(left[at], right[...], NT)
        if extra is not None:
            value = value + dot(extra[0][at], extra[1][...], NT)
        out[...] = value.astype(out.dtype)
        if along is not None:
            summed = jnp.sum(value * along[at].astype(F32), axis=0, keepdims=True)
            total = summed if total is None else total + summed
    return total


def middle_kernel(s, near, got, send, keep):
    rows = send.shape[0]
    send[...] = (near[rows:] + got[rows:].astype(F32)).astype(BF16)
    keep[...] = near[:rows] + got[:rows].astype(F32)


def second_norm_kernel(s, keep, got, x_own, vectors, x_one, h):
    value = x_own[...].astype(F32) + keep[...] + got[...].astype(F32) + vectors[2:3]
    x_one[...] = value
    normed, _ = normalize(value)
    h[...] = (normed * vectors[1:2]).astype(BF16)


def grad_act_kernel(n_blocks, s, p0, p1, p2, p3, *refs):
    blocks, (grad_act, g, w_hidden, w_down, weight, sem) = refs[:n_blocks], refs[n_blocks:]
    copies = fetch(blocks, weight, sem)
    join((p0, p1, p2, p3), g)
    for copy in copies:
        copy.wait()
    split_weight(weight, w_hidden, w_down)
    grad_act[...] = dot(g[...], w_down[...])


def hidden_kernel(s, p0, p1, p2, p3, w_hidden, biases, grad_act, out_far, out_near, act, grad_pre, h):
    join((p0, p1, p2, p3), h)
    pre = dot(h[...], w_hidden[...]) + biases[6:7]
    sigma = jax.nn.sigmoid(pre)
    act[...] = (pre * sigma).astype(BF16)
    grad_pre[...] = (grad_act[...] * (sigma * (1.0 + pre * (1.0 - sigma)))).astype(BF16)
    split_product(grad_pre, w_hidden, out_far, out_near)


def spread_terms(term, keep, sends, depth, order):
    if not sends:
        keep[...] = term[...]
        return
    half = len(order) // len(sends)
    for at, j in enumerate(order):
        keep[pl.ds(at * depth, depth)] = term[pl.ds(2 * j * depth, depth)]
        sends[at // half][pl.ds(at % half * depth, depth)] = term[pl.ds((2 * j + 1) * depth, depth)]


def two_terms(left_one, right_one, left_two, right_two, term):
    first = dot(left_one[...], right_one[...], TN)
    second = dot(left_two[...], right_two[...], TN)
    term[...] = pack(first, second).astype(BF16)


def down_kernel(depth, order, s, h, g, act, grad_pre, w_down, far, near, b_hidden, keep, *refs):
    *sends, term = refs
    two_terms(h, grad_pre, g, act, term)
    spread_terms(term, keep, sends, depth, order)
    b_hidden[...] = jnp.sum(grad_pre[...].astype(F32), axis=0, keepdims=True)
    split_product(act, w_down, far, near)


def pair_kernel(start, s, own, got, *outs):
    depth = outs[0].shape[0]
    for k, out in enumerate(outs):
        value = own[pl.ds((start + k) * depth, depth)].astype(F32) + got[pl.ds(k * depth, depth)].astype(F32)
        out[...] = value.astype(out.dtype)


def owned_kernel(n_got, s, keep, *refs):
    total = keep[...]
    for got in refs[:n_got]:
        total = total + got[...].astype(F32)
    refs[n_got][...], refs[n_got + 1][...] = unpack(total)


def grad_middle_kernel(s, keep, got, x_one, grad, vectors, grad_low, grad_full, sums):
    normed, inverse = normalize(x_one[...])
    grad_h = keep[...] + got[...].astype(F32)
    full = grad[...].astype(F32) + norm_back(grad_h, normed, inverse, vectors[1:2])
    grad_full[...] = full
    grad_low[...] = full.astype(BF16)
    sums[...] = vectors[...]
    sums[5:6] = jnp.sum(full, axis=0, keepdims=True)
    sums[6:7] = jnp.sum(grad_h * normed, axis=0, keepdims=True)


def grad_context_kernel(depth, order, head_size, s, p0, p1, p2, p3, w_output, turned, context, h, *refs):
    grad_context, grad_value, gm, keep, *sends, term = refs
    join((p0, p1, p2, p3), gm)
    grad_context[...] = dot(gm[...], w_output[...]).astype(BF16)
    grad_value[...] = mixed_heads(turned, grad_context[...], head_size, NN).astype(BF16)
    two_terms(h, grad_value, gm, context, term)
    spread_terms(term, keep, sends, depth, order)


def grad_scores_kernel(head_size, s, turned, grad_context, v_low, q_low, k_low, q_raw, biases, *refs):
    grad_qk, sums, grad_q, grad_k, scores = refs
    rows = q_low.shape[0]
    grad_q[...] = jnp.zeros_like(grad_q)
    grad_k[...] = jnp.zeros_like(grad_k)

    def head(number, carry):
        def part(at, m):
            grad_chance = dot(v_low[...], of_head(grad_context[at], number, head_size), NT)
            chance = turned[number, :, at].astype(F32)
            product = chance * grad_chance
            center = jnp.sum(product, axis=0, keepdims=True)
            scores[:, at] = (product - chance * center).astype(BF16)

        tiles(rows, part)
        grad_q[...] += dot(scores[...], of_head(k_low[...], number, head_size), TN)
        grad_k[...] += dot(scores[...], of_head(q_low[...], number, head_size))
        return carry

    lax.fori_loop(0, turned.shape[0], head, 0)
    low = grad_q[...].astype(BF16).astype(F32)
    sums[0:1] = jnp.sum(low * q_raw[...], axis=0, keepdims=True)
    low = (low * biases[7:8]).astype(BF16).astype(F32)
    grad_qk[...] = pack(low, grad_k[...]).astype(BF16)
    sums[1:2] = jnp.sum(low, axis=0, keepdims=True)


def grad_first_kernel(
    n_dp, depth, order, s, grad_qk, w_qk, grad_value, w_value, h, sums_in, sums_q, b_hidden, slope, *refs
):
    far, near, sums, keep, *sends, term = refs
    term[...] = dot(h[...], grad_qk[...], TN).astype(BF16)
    spread_terms(term, keep, sends, depth, order)
    ring, pair, place = s[0], s[1], s[2]
    gained = split_product(grad_qk, w_qk, far, near, (grad_value, w_value), h) / sums_in[0:1]
    row = lax.broadcasted_iota(jnp.int32, sums.shape, 0)
    sums[...] = from_own(jnp.where(row == 7, gained, sums_in[...]), ring, pair, n_dp)
    sums[0:4] = jnp.zeros((4, sums.shape[1]), F32)
    local_width, head_size = sums_q.shape[1], slope.shape[1]
    b_value = jnp.sum(grad_value[...].astype(F32), axis=0, keepdims=True)
    share = jnp.concatenate([sums_q[1:2], b_value, b_hidden[...]], axis=0)
    for number in range(sums.shape[1] // local_width):

        @pl.when(place == number)
        def _():
            sums[0:3, number * local_width : (number + 1) * local_width] = share

    scale = sums_q[0:1]
    total = scale[:, :head_size]
    for number in range(1, local_width // head_size):
        total = total + scale[:, number * head_size : (number + 1) * head_size]
    sums[3:4, :head_size] = total * slope[...]


def last_kernel(n_dp, s, keep, got, x_own, grad_full, sums_in, grad_in):
    normed, inverse = normalize(x_own[...].astype(F32))
    grad_h = keep[...] + got[...].astype(F32)
    full = grad_full[...] + norm_back(grad_h, normed, inverse, sums_in[0:1])
    grad_in[...] = from_own(full, s[0], s[1], n_dp).astype(BF16)


def add_kernel(s, one, two, out):
    out[...] = one[...] + two[...]


def output_kernel(n_dp, s, keep, got, x_one, vectors, out):
    value = x_one[...] + keep[...] + got[...].astype(F32) + vectors[3:4]
    out[...] = from_own(value, s[0], s[1], n_dp).astype(BF16)


def tie(*values):
    return lax.optimization_barrier(values)


class Links:
    def __init__(self, n_dp, n_tensor):
        self.n_dp, self.n_tensor = n_dp, n_tensor
        self.ring = n_dp // 2
        self.wide = self.ring > 4
        order = sorted(range(1, self.ring), key=lambda j: -min(j, self.ring - j))
        self.order = [] if self.wide else order

    def move(self, value, target):
        pairs = []
        for d in range(self.n_dp):
            for t in range(self.n_tensor):
                to_d, to_t = target(d, t)
                pairs.append((d * self.n_tensor + t, to_d * self.n_tensor + to_t))
        return lax.ppermute(value, AXES, pairs)

    def chip(self, value):
        return self.move(value, lambda d, t: (d, t ^ 2))

    def core(self, value):
        return self.move(value, lambda d, t: (d, t ^ 1))

    def pair(self, value):
        return self.move(value, lambda d, t: (d ^ 1, t))

    def shift(self, value, step):
        n = self.ring
        return self.move(value, lambda d, t: (((d // 2 + step) % n) * 2 + d % 2, t))

    def gather_tensor(self, rows):
        near = self.chip(rows)
        return rows, near, self.core(rows), self.core(near)

    def gather_ring(self, shard):
        if self.wide:
            blocks = lax.all_gather(shard, "dp", axis=0)
            place = lax.axis_index("dp")
            blocks = jnp.roll(blocks.reshape(self.ring, 2, *shard.shape), -(place >> 1), axis=0)
            blocks = jnp.where((place & 1) == 1, blocks[:, ::-1], blocks)
            return [blocks.reshape(self.n_dp * shard.shape[0], shard.shape[1])]
        got = {0: shard}
        for j in self.order:
            got[j] = self.shift(shard, -j)
        return [got[j] for j in range(self.ring)]

    def scatter_wide(self, total):
        place = lax.axis_index("dp")
        blocks = total.reshape(self.ring, 2, total.shape[0] // self.n_dp, total.shape[1])
        blocks = jnp.where((place & 1) == 1, blocks[:, ::-1], blocks)
        blocks = jnp.roll(blocks, place >> 1, axis=0).reshape(total.shape).astype(F32)
        return unpack(lax.psum_scatter(blocks, "dp", scatter_dimension=0, tiled=True))

    def steps(self):
        found, bit = [lambda d, t: (d, t ^ 1)], 2
        while bit < self.n_dp:
            found.append(lambda d, t, bit=bit: (d ^ bit, t))
            bit *= 2
        return found + [lambda d, t: (d, t ^ 2), lambda d, t: (d ^ 1, t)]


def body(
    inputs,
    weight_query,
    weight_key,
    weight_value,
    weight_output,
    weight_hidden,
    weight_down,
    bias_query,
    bias_value,
    bias_hidden,
    bias_output,
    bias_final,
    gain_attention,
    gain_mixer,
    query_scale,
    lengths,
    cotangent,
    n_dp,
    n_tensor,
):
    links = Links(n_dp, n_tensor)
    n_ring = n_dp // 2
    local_rows, width = inputs.shape
    all_rows = local_rows * n_tensor
    depth = width // n_dp
    local_width = weight_query.shape[1]
    both = 2 * local_width
    head_size = query_scale.shape[0]
    heads = local_width // head_size
    dp_index = lax.axis_index("dp")
    tensor_index = lax.axis_index("tensor")
    s = jnp.stack([dp_index >> 1, dp_index & 1, tensor_index, lengths[0]])
    product = 2 * all_rows * width * local_width
    mixed = 2 * all_rows * all_rows * local_width

    def run(name, kernel, outs, *arguments, **rest):
        return call(name, kernel, [shaped(*o) for o in outs], s, *arguments, **rest)

    def bind(kernel, *fixed):
        def bound(*refs):
            return kernel(*fixed, *refs)

        return bound

    packed = [((depth, both), BF16)]
    rows_low, rows_full = ((local_rows, width), BF16), ((local_rows, width), F32)
    split = [((all_rows // 2, width), BF16), ((all_rows // 2, width), F32)]
    part = ((all_rows, local_width), BF16)
    part_full = ((all_rows, local_width), F32)
    whole_rows = ((all_rows, width), BF16)
    weight = ((width, local_width), BF16)
    vector = ((8, width), F32)
    halves = [((width // 2, both), BF16)] * 2
    term = [pltpu.VMEM((width, both), BF16)]
    sems = [pltpu.SemaphoreType.DMA((n_dp,))]

    unit = SOFTPLUS_UNIT / jnp.sqrt(F32(head_size))
    scale_wide = jnp.tile(jax.nn.softplus(query_scale) * unit, heads)[None]
    slope = (jax.nn.sigmoid(query_scale) * unit)[None]
    loads = [pltpu.VMEM((depth, local_width), BF16)] * 2 + [pltpu.SemaphoreType.DMA((2,))]

    def apart(value):
        return pltpu.with_memory_space_constraint(value, pltpu.HBM)

    def pack_two(name, one, two):
        return run("pack_" + name, pack_kernel, packed, apart(one), apart(two), remote=2, scratch=loads)[0]

    own_qk = pack_two("qk", weight_query, weight_key)
    ring_qk = links.gather_ring(own_qk)
    given = (gain_attention, gain_mixer, bias_output, bias_final, bias_query, bias_value, bias_hidden)
    scale_wide, slope = tie(scale_wide, slope)
    tall = (width // LANES, LANES)
    h_own, x_own, grad_own, vectors, biases = run(
        "prepare",
        bind(prepare_kernel, n_dp),
        [rows_low, rows_low, rows_low, vector, ((8, local_width), F32)],
        scale_wide,
        *(apart(v) for v in (inputs, cotangent, *(v.reshape(tall) for v in given))),
        remote=9,
        scratch=[pltpu.VMEM((local_rows, width), BF16)] * 2
        + [pltpu.VMEM(tall, F32)] * 7
        + [pltpu.SemaphoreType.DMA((9,))],
    )
    own_vo = pack_two("vo", weight_value, weight_output.T)
    own_hd = pack_two("hd", weight_hidden, weight_down.T)
    order = links.order + [0]
    n_half = len(order) // 2

    def partners(blocks):
        if links.wide:
            return []
        (stacked,) = run("stack", stack_kernel, [((len(blocks) * depth, both), BF16)], *blocks)
        return [links.pair(stacked)]

    first_qk = [] if links.wide else [links.pair(own_qk)]
    h_own, ring_qk, first_qk, own_vo, own_hd = tie(h_own, ring_qk, first_qk, own_vo, own_hd)
    h_one = links.gather_tensor(h_own)
    ring_vo = links.gather_ring(own_vo)
    blocks_qk = ring_qk + first_qk + partners(ring_qk[1:])
    h_one, ring_vo, blocks_qk = tie(h_one, ring_vo, blocks_qk)
    blocks_vo = ring_vo + partners(ring_vo)
    ring_hd = links.gather_ring(own_hd)
    q_raw, q_low, k_low, h_all, w_qk, turned = run(
        "attend",
        bind(attend_kernel, len(blocks_qk), head_size),
        [
            part_full,
            part,
            part,
            whole_rows,
            ((width, both), BF16),
            ((heads, all_rows, all_rows), BF16),
        ],
        *h_one,
        biases,
        *blocks_qk,
        remote=len(blocks_qk),
        scratch=sems,
    )
    grad_own, q_low = tie(grad_own, q_low)
    grad_rows = links.gather_tensor(grad_own)
    turned, blocks_vo, ring_hd = tie(turned, blocks_vo, ring_hd)
    blocks_hd = ring_hd + partners(ring_hd)
    v_low, context, far, near, w_value, w_output = run(
        "context",
        bind(context_kernel, head_size, len(blocks_vo)),
        [part, part, *split, weight, weight],
        h_all,
        turned,
        biases,
        *blocks_vo,
        remote=len(blocks_vo),
        scratch=term + sems,
    )

    def core_half(far, near):
        return run("middle", middle_kernel, [rows_low, rows_full], near, links.core(far))

    send, keep = core_half(far, near)
    got = links.chip(send)
    got, blocks_hd, grad_rows = tie(got, blocks_hd, grad_rows)
    x_one, h_two_own = run("second_norm", second_norm_kernel, [rows_full, rows_low], keep, got, x_own, vectors)
    h_two = links.gather_tensor(h_two_own)
    grad_act, grad_all, w_hidden, w_down = run(
        "grad_act",
        bind(grad_act_kernel, len(blocks_hd)),
        [part_full, whole_rows, weight, weight],
        *grad_rows,
        *blocks_hd,
        remote=len(blocks_hd),
        scratch=term + sems,
    )
    far, near, act, grad_pre, h_two_all = run(
        "hidden",
        hidden_kernel,
        [*split, part, part, whole_rows],
        *h_two,
        w_hidden,
        biases,
        grad_act,
    )
    send, keep = core_half(far, near)
    act, send = tie(act, send)
    got = links.chip(send)
    if links.wide:
        terms = [((width, both), BF16)]
    else:
        terms = [((n_ring * depth, both), BF16)] + [((n_half * depth, both), BF16)] * 2
    far, near, grad_b_hidden, *terms_hd = run(
        "down",
        bind(down_kernel, depth, order),
        [*split, ((1, local_width), F32), *terms],
        h_two_all,
        grad_all,
        act,
        grad_pre,
        w_down,
        scratch=term,
    )
    got, terms_hd = tie(got, terms_hd)

    def pair_sum(name, start, keep, got, last):
        count = got.shape[0] // depth
        outs = packed * count
        if last:
            outs = packed * (count - 1) + [((depth, both), F32)]
        return run("pair_" + name, bind(pair_kernel, start), outs, keep, got)

    def ring_send(parts, start):
        return [links.shift(part, j) for part, j in zip(parts, links.order[start:])]

    def owned(name, parts):
        outs = [((depth, local_width), F32)] * 2
        return run("owned_" + name, bind(owned_kernel, n_ring - 1), outs, *parts)

    sent_hd = [links.pair(part) for part in terms_hd[1:]]
    grad_mid_low, grad_mid, sums = run(
        "grad_middle",
        grad_middle_kernel,
        [rows_low, rows_full, vector],
        keep,
        got,
        x_one,
        grad_own,
        vectors,
    )
    grad_mid_rows = links.gather_tensor(grad_mid_low)
    grad_mid_rows, far = tie(grad_mid_rows, far)
    if not links.wide:
        grad_mid_rows, sent_hd[0] = tie(grad_mid_rows, sent_hd[0])
        parts_hd = ring_send(pair_sum("hd_a", 0, terms_hd[0], sent_hd[0], False), 0)
    mix_send, mix_keep = core_half(far, near)
    mix_got = links.chip(mix_send)
    grad_context, grad_value, _, *terms_vo = run(
        "grad_context",
        bind(grad_context_kernel, depth, order, head_size),
        [part, part, whole_rows, *terms],
        *grad_mid_rows,
        w_output,
        turned,
        context,
        h_all,
        scratch=term,
    )
    grad_context, sent_hd[1:] = tie(grad_context, sent_hd[1:])
    sent_vo = [links.pair(part) for part in terms_vo[1:]]
    if not links.wide:
        *parts, zero_hd = pair_sum("hd_b", n_half, terms_hd[0], sent_hd[1], True)
        grad_context, parts = tie(grad_context, parts)
        parts_hd += ring_send(parts, n_half)
    grad_qk, sums_q = run(
        "grad_scores",
        bind(grad_scores_kernel, head_size),
        [((all_rows, both), BF16), ((8, local_width), F32)],
        turned,
        grad_context,
        v_low,
        q_low,
        k_low,
        q_raw,
        biases,
        scratch=[
            pltpu.VMEM((all_rows, local_width), F32),
            pltpu.VMEM((all_rows, local_width), F32),
            pltpu.VMEM((all_rows, all_rows), BF16),
        ],
    )
    grad_qk, sent_vo, mix_got = tie(grad_qk, sent_vo, mix_got)
    if not links.wide:
        grad_qk, parts_hd = tie(grad_qk, parts_hd)
        parts_vo = ring_send(pair_sum("vo_a", 0, terms_vo[0], sent_vo[0], False), 0)
        *parts, zero_vo = pair_sum("vo_b", n_half, terms_vo[0], sent_vo[1], True)
        parts_vo += ring_send(parts, n_half)
    far, near, sums, *terms_qk = run(
        "grad_first",
        bind(grad_first_kernel, n_dp, depth, order),
        [*split, vector, *terms],
        grad_qk,
        w_qk,
        grad_value,
        w_value,
        h_all,
        sums,
        sums_q,
        grad_b_hidden,
        slope,
        scratch=term,
    )
    sent_qk = [links.pair(part) for part in terms_qk[1:]]
    send, keep = core_half(far, near)
    got = links.chip(send)
    steps = links.steps()
    total = sums

    def exchange(value, step):
        return run("add", add_kernel, [vector], value, links.move(value, step))[0]

    for step in steps[:-2]:
        total = exchange(total, step)
    if not links.wide:
        got, sent_qk[0], parts_vo = tie(got, sent_qk[0], parts_vo)
        parts = pair_sum("qk_a", 0, terms_qk[0], sent_qk[0], False)
        got, parts = tie(got, parts)
        parts_qk = ring_send(parts, 0)
    (grad_in,) = run("last", bind(last_kernel, n_dp), [rows_low], keep, got, x_own, grad_mid, vectors)
    total, grad_in = tie(total, grad_in)
    total = exchange(total, steps[-2])
    if not links.wide:
        total, sent_qk[1] = tie(total, sent_qk[1])
        *parts, zero_qk = pair_sum("qk_b", n_half, terms_qk[0], sent_qk[1], True)
        total, parts = tie(total, parts)
        parts_qk += ring_send(parts, n_half)
    total = exchange(total, steps[-1])
    (output,) = run("output", bind(output_kernel, n_dp), [rows_low], mix_keep, mix_got, x_one, vectors)
    if links.wide:
        grad_hidden, grad_down = links.scatter_wide(terms_hd[0])
        grad_output_v, grad_output_o = links.scatter_wide(terms_vo[0])
        grad_query, grad_key = links.scatter_wide(terms_qk[0])
    else:
        grad_hidden, grad_down = owned("hd", [zero_hd, *parts_hd])
        grad_output_v, grad_output_o = owned("vo", [zero_vo, *parts_vo])
        grad_query, grad_key = owned("qk", [zero_qk, *parts_qk])
    return (
        output,
        grad_in,
        grad_query,
        grad_key,
        grad_output_v,
        grad_output_o.T,
        grad_hidden,
        grad_down.T,
        total[0],
        total[1],
        total[2],
        total[5],
        total[4],
        total[7],
        total[6],
        total[3, :head_size],
    )


def solution(mesh):
    n_dp, n_tensor = mesh.shape["dp"], mesh.shape["tensor"]

    def local(*arguments):
        return body(*arguments, n_dp, n_tensor)

    rows = P(("dp", "tensor"), None)
    into, out_of = P("dp", "tensor"), P("tensor", "dp")
    return jax.shard_map(
        local,
        mesh=mesh,
        in_specs=(rows, into, into, into, out_of, into, out_of, *[P()] * 8, P("dp"), rows),
        out_specs=(rows, rows, into, into, into, out_of, into, out_of, *[P()] * 8),
        check_vma=False,
    )
```

profile of v0, /device:TPU:0, one launch (start us, length us, event | category | flops | bytes accessed | tf_op | source)
XLA Modules:
  0.0 246.1 jit_solution(3744633206000391115)
XLA Ops:
  3.0 3.0 %collective-permute-start.3 = (bf16[160,640]{1,0:T(8,128)(2,1)S(1)}, bf16[160,640]{1,0:T(8,128)(2,1)S(1)}, u32[]{:S(2)}, u32[]{:S(2)}) collective-permute-start(bf16[160,640]{1,0:T(8,128)(2,1)S(1)} %pack_qk.1.refs_6_), channel_id=1, source_target_pairs={{0,4},{1,5},{2,6},{3,7},{4,0},{5,1},{6,2},{7,3},{8,12},{9,13},{10,... | collective-permute-start | bytes 614408 | tf_op jit(solution)/shard_map/ppermute | solution.py:448
  7.6 2.6 %collective-permute-start.1 = (bf16[160,640]{1,0:T(8,128)(2,1)S(1)}, bf16[160,640]{1,0:T(8,128)(2,1)S(1)}, u32[]{:S(2)}, u32[]{:S(2)}) collective-permute-start(bf16[160,640]{1,0:T(8,128)(2,1)S(1)} %pack_qk.1.refs_6_), channel_id=1, source_target_pairs={{0,16},{1,17},{2,18},{3,19},{4,20},{5,21},{6,22},{7,23},{8,24},{9,... | collective-permute-start | bytes 614408 | tf_op jit(solution)/shard_map/ppermute | solution.py:448
  15.5 3.1 %prepare.1 = (bf16[128,1280]{1,0:T(8,128)(2,1)S(1)}, bf16[128,1280]{1,0:T(8,128)(2,1)S(1)}, bf16[128,1280]{1,0:T(8,128)(2,1)S(1)}, f32[8,1280]{1,0:T(8,128)S(1)}, f32[8,320]{1,0:T(8,128)S(1)}) custom-call(s32[4]{0:T(128)S(1)} %pad_add_fusion.refs_0_.s, f32[1,320]{1,0:T(1,128)S(1)} %broadcast_in_dim_tile.3.refs_1_, bf16[128,1280]{1,0:T(8,128)(2,1)} %refs_2_.1, ...), custom_call_target="tpu_custom_call" | custom-call | flops 1000000 | bytes 1726720 | tf_op jit(solution)/shard_map/prepare/pallas_call | solution.py:30
  18.6 4.7 %collective-permute-done.1.refs_1_.refs_8_ = bf16[160,640]{1,0:T(8,128)(2,1)S(1)} collective-permute-done((bf16[160,640]{1,0:T(8,128)(2,1)S(1)}, bf16[160,640]{1,0:T(8,128)(2,1)S(1)}, u32[]{:S(2)}, u32[]{:S(2)}) %collective-permute-start.1) | collective-permute-done | bytes 204832 | tf_op jit(solution)/shard_map/ppermute | solution.py:448
  26.0 4.9 %collective-permute-start.9 = (bf16[160,640]{1,0:T(8,128)(2,1)S(1)}, bf16[160,640]{1,0:T(8,128)(2,1)S(1)}, u32[]{:S(2)}, u32[]{:S(2)}) collective-permute-start(bf16[160,640]{1,0:T(8,128)(2,1)S(1)} %pack_vo.1.refs_0_.refs_4_), channel_id=1, source_target_pairs={{0,8},{1,9},{2,10},{3,11},{4,12},{5,13},{6,14},{7,15},{8,16},{9,17... | collective-permute-start | bytes 614408 | tf_op jit(solution)/shard_map/ppermute | solution.py:448
  32.8 3.9 %collective-permute-start.8 = (bf16[160,640]{1,0:T(8,128)(2,1)S(1)}, bf16[160,640]{1,0:T(8,128)(2,1)S(1)}, u32[]{:S(2)}, u32[]{:S(2)}) collective-permute-start(bf16[160,640]{1,0:T(8,128)(2,1)S(1)} %pack_vo.1.refs_0_.refs_4_), channel_id=1, source_target_pairs={{0,16},{1,17},{2,18},{3,19},{4,20},{5,21},{6,22},{7,23},{8,24},{9,... | collective-permute-start | bytes 614408 | tf_op jit(solution)/shard_map/ppermute | solution.py:448
  36.8 3.4 %collective-permute-start.7 = (bf16[160,640]{1,0:T(8,128)(2,1)S(1)}, bf16[160,640]{1,0:T(8,128)(2,1)S(1)}, u32[]{:S(2)}, u32[]{:S(2)}) collective-permute-start(bf16[160,640]{1,0:T(8,128)(2,1)S(1)} %pack_vo.1.refs_0_.refs_4_), channel_id=1, source_target_pairs={{0,24},{1,25},{2,26},{3,27},{4,28},{5,29},{6,30},{7,31},{8,0},{9,1... | collective-permute-start | bytes 614408 | tf_op jit(solution)/shard_map/ppermute | solution.py:448
  40.2 6.9 %collective-permute-done.8.refs_2_.refs_6_ = bf16[160,640]{1,0:T(8,128)(2,1)S(1)} collective-permute-done((bf16[160,640]{1,0:T(8,128)(2,1)S(1)}, bf16[160,640]{1,0:T(8,128)(2,1)S(1)}, u32[]{:S(2)}, u32[]{:S(2)}) %collective-permute-start.8) | collective-permute-done | bytes 204832 | tf_op jit(solution)/shard_map/ppermute | solution.py:448
  48.3 4.8 %collective-permute-start.14 = (bf16[160,640]{1,0:T(8,128)(2,1)S(1)}, bf16[160,640]{1,0:T(8,128)(2,1)S(1)}, u32[]{:S(2)}, u32[]{:S(2)}) collective-permute-start(bf16[160,640]{1,0:T(8,128)(2,1)S(1)} %pack_hd.1.refs_0_.refs_5_), channel_id=1, source_target_pairs={{0,8},{1,9},{2,10},{3,11},{4,12},{5,13},{6,14},{7,15},{8,16},{9,17... | collective-permute-start | bytes 614408 | tf_op jit(solution)/shard_map/ppermute | solution.py:448
  53.1 3.4 %collective-permute-start.13 = (bf16[160,640]{1,0:T(8,128)(2,1)S(1)}, bf16[160,640]{1,0:T(8,128)(2,1)S(1)}, u32[]{:S(2)}, u32[]{:S(2)}) collective-permute-start(bf16[160,640]{1,0:T(8,128)(2,1)S(1)} %pack_hd.1.refs_0_.refs_5_), channel_id=1, source_target_pairs={{0,16},{1,17},{2,18},{3,19},{4,20},{5,21},{6,22},{7,23},{8,24},{9,... | collective-permute-start | bytes 614408 | tf_op jit(solution)/shard_map/ppermute | solution.py:448
  56.5 10.6 %attend.1 = (f32[512,320]{1,0:T(8,128)S(1)}, bf16[512,320]{1,0:T(8,128)(2,1)S(1)}, bf16[512,320]{1,0:T(8,128)(2,1)S(1)}, bf16[512,1280]{1,0:T(8,128)(2,1)S(1)}, ...) custom-call(s32[4]{0:T(128)S(1)} %pad_add_fusion.refs_0_.s, ...), custom_call_target="tpu_custom_call" | custom-call | flops 1000000 | bytes 9316352 | tf_op jit(solution)/shard_map/attend/pallas_call | solution.py:30
  69.6 6.3 %context.1 = (bf16[512,320]{1,0:T(8,128)(2,1)S(1)}, bf16[512,320]{1,0:T(8,128)(2,1)S(1)}, bf16[256,1280]{1,0:T(8,128)(2,1)S(1)}, f32[256,1280]{1,0:T(8,128)S(1)}...) custom-call(s32[4]{0:T(128)S(1)} %pad_add_fusion.refs_0_.s, ...), custom_call_target="tpu_custom_call" | custom-call | flops 1000000 | bytes 9316352 | tf_op jit(solution)/shard_map/context/pallas_call | solution.py:30
  79.7 8.3 %collective-permute-done.18.refs_2_ = bf16[128,1280]{1,0:T(8,128)(2,1)S(1)} collective-permute-done((bf16[128,1280]{1,0:T(8,128)(2,1)S(1)}, bf16[128,1280]{1,0:T(8,128)(2,1)S(1)}, u32[]{:S(2)}, u32[]{:S(2)}) %collective-permute-start.18) | collective-permute-done | bytes 327712 | tf_op jit(solution)/shard_map/ppermute | solution.py:448
  90.3 7.0 %collective-permute-done.17.refs_9_ = bf16[640,640]{1,0:T(8,128)(2,1)S(1)} collective-permute-done((bf16[640,640]{1,0:T(8,128)(2,1)S(1)}, bf16[640,640]{1,0:T(8,128)(2,1)S(1)}, u32[]{:S(2)}, u32[]{:S(2)}) %collective-permute-start.17) | collective-permute-done | bytes 819232 | tf_op jit(solution)/shard_map/ppermute | solution.py:448
  101.3 7.8 %collective-permute-done.21.p1 = bf16[128,1280]{1,0:T(8,128)(2,1)S(1)} collective-permute-done((bf16[128,1280]{1,0:T(8,128)(2,1)S(1)}, bf16[128,1280]{1,0:T(8,128)(2,1)S(1)}, u32[]{:S(2)}, u32[]{:S(2)}) %collective-permute-start.21) | collective-permute-done | bytes 327712 | tf_op jit(solution)/shard_map/ppermute | solution.py:448
  109.1 4.7 %grad_act.1 = (f32[512,320]{1,0:T(8,128)S(1)}, bf16[512,1280]{1,0:T(8,128)(2,1)S(1)}, bf16[1280,320]{1,0:T(8,128)(2,1)S(1)}, bf16[1280,320]{1,0:T(8,128)(2,1)S(1)}) custom-call(s32[4]{0:T(128)S(1)} %pad_add_fusion.refs_0_.s, bf16[128,1280]{1,0:T(8,128)(2,1)S(1)} %get-tuple-element.228.refs_1_.grad, bf16[128,1280]{1,0:T(8,128)(2,1)S(1)} %collective-permute-done.18.refs_2_, ...), custom_call_target="tpu_custom_call" | custom-call | flops 1000000 | bytes 6553600 | tf_op jit(solution)/shard_map/grad_act/pallas_call | solution.py:30
  120.7 2.9 %down.1 = (bf16[256,1280]{1,0:T(8,128)(2,1)S(1)}, f32[256,1280]{1,0:T(8,128)S(1)}, f32[1,320]{1,0:T(1,128)S(1)}, bf16[640,640]{1,0:T(8,128)(2,1)S(1)}, bf16[320,...) custom-call(s32[4]{0:T(128)S(1)} %pad_add_fusion.refs_0_.s, bf16[512,1280]{1,0:T(8,128)(2,1)S(1)} %get-tuple-element.239.refs_1_, ...), custom_call_target="tpu_custom_call" | custom-call | flops 1000000 | bytes 7701760 | tf_op jit(solution)/shard_map/down/pallas_call | solution.py:30
  123.6 5.6 %collective-permute-done.25.got = bf16[128,1280]{1,0:T(8,128)(2,1)S(1)} collective-permute-done((bf16[128,1280]{1,0:T(8,128)(2,1)S(1)}, bf16[128,1280]{1,0:T(8,128)(2,1)S(1)}, u32[]{:S(2)}, u32[]{:S(2)}) %collective-permute-start.25) | collective-permute-done | bytes 327712 | tf_op jit(solution)/shard_map/ppermute | solution.py:448
  131.7 7.7 %collective-permute-done.26.refs_2_ = bf16[128,1280]{1,0:T(8,128)(2,1)S(1)} collective-permute-done((bf16[128,1280]{1,0:T(8,128)(2,1)S(1)}, bf16[128,1280]{1,0:T(8,128)(2,1)S(1)}, u32[]{:S(2)}, u32[]{:S(2)}) %collective-permute-start.26) | collective-permute-done | bytes 327712 | tf_op jit(solution)/shard_map/ppermute | solution.py:448
  141.7 10.0 %collective-permute-done.30.refs_2_ = bf16[320,640]{1,0:T(8,128)(2,1)S(1)} collective-permute-done((bf16[320,640]{1,0:T(8,128)(2,1)S(1)}, bf16[320,640]{1,0:T(8,128)(2,1)S(1)}, u32[]{:S(2)}, u32[]{:S(2)}) %collective-permute-start.30) | collective-permute-done | bytes 409632 | tf_op jit(solution)/shard_map/ppermute | solution.py:448
  151.7 4.3 %grad_context.1 = (bf16[512,320]{1,0:T(8,128)(2,1)S(1)}, bf16[512,320]{1,0:T(8,128)(2,1)S(1)}, bf16[512,1280]{1,0:T(8,128)(2,1)}, bf16[640,640]{1,0:T(8,128)(2,1...) custom-call(s32[4]{0:T(128)S(1)} %pad_add_fusion.refs_0_.s, ...), custom_call_target="tpu_custom_call" | custom-call | flops 1000000 | bytes 9469952 | tf_op jit(solution)/shard_map/grad_context/pallas_call | solution.py:30
  160.9 3.9 %collective-permute-start.35 = (bf16[160,640]{1,0:T(8,128)(2,1)S(1)}, bf16[160,640]{1,0:T(8,128)(2,1)S(1)}, u32[]{:S(2)}, u32[]{:S(2)}) collective-permute-start(bf16[160,640]{1,0:T(8,128)(2,1)S(1)} %get-tuple-element.289), channel_id=1, source_target_pairs={{0,16},{1,17},{2,18},{3,19},{4,20},{5,21},{6,22},{7,23},{8,24},{9,... | collective-permute-start | bytes 614408 | tf_op jit(solution)/shard_map/ppermute | solution.py:448
  169.2 4.8 %collective-permute-start.37 = (bf16[160,640]{1,0:T(8,128)(2,1)S(1)}, bf16[160,640]{1,0:T(8,128)(2,1)S(1)}, u32[]{:S(2)}, u32[]{:S(2)}) collective-permute-start(bf16[160,640]{1,0:T(8,128)(2,1)S(1)} %get-tuple-element.291), channel_id=1, source_target_pairs={{0,24},{1,25},{2,26},{3,27},{4,28},{5,29},{6,30},{7,31},{8,0},{9,1... | collective-permute-start | bytes 614408 | tf_op jit(solution)/shard_map/ppermute | solution.py:448
  174.0 9.8 %grad_scores.1 = (bf16[512,640]{1,0:T(8,128)(2,1)S(1)}, f32[8,320]{1,0:T(8,128)S(1)}) custom-call(s32[4]{0:T(128)S(1)} %pad_add_fusion.refs_0_.s, bf16[4,512,512]{2,1,0:T(8,128)(2,1)S(1)} %get-tuple-element.207.refs_2_.refs_6_.refs_1_, bf16[512,320]{1,0:T(8,128)(2,1)S(1)} %get-tuple-element.277.refs_2_, bf16[512,320]{1,0:T(8,128)(2,1)S(1)} %get-tuple-element.278.refs_3_, ...), custom_call_target="tpu_custom_call" | custom-call | flops 1000000 | bytes 4739072 | tf_op jit(solution)/shard_map/grad_scores/pallas_call | solution.py:30
  183.8 3.9 %grad_first.1 = (bf16[256,1280]{1,0:T(8,128)(2,1)S(1)}, f32[256,1280]{1,0:T(8,128)S(1)}, f32[8,1280]{1,0:T(8,128)S(1)}, bf16[640,640]{1,0:T(8,128)(2,1)S(1)}, bf...) custom-call(s32[4]{0:T(128)S(1)} %pad_add_fusion.refs_0_.s, bf16[512,640]{1,0:T(8,128)(2,1)S(1)} %get-tuple-element.292.refs_1_, ...), custom_call_target="tpu_custom_call" | custom-call | flops 1000000 | bytes 8449600 | tf_op jit(solution)/shard_map/grad_first/pallas_call | solution.py:30
  194.9 6.7 %collective-permute-done.39.two = f32[8,1280]{1,0:T(8,128)S(1)} collective-permute-done((f32[8,1280]{1,0:T(8,128)S(1)}, f32[8,1280]{1,0:T(8,128)S(1)}, u32[]{:S(2)}, u32[]{:S(2)}) %collective-permute-start.39) | collective-permute-done | bytes 40992 | tf_op jit(solution)/shard_map/ppermute | solution.py:448
  202.9 4.2 %collective-permute-done.40.two = f32[8,1280]{1,0:T(8,128)S(1)} collective-permute-done((f32[8,1280]{1,0:T(8,128)S(1)}, f32[8,1280]{1,0:T(8,128)S(1)}, u32[]{:S(2)}, u32[]{:S(2)}) %collective-permute-start.40) | collective-permute-done | bytes 40992 | tf_op jit(solution)/shard_map/ppermute | solution.py:448
  207.1 3.8 %collective-permute-start.46 = (bf16[160,640]{1,0:T(8,128)(2,1)S(1)}, bf16[160,640]{1,0:T(8,128)(2,1)S(1)}, u32[]{:S(2)}, u32[]{:S(2)}) collective-permute-start(bf16[160,640]{1,0:T(8,128)(2,1)S(1)} %get-tuple-element.311), channel_id=1, source_target_pairs={{0,24},{1,25},{2,26},{3,27},{4,28},{5,29},{6,30},{7,31},{8,0},{9,1... | collective-permute-start | bytes 614408 | tf_op jit(solution)/shard_map/ppermute | solution.py:448
  211.5 5.4 %collective-permute-done.45.refs_3_ = bf16[160,640]{1,0:T(8,128)(2,1)S(1)} collective-permute-done((bf16[160,640]{1,0:T(8,128)(2,1)S(1)}, bf16[160,640]{1,0:T(8,128)(2,1)S(1)}, u32[]{:S(2)}, u32[]{:S(2)}) %collective-permute-start.45) | collective-permute-done | bytes 204832 | tf_op jit(solution)/shard_map/ppermute | solution.py:448
  222.0 2.5 %collective-permute-done.47.two = f32[8,1280]{1,0:T(8,128)S(1)} collective-permute-done((f32[8,1280]{1,0:T(8,128)S(1)}, f32[8,1280]{1,0:T(8,128)S(1)}, u32[]{:S(2)}, u32[]{:S(2)}) %collective-permute-start.47) | collective-permute-done | bytes 40992 | tf_op jit(solution)/shard_map/ppermute | solution.py:448
  233.5 3.6 %collective-permute-start.51 = (bf16[160,640]{1,0:T(8,128)(2,1)S(1)}, bf16[160,640]{1,0:T(8,128)(2,1)S(1)}, u32[]{:S(2)}, u32[]{:S(2)}) collective-permute-start(bf16[160,640]{1,0:T(8,128)(2,1)S(1)} %get-tuple-element.328), channel_id=1, source_target_pairs={{0,24},{1,25},{2,26},{3,27},{4,28},{5,29},{6,30},{7,31},{8,0},{9,1... | collective-permute-start | bytes 614408 | tf_op jit(solution)/shard_map/ppermute | solution.py:448
  238.8 5.6 %collective-permute-done.49.refs_2_ = bf16[160,640]{1,0:T(8,128)(2,1)S(1)} collective-permute-done((bf16[160,640]{1,0:T(8,128)(2,1)S(1)}, bf16[160,640]{1,0:T(8,128)(2,1)S(1)}, u32[]{:S(2)}, u32[]{:S(2)}) %collective-permute-start.49) | collective-permute-done | bytes 204832 | tf_op jit(solution)/shard_map/ppermute | solution.py:448
  (117 shorter events, 74.3 us)
Async XLA Ops:
  3.0 15.6 %collective-permute-start.3 = (bf16[160,640]{1,0:T(8,128)(2,1)S(1)}, bf16[160,640]{1,0:T(8,128)(2,1)S(1)}, u32[]{:S(2)}, u32[]{:S(2)}) collective-permute-start(bf16[160,640]{1,0:T(8,128)(2,1)S(1)} %pack_qk.1.refs_6_), channel_id=1, source_target_pairs={{0,4},{1,5},{2,6},{3,7},{4,0},{5,1},{6,2},{7,3},{8,12},{9,13},{10,... | collective-permute-start | bytes 614408 | tf_op jit(solution)/shard_map/ppermute | solution.py:448
  6.0 12.6 %collective-permute-start.2 = (bf16[160,640]{1,0:T(8,128)(2,1)S(1)}, bf16[160,640]{1,0:T(8,128)(2,1)S(1)}, u32[]{:S(2)}, u32[]{:S(2)}) collective-permute-start(bf16[160,640]{1,0:T(8,128)(2,1)S(1)} %pack_qk.1.refs_6_), channel_id=1, source_target_pairs={{0,8},{1,9},{2,10},{3,11},{4,12},{5,13},{6,14},{7,15},{8,16},{9,17... | collective-permute-start | bytes 614408 | tf_op jit(solution)/shard_map/ppermute | solution.py:448
  7.6 15.7 %collective-permute-start.1 = (bf16[160,640]{1,0:T(8,128)(2,1)S(1)}, bf16[160,640]{1,0:T(8,128)(2,1)S(1)}, u32[]{:S(2)}, u32[]{:S(2)}) collective-permute-start(bf16[160,640]{1,0:T(8,128)(2,1)S(1)} %pack_qk.1.refs_6_), channel_id=1, source_target_pairs={{0,16},{1,17},{2,18},{3,19},{4,20},{5,21},{6,22},{7,23},{8,24},{9,... | collective-permute-start | bytes 614408 | tf_op jit(solution)/shard_map/ppermute | solution.py:448
  10.2 13.1 %collective-permute-start = (bf16[160,640]{1,0:T(8,128)(2,1)S(1)}, bf16[160,640]{1,0:T(8,128)(2,1)S(1)}, u32[]{:S(2)}, u32[]{:S(2)}) collective-permute-start(bf16[160,640]{1,0:T(8,128)(2,1)S(1)} %pack_qk.1.refs_6_), channel_id=1, source_target_pairs={{0,24},{1,25},{2,26},{3,27},{4,28},{5,29},{6,30},{7,31},{8,0},{9,1... | collective-permute-start | bytes 614408 | tf_op jit(solution)/shard_map/ppermute | solution.py:448
  25.4 21.7 %collective-permute-start.10 = (bf16[480,640]{1,0:T(8,128)(2,1)S(1)}, bf16[480,640]{1,0:T(8,128)(2,1)S(1)}, u32[]{:S(2)}, u32[]{:S(2)}) collective-permute-start(bf16[480,640]{1,0:T(8,128)(2,1)S(1)} %stack.19), channel_id=1, source_target_pairs={{0,4},{1,5},{2,6},{3,7},{4,0},{5,1},{6,2},{7,3},{8,12},{9,13},{10,... | collective-permute-start | bytes 1843208 | tf_op jit(solution)/shard_map/ppermute | solution.py:448
  30.8 16.3 %collective-permute-start.5 = (bf16[128,1280]{1,0:T(8,128)(2,1)S(1)}, bf16[128,1280]{1,0:T(8,128)(2,1)S(1)}, u32[]{:S(2)}, u32[]{:S(2)}) collective-permute-start(bf16[128,1280]{1,0:T(8,128)(2,1)S(1)} %get-tuple-element.189.refs_1_), channel_id=1, source_target_pairs={{0,1},{1,0},{2,3},{3,2},{4,5},{5,4},{6,7},{7,6},{8,9},{9,8},{10,11... | collective-permute-start | bytes 983048 | tf_op jit(solution)/shard_map/ppermute | solution.py:448
  32.8 14.3 %collective-permute-start.6 = (bf16[128,1280]{1,0:T(8,128)(2,1)S(1)}, bf16[128,1280]{1,0:T(8,128)(2,1)S(1)}, u32[]{:S(2)}, u32[]{:S(2)}) collective-permute-start(bf16[128,1280]{1,0:T(8,128)(2,1)S(1)} %collective-permute-done.4.refs_2_), channel_id=1, source_target_pairs={{0,1},{1,0},{2,3},{3,2},{4,5},{5,4},{6,7},{7,6},{8,9},{9,8},{10,11... | collective-permute-start | bytes 983048 | tf_op jit(solution)/shard_map/ppermute | solution.py:448
  32.8 14.3 %collective-permute-start.8 = (bf16[160,640]{1,0:T(8,128)(2,1)S(1)}, bf16[160,640]{1,0:T(8,128)(2,1)S(1)}, u32[]{:S(2)}, u32[]{:S(2)}) collective-permute-start(bf16[160,640]{1,0:T(8,128)(2,1)S(1)} %pack_vo.1.refs_0_.refs_4_), channel_id=1, source_target_pairs={{0,16},{1,17},{2,18},{3,19},{4,20},{5,21},{6,22},{7,23},{8,24},{9,... | collective-permute-start | bytes 614408 | tf_op jit(solution)/shard_map/ppermute | solution.py:448
  47.7 21.9 %collective-permute-start.11 = (bf16[640,640]{1,0:T(8,128)(2,1)S(1)}, bf16[640,640]{1,0:T(8,128)(2,1)S(1)}, u32[]{:S(2)}, u32[]{:S(2)}) collective-permute-start(bf16[640,640]{1,0:T(8,128)(2,1)S(1)} %stack.20), channel_id=1, source_target_pairs={{0,4},{1,5},{2,6},{3,7},{4,0},{5,1},{6,2},{7,3},{8,12},{9,13},{10,... | collective-permute-start | bytes 2457608 | tf_op jit(solution)/shard_map/ppermute | solution.py:448
  48.3 18.8 %collective-permute-start.14 = (bf16[160,640]{1,0:T(8,128)(2,1)S(1)}, bf16[160,640]{1,0:T(8,128)(2,1)S(1)}, u32[]{:S(2)}, u32[]{:S(2)}) collective-permute-start(bf16[160,640]{1,0:T(8,128)(2,1)S(1)} %pack_hd.1.refs_0_.refs_5_), channel_id=1, source_target_pairs={{0,8},{1,9},{2,10},{3,11},{4,12},{5,13},{6,14},{7,15},{8,16},{9,17... | collective-permute-start | bytes 614408 | tf_op jit(solution)/shard_map/ppermute | solution.py:448
  53.1 16.5 %collective-permute-start.13 = (bf16[160,640]{1,0:T(8,128)(2,1)S(1)}, bf16[160,640]{1,0:T(8,128)(2,1)S(1)}, u32[]{:S(2)}, u32[]{:S(2)}) collective-permute-start(bf16[160,640]{1,0:T(8,128)(2,1)S(1)} %pack_hd.1.refs_0_.refs_5_), channel_id=1, source_target_pairs={{0,16},{1,17},{2,18},{3,19},{4,20},{5,21},{6,22},{7,23},{8,24},{9,... | collective-permute-start | bytes 614408 | tf_op jit(solution)/shard_map/ppermute | solution.py:448
  56.5 13.1 %collective-permute-start.12 = (bf16[160,640]{1,0:T(8,128)(2,1)S(1)}, bf16[160,640]{1,0:T(8,128)(2,1)S(1)}, u32[]{:S(2)}, u32[]{:S(2)}) collective-permute-start(bf16[160,640]{1,0:T(8,128)(2,1)S(1)} %pack_hd.1.refs_0_.refs_5_), channel_id=1, source_target_pairs={{0,24},{1,25},{2,26},{3,27},{4,28},{5,29},{6,30},{7,31},{8,0},{9,1... | collective-permute-start | bytes 614408 | tf_op jit(solution)/shard_map/ppermute | solution.py:448
  75.9 12.1 %collective-permute-start.15 = (bf16[256,1280]{1,0:T(8,128)(2,1)S(1)}, bf16[256,1280]{1,0:T(8,128)(2,1)S(1)}, u32[]{:S(2)}, u32[]{:S(2)}) collective-permute-start(bf16[256,1280]{1,0:T(8,128)(2,1)S(1)} %get-tuple-element.214), channel_id=1, source_target_pairs={{0,1},{1,0},{2,3},{3,2},{4,5},{5,4},{6,7},{7,6},{8,9},{9,8},{10,11... | collective-permute-start | bytes 1966088 | tf_op jit(solution)/shard_map/ppermute | solution.py:448
  76.6 20.7 %collective-permute-start.17 = (bf16[640,640]{1,0:T(8,128)(2,1)S(1)}, bf16[640,640]{1,0:T(8,128)(2,1)S(1)}, u32[]{:S(2)}, u32[]{:S(2)}) collective-permute-start(bf16[640,640]{1,0:T(8,128)(2,1)S(1)} %stack.21), channel_id=1, source_target_pairs={{0,4},{1,5},{2,6},{3,7},{4,0},{5,1},{6,2},{7,3},{8,12},{9,13},{10,... | collective-permute-start | bytes 2457608 | tf_op jit(solution)/shard_map/ppermute | solution.py:448
  101.3 12.5 %collective-permute-start.22 = (bf16[128,1280]{1,0:T(8,128)(2,1)S(1)}, bf16[128,1280]{1,0:T(8,128)(2,1)S(1)}, u32[]{:S(2)}, u32[]{:S(2)}) collective-permute-start(bf16[128,1280]{1,0:T(8,128)(2,1)S(1)} %get-tuple-element.227.p0), channel_id=1, source_target_pairs={{0,1},{1,0},{2,3},{3,2},{4,5},{5,4},{6,7},{7,6},{8,9},{9,8},{10,11... | collective-permute-start | bytes 983048 | tf_op jit(solution)/shard_map/ppermute | solution.py:448
  139.4 12.3 %collective-permute-start.30 = (bf16[320,640]{1,0:T(8,128)(2,1)S(1)}, bf16[320,640]{1,0:T(8,128)(2,1)S(1)}, u32[]{:S(2)}, u32[]{:S(2)}) collective-permute-start(bf16[320,640]{1,0:T(8,128)(2,1)S(1)} %get-tuple-element.264), channel_id=1, source_target_pairs={{0,4},{1,5},{2,6},{3,7},{4,0},{5,1},{6,2},{7,3},{8,12},{9,13},{10,... | collective-permute-start | bytes 1228808 | tf_op jit(solution)/shard_map/ppermute | solution.py:448
  141.0 17.0 %collective-permute-start.29 = (bf16[256,1280]{1,0:T(8,128)(2,1)S(1)}, bf16[256,1280]{1,0:T(8,128)(2,1)S(1)}, u32[]{:S(2)}, u32[]{:S(2)}) collective-permute-start(bf16[256,1280]{1,0:T(8,128)(2,1)S(1)} %get-tuple-element.258), channel_id=1, source_target_pairs={{0,1},{1,0},{2,3},{3,2},{4,5},{5,4},{6,7},{7,6},{8,9},{9,8},{10,11... | collective-permute-start | bytes 1966088 | tf_op jit(solution)/shard_map/ppermute | solution.py:448
  141.2 23.6 %collective-permute-start.31 = (bf16[320,640]{1,0:T(8,128)(2,1)S(1)}, bf16[320,640]{1,0:T(8,128)(2,1)S(1)}, u32[]{:S(2)}, u32[]{:S(2)}) collective-permute-start(bf16[320,640]{1,0:T(8,128)(2,1)S(1)} %get-tuple-element.272), channel_id=1, source_target_pairs={{0,4},{1,5},{2,6},{3,7},{4,0},{5,1},{6,2},{7,3},{8,12},{9,13},{10,... | collective-permute-start | bytes 1228808 | tf_op jit(solution)/shard_map/ppermute | solution.py:448
  155.9 13.3 %collective-permute-start.32 = (bf16[320,640]{1,0:T(8,128)(2,1)S(1)}, bf16[320,640]{1,0:T(8,128)(2,1)S(1)}, u32[]{:S(2)}, u32[]{:S(2)}) collective-permute-start(bf16[320,640]{1,0:T(8,128)(2,1)S(1)} %get-tuple-element.283), channel_id=1, source_target_pairs={{0,4},{1,5},{2,6},{3,7},{4,0},{5,1},{6,2},{7,3},{8,12},{9,13},{10,... | collective-permute-start | bytes 1228808 | tf_op jit(solution)/shard_map/ppermute | solution.py:448
  156.5 27.3 %collective-permute-start.33 = (bf16[320,640]{1,0:T(8,128)(2,1)S(1)}, bf16[320,640]{1,0:T(8,128)(2,1)S(1)}, u32[]{:S(2)}, u32[]{:S(2)}) collective-permute-start(bf16[320,640]{1,0:T(8,128)(2,1)S(1)} %get-tuple-element.284), channel_id=1, source_target_pairs={{0,4},{1,5},{2,6},{3,7},{4,0},{5,1},{6,2},{7,3},{8,12},{9,13},{10,... | collective-permute-start | bytes 1228808 | tf_op jit(solution)/shard_map/ppermute | solution.py:448
  158.7 25.1 %collective-permute-start.34 = (bf16[128,1280]{1,0:T(8,128)(2,1)S(1)}, bf16[128,1280]{1,0:T(8,128)(2,1)S(1)}, u32[]{:S(2)}, u32[]{:S(2)}) collective-permute-start(bf16[128,1280]{1,0:T(8,128)(2,1)S(1)} %get-tuple-element.285), channel_id=1, source_target_pairs={{0,2},{1,3},{2,0},{3,1},{4,6},{5,7},{6,4},{7,5},{8,10},{9,11},{10,... | collective-permute-start | bytes 983048 | tf_op jit(solution)/shard_map/ppermute | solution.py:448
  160.9 22.9 %collective-permute-start.35 = (bf16[160,640]{1,0:T(8,128)(2,1)S(1)}, bf16[160,640]{1,0:T(8,128)(2,1)S(1)}, u32[]{:S(2)}, u32[]{:S(2)}) collective-permute-start(bf16[160,640]{1,0:T(8,128)(2,1)S(1)} %get-tuple-element.289), channel_id=1, source_target_pairs={{0,16},{1,17},{2,18},{3,19},{4,20},{5,21},{6,22},{7,23},{8,24},{9,... | collective-permute-start | bytes 614408 | tf_op jit(solution)/shard_map/ppermute | solution.py:448
  164.8 19.0 %collective-permute-start.36 = (bf16[160,640]{1,0:T(8,128)(2,1)S(1)}, bf16[160,640]{1,0:T(8,128)(2,1)S(1)}, u32[]{:S(2)}, u32[]{:S(2)}) collective-permute-start(bf16[160,640]{1,0:T(8,128)(2,1)S(1)} %get-tuple-element.290), channel_id=1, source_target_pairs={{0,8},{1,9},{2,10},{3,11},{4,12},{5,13},{6,14},{7,15},{8,16},{9,17... | collective-permute-start | bytes 614408 | tf_op jit(solution)/shard_map/ppermute | solution.py:448
  169.2 14.6 %collective-permute-start.37 = (bf16[160,640]{1,0:T(8,128)(2,1)S(1)}, bf16[160,640]{1,0:T(8,128)(2,1)S(1)}, u32[]{:S(2)}, u32[]{:S(2)}) collective-permute-start(bf16[160,640]{1,0:T(8,128)(2,1)S(1)} %get-tuple-element.291), channel_id=1, source_target_pairs={{0,24},{1,25},{2,26},{3,27},{4,28},{5,29},{6,30},{7,31},{8,0},{9,1... | collective-permute-start | bytes 614408 | tf_op jit(solution)/shard_map/ppermute | solution.py:448
  188.4 18.7 %collective-permute-start.44 = (bf16[160,640]{1,0:T(8,128)(2,1)S(1)}, bf16[160,640]{1,0:T(8,128)(2,1)S(1)}, u32[]{:S(2)}, u32[]{:S(2)}) collective-permute-start(bf16[160,640]{1,0:T(8,128)(2,1)S(1)} %get-tuple-element.308), channel_id=1, source_target_pairs={{0,16},{1,17},{2,18},{3,19},{4,20},{5,21},{6,22},{7,23},{8,24},{9,... | collective-permute-start | bytes 614408 | tf_op jit(solution)/shard_map/ppermute | solution.py:448
  190.0 27.8 %collective-permute-start.43 = (bf16[320,640]{1,0:T(8,128)(2,1)S(1)}, bf16[320,640]{1,0:T(8,128)(2,1)S(1)}, u32[]{:S(2)}, u32[]{:S(2)}) collective-permute-start(bf16[320,640]{1,0:T(8,128)(2,1)S(1)} %get-tuple-element.305), channel_id=1, source_target_pairs={{0,4},{1,5},{2,6},{3,7},{4,0},{5,1},{6,2},{7,3},{8,12},{9,13},{10,... | collective-permute-start | bytes 1228808 | tf_op jit(solution)/shard_map/ppermute | solution.py:448
  190.5 34.5 %collective-permute-start.48 = (bf16[320,640]{1,0:T(8,128)(2,1)S(1)}, bf16[320,640]{1,0:T(8,128)(2,1)S(1)}, u32[]{:S(2)}, u32[]{:S(2)}) collective-permute-start(bf16[320,640]{1,0:T(8,128)(2,1)S(1)} %get-tuple-element.321), channel_id=1, source_target_pairs={{0,4},{1,5},{2,6},{3,7},{4,0},{5,1},{6,2},{7,3},{8,12},{9,13},{10,... | collective-permute-start | bytes 1228808 | tf_op jit(solution)/shard_map/ppermute | solution.py:448
  192.7 25.1 %collective-permute-start.42 = (bf16[128,1280]{1,0:T(8,128)(2,1)S(1)}, bf16[128,1280]{1,0:T(8,128)(2,1)S(1)}, u32[]{:S(2)}, u32[]{:S(2)}) collective-permute-start(bf16[128,1280]{1,0:T(8,128)(2,1)S(1)} %get-tuple-element.304), channel_id=1, source_target_pairs={{0,2},{1,3},{2,0},{3,1},{4,6},{5,7},{6,4},{7,5},{8,10},{9,11},{10,... | collective-permute-start | bytes 983048 | tf_op jit(solution)/shard_map/ppermute | solution.py:448
  225.7 11.3 %collective-permute-start.52 = (f32[8,1280]{1,0:T(8,128)S(1)}, f32[8,1280]{1,0:T(8,128)S(1)}, u32[]{:S(2)}, u32[]{:S(2)}) collective-permute-start(f32[8,1280]{1,0:T(8,128)S(1)} %add.32.one), channel_id=1, source_target_pairs={{0,4},{1,5},{2,6},{3,7},{4,0},{5,1},{6,2},{7,3},{8,12},{9,13},{10,... | collective-permute-start | bytes 122888 | tf_op jit(solution)/shard_map/ppermute | solution.py:448
  229.4 15.0 %collective-permute-start.49 = (bf16[160,640]{1,0:T(8,128)(2,1)S(1)}, bf16[160,640]{1,0:T(8,128)(2,1)S(1)}, u32[]{:S(2)}, u32[]{:S(2)}) collective-permute-start(bf16[160,640]{1,0:T(8,128)(2,1)S(1)} %get-tuple-element.324), channel_id=1, source_target_pairs={{0,16},{1,17},{2,18},{3,19},{4,20},{5,21},{6,22},{7,23},{8,24},{9,... | collective-permute-start | bytes 614408 | tf_op jit(solution)/shard_map/ppermute | solution.py:448
  231.8 12.6 %collective-permute-start.50 = (bf16[160,640]{1,0:T(8,128)(2,1)S(1)}, bf16[160,640]{1,0:T(8,128)(2,1)S(1)}, u32[]{:S(2)}, u32[]{:S(2)}) collective-permute-start(bf16[160,640]{1,0:T(8,128)(2,1)S(1)} %get-tuple-element.325), channel_id=1, source_target_pairs={{0,8},{1,9},{2,10},{3,11},{4,12},{5,13},{6,14},{7,15},{8,16},{9,17... | collective-permute-start | bytes 614408 | tf_op jit(solution)/shard_map/ppermute | solution.py:448
  233.5 11.3 %collective-permute-start.51 = (bf16[160,640]{1,0:T(8,128)(2,1)S(1)}, bf16[160,640]{1,0:T(8,128)(2,1)S(1)}, u32[]{:S(2)}, u32[]{:S(2)}) collective-permute-start(bf16[160,640]{1,0:T(8,128)(2,1)S(1)} %get-tuple-element.328), channel_id=1, source_target_pairs={{0,24},{1,25},{2,26},{3,27},{4,28},{5,29},{6,30},{7,31},{8,0},{9,1... | collective-permute-start | bytes 614408 | tf_op jit(solution)/shard_map/ppermute | solution.py:448
  (21 other events, 151.8 us)
where the time goes:
time: 247 us; the launch traced here: 246 us
  waiting for transfers between devices  95 us (38%)
  starting transfers between devices  73.9 us (30%)
  Pallas kernels  73.4 us (30%)
    ppermute x53, waiting for transfers between devices, move(): return lax.ppermute(value, AXES, pairs)  95 us
    ppermute x53, starting transfers between devices, move(): return lax.ppermute(value, AXES, pairs)  73.9 us
    pallas_call x37, Pallas kernels, call(): pl.pallas_call(kernel, name=name, out_shape=outs, in_specs=[pl.BlockSpec(...  73.4 us
  transfers between devices with their start and end apart: 53, of which 21 were waited for; matrix products, arithmetic and copies ran while one was open for 1% of the time, Pallas kernels for 22%

commit v1 on v0

--- a/solution.py
+++ b/solution.py
@@ -56,35 +56,17 @@
     return first, second
 
 
-def to_own(value, ring, pair, n_dp):
+def reorder(value, place, n_dp):
     width = value.shape[1]
-    depth = width // n_dp
-    value = swap_pairs(value, pair, depth)
+    lane = lax.broadcasted_iota(jnp.int32, (1, width), 1)
+    span = width // n_dp
     bit = 1
-    while bit < n_dp // 2:
-        moved = pltpu.roll(value, width - bit * 2 * depth, 1)
-        value = jnp.where((ring & bit) != 0, moved, value)
-        bit *= 2
+    while bit < n_dp:
+        low = lax.rem(lane, 2 * span) < span
+        other = jnp.where(low, pltpu.roll(value, width - span, 1), pltpu.roll(value, span, 1))
+        value = jnp.where((place & bit) != 0, other, value)
+        bit, span = 2 * bit, 2 * span
     return value
-
-
-def from_own(value, ring, pair, n_dp):
-    width = value.shape[1]
-    depth = width // n_dp
-    bit = 1
-    while bit < n_dp // 2:
-        moved = pltpu.roll(value, bit * 2 * depth, 1)
-        value = jnp.where((ring & bit) != 0, moved, value)
-        bit *= 2
-    return swap_pairs(value, pair, depth)
-
-
-def swap_pairs(value, pair, depth):
-    width = value.shape[1]
-    lane = lax.broadcasted_iota(jnp.int32, value.shape, 1)
-    low = lax.rem(lane, 2 * depth) < depth
-    other = jnp.where(low, pltpu.roll(value, width - depth, 1), pltpu.roll(value, depth, 1))
-    return jnp.where(pair != 0, other, value)
 
 
 def row_mean(value):
@@ -122,22 +104,22 @@
     sources, (h, x_own, grad, vectors, biases) = refs[:9], refs[9:14]
     x, cotangent, *given = refs[14:23]
     load(sources, refs[14:23], refs[23])
-    ring, pair, place, length = s[0], s[1], s[2], s[3]
-    value = to_own(x[...].astype(F32), ring, pair, n_dp)
+    mine, place, length = s[0], s[1], s[2]
+    value = reorder(x[...].astype(F32), mine, n_dp)
     stacked = jnp.concatenate([row_of(given[k]) for k in (0, 1, 2, 3, 4, 5, 6, 6)], axis=0)
     width = biases.shape[1]
-    mine = stacked[:, :width]
+    slices = stacked[:, :width]
     for number in range(1, stacked.shape[1] // width):
-        mine = jnp.where(place == number, stacked[:, number * width : (number + 1) * width], mine)
-    biases[...] = mine
+        slices = jnp.where(place == number, stacked[:, number * width : (number + 1) * width], slices)
+    biases[...] = slices
     biases[7:8] = scale[...]
-    stacked = to_own(stacked, ring, pair, n_dp)
+    stacked = reorder(stacked, mine, n_dp)
     normed, _ = normalize(value)
     h[...] = (normed * stacked[0:1]).astype(BF16)
     x_own[...] = value.astype(BF16)
     rows = value.shape[0]
     row = lax.broadcasted_iota(jnp.int32, value.shape, 0) + place * rows
-    g = jnp.where(row < length, to_own(cotangent[...].astype(F32), ring, pair, n_dp), 0.0)
+    g = jnp.where(row < length, reorder(cotangent[...].astype(F32), mine, n_dp), 0.0)
     grad[...] = g.astype(BF16)
     vectors[...] = stacked
     vectors[4:5] = jnp.sum(g, axis=0, keepdims=True)
@@ -165,24 +147,18 @@
     return ((place ^ turned) << shift) + (row & (local - 1))
 
 
-def fetch(blocks, out, sem):
-    depth = blocks[0].shape[0]
-    n_ring = out.shape[0] // (2 * depth)
+def fetch(even, odd, out, depth, sem):
     copies = []
-
-    def copy(source, row):
-        copies.append(pltpu.make_async_copy(source, out.at[pl.ds(row, depth)], sem.at[len(copies)]))
-
-    if n_ring == 0:
-        copy(blocks[0], 0)
+    if not odd:
+        copies.append(pltpu.make_async_copy(even[0], out, sem.at[0]))
     else:
-        for j in range(n_ring):
-            copy(blocks[j], 2 * j * depth)
-        j = 0
-        for block in blocks[n_ring:]:
-            for k in range(block.shape[0] // depth):
-                copy(block.at[pl.ds(k * depth, depth)], (2 * j + 1) * depth)
-                j += 1
+        for start, blocks in enumerate((even, odd)):
+            row = start * depth
+            for block in blocks:
+                for k in range(block.shape[0] // depth):
+                    source, target = block.at[pl.ds(k * depth, depth)], out.at[pl.ds(row, depth)]
+                    copies.append(pltpu.make_async_copy(source, target, sem.at[len(copies)]))
+                    row += 2 * depth
     for one in copies:
         one.start()
     return copies
@@ -197,9 +173,10 @@
     return jnp.where(lanes == number, value, jnp.zeros((), value.dtype))
 
 
-def attend_kernel(n_blocks, head_size, s, p0, p1, p2, p3, biases, *refs):
-    blocks, (q_raw, q_low, k_low, h, weight, turned, sem) = refs[:n_blocks], refs[n_blocks:]
-    copies = fetch(blocks, weight, sem)
+def attend_kernel(counts, depth, head_size, s, p0, p1, p2, p3, biases, *refs):
+    even, odd = refs[: counts[0]], refs[counts[0] : counts[1]]
+    q_raw, q_low, k_low, h, weight, turned, sem = refs[counts[1] :]
+    copies = fetch(even, odd, weight, depth, sem)
     join((p0, p1, p2, p3), h)
     for copy in copies:
         copy.wait()
@@ -208,24 +185,21 @@
     q_raw[...] = first
     q_low[...] = (first * biases[7:8]).astype(BF16)
     k_low[...] = second.astype(BF16)
-    place, length = s[2], s[3]
+    place, length = s[1], s[2]
     rows, local = q_low.shape[0], p0.shape[0]
     key_place = positions((rows, 1), 0, place, local)
+    last = jnp.minimum(positions((1, rows), 1, place, local), length - 1)
 
     def head(number, carry):
-        def part(at, m):
-            score = dot(k_low[...], of_head(q_low[at], number, head_size), NT)
-            query_place = positions((1, 128), 1, place, local, m * 128)
-            last = jnp.minimum(query_place, length - 1)
-            score = jnp.where(key_place <= last, score, -1e30)
-            raised = jnp.exp(score - jnp.max(score, axis=0, keepdims=True))
-            share = 1.0 / jnp.sum(raised, axis=0, keepdims=True)
-            turned[number, :, at] = (raised * share).astype(BF16)
-
-        tiles(rows, part)
+        score = dot(k_low[...], of_head(q_low[...], number, head_size), NT)
+        score = jnp.where(key_place <= last, score, -1e30)
+        raised = jnp.exp(score - jnp.max(score, axis=0, keepdims=True))
+        share = 1.0 / jnp.sum(raised, axis=0, keepdims=True)
+        turned[number] = (raised * share).astype(BF16)
         return carry
 
-    lax.fori_loop(0, turned.shape[0], head, 0)
+    for number in range(turned.shape[0]):
+        head(number, 0)
 
 
 def mixed_heads(turned, value, head_size, dims):
@@ -237,15 +211,13 @@
 
 
 def split_weight(weight, one, two):
-    def body(at, m):
-        one[at], two[at] = unpack(weight[at])
-
-    tiles(weight.shape[0], body)
-
-
-def context_kernel(head_size, n_blocks, s, h, turned, biases, *refs):
-    blocks, (v_low, context, far, near, w_value, w_output, weight, sem) = refs[:n_blocks], refs[n_blocks:]
-    for copy in fetch(blocks, weight, sem):
+    one[...], two[...] = unpack(weight[...])
+
+
+def context_kernel(counts, depth, head_size, s, h, turned, biases, *refs):
+    even, odd = refs[: counts[0]], refs[counts[0] : counts[1]]
+    v_low, context, far, near, w_value, w_output, weight, sem = refs[counts[1] :]
+    for copy in fetch(even, odd, weight, depth, sem):
         copy.wait()
     split_weight(weight, w_value, w_output)
     v_low[...] = (dot(h[...], w_value[...]) + biases[5:6]).astype(BF16)
@@ -280,9 +252,10 @@
     h[...] = (normed * vectors[1:2]).astype(BF16)
 
 
-def grad_act_kernel(n_blocks, s, p0, p1, p2, p3, *refs):
-    blocks, (grad_act, g, w_hidden, w_down, weight, sem) = refs[:n_blocks], refs[n_blocks:]
-    copies = fetch(blocks, weight, sem)
+def grad_act_kernel(counts, depth, s, p0, p1, p2, p3, *refs):
+    even, odd = refs[: counts[0]], refs[counts[0] : counts[1]]
+    grad_act, g, w_hidden, w_down, weight, sem = refs[counts[1] :]
+    copies = fetch(even, odd, weight, depth, sem)
     join((p0, p1, p2, p3), g)
     for copy in copies:
         copy.wait()
@@ -323,17 +296,22 @@
     split_product(act, w_down, far, near)
 
 
-def pair_kernel(start, s, own, got, *outs):
-    depth = outs[0].shape[0]
-    for k, out in enumerate(outs):
-        value = own[pl.ds((start + k) * depth, depth)].astype(F32) + got[pl.ds(k * depth, depth)].astype(F32)
+def pair_kernel(start, count, s, own, *refs):
+    gots, outs = refs[:count], refs[count:]
+    row = 0
+    for out in outs:
+        rows = out.shape[0]
+        value = own[pl.ds(start + row, rows)].astype(F32)
+        for got in gots:
+            value = value + got[pl.ds(row, rows)].astype(F32)
         out[...] = value.astype(out.dtype)
+        row += rows
 
 
 def owned_kernel(n_got, s, keep, *refs):
     total = keep[...]
     for got in refs[:n_got]:
-        total = total + got[...].astype(F32)
+        total = total + got[pl.ds(0, total.shape[0])].astype(F32)
     refs[n_got][...], refs[n_got + 1][...] = unpack(total)
 
 
@@ -364,19 +342,17 @@
     grad_k[...] = jnp.zeros_like(grad_k)
 
     def head(number, carry):
-        def part(at, m):
-            grad_chance = dot(v_low[...], of_head(grad_context[at], number, head_size), NT)
-            chance = turned[number, :, at].astype(F32)
-            product = chance * grad_chance
-            center = jnp.sum(product, axis=0, keepdims=True)
-            scores[:, at] = (product - chance * center).astype(BF16)
-
-        tiles(rows, part)
+        grad_chance = dot(v_low[...], of_head(grad_context[...], number, head_size), NT)
+        chance = turned[number].astype(F32)
+        product = chance * grad_chance
+        center = jnp.sum(product, axis=0, keepdims=True)
+        scores[...] = (product - chance * center).astype(BF16)
         grad_q[...] += dot(scores[...], of_head(k_low[...], number, head_size), TN)
         grad_k[...] += dot(scores[...], of_head(q_low[...], number, head_size))
         return carry
 
-    lax.fori_loop(0, turned.shape[0], head, 0)
+    for number in range(turned.shape[0]):
+        head(number, 0)
     low = grad_q[...].astype(BF16).astype(F32)
     sums[0:1] = jnp.sum(low * q_raw[...], axis=0, keepdims=True)
     low = (low * biases[7:8]).astype(BF16).astype(F32)
@@ -390,10 +366,10 @@
     far, near, sums, keep, *sends, term = refs
     term[...] = dot(h[...], grad_qk[...], TN).astype(BF16)
     spread_terms(term, keep, sends, depth, order)
-    ring, pair, place = s[0], s[1], s[2]
+    mine, place = s[0], s[1]
     gained = split_product(grad_qk, w_qk, far, near, (grad_value, w_value), h) / sums_in[0:1]
     row = lax.broadcasted_iota(jnp.int32, sums.shape, 0)
-    sums[...] = from_own(jnp.where(row == 7, gained, sums_in[...]), ring, pair, n_dp)
+    sums[...] = reorder(jnp.where(row == 7, gained, sums_in[...]), mine, n_dp)
     sums[0:4] = jnp.zeros((4, sums.shape[1]), F32)
     local_width, head_size = sums_q.shape[1], slope.shape[1]
     b_value = jnp.sum(grad_value[...].astype(F32), axis=0, keepdims=True)
@@ -409,13 +385,60 @@
     for number in range(1, local_width // head_size):
         total = total + scale[:, number * head_size : (number + 1) * head_size]
     sums[3:4, :head_size] = total * slope[...]
+    if sends:
+        sends[0][pl.ds(sends[0].shape[0] - 16, 16)] = fold(sums[...])
+
+
+def fold(vectors):
+    half = vectors.shape[1] // 2
+    return jnp.concatenate([vectors[:, :half], vectors[:, half:]], axis=0).astype(BF16)
+
+
+def unfold(rows):
+    return jnp.concatenate([rows[:8], rows[8:]], axis=1)
+
+
+def pair_first_kernel(depth, s, own, got, vectors, one, two, small):
+    last = got.shape[0] - 16
+    low = fold(vectors[...]).astype(F32) + got[pl.ds(last, 16)].astype(F32)
+    low = low.astype(BF16)
+    small[...] = low
+    for row, out in ((0, one), (depth, two)):
+        value = own[pl.ds(row, depth)].astype(F32) + got[pl.ds(row, depth)].astype(F32)
+        out[pl.ds(0, depth)] = value.astype(BF16)
+        out[pl.ds(depth, 16)] = low
+
+
+def pair_last_kernel(depth, start, s, own, got, small, out, zero):
+    value = own[pl.ds(start, 2 * depth)].astype(F32) + got[...].astype(F32)
+    out[pl.ds(0, depth)] = value[:depth].astype(BF16)
+    out[pl.ds(depth, 16)] = small[...]
+    zero[...] = value[depth:]
+
+
+def vector_far_kernel(depth, s, three, two, out):
+    at = pl.ds(depth, 16)
+    out[...] = two[at].astype(F32) + three[at].astype(F32)
+
+
+def vector_kernel(depth, s, small, far, one, out):
+    near = small[...].astype(F32) + one[pl.ds(depth, 16)].astype(F32)
+    out[...] = unfold(near + far[...])
+
+
+def total_kernel(s, one, two, *outs):
+    total = one[...] + two[...]
+    for out, row in zip(outs[:7], (0, 1, 2, 6, 4, 5, 7)):
+        for k in range(out.shape[0]):
+            out[k : k + 1] = total[row : row + 1, k * LANES : (k + 1) * LANES]
+    outs[7][...] = total[3:4, : outs[7].shape[1]]
 
 
 def last_kernel(n_dp, s, keep, got, x_own, grad_full, sums_in, grad_in):
     normed, inverse = normalize(x_own[...].astype(F32))
     grad_h = keep[...] + got[...].astype(F32)
     full = grad_full[...] + norm_back(grad_h, normed, inverse, sums_in[0:1])
-    grad_in[...] = from_own(full, s[0], s[1], n_dp).astype(BF16)
+    grad_in[...] = reorder(full, s[0], n_dp).astype(BF16)
 
 
 def add_kernel(s, one, two, out):
@@ -424,7 +447,7 @@
 
 def output_kernel(n_dp, s, keep, got, x_one, vectors, out):
     value = x_one[...] + keep[...] + got[...].astype(F32) + vectors[3:4]
-    out[...] = from_own(value, s[0], s[1], n_dp).astype(BF16)
+    out[...] = reorder(value, s[0], n_dp).astype(BF16)
 
 
 def tie(*values):
@@ -434,10 +457,7 @@
 class Links:
     def __init__(self, n_dp, n_tensor):
         self.n_dp, self.n_tensor = n_dp, n_tensor
-        self.ring = n_dp // 2
-        self.wide = self.ring > 4
-        order = sorted(range(1, self.ring), key=lambda j: -min(j, self.ring - j))
-        self.order = [] if self.wide else order
+        self.wide = n_dp > 8
 
     def move(self, value, target):
         pairs = []
@@ -454,41 +474,31 @@
         return self.move(value, lambda d, t: (d, t ^ 1))
 
     def pair(self, value):
-        return self.move(value, lambda d, t: (d ^ 1, t))
-
-    def shift(self, value, step):
-        n = self.ring
-        return self.move(value, lambda d, t: (((d // 2 + step) % n) * 2 + d % 2, t))
+        return self.along(value, 1)
+
+    def along(self, value, bits):
+        return self.move(value, lambda d, t: (d ^ bits, t))
 
     def gather_tensor(self, rows):
         near = self.chip(rows)
         return rows, near, self.core(rows), self.core(near)
 
-    def gather_ring(self, shard):
-        if self.wide:
-            blocks = lax.all_gather(shard, "dp", axis=0)
-            place = lax.axis_index("dp")
-            blocks = jnp.roll(blocks.reshape(self.ring, 2, *shard.shape), -(place >> 1), axis=0)
-            blocks = jnp.where((place & 1) == 1, blocks[:, ::-1], blocks)
-            return [blocks.reshape(self.n_dp * shard.shape[0], shard.shape[1])]
-        got = {0: shard}
-        for j in self.order:
-            got[j] = self.shift(shard, -j)
-        return [got[j] for j in range(self.ring)]
+    def gather_wide(self, shard):
+        blocks, place = lax.all_gather(shard, "dp", axis=0), lax.axis_index("dp")
+        return jnp.take(blocks, lax.iota(jnp.int32, self.n_dp) ^ place, axis=0).reshape(-1, shard.shape[1])
 
     def scatter_wide(self, total):
         place = lax.axis_index("dp")
-        blocks = total.reshape(self.ring, 2, total.shape[0] // self.n_dp, total.shape[1])
-        blocks = jnp.where((place & 1) == 1, blocks[:, ::-1], blocks)
-        blocks = jnp.roll(blocks, place >> 1, axis=0).reshape(total.shape).astype(F32)
-        return unpack(lax.psum_scatter(blocks, "dp", scatter_dimension=0, tiled=True))
+        blocks = total.reshape(self.n_dp, total.shape[0] // self.n_dp, total.shape[1])
+        blocks = jnp.take(blocks, lax.iota(jnp.int32, self.n_dp) ^ place, axis=0).astype(F32)
+        return unpack(lax.psum_scatter(blocks.reshape(total.shape), "dp", scatter_dimension=0, tiled=True))
 
     def steps(self):
-        found, bit = [lambda d, t: (d, t ^ 1)], 2
-        while bit < self.n_dp:
+        found, bit = [], 1
+        while bit < self.n_dp and self.wide:
             found.append(lambda d, t, bit=bit: (d ^ bit, t))
             bit *= 2
-        return found + [lambda d, t: (d, t ^ 2), lambda d, t: (d ^ 1, t)]
+        return found + [lambda d, t: (d, t ^ 1), lambda d, t: (d, t ^ 2)]
 
 
 def body(
@@ -513,7 +523,7 @@
     n_tensor,
 ):
     links = Links(n_dp, n_tensor)
-    n_ring = n_dp // 2
+    wide = links.wide
     local_rows, width = inputs.shape
     all_rows = local_rows * n_tensor
     depth = width // n_dp
@@ -523,7 +533,7 @@
     heads = local_width // head_size
     dp_index = lax.axis_index("dp")
     tensor_index = lax.axis_index("tensor")
-    s = jnp.stack([dp_index >> 1, dp_index & 1, tensor_index, lengths[0]])
+    s = jnp.stack([dp_index, tensor_index, lengths[0]])
     product = 2 * all_rows * width * local_width
     mixed = 2 * all_rows * all_rows * local_width
 
@@ -560,7 +570,6 @@
         return run("pack_" + name, pack_kernel, packed, apart(one), apart(two), remote=2, scratch=loads)[0]
 
     own_qk = pack_two("qk", weight_query, weight_key)
-    ring_qk = links.gather_ring(own_qk)
     given = (gain_attention, gain_mixer, bias_output, bias_final, bias_query, bias_value, bias_hidden)
     scale_wide, slope = tie(scale_wide, slope)
     tall = (width // LANES, LANES)
@@ -577,26 +586,37 @@
     )
     own_vo = pack_two("vo", weight_value, weight_output.T)
     own_hd = pack_two("hd", weight_hidden, weight_down.T)
-    order = links.order + [0]
-    n_half = len(order) // 2
-
-    def partners(blocks):
-        if links.wide:
-            return []
-        (stacked,) = run("stack", stack_kernel, [((len(blocks) * depth, both), BF16)], *blocks)
-        return [links.pair(stacked)]
-
-    first_qk = [] if links.wide else [links.pair(own_qk)]
-    h_own, ring_qk, first_qk, own_vo, own_hd = tie(h_own, ring_qk, first_qk, own_vo, own_hd)
-    h_one = links.gather_tensor(h_own)
-    ring_vo = links.gather_ring(own_vo)
-    blocks_qk = ring_qk + first_qk + partners(ring_qk[1:])
-    h_one, ring_vo, blocks_qk = tie(h_one, ring_vo, blocks_qk)
-    blocks_vo = ring_vo + partners(ring_vo)
-    ring_hd = links.gather_ring(own_hd)
+    order = (3, 2, 1, 0)
+
+    def stack(*blocks):
+        rows = sum(block.shape[0] for block in blocks)
+        return run("stack", stack_kernel, [((rows, both), BF16)], *blocks)[0]
+
+    if wide:
+        qk, vo, hd = (([links.gather_wide(own)], []) for own in (own_qk, own_vo, own_hd))
+        h_one, grad_rows = links.gather_tensor(h_own), links.gather_tensor(grad_own)
+    else:
+        qk_one, qk_two = links.along(own_qk, 2), links.along(own_qk, 4)
+        h_own, own_vo, own_hd, qk_one, qk_two = tie(h_own, own_vo, own_hd, qk_one, qk_two)
+        h_chip = links.chip(h_own)
+        qk_three = links.along(qk_one, 4)
+        near_qk_pair = links.pair(stack(own_qk, qk_one))
+        own_vo, qk_three = tie(own_vo, qk_three)
+        far_stack = stack(qk_two, qk_three)
+        far_stack, near_qk_pair, h_chip = tie(far_stack, near_qk_pair, h_chip)
+        h_one = h_own, h_chip, links.core(h_own), links.core(h_chip)
+        far_qk_pair = links.pair(far_stack)
+        vo_one, vo_two = links.along(own_vo, 2), links.along(own_vo, 4)
+        qk = [own_qk, qk_one, qk_two, qk_three], [near_qk_pair, far_qk_pair]
+        h_one, qk, vo_one, vo_two = tie(h_one, qk, vo_one, vo_two)
+        near_vo_pair = links.pair(stack(own_vo, vo_one))
+        vo_three = links.along(vo_one, 4)
+        hd_one = links.along(own_hd, 2)
+        grad_chip = links.chip(grad_own)
+    n_qk = len(qk[0]), len(qk[0]) + len(qk[1])
     q_raw, q_low, k_low, h_all, w_qk, turned = run(
         "attend",
-        bind(attend_kernel, len(blocks_qk), head_size),
+        bind(attend_kernel, n_qk, depth, head_size),
         [
             part_full,
             part,
@@ -607,41 +627,59 @@
         ],
         *h_one,
         biases,
-        *blocks_qk,
-        remote=len(blocks_qk),
+        *qk[0],
+        *qk[1],
+        remote=n_qk[1],
         scratch=sems,
     )
-    grad_own, q_low = tie(grad_own, q_low)
-    grad_rows = links.gather_tensor(grad_own)
-    turned, blocks_vo, ring_hd = tie(turned, blocks_vo, ring_hd)
-    blocks_hd = ring_hd + partners(ring_hd)
+    if not wide:
+        turned, near_vo_pair, vo_three, hd_one, grad_chip = tie(
+            turned, near_vo_pair, vo_three, hd_one, grad_chip
+        )
+        far_vo_pair = links.pair(stack(vo_two, vo_three))
+        hd_two = links.along(own_hd, 4)
+        grad_rows = grad_own, grad_chip, links.core(grad_own), links.core(grad_chip)
+        vo = [own_vo, vo_one, vo_two, vo_three], [near_vo_pair, far_vo_pair]
+        grad_rows, own_hd, hd_one, hd_two = tie(grad_rows, own_hd, hd_one, hd_two)
+        near_hd_pair = links.pair(stack(own_hd, hd_one))
+        hd_three = links.along(hd_one, 4)
+        turned, vo, grad_rows = tie(turned, vo, grad_rows)
+    n_vo = len(vo[0]), len(vo[0]) + len(vo[1])
     v_low, context, far, near, w_value, w_output = run(
         "context",
-        bind(context_kernel, head_size, len(blocks_vo)),
+        bind(context_kernel, n_vo, depth, head_size),
         [part, part, *split, weight, weight],
         h_all,
         turned,
         biases,
-        *blocks_vo,
-        remote=len(blocks_vo),
+        *vo[0],
+        *vo[1],
+        remote=n_vo[1],
         scratch=term + sems,
     )
 
     def core_half(far, near):
         return run("middle", middle_kernel, [rows_low, rows_full], near, links.core(far))
 
+    if not wide:
+        far, hd_three, near_hd_pair = tie(far, hd_three, near_hd_pair)
     send, keep = core_half(far, near)
     got = links.chip(send)
-    got, blocks_hd, grad_rows = tie(got, blocks_hd, grad_rows)
+    if not wide:
+        far_hd_pair = links.pair(stack(hd_two, hd_three))
+        hd = [own_hd, hd_one, hd_two, hd_three], [near_hd_pair, far_hd_pair]
+        got, hd = tie(got, hd)
+    n_hd = len(hd[0]), len(hd[0]) + len(hd[1])
     x_one, h_two_own = run("second_norm", second_norm_kernel, [rows_full, rows_low], keep, got, x_own, vectors)
     h_two = links.gather_tensor(h_two_own)
     grad_act, grad_all, w_hidden, w_down = run(
         "grad_act",
-        bind(grad_act_kernel, len(blocks_hd)),
+        bind(grad_act_kernel, n_hd, depth),
         [part_full, whole_rows, weight, weight],
         *grad_rows,
-        *blocks_hd,
-        remote=len(blocks_hd),
+        *hd[0],
+        *hd[1],
+        remote=n_hd[1],
         scratch=term + sems,
     )
     far, near, act, grad_pre, h_two_all = run(
@@ -656,10 +694,9 @@
     send, keep = core_half(far, near)
     act, send = tie(act, send)
     got = links.chip(send)
-    if links.wide:
-        terms = [((width, both), BF16)]
-    else:
-        terms = [((n_ring * depth, both), BF16)] + [((n_half * depth, both), BF16)] * 2
+    half = ((n_dp // 4 * depth, both), BF16)
+    ridden = ((depth + 16, both), BF16)
+    terms = [((width, both), BF16)] if wide else [((n_dp // 2 * depth, both), BF16), half, half]
     far, near, grad_b_hidden, *terms_hd = run(
         "down",
         bind(down_kernel, depth, order),
@@ -673,19 +710,20 @@
     )
     got, terms_hd = tie(got, terms_hd)
 
-    def pair_sum(name, start, keep, got, last):
-        count = got.shape[0] // depth
-        outs = packed * count
-        if last:
-            outs = packed * (count - 1) + [((depth, both), F32)]
-        return run("pair_" + name, bind(pair_kernel, start), outs, keep, got)
-
-    def ring_send(parts, start):
-        return [links.shift(part, j) for part, j in zip(parts, links.order[start:])]
-
-    def owned(name, parts):
+    def pair_sum(name, start, outs, own, *gots):
+        return run("pair_" + name, bind(pair_kernel, start, len(gots)), outs, own, *gots)
+
+    def owned(name, *parts):
         outs = [((depth, local_width), F32)] * 2
-        return run("owned_" + name, bind(owned_kernel, n_ring - 1), outs, *parts)
+        return run("owned_" + name, bind(owned_kernel, len(parts) - 1), outs, *parts)
+
+    def first_far(name, terms, got):
+        return pair_sum(name + "_a", 0, [half], terms[0], got)[0]
+
+    def then_near(name, terms, got_pair, got_far):
+        outs = packed + [((depth, both), F32)]
+        sent, zero = pair_sum(name + "_b", half[0][0], outs, terms[0], got_pair, got_far)
+        return zero, links.along(sent, 2)
 
     sent_hd = [links.pair(part) for part in terms_hd[1:]]
     grad_mid_low, grad_mid, sums = run(
@@ -698,11 +736,14 @@
         grad_own,
         vectors,
     )
-    grad_mid_rows = links.gather_tensor(grad_mid_low)
+    if wide:
+        grad_mid_rows = links.gather_tensor(grad_mid_low)
+    else:
+        grad_mid_chip = links.chip(grad_mid_low)
+        grad_mid_chip, sent_hd[0] = tie(grad_mid_chip, sent_hd[0])
+        far_sum = links.along(first_far("hd", terms_hd, sent_hd[0]), 4)
+        grad_mid_rows = grad_mid_low, grad_mid_chip, links.core(grad_mid_low), links.core(grad_mid_chip)
     grad_mid_rows, far = tie(grad_mid_rows, far)
-    if not links.wide:
-        grad_mid_rows, sent_hd[0] = tie(grad_mid_rows, sent_hd[0])
-        parts_hd = ring_send(pair_sum("hd_a", 0, terms_hd[0], sent_hd[0], False), 0)
     mix_send, mix_keep = core_half(far, near)
     mix_got = links.chip(mix_send)
     grad_context, grad_value, _, *terms_vo = run(
@@ -717,11 +758,7 @@
         scratch=term,
     )
     grad_context, sent_hd[1:] = tie(grad_context, sent_hd[1:])
-    sent_vo = [links.pair(part) for part in terms_vo[1:]]
-    if not links.wide:
-        *parts, zero_hd = pair_sum("hd_b", n_half, terms_hd[0], sent_hd[1], True)
-        grad_context, parts = tie(grad_context, parts)
-        parts_hd += ring_send(parts, n_half)
+    sent_vo = [links.pair(part) for part in terms_vo[1:2]]
     grad_qk, sums_q = run(
         "grad_scores",
         bind(grad_scores_kernel, head_size),
@@ -739,16 +776,21 @@
             pltpu.VMEM((all_rows, all_rows), BF16),
         ],
     )
-    grad_qk, sent_vo, mix_got = tie(grad_qk, sent_vo, mix_got)
-    if not links.wide:
-        grad_qk, parts_hd = tie(grad_qk, parts_hd)
-        parts_vo = ring_send(pair_sum("vo_a", 0, terms_vo[0], sent_vo[0], False), 0)
-        *parts, zero_vo = pair_sum("vo_b", n_half, terms_vo[0], sent_vo[1], True)
-        parts_vo += ring_send(parts, n_half)
+    if wide:
+        grad_qk, mix_got = tie(grad_qk, mix_got)
+    else:
+        grad_qk, sent_vo[0], mix_got, far_sum = tie(grad_qk, sent_vo[0], mix_got, far_sum)
+        zero_hd, part_hd = then_near("hd", terms_hd, sent_hd[1], far_sum)
+        sent = first_far("vo", terms_vo, sent_vo[0])
+        grad_qk, zero_hd, sent = tie(grad_qk, zero_hd, sent)
+        far_sum = links.along(sent, 4)
+    terms_first = list(terms)
+    if not wide:
+        terms_first[1] = ((half[0][0] + 16, both), BF16)
     far, near, sums, *terms_qk = run(
         "grad_first",
         bind(grad_first_kernel, n_dp, depth, order),
-        [*split, vector, *terms],
+        [*split, vector, *terms_first],
         grad_qk,
         w_qk,
         grad_value,
@@ -760,40 +802,70 @@
         slope,
         scratch=term,
     )
-    sent_qk = [links.pair(part) for part in terms_qk[1:]]
+    def exchange(value, step):
+        return run("add", add_kernel, [vector], value, links.move(value, step))[0]
+
+    if not wide:
+        far, sent_qk = tie(far, terms_qk[1:])
+        sent_qk = [links.pair(part) for part in sent_qk]
+        sent_qk[0], last_vo = tie(sent_qk[0], terms_vo[2])
+        sent_vo.append(links.pair(last_vo))
     send, keep = core_half(far, near)
     got = links.chip(send)
+    if wide:
+        total = sums
+    else:
+        got, sent_qk[0] = tie(got, sent_qk[0])
+        one, two, small = run(
+            "pair_qk_a",
+            bind(pair_first_kernel, depth),
+            [ridden, ridden, ((16, both), BF16)],
+            terms_qk[0],
+            sent_qk[0],
+            sums,
+        )
+        got, one, two = tie(got, one, two)
+        three, two = links.along(one, 6), links.along(two, 4)
+    (grad_in,) = run("last", bind(last_kernel, n_dp), [rows_low], keep, got, x_own, grad_mid, vectors)
+    if not wide:
+        grad_in, sent_qk[1] = tie(grad_in, sent_qk[1])
+        one, zero_qk = run(
+            "pair_qk_b",
+            bind(pair_last_kernel, depth, half[0][0]),
+            [ridden, ((depth, both), F32)],
+            terms_qk[0],
+            sent_qk[1],
+            small,
+        )
+        one = links.along(one, 2)
+        zero_qk, far_sum = tie(zero_qk, far_sum)
+        zero_vo, part_vo = then_near("vo", terms_vo, sent_vo[1], far_sum)
+        mix_got, zero_vo = tie(mix_got, zero_vo)
+    (output,) = run("output", bind(output_kernel, n_dp), [rows_low], mix_keep, mix_got, x_one, vectors)
+    if not wide:
+        part_hd, output = tie(part_hd, output)
+        grad_hidden, grad_down = owned("hd", zero_hd, part_hd)
+        three, two, grad_hidden = tie(three, two, grad_hidden)
+        (far_rows,) = run("vector_a", bind(vector_far_kernel, depth), [((16, both), F32)], three, two)
+        (total,) = run("vector_b", bind(vector_kernel, depth), [vector], small, far_rows, one)
     steps = links.steps()
-    total = sums
-
-    def exchange(value, step):
-        return run("add", add_kernel, [vector], value, links.move(value, step))[0]
-
-    for step in steps[:-2]:
+    for step in steps[:-1]:
         total = exchange(total, step)
-    if not links.wide:
-        got, sent_qk[0], parts_vo = tie(got, sent_qk[0], parts_vo)
-        parts = pair_sum("qk_a", 0, terms_qk[0], sent_qk[0], False)
-        got, parts = tie(got, parts)
-        parts_qk = ring_send(parts, 0)
-    (grad_in,) = run("last", bind(last_kernel, n_dp), [rows_low], keep, got, x_own, grad_mid, vectors)
-    total, grad_in = tie(total, grad_in)
-    total = exchange(total, steps[-2])
-    if not links.wide:
-        total, sent_qk[1] = tie(total, sent_qk[1])
-        *parts, zero_qk = pair_sum("qk_b", n_half, terms_qk[0], sent_qk[1], True)
-        total, parts = tie(total, parts)
-        parts_qk += ring_send(parts, n_half)
-    total = exchange(total, steps[-1])
-    (output,) = run("output", bind(output_kernel, n_dp), [rows_low], mix_keep, mix_got, x_one, vectors)
-    if links.wide:
+    if not wide:
+        total, zero_qk = tie(total, zero_qk)
+    moved = links.move(total, steps[-1])
+    tall_vector = (tall, F32)
+    *totals, total_scale = run(
+        "total", total_kernel, [tall_vector] * 7 + [((1, head_size), F32)], total, moved
+    )
+    totals = [v.reshape(width) for v in totals]
+    if wide:
         grad_hidden, grad_down = links.scatter_wide(terms_hd[0])
         grad_output_v, grad_output_o = links.scatter_wide(terms_vo[0])
         grad_query, grad_key = links.scatter_wide(terms_qk[0])
     else:
-        grad_hidden, grad_down = owned("hd", [zero_hd, *parts_hd])
-        grad_output_v, grad_output_o = owned("vo", [zero_vo, *parts_vo])
-        grad_query, grad_key = owned("qk", [zero_qk, *parts_qk])
+        grad_output_v, grad_output_o = owned("vo", zero_vo, part_vo)
+        grad_query, grad_key = owned("qk", zero_qk, three, two, one)
     return (
         output,
         grad_in,
@@ -803,14 +875,14 @@
         grad_output_o.T,
         grad_hidden,
         grad_down.T,
-        total[0],
-        total[1],
-        total[2],
-        total[5],
-        total[4],
-        total[7],
-        total[6],
-        total[3, :head_size],
+        totals[0],
+        totals[1],
+        totals[2],
+        totals[5],
+        totals[4],
+        totals[6],
+        totals[3],
+        total_scale.reshape(head_size),
     )
 
 

time: 247 us -> 222 us (0.90)
  starting transfers between devices: 73.9 us -> 45.1 us
  waiting for transfers between devices: 95 us -> 108 us
  Pallas kernels: 73.4 us -> 65.5 us
    ppermute x53 -> x50, starting transfers between devices: 73.9 us -> 45.1 us  [move(): return lax.ppermute(value, AXES, pairs)]
    ppermute x53 -> x50, waiting for transfers between devices: 95 us -> 108 us  [move(): return lax.ppermute(value, AXES, pairs)]
    pallas_call x37 -> x39, Pallas kernels: 73.4 us -> 65.5 us  [call(): pl.pallas_call(kernel, name=name, out_shape=outs, in_specs=[pl.BlockSpec(...]
  transfers between devices with their start and end apart: 53 -> 50, of which waited for: 21 -> 24; matrix products, arithmetic and copies ran while one was open for 1% -> 0% of each run, Pallas kernels for 22% -> 24%
where the time goes in v1:
time: 222 us; the launch traced here: 221 us
  waiting for transfers between devices  108 us (49%)
  Pallas kernels  65.5 us (30%)
  starting transfers between devices  45.1 us (20%)
    ppermute x50, waiting for transfers between devices, move(): return lax.ppermute(value, AXES, pairs)  108 us
    pallas_call x39, Pallas kernels, call(): pl.pallas_call(kernel, name=name, out_shape=outs, in_specs=[pl.BlockSpec(...  65.5 us
    ppermute x50, starting transfers between devices, move(): return lax.ppermute(value, AXES, pairs)  45.1 us
  transfers between devices with their start and end apart: 50, of which 24 were waited for; matrix products, arithmetic and copies ran while one was open for 0% of the time, Pallas kernels for 24%

profile of v1, /device:TPU:0, one launch (start us, length us, event | category | flops | bytes accessed | tf_op | source)
XLA Modules:
  0.0 221.4 jit_solution(4501185767110489299)
XLA Ops:
  3.0 4.1 %collective-permute-start.1 = (bf16[160,640]{1,0:T(8,128)(2,1)S(1)}, bf16[160,640]{1,0:T(8,128)(2,1)S(1)}, u32[]{:S(2)}, u32[]{:S(2)}) collective-permute-start(bf16[160,640]{1,0:T(8,128)(2,1)S(1)} %pack_qk.1.refs_0_.refs_6_), channel_id=1, source_target_pairs={{0,16},{1,17},{2,18},{3,19},{4,20},{5,21},{6,22},{7,23},{8,24},{9,... | collective-permute-start | bytes 614408 | tf_op jit(solution)/shard_map/ppermute | solution.py:468
  12.7 3.2 %prepare.1 = (bf16[128,1280]{1,0:T(8,128)(2,1)S(1)}, bf16[128,1280]{1,0:T(8,128)(2,1)S(1)}, bf16[128,1280]{1,0:T(8,128)(2,1)S(1)}, f32[8,1280]{1,0:T(8,128)S(1)}, f32[8,320]{1,0:T(8,128)S(1)}) custom-call(s32[3]{0:T(128)S(1)} %pad_add_fusion.refs_0_.s, f32[1,320]{1,0:T(1,128)S(1)} %broadcast_in_dim_tile.3.refs_1_, bf16[128,1280]{1,0:T(8,128)(2,1)} %refs_2_.1, ...), custom_call_target="tpu_custom_call" | custom-call | flops 1000000 | bytes 1726720 | tf_op jit(solution)/shard_map/prepare/pallas_call | solution.py:30
  21.9 9.1 %collective-permute-done.2.refs_1_.refs_9_ = bf16[160,640]{1,0:T(8,128)(2,1)S(1)} collective-permute-done((bf16[160,640]{1,0:T(8,128)(2,1)S(1)}, bf16[160,640]{1,0:T(8,128)(2,1)S(1)}, u32[]{:S(2)}, u32[]{:S(2)}) %collective-permute-start.2) | collective-permute-done | bytes 204832 | tf_op jit(solution)/shard_map/ppermute | solution.py:468
  32.7 3.1 %collective-permute-start.8 = (bf16[160,640]{1,0:T(8,128)(2,1)S(1)}, bf16[160,640]{1,0:T(8,128)(2,1)S(1)}, u32[]{:S(2)}, u32[]{:S(2)}) collective-permute-start(bf16[160,640]{1,0:T(8,128)(2,1)S(1)} %pack_vo.1.refs_0_.refs_4_), channel_id=1, source_target_pairs={{0,8},{1,9},{2,10},{3,11},{4,12},{5,13},{6,14},{7,15},{8,0},{9,1},... | collective-permute-start | bytes 614408 | tf_op jit(solution)/shard_map/ppermute | solution.py:468
  35.8 9.2 %collective-permute-done.9.refs_0_.refs_6_ = bf16[160,640]{1,0:T(8,128)(2,1)S(1)} collective-permute-done((bf16[160,640]{1,0:T(8,128)(2,1)S(1)}, bf16[160,640]{1,0:T(8,128)(2,1)S(1)}, u32[]{:S(2)}, u32[]{:S(2)}) %collective-permute-start.9) | collective-permute-done | bytes 204832 | tf_op jit(solution)/shard_map/ppermute | solution.py:468
  47.8 2.0 collective-permute-start.11
  49.8 6.3 %attend.1 = (f32[512,320]{1,0:T(8,128)S(1)}, bf16[512,320]{1,0:T(8,128)(2,1)S(1)}, bf16[512,320]{1,0:T(8,128)(2,1)S(1)}, bf16[512,1280]{1,0:T(8,128)(2,1)S(1)}, ...) custom-call(s32[3]{0:T(128)S(1)} %pad_add_fusion.refs_0_.s, ...), custom_call_target="tpu_custom_call" | custom-call | flops 1000000 | bytes 9316352 | tf_op jit(solution)/shard_map/attend/pallas_call | solution.py:30
  57.2 2.2 collective-permute-done.11.refs_1_.refs_7_
  60.9 10.1 %collective-permute-done.17.refs_0_.refs_7_ = bf16[160,640]{1,0:T(8,128)(2,1)S(1)} collective-permute-done((bf16[160,640]{1,0:T(8,128)(2,1)S(1)}, bf16[160,640]{1,0:T(8,128)(2,1)S(1)}, u32[]{:S(2)}, u32[]{:S(2)}) %collective-permute-start.17) | collective-permute-done | bytes 204832 | tf_op jit(solution)/shard_map/ppermute | solution.py:468
  72.3 5.6 %context.1 = (bf16[512,320]{1,0:T(8,128)(2,1)S(1)}, bf16[512,320]{1,0:T(8,128)(2,1)S(1)}, bf16[256,1280]{1,0:T(8,128)(2,1)S(1)}, f32[256,1280]{1,0:T(8,128)S(1)}...) custom-call(s32[3]{0:T(128)S(1)} %pad_add_fusion.refs_0_.s, ...), custom_call_target="tpu_custom_call" | custom-call | flops 1000000 | bytes 9316352 | tf_op jit(solution)/shard_map/context/pallas_call | solution.py:30
  77.9 6.1 %collective-permute-done.18.refs_1_.refs_8_ = bf16[160,640]{1,0:T(8,128)(2,1)S(1)} collective-permute-done((bf16[160,640]{1,0:T(8,128)(2,1)S(1)}, bf16[160,640]{1,0:T(8,128)(2,1)S(1)}, u32[]{:S(2)}, u32[]{:S(2)}) %collective-permute-start.18) | collective-permute-done | bytes 204832 | tf_op jit(solution)/shard_map/ppermute | solution.py:468
  88.4 8.1 %collective-permute-done.22.refs_10_ = bf16[320,640]{1,0:T(8,128)(2,1)S(1)} collective-permute-done((bf16[320,640]{1,0:T(8,128)(2,1)S(1)}, bf16[320,640]{1,0:T(8,128)(2,1)S(1)}, u32[]{:S(2)}, u32[]{:S(2)}) %collective-permute-start.22) | collective-permute-done | bytes 409632 | tf_op jit(solution)/shard_map/ppermute | solution.py:468
  99.1 7.6 %collective-permute-done.23.p1 = bf16[128,1280]{1,0:T(8,128)(2,1)S(1)} collective-permute-done((bf16[128,1280]{1,0:T(8,128)(2,1)S(1)}, bf16[128,1280]{1,0:T(8,128)(2,1)S(1)}, u32[]{:S(2)}, u32[]{:S(2)}) %collective-permute-start.23) | collective-permute-done | bytes 327712 | tf_op jit(solution)/shard_map/ppermute | solution.py:468
  106.7 4.0 %grad_act.1 = (f32[512,320]{1,0:T(8,128)S(1)}, bf16[512,1280]{1,0:T(8,128)(2,1)S(1)}, bf16[1280,320]{1,0:T(8,128)(2,1)S(1)}, bf16[1280,320]{1,0:T(8,128)(2,1)S(1)}) custom-call(s32[3]{0:T(128)S(1)} %pad_add_fusion.refs_0_.s, bf16[128,1280]{1,0:T(8,128)(2,1)S(1)} %get-tuple-element.257.refs_1_.grad, bf16[128,1280]{1,0:T(8,128)(2,1)S(1)} %collective-permute-done.13.refs_2_, ...), custom_call_target="tpu_custom_call" | custom-call | flops 1000000 | bytes 6553600 | tf_op jit(solution)/shard_map/grad_act/pallas_call | solution.py:30
  110.7 2.3 %hidden.1 = (bf16[256,1280]{1,0:T(8,128)(2,1)S(1)}, f32[256,1280]{1,0:T(8,128)S(1)}, bf16[512,320]{1,0:T(8,128)(2,1)S(1)}, bf16[512,320]{1,0:T(8,128)(2,1)S(1)}, bf16[512,1280]{1,0:T(8,128)(2,1)S(1)}) custom-call(s32[3]{0:T(128)S(1)} %pad_add_fusion.refs_0_.s, bf16[128,1280]{1,0:T(8,128)(2,1)S(1)} %get-tuple-element.256.p0, ...), custom_call_target="tpu_custom_call" | custom-call | flops 1000000 | bytes 6727680 | tf_op jit(solution)/shard_map/hidden/pallas_call | solution.py:30
  113.6 1.7 collective-permute-done.26.got
  117.6 2.9 %down.1 = (bf16[256,1280]{1,0:T(8,128)(2,1)S(1)}, f32[256,1280]{1,0:T(8,128)S(1)}, f32[1,320]{1,0:T(1,128)S(1)}, bf16[640,640]{1,0:T(8,128)(2,1)S(1)}, bf16[320,...) custom-call(s32[3]{0:T(128)S(1)} %pad_add_fusion.refs_0_.s, bf16[512,1280]{1,0:T(8,128)(2,1)S(1)} %get-tuple-element.274.refs_1_, ...), custom_call_target="tpu_custom_call" | custom-call | flops 1000000 | bytes 7701760 | tf_op jit(solution)/shard_map/down/pallas_call | solution.py:30
  120.5 5.6 %collective-permute-done.27.got = bf16[128,1280]{1,0:T(8,128)(2,1)S(1)} collective-permute-done((bf16[128,1280]{1,0:T(8,128)(2,1)S(1)}, bf16[128,1280]{1,0:T(8,128)(2,1)S(1)}, u32[]{:S(2)}, u32[]{:S(2)}) %collective-permute-start.27) | collective-permute-done | bytes 327712 | tf_op jit(solution)/shard_map/ppermute | solution.py:468
  130.1 7.4 %collective-permute-done.28.refs_2_ = bf16[128,1280]{1,0:T(8,128)(2,1)S(1)} collective-permute-done((bf16[128,1280]{1,0:T(8,128)(2,1)S(1)}, bf16[128,1280]{1,0:T(8,128)(2,1)S(1)}, u32[]{:S(2)}, u32[]{:S(2)}) %collective-permute-start.28) | collective-permute-done | bytes 327712 | tf_op jit(solution)/shard_map/ppermute | solution.py:468
  141.0 4.3 %grad_context.1 = (bf16[512,320]{1,0:T(8,128)(2,1)S(1)}, bf16[512,320]{1,0:T(8,128)(2,1)S(1)}, bf16[512,1280]{1,0:T(8,128)(2,1)}, bf16[640,640]{1,0:T(8,128)(2,1...) custom-call(s32[3]{0:T(128)S(1)} %pad_add_fusion.refs_0_.s, ...), custom_call_target="tpu_custom_call" | custom-call | flops 1000000 | bytes 9469952 | tf_op jit(solution)/shard_map/grad_context/pallas_call | solution.py:30
  148.6 3.0 %collective-permute-done.32.refs_2_ = bf16[320,640]{1,0:T(8,128)(2,1)S(1)} collective-permute-done((bf16[320,640]{1,0:T(8,128)(2,1)S(1)}, bf16[320,640]{1,0:T(8,128)(2,1)S(1)}, u32[]{:S(2)}, u32[]{:S(2)}) %collective-permute-start.32) | collective-permute-done | bytes 409632 | tf_op jit(solution)/shard_map/ppermute | solution.py:468
  151.6 5.5 %grad_scores.1 = (bf16[512,640]{1,0:T(8,128)(2,1)S(1)}, f32[8,320]{1,0:T(8,128)S(1)}) custom-call(s32[3]{0:T(128)S(1)} %pad_add_fusion.refs_0_.s, bf16[4,512,512]{2,1,0:T(8,128)(2,1)S(1)} %get-tuple-element.236.refs_2_.refs_6_.refs_1_, bf16[512,320]{1,0:T(8,128)(2,1)S(1)} %get-tuple-element.299.refs_2_, bf16[512,320]{1,0:T(8,128)(2,1)S(1)} %get-tuple-element.300.refs_3_, ...), custom_call_target="tpu_custom_call" | custom-call | flops 1000000 | bytes 4739072 | tf_op jit(solution)/shard_map/grad_scores/pallas_call | solution.py:30
  157.1 3.8 %collective-permute-done.36.refs_3_ = bf16[320,640]{1,0:T(8,128)(2,1)S(1)} collective-permute-done((bf16[320,640]{1,0:T(8,128)(2,1)S(1)}, bf16[320,640]{1,0:T(8,128)(2,1)S(1)}, u32[]{:S(2)}, u32[]{:S(2)}) %collective-permute-start.36) | collective-permute-done | bytes 409632 | tf_op jit(solution)/shard_map/ppermute | solution.py:468
  162.3 3.9 %grad_first.1 = (bf16[256,1280]{1,0:T(8,128)(2,1)S(1)}, f32[256,1280]{1,0:T(8,128)S(1)}, f32[8,1280]{1,0:T(8,128)S(1)}, bf16[640,640]{1,0:T(8,128)(2,1)S(1)}, bf...) custom-call(s32[3]{0:T(128)S(1)} %pad_add_fusion.refs_0_.s, bf16[512,640]{1,0:T(8,128)(2,1)S(1)} %get-tuple-element.318.refs_1_, ...), custom_call_target="tpu_custom_call" | custom-call | flops 1000000 | bytes 8470080 | tf_op jit(solution)/shard_map/grad_first/pallas_call | solution.py:30
  170.5 8.5 %collective-permute-done.38.refs_2_ = bf16[336,640]{1,0:T(8,128)(2,1)S(1)} collective-permute-done((bf16[336,640]{1,0:T(8,128)(2,1)S(1)}, bf16[336,640]{1,0:T(8,128)(2,1)S(1)}, u32[]{:S(2)}, u32[]{:S(2)}) %collective-permute-start.38) | collective-permute-done | bytes 430112 | tf_op jit(solution)/shard_map/ppermute | solution.py:468
  180.7 2.5 %collective-permute-start.44 = (bf16[176,640]{1,0:T(8,128)(2,1)S(1)}, bf16[176,640]{1,0:T(8,128)(2,1)S(1)}, u32[]{:S(2)}, u32[]{:S(2)}) collective-permute-start(bf16[176,640]{1,0:T(8,128)(2,1)S(1)} %get-tuple-element.355), channel_id=1, source_target_pairs={{0,24},{1,25},{2,26},{3,27},{4,28},{5,29},{6,30},{7,31},{8,16},{9,... | collective-permute-start | bytes 675848 | tf_op jit(solution)/shard_map/ppermute | solution.py:468
  183.4 2.1 last.1
  185.5 2.3 %collective-permute-done.42.refs_2_ = bf16[320,640]{1,0:T(8,128)(2,1)S(1)} collective-permute-done((bf16[320,640]{1,0:T(8,128)(2,1)S(1)}, bf16[320,640]{1,0:T(8,128)(2,1)S(1)}, u32[]{:S(2)}, u32[]{:S(2)}) %collective-permute-start.42) | collective-permute-done | bytes 409632 | tf_op jit(solution)/shard_map/ppermute | solution.py:468
  188.5 10.3 %collective-permute-done.43.refs_3_ = bf16[320,640]{1,0:T(8,128)(2,1)S(1)} collective-permute-done((bf16[320,640]{1,0:T(8,128)(2,1)S(1)}, bf16[320,640]{1,0:T(8,128)(2,1)S(1)}, u32[]{:S(2)}, u32[]{:S(2)}) %collective-permute-start.43) | collective-permute-done | bytes 409632 | tf_op jit(solution)/shard_map/ppermute | solution.py:468
  199.5 2.1 collective-permute-start.48
  201.6 1.8 output.1
  203.4 8.2 %collective-permute-done.37.refs_2_ = bf16[160,640]{1,0:T(8,128)(2,1)S(1)} collective-permute-done((bf16[160,640]{1,0:T(8,128)(2,1)S(1)}, bf16[160,640]{1,0:T(8,128)(2,1)S(1)}, u32[]{:S(2)}, u32[]{:S(2)}) %collective-permute-start.37) | collective-permute-done | bytes 204832 | tf_op jit(solution)/shard_map/ppermute | solution.py:468
  (111 shorter events, 61.0 us)
Async XLA Ops:
  3.0 13.7 %collective-permute-start.1 = (bf16[160,640]{1,0:T(8,128)(2,1)S(1)}, bf16[160,640]{1,0:T(8,128)(2,1)S(1)}, u32[]{:S(2)}, u32[]{:S(2)}) collective-permute-start(bf16[160,640]{1,0:T(8,128)(2,1)S(1)} %pack_qk.1.refs_0_.refs_6_), channel_id=1, source_target_pairs={{0,16},{1,17},{2,18},{3,19},{4,20},{5,21},{6,22},{7,23},{8,24},{9,... | collective-permute-start | bytes 614408 | tf_op jit(solution)/shard_map/ppermute | solution.py:468
  17.4 14.2 %collective-permute-start.3 = (bf16[320,640]{1,0:T(8,128)(2,1)S(1)}, bf16[320,640]{1,0:T(8,128)(2,1)S(1)}, u32[]{:S(2)}, u32[]{:S(2)}) collective-permute-start(bf16[320,640]{1,0:T(8,128)(2,1)S(1)} %stack.19), channel_id=1, source_target_pairs={{0,4},{1,5},{2,6},{3,7},{4,0},{5,1},{6,2},{7,3},{8,12},{9,13},{10,... | collective-permute-start | bytes 1228808 | tf_op jit(solution)/shard_map/ppermute | solution.py:468
  19.1 12.5 %collective-permute-start.4 = (bf16[128,1280]{1,0:T(8,128)(2,1)S(1)}, bf16[128,1280]{1,0:T(8,128)(2,1)S(1)}, u32[]{:S(2)}, u32[]{:S(2)}) collective-permute-start(bf16[128,1280]{1,0:T(8,128)(2,1)S(1)} %get-tuple-element.210.refs_1_), channel_id=1, source_target_pairs={{0,2},{1,3},{2,0},{3,1},{4,6},{5,7},{6,4},{7,5},{8,10},{9,11},{10,... | collective-permute-start | bytes 983048 | tf_op jit(solution)/shard_map/ppermute | solution.py:468
  31.6 13.5 %collective-permute-start.7 = (bf16[320,640]{1,0:T(8,128)(2,1)S(1)}, bf16[320,640]{1,0:T(8,128)(2,1)S(1)}, u32[]{:S(2)}, u32[]{:S(2)}) collective-permute-start(bf16[320,640]{1,0:T(8,128)(2,1)S(1)} %stack.18), channel_id=1, source_target_pairs={{0,4},{1,5},{2,6},{3,7},{4,0},{5,1},{6,2},{7,3},{8,12},{9,13},{10,... | collective-permute-start | bytes 1228808 | tf_op jit(solution)/shard_map/ppermute | solution.py:468
  32.2 12.9 %collective-permute-start.6 = (bf16[128,1280]{1,0:T(8,128)(2,1)S(1)}, bf16[128,1280]{1,0:T(8,128)(2,1)S(1)}, u32[]{:S(2)}, u32[]{:S(2)}) collective-permute-start(bf16[128,1280]{1,0:T(8,128)(2,1)S(1)} %collective-permute-done.4.refs_2_), channel_id=1, source_target_pairs={{0,1},{1,0},{2,3},{3,2},{4,5},{5,4},{6,7},{7,6},{8,9},{9,8},{10,11... | collective-permute-start | bytes 983048 | tf_op jit(solution)/shard_map/ppermute | solution.py:468
  32.7 12.2 %collective-permute-start.9 = (bf16[160,640]{1,0:T(8,128)(2,1)S(1)}, bf16[160,640]{1,0:T(8,128)(2,1)S(1)}, u32[]{:S(2)}, u32[]{:S(2)}) collective-permute-start(bf16[160,640]{1,0:T(8,128)(2,1)S(1)} %pack_vo.1.refs_0_.refs_4_), channel_id=1, source_target_pairs={{0,16},{1,17},{2,18},{3,19},{4,20},{5,21},{6,22},{7,23},{8,24},{9,... | collective-permute-start | bytes 614408 | tf_op jit(solution)/shard_map/ppermute | solution.py:468
  32.7 12.4 %collective-permute-start.8 = (bf16[160,640]{1,0:T(8,128)(2,1)S(1)}, bf16[160,640]{1,0:T(8,128)(2,1)S(1)}, u32[]{:S(2)}, u32[]{:S(2)}) collective-permute-start(bf16[160,640]{1,0:T(8,128)(2,1)S(1)} %pack_vo.1.refs_0_.refs_4_), channel_id=1, source_target_pairs={{0,8},{1,9},{2,10},{3,11},{4,12},{5,13},{6,14},{7,15},{8,0},{9,1},... | collective-permute-start | bytes 614408 | tf_op jit(solution)/shard_map/ppermute | solution.py:468
  45.7 13.7 %collective-permute-start.10 = (bf16[320,640]{1,0:T(8,128)(2,1)S(1)}, bf16[320,640]{1,0:T(8,128)(2,1)S(1)}, u32[]{:S(2)}, u32[]{:S(2)}) collective-permute-start(bf16[320,640]{1,0:T(8,128)(2,1)S(1)} %stack.20), channel_id=1, source_target_pairs={{0,4},{1,5},{2,6},{3,7},{4,0},{5,1},{6,2},{7,3},{8,12},{9,13},{10,... | collective-permute-start | bytes 1228808 | tf_op jit(solution)/shard_map/ppermute | solution.py:468
  47.8 11.6 %collective-permute-start.11 = (bf16[160,640]{1,0:T(8,128)(2,1)S(1)}, bf16[160,640]{1,0:T(8,128)(2,1)S(1)}, u32[]{:S(2)}, u32[]{:S(2)}) collective-permute-start(bf16[160,640]{1,0:T(8,128)(2,1)S(1)} %collective-permute-done.8.refs_1_.refs_5_), channel_id=1, source_target_pairs={{0,16},{1,17},{2,18},{3,19},{4,20},{5,21},{6,22},{7,23},{8,24},{9,... | collective-permute-start | bytes 614408 | tf_op jit(solution)/shard_map/ppermute | solution.py:468
  49.8 11.0 %collective-permute-start.15 = (bf16[128,1280]{1,0:T(8,128)(2,1)S(1)}, bf16[128,1280]{1,0:T(8,128)(2,1)S(1)}, u32[]{:S(2)}, u32[]{:S(2)}) collective-permute-start(bf16[128,1280]{1,0:T(8,128)(2,1)S(1)} %get-tuple-element.257.refs_1_.grad), channel_id=1, source_target_pairs={{0,1},{1,0},{2,3},{3,2},{4,5},{5,4},{6,7},{7,6},{8,9},{9,8},{10,11... | collective-permute-start | bytes 983048 | tf_op jit(solution)/shard_map/ppermute | solution.py:468
  59.4 11.6 %collective-permute-start.16 = (bf16[128,1280]{1,0:T(8,128)(2,1)S(1)}, bf16[128,1280]{1,0:T(8,128)(2,1)S(1)}, u32[]{:S(2)}, u32[]{:S(2)}) collective-permute-start(bf16[128,1280]{1,0:T(8,128)(2,1)S(1)} %collective-permute-done.13.refs_2_), channel_id=1, source_target_pairs={{0,1},{1,0},{2,3},{3,2},{4,5},{5,4},{6,7},{7,6},{8,9},{9,8},{10,11... | collective-permute-start | bytes 983048 | tf_op jit(solution)/shard_map/ppermute | solution.py:468
  59.4 11.6 %collective-permute-start.17 = (bf16[160,640]{1,0:T(8,128)(2,1)S(1)}, bf16[160,640]{1,0:T(8,128)(2,1)S(1)}, u32[]{:S(2)}, u32[]{:S(2)}) collective-permute-start(bf16[160,640]{1,0:T(8,128)(2,1)S(1)} %pack_hd.1.refs_0_.refs_5_), channel_id=1, source_target_pairs={{0,16},{1,17},{2,18},{3,19},{4,20},{5,21},{6,22},{7,23},{8,24},{9,... | collective-permute-start | bytes 614408 | tf_op jit(solution)/shard_map/ppermute | solution.py:468
  60.3 12.0 %collective-permute-start.14 = (bf16[320,640]{1,0:T(8,128)(2,1)S(1)}, bf16[320,640]{1,0:T(8,128)(2,1)S(1)}, u32[]{:S(2)}, u32[]{:S(2)}) collective-permute-start(bf16[320,640]{1,0:T(8,128)(2,1)S(1)} %stack.21), channel_id=1, source_target_pairs={{0,4},{1,5},{2,6},{3,7},{4,0},{5,1},{6,2},{7,3},{8,12},{9,13},{10,... | collective-permute-start | bytes 1228808 | tf_op jit(solution)/shard_map/ppermute | solution.py:468
  71.6 12.4 %collective-permute-start.19 = (bf16[320,640]{1,0:T(8,128)(2,1)S(1)}, bf16[320,640]{1,0:T(8,128)(2,1)S(1)}, u32[]{:S(2)}, u32[]{:S(2)}) collective-permute-start(bf16[320,640]{1,0:T(8,128)(2,1)S(1)} %stack.22), channel_id=1, source_target_pairs={{0,4},{1,5},{2,6},{3,7},{4,0},{5,1},{6,2},{7,3},{8,12},{9,13},{10,... | collective-permute-start | bytes 1228808 | tf_op jit(solution)/shard_map/ppermute | solution.py:468
  72.3 11.7 %collective-permute-start.18 = (bf16[160,640]{1,0:T(8,128)(2,1)S(1)}, bf16[160,640]{1,0:T(8,128)(2,1)S(1)}, u32[]{:S(2)}, u32[]{:S(2)}) collective-permute-start(bf16[160,640]{1,0:T(8,128)(2,1)S(1)} %collective-permute-done.12.refs_1_.refs_6_), channel_id=1, source_target_pairs={{0,16},{1,17},{2,18},{3,19},{4,20},{5,21},{6,22},{7,23},{8,24},{9,... | collective-permute-start | bytes 614408 | tf_op jit(solution)/shard_map/ppermute | solution.py:468
  84.6 11.9 %collective-permute-start.22 = (bf16[320,640]{1,0:T(8,128)(2,1)S(1)}, bf16[320,640]{1,0:T(8,128)(2,1)S(1)}, u32[]{:S(2)}, u32[]{:S(2)}) collective-permute-start(bf16[320,640]{1,0:T(8,128)(2,1)S(1)} %stack.23), channel_id=1, source_target_pairs={{0,4},{1,5},{2,6},{3,7},{4,0},{5,1},{6,2},{7,3},{8,12},{9,13},{10,... | collective-permute-start | bytes 1228808 | tf_op jit(solution)/shard_map/ppermute | solution.py:468
  99.1 11.6 %collective-permute-start.24 = (bf16[128,1280]{1,0:T(8,128)(2,1)S(1)}, bf16[128,1280]{1,0:T(8,128)(2,1)S(1)}, u32[]{:S(2)}, u32[]{:S(2)}) collective-permute-start(bf16[128,1280]{1,0:T(8,128)(2,1)S(1)} %get-tuple-element.256.p0), channel_id=1, source_target_pairs={{0,1},{1,0},{2,3},{3,2},{4,5},{5,4},{6,7},{7,6},{8,9},{9,8},{10,11... | collective-permute-start | bytes 983048 | tf_op jit(solution)/shard_map/ppermute | solution.py:468
  126.1 11.4 %collective-permute-start.29 = (bf16[320,640]{1,0:T(8,128)(2,1)S(1)}, bf16[320,640]{1,0:T(8,128)(2,1)S(1)}, u32[]{:S(2)}, u32[]{:S(2)}) collective-permute-start(bf16[320,640]{1,0:T(8,128)(2,1)S(1)} %get-tuple-element.287), channel_id=1, source_target_pairs={{0,4},{1,5},{2,6},{3,7},{4,0},{5,1},{6,2},{7,3},{8,12},{9,13},{10,... | collective-permute-start | bytes 1228808 | tf_op jit(solution)/shard_map/ppermute | solution.py:468
  139.3 12.3 %collective-permute-start.32 = (bf16[320,640]{1,0:T(8,128)(2,1)S(1)}, bf16[320,640]{1,0:T(8,128)(2,1)S(1)}, u32[]{:S(2)}, u32[]{:S(2)}) collective-permute-start(bf16[320,640]{1,0:T(8,128)(2,1)S(1)} %get-tuple-element.297), channel_id=1, source_target_pairs={{0,4},{1,5},{2,6},{3,7},{4,0},{5,1},{6,2},{7,3},{8,12},{9,13},{10,... | collective-permute-start | bytes 1228808 | tf_op jit(solution)/shard_map/ppermute | solution.py:468
  141.0 20.0 %collective-permute-start.36 = (bf16[320,640]{1,0:T(8,128)(2,1)S(1)}, bf16[320,640]{1,0:T(8,128)(2,1)S(1)}, u32[]{:S(2)}, u32[]{:S(2)}) collective-permute-start(bf16[320,640]{1,0:T(8,128)(2,1)S(1)} %pair_hd_a.1), channel_id=1, source_target_pairs={{0,16},{1,17},{2,18},{3,19},{4,20},{5,21},{6,22},{7,23},{8,24},{9,... | collective-permute-start | bytes 1228808 | tf_op jit(solution)/shard_map/ppermute | solution.py:468
  145.3 15.6 %collective-permute-start.33 = (bf16[320,640]{1,0:T(8,128)(2,1)S(1)}, bf16[320,640]{1,0:T(8,128)(2,1)S(1)}, u32[]{:S(2)}, u32[]{:S(2)}) collective-permute-start(bf16[320,640]{1,0:T(8,128)(2,1)S(1)} %get-tuple-element.305), channel_id=1, source_target_pairs={{0,4},{1,5},{2,6},{3,7},{4,0},{5,1},{6,2},{7,3},{8,12},{9,13},{10,... | collective-permute-start | bytes 1228808 | tf_op jit(solution)/shard_map/ppermute | solution.py:468
  147.1 13.9 %collective-permute-start.35 = (bf16[128,1280]{1,0:T(8,128)(2,1)S(1)}, bf16[128,1280]{1,0:T(8,128)(2,1)S(1)}, u32[]{:S(2)}, u32[]{:S(2)}) collective-permute-start(bf16[128,1280]{1,0:T(8,128)(2,1)S(1)} %get-tuple-element.308), channel_id=1, source_target_pairs={{0,2},{1,3},{2,0},{3,1},{4,6},{5,7},{6,4},{7,5},{8,10},{9,11},{10,... | collective-permute-start | bytes 983048 | tf_op jit(solution)/shard_map/ppermute | solution.py:468
  166.3 12.7 %collective-permute-start.38 = (bf16[336,640]{1,0:T(8,128)(2,1)S(1)}, bf16[336,640]{1,0:T(8,128)(2,1)S(1)}, u32[]{:S(2)}, u32[]{:S(2)}) collective-permute-start(bf16[336,640]{1,0:T(8,128)(2,1)S(1)} %get-tuple-element.329), channel_id=1, source_target_pairs={{0,4},{1,5},{2,6},{3,7},{4,0},{5,1},{6,2},{7,3},{8,12},{9,13},{10,... | collective-permute-start | bytes 1290248 | tf_op jit(solution)/shard_map/ppermute | solution.py:468
  167.3 20.5 %collective-permute-start.42 = (bf16[320,640]{1,0:T(8,128)(2,1)S(1)}, bf16[320,640]{1,0:T(8,128)(2,1)S(1)}, u32[]{:S(2)}, u32[]{:S(2)}) collective-permute-start(bf16[320,640]{1,0:T(8,128)(2,1)S(1)} %get-tuple-element.345), channel_id=1, source_target_pairs={{0,4},{1,5},{2,6},{3,7},{4,0},{5,1},{6,2},{7,3},{8,12},{9,13},{10,... | collective-permute-start | bytes 1228808 | tf_op jit(solution)/shard_map/ppermute | solution.py:468
  168.3 30.5 %collective-permute-start.43 = (bf16[320,640]{1,0:T(8,128)(2,1)S(1)}, bf16[320,640]{1,0:T(8,128)(2,1)S(1)}, u32[]{:S(2)}, u32[]{:S(2)}) collective-permute-start(bf16[320,640]{1,0:T(8,128)(2,1)S(1)} %pair_vo_a.1), channel_id=1, source_target_pairs={{0,16},{1,17},{2,18},{3,19},{4,20},{5,21},{6,22},{7,23},{8,24},{9,... | collective-permute-start | bytes 1228808 | tf_op jit(solution)/shard_map/ppermute | solution.py:468
  169.0 11.0 %collective-permute-start.41 = (bf16[128,1280]{1,0:T(8,128)(2,1)S(1)}, bf16[128,1280]{1,0:T(8,128)(2,1)S(1)}, u32[]{:S(2)}, u32[]{:S(2)}) collective-permute-start(bf16[128,1280]{1,0:T(8,128)(2,1)S(1)} %get-tuple-element.336), channel_id=1, source_target_pairs={{0,2},{1,3},{2,0},{3,1},{4,6},{5,7},{6,4},{7,5},{8,10},{9,11},{10,... | collective-permute-start | bytes 983048 | tf_op jit(solution)/shard_map/ppermute | solution.py:468
  179.0 19.8 %collective-permute-start.39 = (bf16[320,640]{1,0:T(8,128)(2,1)S(1)}, bf16[320,640]{1,0:T(8,128)(2,1)S(1)}, u32[]{:S(2)}, u32[]{:S(2)}) collective-permute-start(bf16[320,640]{1,0:T(8,128)(2,1)S(1)} %get-tuple-element.331), channel_id=1, source_target_pairs={{0,4},{1,5},{2,6},{3,7},{4,0},{5,1},{6,2},{7,3},{8,12},{9,13},{10,... | collective-permute-start | bytes 1228808 | tf_op jit(solution)/shard_map/ppermute | solution.py:468
  180.7 32.3 %collective-permute-start.44 = (bf16[176,640]{1,0:T(8,128)(2,1)S(1)}, bf16[176,640]{1,0:T(8,128)(2,1)S(1)}, u32[]{:S(2)}, u32[]{:S(2)}) collective-permute-start(bf16[176,640]{1,0:T(8,128)(2,1)S(1)} %get-tuple-element.355), channel_id=1, source_target_pairs={{0,24},{1,25},{2,26},{3,27},{4,28},{5,29},{6,30},{7,31},{8,16},{9,... | collective-permute-start | bytes 675848 | tf_op jit(solution)/shard_map/ppermute | solution.py:468
  183.2 29.8 %collective-permute-start.45 = (bf16[176,640]{1,0:T(8,128)(2,1)S(1)}, bf16[176,640]{1,0:T(8,128)(2,1)S(1)}, u32[]{:S(2)}, u32[]{:S(2)}) collective-permute-start(bf16[176,640]{1,0:T(8,128)(2,1)S(1)} %get-tuple-element.356), channel_id=1, source_target_pairs={{0,16},{1,17},{2,18},{3,19},{4,20},{5,21},{6,22},{7,23},{8,24},{9,... | collective-permute-start | bytes 675848 | tf_op jit(solution)/shard_map/ppermute | solution.py:468
  188.4 25.1 %collective-permute-start.46 = (bf16[176,640]{1,0:T(8,128)(2,1)S(1)}, bf16[176,640]{1,0:T(8,128)(2,1)S(1)}, u32[]{:S(2)}, u32[]{:S(2)}) collective-permute-start(bf16[176,640]{1,0:T(8,128)(2,1)S(1)} %get-tuple-element.362), channel_id=1, source_target_pairs={{0,8},{1,9},{2,10},{3,11},{4,12},{5,13},{6,14},{7,15},{8,0},{9,1},... | collective-permute-start | bytes 675848 | tf_op jit(solution)/shard_map/ppermute | solution.py:468
  198.8 12.8 %collective-permute-start.37 = (bf16[160,640]{1,0:T(8,128)(2,1)S(1)}, bf16[160,640]{1,0:T(8,128)(2,1)S(1)}, u32[]{:S(2)}, u32[]{:S(2)}) collective-permute-start(bf16[160,640]{1,0:T(8,128)(2,1)S(1)} %get-tuple-element.311), channel_id=1, source_target_pairs={{0,8},{1,9},{2,10},{3,11},{4,12},{5,13},{6,14},{7,15},{8,0},{9,1},... | collective-permute-start | bytes 614408 | tf_op jit(solution)/shard_map/ppermute | solution.py:468
  199.5 17.9 %collective-permute-start.48 = (bf16[160,640]{1,0:T(8,128)(2,1)S(1)}, bf16[160,640]{1,0:T(8,128)(2,1)S(1)}, u32[]{:S(2)}, u32[]{:S(2)}) collective-permute-start(bf16[160,640]{1,0:T(8,128)(2,1)S(1)} %get-tuple-element.368), channel_id=1, source_target_pairs={{0,8},{1,9},{2,10},{3,11},{4,12},{5,13},{6,14},{7,15},{8,0},{9,1},... | collective-permute-start | bytes 614408 | tf_op jit(solution)/shard_map/ppermute | solution.py:468
  (18 other events, 112.8 us)

commit v2 on v1

--- a/solution.py
+++ b/solution.py
@@ -272,14 +272,27 @@
     split_product(grad_pre, w_hidden, out_far, out_near)
 
 
-def spread_terms(term, keep, sends, depth, order):
-    if not sends:
-        keep[...] = term[...]
+PAIR_FIRST = (3, 1, 2, 0)
+RING_SENT, RING_KEPT = ((3, 1), (1, 1), (3, 0), (1, 0)), ((2, 1), (0, 1), (2, 0), (0, 0))
+
+
+def spread_terms(term, outs, depth):
+    if len(outs) == 1:
+        outs[0][...] = term[...]
         return
-    half = len(order) // len(sends)
-    for at, j in enumerate(order):
-        keep[pl.ds(at * depth, depth)] = term[pl.ds(2 * j * depth, depth)]
-        sends[at // half][pl.ds(at % half * depth, depth)] = term[pl.ds((2 * j + 1) * depth, depth)]
+    pair_sent, pair_kept, ring_sent, ring_kept = outs
+    cut = pair_kept.shape[1]
+
+    def copy(out, at, block, columns):
+        out[pl.ds(at * depth, depth)] = term[pl.ds(block * depth, depth), columns]
+
+    for at, j in enumerate(PAIR_FIRST):
+        copy(pair_sent, at, 2 * j + 1, slice(0, cut))
+        copy(pair_kept, at, 2 * j, slice(0, cut))
+    for at in range(4):
+        (j, i), (k, m) = RING_SENT[at], RING_KEPT[at]
+        copy(ring_sent, at, 2 * j + i, slice(cut, None))
+        copy(ring_kept, at, 2 * k + m, slice(cut, None))
 
 
 def two_terms(left_one, right_one, left_two, right_two, term):
@@ -288,24 +301,12 @@
     term[...] = pack(first, second).astype(BF16)
 
 
-def down_kernel(depth, order, s, h, g, act, grad_pre, w_down, far, near, b_hidden, keep, *refs):
-    *sends, term = refs
+def down_kernel(depth, s, h, g, act, grad_pre, w_down, far, near, b_hidden, *refs):
+    *outs, term = refs
     two_terms(h, grad_pre, g, act, term)
-    spread_terms(term, keep, sends, depth, order)
+    spread_terms(term, outs, depth)
     b_hidden[...] = jnp.sum(grad_pre[...].astype(F32), axis=0, keepdims=True)
     split_product(act, w_down, far, near)
-
-
-def pair_kernel(start, count, s, own, *refs):
-    gots, outs = refs[:count], refs[count:]
-    row = 0
-    for out in outs:
-        rows = out.shape[0]
-        value = own[pl.ds(start + row, rows)].astype(F32)
-        for got in gots:
-            value = value + got[pl.ds(row, rows)].astype(F32)
-        out[...] = value.astype(out.dtype)
-        row += rows
 
 
 def owned_kernel(n_got, s, keep, *refs):
@@ -326,13 +327,13 @@
     sums[6:7] = jnp.sum(grad_h * normed, axis=0, keepdims=True)
 
 
-def grad_context_kernel(depth, order, head_size, s, p0, p1, p2, p3, w_output, turned, context, h, *refs):
-    grad_context, grad_value, gm, keep, *sends, term = refs
+def grad_context_kernel(depth, head_size, s, p0, p1, p2, p3, w_output, turned, context, h, *refs):
+    grad_context, grad_value, gm, *outs, term = refs
     join((p0, p1, p2, p3), gm)
     grad_context[...] = dot(gm[...], w_output[...]).astype(BF16)
     grad_value[...] = mixed_heads(turned, grad_context[...], head_size, NN).astype(BF16)
     two_terms(h, grad_value, gm, context, term)
-    spread_terms(term, keep, sends, depth, order)
+    spread_terms(term, outs, depth)
 
 
 def grad_scores_kernel(head_size, s, turned, grad_context, v_low, q_low, k_low, q_raw, biases, *refs):
@@ -361,11 +362,11 @@
 
 
 def grad_first_kernel(
-    n_dp, depth, order, s, grad_qk, w_qk, grad_value, w_value, h, sums_in, sums_q, b_hidden, slope, *refs
+    n_dp, depth, s, grad_qk, w_qk, grad_value, w_value, h, sums_in, sums_q, b_hidden, slope, *refs
 ):
-    far, near, sums, keep, *sends, term = refs
+    far, near, sums, *outs, term = refs
     term[...] = dot(h[...], grad_qk[...], TN).astype(BF16)
-    spread_terms(term, keep, sends, depth, order)
+    spread_terms(term, outs, depth)
     mine, place = s[0], s[1]
     gained = split_product(grad_qk, w_qk, far, near, (grad_value, w_value), h) / sums_in[0:1]
     row = lax.broadcasted_iota(jnp.int32, sums.shape, 0)
@@ -385,45 +386,44 @@
     for number in range(1, local_width // head_size):
         total = total + scale[:, number * head_size : (number + 1) * head_size]
     sums[3:4, :head_size] = total * slope[...]
-    if sends:
-        sends[0][pl.ds(sends[0].shape[0] - 16, 16)] = fold(sums[...])
-
-
-def fold(vectors):
-    half = vectors.shape[1] // 2
-    return jnp.concatenate([vectors[:, :half], vectors[:, half:]], axis=0).astype(BF16)
-
-
-def unfold(rows):
-    return jnp.concatenate([rows[:8], rows[8:]], axis=1)
-
-
-def pair_first_kernel(depth, s, own, got, vectors, one, two, small):
-    last = got.shape[0] - 16
-    low = fold(vectors[...]).astype(F32) + got[pl.ds(last, 16)].astype(F32)
-    low = low.astype(BF16)
-    small[...] = low
-    for row, out in ((0, one), (depth, two)):
-        value = own[pl.ds(row, depth)].astype(F32) + got[pl.ds(row, depth)].astype(F32)
-        out[pl.ds(0, depth)] = value.astype(BF16)
-        out[pl.ds(depth, 16)] = low
-
-
-def pair_last_kernel(depth, start, s, own, got, small, out, zero):
-    value = own[pl.ds(start, 2 * depth)].astype(F32) + got[...].astype(F32)
-    out[pl.ds(0, depth)] = value[:depth].astype(BF16)
-    out[pl.ds(depth, 16)] = small[...]
-    zero[...] = value[depth:]
-
-
-def vector_far_kernel(depth, s, three, two, out):
-    at = pl.ds(depth, 16)
-    out[...] = two[at].astype(F32) + three[at].astype(F32)
-
-
-def vector_kernel(depth, s, small, far, one, out):
-    near = small[...].astype(F32) + one[pl.ds(depth, 16)].astype(F32)
-    out[...] = unfold(near + far[...])
+    if len(outs) > 1:
+        outs[0][pl.ds(4 * depth, 32)] = fold(sums[...], outs[0].shape[1])
+
+
+def fold(vectors, width):
+    part = vectors.shape[1] // 4
+    rows = jnp.concatenate([vectors[:, k * part : (k + 1) * part] for k in range(4)], axis=0)
+    return jnp.concatenate([rows, jnp.zeros((32, width - part), F32)], axis=1).astype(BF16)
+
+
+def unfold(rows, part):
+    return jnp.concatenate([rows[8 * k : 8 * k + 8, :part] for k in range(4)], axis=1)
+
+
+def first_sum_kernel(s, pair_kept, pair_got, ring_kept, ring_got, *refs):
+    *given, pair_out, pair_mid, ring_out, ring_mid = refs
+    half = pair_mid.shape[0]
+    value = pair_kept[...].astype(F32) + pair_got[pl.ds(0, 2 * half)].astype(F32)
+    pair_out[pl.ds(0, half)] = value[:half].astype(BF16)
+    pair_mid[...] = value[half:]
+    value = ring_kept[...].astype(F32) + ring_got[...].astype(F32)
+    ring_out[...] = value[:half].astype(BF16)
+    ring_mid[...] = value[half:]
+    if given:
+        low = fold(given[0][...], pair_out.shape[1]).astype(F32) + pair_got[pl.ds(2 * half, 32)].astype(F32)
+        pair_out[pl.ds(half, 32)] = low.astype(BF16)
+
+
+def second_sum_kernel(s, pair_mid, pair_got, ring_mid, ring_got, *refs):
+    half, depth, cut = pair_mid.shape[0], pair_mid.shape[0] // 2, pair_mid.shape[1]
+    given, out, zero = refs[: len(refs) // 3], refs[len(refs) // 3], refs[len(refs) // 3 + 1]
+    pair = pair_mid[...] + pair_got[pl.ds(0, half)].astype(F32)
+    ring = ring_mid[...] + ring_got[...].astype(F32)
+    out[:, :cut], out[:, cut:] = pair[:depth].astype(BF16), ring[:depth].astype(BF16)
+    zero[:, :cut], zero[:, cut:] = pair[depth:], ring[depth:]
+    if given:
+        at, vectors = pl.ds(half, 32), refs[-1]
+        vectors[...] = unfold(given[0][at].astype(F32) + pair_got[at].astype(F32), vectors.shape[1] // 4)
 
 
 def total_kernel(s, one, two, *outs):
@@ -498,7 +498,8 @@
         while bit < self.n_dp and self.wide:
             found.append(lambda d, t, bit=bit: (d ^ bit, t))
             bit *= 2
-        return found + [lambda d, t: (d, t ^ 1), lambda d, t: (d, t ^ 2)]
+        far = [] if self.wide else [lambda d, t: (d ^ 4, t)]
+        return found + [lambda d, t: (d, t ^ 1), lambda d, t: (d, t ^ 2)] + far
 
 
 def body(
@@ -586,7 +587,6 @@
     )
     own_vo = pack_two("vo", weight_value, weight_output.T)
     own_hd = pack_two("hd", weight_hidden, weight_down.T)
-    order = (3, 2, 1, 0)
 
     def stack(*blocks):
         rows = sum(block.shape[0] for block in blocks)
@@ -599,19 +599,19 @@
         qk_one, qk_two = links.along(own_qk, 2), links.along(own_qk, 4)
         h_own, own_vo, own_hd, qk_one, qk_two = tie(h_own, own_vo, own_hd, qk_one, qk_two)
         h_chip = links.chip(h_own)
-        qk_three = links.along(qk_one, 4)
+        qk_three = links.along(qk_two, 2)
         near_qk_pair = links.pair(stack(own_qk, qk_one))
-        own_vo, qk_three = tie(own_vo, qk_three)
+        vo_one, vo_two = links.along(own_vo, 2), links.along(own_vo, 4)
         far_stack = stack(qk_two, qk_three)
-        far_stack, near_qk_pair, h_chip = tie(far_stack, near_qk_pair, h_chip)
+        far_stack, near_qk_pair, h_chip, vo_one, vo_two = tie(far_stack, near_qk_pair, h_chip, vo_one, vo_two)
         h_one = h_own, h_chip, links.core(h_own), links.core(h_chip)
         far_qk_pair = links.pair(far_stack)
-        vo_one, vo_two = links.along(own_vo, 2), links.along(own_vo, 4)
+        vo_three = links.along(vo_two, 2)
+        near_vo = stack(own_vo, vo_one)
         qk = [own_qk, qk_one, qk_two, qk_three], [near_qk_pair, far_qk_pair]
-        h_one, qk, vo_one, vo_two = tie(h_one, qk, vo_one, vo_two)
-        near_vo_pair = links.pair(stack(own_vo, vo_one))
-        vo_three = links.along(vo_one, 4)
-        hd_one = links.along(own_hd, 2)
+        h_one, qk, vo_three, near_vo = tie(h_one, qk, vo_three, near_vo)
+        near_vo_pair = links.pair(near_vo)
+        hd_one, hd_two = links.along(own_hd, 2), links.along(own_hd, 4)
         grad_chip = links.chip(grad_own)
     n_qk = len(qk[0]), len(qk[0]) + len(qk[1])
     q_raw, q_low, k_low, h_all, w_qk, turned = run(
@@ -633,17 +633,13 @@
         scratch=sems,
     )
     if not wide:
-        turned, near_vo_pair, vo_three, hd_one, grad_chip = tie(
-            turned, near_vo_pair, vo_three, hd_one, grad_chip
-        )
+        turned, near_vo_pair, hd_one, hd_two, grad_chip = tie(turned, near_vo_pair, hd_one, hd_two, grad_chip)
         far_vo_pair = links.pair(stack(vo_two, vo_three))
-        hd_two = links.along(own_hd, 4)
+        hd_three = links.along(hd_two, 2)
         grad_rows = grad_own, grad_chip, links.core(grad_own), links.core(grad_chip)
         vo = [own_vo, vo_one, vo_two, vo_three], [near_vo_pair, far_vo_pair]
-        grad_rows, own_hd, hd_one, hd_two = tie(grad_rows, own_hd, hd_one, hd_two)
+        turned, vo, grad_rows, hd_three = tie(turned, vo, grad_rows, hd_three)
         near_hd_pair = links.pair(stack(own_hd, hd_one))
-        hd_three = links.along(hd_one, 4)
-        turned, vo, grad_rows = tie(turned, vo, grad_rows)
     n_vo = len(vo[0]), len(vo[0]) + len(vo[1])
     v_low, context, far, near, w_value, w_output = run(
         "context",
@@ -658,14 +654,17 @@
         scratch=term + sems,
     )
 
-    def core_half(far, near):
-        return run("middle", middle_kernel, [rows_low, rows_full], near, links.core(far))
-
-    if not wide:
-        far, hd_three, near_hd_pair = tie(far, hd_three, near_hd_pair)
-    send, keep = core_half(far, near)
-    got = links.chip(send)
-    if not wide:
+    def core_half(far, near, *extra):
+        got, *extra = tie(links.core(far), *extra)
+        return list(run("middle", middle_kernel, [rows_low, rows_full], near, got)) + list(extra)
+
+    if wide:
+        send, keep = core_half(far, near)
+        got = links.chip(send)
+    else:
+        far, near_hd_pair = tie(far, near_hd_pair)
+        send, keep = core_half(far, near)
+        got = links.chip(send)
         far_hd_pair = links.pair(stack(hd_two, hd_three))
         hd = [own_hd, hd_one, hd_two, hd_three], [near_hd_pair, far_hd_pair]
         got, hd = tie(got, hd)
@@ -691,15 +690,14 @@
         biases,
         grad_act,
     )
-    send, keep = core_half(far, near)
-    act, send = tie(act, send)
-    got = links.chip(send)
-    half = ((n_dp // 4 * depth, both), BF16)
-    ridden = ((depth + 16, both), BF16)
-    terms = [((width, both), BF16)] if wide else [((n_dp // 2 * depth, both), BF16), half, half]
-    far, near, grad_b_hidden, *terms_hd = run(
+    cut = 3 * both // 5
+    tall_sent = n_dp // 2 * depth
+    terms = [((width, both), BF16)]
+    if not wide:
+        terms = [((tall_sent, c), BF16) for c in (cut, cut, both - cut, both - cut)]
+    mix_far, mix_near, grad_b_hidden, *terms_hd = run(
         "down",
-        bind(down_kernel, depth, order),
+        bind(down_kernel, depth),
         [*split, ((1, local_width), F32), *terms],
         h_two_all,
         grad_all,
@@ -708,24 +706,33 @@
         w_down,
         scratch=term,
     )
-    got, terms_hd = tie(got, terms_hd)
-
-    def pair_sum(name, start, outs, own, *gots):
-        return run("pair_" + name, bind(pair_kernel, start, len(gots)), outs, own, *gots)
+    send, keep, terms_hd = core_half(far, near, terms_hd)
+    got = links.chip(send)
+
+    def first_send(terms):
+        return [links.pair(terms[0]), links.along(terms[2], 2)]
+
+    def first_sum(name, terms, got, given=()):
+        rows = tall_sent // 2
+        extra = 32 if given else 0
+        outs = [((rows + extra, cut), BF16), ((rows, cut), F32), ((rows, both - cut), BF16), ((rows, both - cut), F32)]
+        return run("first_" + name, first_sum_kernel, outs, terms[1], got[0], terms[3], got[1], *given)
+
+    def second_send(sums):
+        return [links.along(sums[0], 2), links.pair(sums[2])]
+
+    def second_sum(name, sums, got, given=False):
+        outs = packed + [((depth, both), F32)] + ([vector] if given else [])
+        more = sums[:1] if given else []
+        return run("second_" + name, second_sum_kernel, outs, sums[1], got[0], sums[3], got[1], *more)
 
     def owned(name, *parts):
         outs = [((depth, local_width), F32)] * 2
         return run("owned_" + name, bind(owned_kernel, len(parts) - 1), outs, *parts)
 
-    def first_far(name, terms, got):
-        return pair_sum(name + "_a", 0, [half], terms[0], got)[0]
-
-    def then_near(name, terms, got_pair, got_far):
-        outs = packed + [((depth, both), F32)]
-        sent, zero = pair_sum(name + "_b", half[0][0], outs, terms[0], got_pair, got_far)
-        return zero, links.along(sent, 2)
-
-    sent_hd = [links.pair(part) for part in terms_hd[1:]]
+    if not wide:
+        got_hd = first_send(terms_hd)
+        got, got_hd = tie(got, got_hd)
     grad_mid_low, grad_mid, sums = run(
         "grad_middle",
         grad_middle_kernel,
@@ -740,15 +747,17 @@
         grad_mid_rows = links.gather_tensor(grad_mid_low)
     else:
         grad_mid_chip = links.chip(grad_mid_low)
-        grad_mid_chip, sent_hd[0] = tie(grad_mid_chip, sent_hd[0])
-        far_sum = links.along(first_far("hd", terms_hd, sent_hd[0]), 4)
+        sums_hd = first_sum("hd", terms_hd, got_hd)
+        got_hd = second_send(sums_hd)
+        grad_mid_chip, got_hd = tie(grad_mid_chip, got_hd)
+        sent_hd, zero_hd = second_sum("hd", sums_hd, got_hd)
         grad_mid_rows = grad_mid_low, grad_mid_chip, links.core(grad_mid_low), links.core(grad_mid_chip)
-    grad_mid_rows, far = tie(grad_mid_rows, far)
-    mix_send, mix_keep = core_half(far, near)
+    grad_mid_rows, mix_far = tie(grad_mid_rows, mix_far)
+    mix_send, mix_keep = core_half(mix_far, mix_near)
     mix_got = links.chip(mix_send)
     grad_context, grad_value, _, *terms_vo = run(
         "grad_context",
-        bind(grad_context_kernel, depth, order, head_size),
+        bind(grad_context_kernel, depth, head_size),
         [part, part, whole_rows, *terms],
         *grad_mid_rows,
         w_output,
@@ -757,8 +766,10 @@
         h_all,
         scratch=term,
     )
-    grad_context, sent_hd[1:] = tie(grad_context, sent_hd[1:])
-    sent_vo = [links.pair(part) for part in terms_vo[1:2]]
+    if not wide:
+        got_vo = first_send(terms_vo)
+        grad_context, sent_hd = tie(grad_context, sent_hd)
+        part_hd = links.along(sent_hd, 4)
     grad_qk, sums_q = run(
         "grad_scores",
         bind(grad_scores_kernel, head_size),
@@ -779,17 +790,16 @@
     if wide:
         grad_qk, mix_got = tie(grad_qk, mix_got)
     else:
-        grad_qk, sent_vo[0], mix_got, far_sum = tie(grad_qk, sent_vo[0], mix_got, far_sum)
-        zero_hd, part_hd = then_near("hd", terms_hd, sent_hd[1], far_sum)
-        sent = first_far("vo", terms_vo, sent_vo[0])
-        grad_qk, zero_hd, sent = tie(grad_qk, zero_hd, sent)
-        far_sum = links.along(sent, 4)
+        grad_qk, mix_got, part_hd, got_vo = tie(grad_qk, mix_got, part_hd, got_vo)
+        sums_vo = first_sum("vo", terms_vo, got_vo)
+        grad_qk, *sums_vo = tie(grad_qk, *sums_vo)
+        got_vo = second_send(sums_vo)
     terms_first = list(terms)
     if not wide:
-        terms_first[1] = ((half[0][0] + 16, both), BF16)
+        terms_first[0] = ((tall_sent + 32, cut), BF16)
     far, near, sums, *terms_qk = run(
         "grad_first",
-        bind(grad_first_kernel, n_dp, depth, order),
+        bind(grad_first_kernel, n_dp, depth),
         [*split, vector, *terms_first],
         grad_qk,
         w_qk,
@@ -805,54 +815,32 @@
     def exchange(value, step):
         return run("add", add_kernel, [vector], value, links.move(value, step))[0]
 
-    if not wide:
-        far, sent_qk = tie(far, terms_qk[1:])
-        sent_qk = [links.pair(part) for part in sent_qk]
-        sent_qk[0], last_vo = tie(sent_qk[0], terms_vo[2])
-        sent_vo.append(links.pair(last_vo))
-    send, keep = core_half(far, near)
-    got = links.chip(send)
+    total = sums
     if wide:
-        total = sums
+        send, keep = core_half(far, near)
+        got = links.chip(send)
     else:
-        got, sent_qk[0] = tie(got, sent_qk[0])
-        one, two, small = run(
-            "pair_qk_a",
-            bind(pair_first_kernel, depth),
-            [ridden, ridden, ((16, both), BF16)],
-            terms_qk[0],
-            sent_qk[0],
-            sums,
-        )
-        got, one, two = tie(got, one, two)
-        three, two = links.along(one, 6), links.along(two, 4)
+        got_qk = first_send(terms_qk)
+        far, got_vo = tie(far, got_vo)
+        sent_vo, zero_vo = second_sum("vo", sums_vo, got_vo)
+        send, keep, sent_vo = core_half(far, near, sent_vo)
+        got = links.chip(send)
+        part_vo = links.along(sent_vo, 4)
+        (output,) = run("output", bind(output_kernel, n_dp), [rows_low], mix_keep, mix_got, x_one, vectors)
+        grad_hidden, grad_down = owned("hd", zero_hd, part_hd)
+        got, output, grad_hidden = tie(got, output, grad_hidden)
+        got_qk, part_vo = tie(got_qk, part_vo)
+        sums_qk = first_sum("qk", terms_qk, got_qk, [sums])
+        got_qk = second_send(sums_qk)
+        sent_qk, zero_qk, total = second_sum("qk", sums_qk, got_qk, True)
+        far_qk = links.along(sent_qk, 4)
+        got, zero_vo, total = tie(got, zero_vo, total)
     (grad_in,) = run("last", bind(last_kernel, n_dp), [rows_low], keep, got, x_own, grad_mid, vectors)
-    if not wide:
-        grad_in, sent_qk[1] = tie(grad_in, sent_qk[1])
-        one, zero_qk = run(
-            "pair_qk_b",
-            bind(pair_last_kernel, depth, half[0][0]),
-            [ridden, ((depth, both), F32)],
-            terms_qk[0],
-            sent_qk[1],
-            small,
-        )
-        one = links.along(one, 2)
-        zero_qk, far_sum = tie(zero_qk, far_sum)
-        zero_vo, part_vo = then_near("vo", terms_vo, sent_vo[1], far_sum)
-        mix_got, zero_vo = tie(mix_got, zero_vo)
-    (output,) = run("output", bind(output_kernel, n_dp), [rows_low], mix_keep, mix_got, x_one, vectors)
-    if not wide:
-        part_hd, output = tie(part_hd, output)
-        grad_hidden, grad_down = owned("hd", zero_hd, part_hd)
-        three, two, grad_hidden = tie(three, two, grad_hidden)
-        (far_rows,) = run("vector_a", bind(vector_far_kernel, depth), [((16, both), F32)], three, two)
-        (total,) = run("vector_b", bind(vector_kernel, depth), [vector], small, far_rows, one)
+    if wide:
+        (output,) = run("output", bind(output_kernel, n_dp), [rows_low], mix_keep, mix_got, x_one, vectors)
     steps = links.steps()
     for step in steps[:-1]:
         total = exchange(total, step)
-    if not wide:
-        total, zero_qk = tie(total, zero_qk)
     moved = links.move(total, steps[-1])
     tall_vector = (tall, F32)
     *totals, total_scale = run(
@@ -865,7 +853,7 @@
         grad_query, grad_key = links.scatter_wide(terms_qk[0])
     else:
         grad_output_v, grad_output_o = owned("vo", zero_vo, part_vo)
-        grad_query, grad_key = owned("qk", zero_qk, three, two, one)
+        grad_query, grad_key = owned("qk", zero_qk, far_qk)
     return (
         output,
         grad_in,

time: 222 us -> 204 us (0.919)
  waiting for transfers between devices: 108 us -> 81.3 us
  starting transfers between devices: 45.1 us -> 54 us
    ppermute x50 -> x53, waiting for transfers between devices: 108 us -> 81.3 us  [move(): return lax.ppermute(value, AXES, pairs)]
    ppermute x50 -> x53, starting transfers between devices: 45.1 us -> 54 us  [move(): return lax.ppermute(value, AXES, pairs)]
    pallas_call x39 -> x38, Pallas kernels: 65.5 us -> 66.3 us  [call(): pl.pallas_call(kernel, name=name, out_shape=outs, in_specs=[pl.BlockSpec(...]
  transfers between devices with their start and end apart: 50 -> 53, of which waited for: 24 -> 25; matrix products, arithmetic and copies ran while one was open for 0% -> 0% of each run, Pallas kernels for 24% -> 28%
where the time goes in v2:
time: 204 us
  waiting for transfers between devices  81.3 us (40%)
  Pallas kernels  66.3 us (32%)
  starting transfers between devices  54 us (26%)
    ppermute x53, waiting for transfers between devices, move(): return lax.ppermute(value, AXES, pairs)  81.3 us
    pallas_call x38, Pallas kernels, call(): pl.pallas_call(kernel, name=name, out_shape=outs, in_specs=[pl.BlockSpec(...  66.3 us
    ppermute x53, starting transfers between devices, move(): return lax.ppermute(value, AXES, pairs)  54 us
  transfers between devices with their start and end apart: 53, of which 25 were waited for; matrix products, arithmetic and copies ran while one was open for 0% of the time, Pallas kernels for 28%

profile of v2, /device:TPU:0, one launch (start us, length us, event | category | flops | bytes accessed | tf_op | source)
XLA Modules:
  0.0 204.0 jit_solution(9902283723837351841)
XLA Ops:
  3.0 4.1 %collective-permute-start.1 = (bf16[160,640]{1,0:T(8,128)(2,1)S(1)}, bf16[160,640]{1,0:T(8,128)(2,1)S(1)}, u32[]{:S(2)}, u32[]{:S(2)}) collective-permute-start(bf16[160,640]{1,0:T(8,128)(2,1)S(1)} %pack_qk.1.refs_0_.refs_6_), channel_id=1, source_target_pairs={{0,16},{1,17},{2,18},{3,19},{4,20},{5,21},{6,22},{7,23},{8,24},{9,... | collective-permute-start | bytes 614408 | tf_op jit(solution)/shard_map/ppermute | solution.py:468
  12.7 3.2 %prepare.1 = (bf16[128,1280]{1,0:T(8,128)(2,1)S(1)}, bf16[128,1280]{1,0:T(8,128)(2,1)S(1)}, bf16[128,1280]{1,0:T(8,128)(2,1)S(1)}, f32[8,1280]{1,0:T(8,128)S(1)}, f32[8,320]{1,0:T(8,128)S(1)}) custom-call(s32[3]{0:T(128)S(1)} %pad_add_fusion.refs_0_.s, f32[1,320]{1,0:T(1,128)S(1)} %broadcast_in_dim_tile.3.refs_1_, bf16[128,1280]{1,0:T(8,128)(2,1)} %refs_2_.1, ...), custom_call_target="tpu_custom_call" | custom-call | flops 1000000 | bytes 1726720 | tf_op jit(solution)/shard_map/prepare/pallas_call | solution.py:30
  17.4 1.6 collective-permute-start.3
  22.0 2.3 %collective-permute-start.6 = (bf16[160,640]{1,0:T(8,128)(2,1)S(1)}, bf16[160,640]{1,0:T(8,128)(2,1)S(1)}, u32[]{:S(2)}, u32[]{:S(2)}) collective-permute-start(bf16[160,640]{1,0:T(8,128)(2,1)S(1)} %pack_vo.1.refs_0_.refs_4_), channel_id=1, source_target_pairs={{0,16},{1,17},{2,18},{3,19},{4,20},{5,21},{6,22},{7,23},{8,24},{9,... | collective-permute-start | bytes 614408 | tf_op jit(solution)/shard_map/ppermute | solution.py:468
  24.3 8.3 %collective-permute-done.2.refs_1_.refs_9_ = bf16[160,640]{1,0:T(8,128)(2,1)S(1)} collective-permute-done((bf16[160,640]{1,0:T(8,128)(2,1)S(1)}, bf16[160,640]{1,0:T(8,128)(2,1)S(1)}, u32[]{:S(2)}, u32[]{:S(2)}) %collective-permute-start.2) | collective-permute-done | bytes 204832 | tf_op jit(solution)/shard_map/ppermute | solution.py:468
  33.2 1.9 collective-permute-done.5.refs_1_.refs_5_
  38.1 5.0 %collective-permute-done.10.refs_1_.refs_7_ = bf16[160,640]{1,0:T(8,128)(2,1)S(1)} collective-permute-done((bf16[160,640]{1,0:T(8,128)(2,1)S(1)}, bf16[160,640]{1,0:T(8,128)(2,1)S(1)}, u32[]{:S(2)}, u32[]{:S(2)}) %collective-permute-start.10) | collective-permute-done | bytes 204832 | tf_op jit(solution)/shard_map/ppermute | solution.py:468
  45.8 3.3 %collective-permute-start.13 = (bf16[160,640]{1,0:T(8,128)(2,1)S(1)}, bf16[160,640]{1,0:T(8,128)(2,1)S(1)}, u32[]{:S(2)}, u32[]{:S(2)}) collective-permute-start(bf16[160,640]{1,0:T(8,128)(2,1)S(1)} %pack_hd.1.refs_0_.refs_5_), channel_id=1, source_target_pairs={{0,16},{1,17},{2,18},{3,19},{4,20},{5,21},{6,22},{7,23},{8,24},{9,... | collective-permute-start | bytes 614408 | tf_op jit(solution)/shard_map/ppermute | solution.py:468
  49.1 1.9 collective-permute-start.12
  53.2 6.3 %attend.1 = (f32[512,320]{1,0:T(8,128)S(1)}, bf16[512,320]{1,0:T(8,128)(2,1)S(1)}, bf16[512,320]{1,0:T(8,128)(2,1)S(1)}, bf16[512,1280]{1,0:T(8,128)(2,1)S(1)}, ...) custom-call(s32[3]{0:T(128)S(1)} %pad_add_fusion.refs_0_.s, ...), custom_call_target="tpu_custom_call" | custom-call | flops 1000000 | bytes 9316352 | tf_op jit(solution)/shard_map/attend/pallas_call | solution.py:30
  62.3 2.4 %collective-permute-done.15.refs_9_ = bf16[320,640]{1,0:T(8,128)(2,1)S(1)} collective-permute-done((bf16[320,640]{1,0:T(8,128)(2,1)S(1)}, bf16[320,640]{1,0:T(8,128)(2,1)S(1)}, u32[]{:S(2)}, u32[]{:S(2)}) %collective-permute-start.15) | collective-permute-done | bytes 409632 | tf_op jit(solution)/shard_map/ppermute | solution.py:468
  64.7 3.4 %collective-permute-done.18.refs_1_.refs_8_ = bf16[160,640]{1,0:T(8,128)(2,1)S(1)} collective-permute-done((bf16[160,640]{1,0:T(8,128)(2,1)S(1)}, bf16[160,640]{1,0:T(8,128)(2,1)S(1)}, u32[]{:S(2)}, u32[]{:S(2)}) %collective-permute-start.18) | collective-permute-done | bytes 204832 | tf_op jit(solution)/shard_map/ppermute | solution.py:468
  68.2 5.6 %context.1 = (bf16[512,320]{1,0:T(8,128)(2,1)S(1)}, bf16[512,320]{1,0:T(8,128)(2,1)S(1)}, bf16[256,1280]{1,0:T(8,128)(2,1)S(1)}, f32[256,1280]{1,0:T(8,128)S(1)}...) custom-call(s32[3]{0:T(128)S(1)} %pad_add_fusion.refs_0_.s, ...), custom_call_target="tpu_custom_call" | custom-call | flops 1000000 | bytes 9316352 | tf_op jit(solution)/shard_map/context/pallas_call | solution.py:30
  78.3 8.1 %collective-permute-done.22.refs_10_ = bf16[320,640]{1,0:T(8,128)(2,1)S(1)} collective-permute-done((bf16[320,640]{1,0:T(8,128)(2,1)S(1)}, bf16[320,640]{1,0:T(8,128)(2,1)S(1)}, u32[]{:S(2)}, u32[]{:S(2)}) %collective-permute-start.22) | collective-permute-done | bytes 409632 | tf_op jit(solution)/shard_map/ppermute | solution.py:468
  89.0 7.6 %collective-permute-done.23.p1 = bf16[128,1280]{1,0:T(8,128)(2,1)S(1)} collective-permute-done((bf16[128,1280]{1,0:T(8,128)(2,1)S(1)}, bf16[128,1280]{1,0:T(8,128)(2,1)S(1)}, u32[]{:S(2)}, u32[]{:S(2)}) %collective-permute-start.23) | collective-permute-done | bytes 327712 | tf_op jit(solution)/shard_map/ppermute | solution.py:468
  96.6 4.0 %grad_act.1 = (f32[512,320]{1,0:T(8,128)S(1)}, bf16[512,1280]{1,0:T(8,128)(2,1)S(1)}, bf16[1280,320]{1,0:T(8,128)(2,1)S(1)}, bf16[1280,320]{1,0:T(8,128)(2,1)S(1)}) custom-call(s32[3]{0:T(128)S(1)} %pad_add_fusion.refs_0_.s, bf16[128,1280]{1,0:T(8,128)(2,1)S(1)} %get-tuple-element.253.refs_1_.grad, bf16[128,1280]{1,0:T(8,128)(2,1)S(1)} %collective-permute-done.14.refs_2_, ...), custom_call_target="tpu_custom_call" | custom-call | flops 1000000 | bytes 6553600 | tf_op jit(solution)/shard_map/grad_act/pallas_call | solution.py:30
  100.6 2.3 %hidden.1 = (bf16[256,1280]{1,0:T(8,128)(2,1)S(1)}, f32[256,1280]{1,0:T(8,128)S(1)}, bf16[512,320]{1,0:T(8,128)(2,1)S(1)}, bf16[512,320]{1,0:T(8,128)(2,1)S(1)}, bf16[512,1280]{1,0:T(8,128)(2,1)S(1)}) custom-call(s32[3]{0:T(128)S(1)} %pad_add_fusion.refs_0_.s, bf16[128,1280]{1,0:T(8,128)(2,1)S(1)} %get-tuple-element.252.p0, ...), custom_call_target="tpu_custom_call" | custom-call | flops 1000000 | bytes 6727680 | tf_op jit(solution)/shard_map/hidden/pallas_call | solution.py:30
  103.5 3.0 %down.1 = (bf16[256,1280]{1,0:T(8,128)(2,1)S(1)}, f32[256,1280]{1,0:T(8,128)S(1)}, f32[1,320]{1,0:T(1,128)S(1)}, bf16[640,384]{1,0:T(8,128)(2,1)S(1)}, bf16[640,...) custom-call(s32[3]{0:T(128)S(1)} %pad_add_fusion.refs_0_.s, ...), custom_call_target="tpu_custom_call" | custom-call | flops 1000000 | bytes 7701760 | tf_op jit(solution)/shard_map/down/pallas_call | solution.py:30
  110.6 7.6 %collective-permute-done.27.got = bf16[128,1280]{1,0:T(8,128)(2,1)S(1)} collective-permute-done((bf16[128,1280]{1,0:T(8,128)(2,1)S(1)}, bf16[128,1280]{1,0:T(8,128)(2,1)S(1)}, u32[]{:S(2)}, u32[]{:S(2)}) %collective-permute-start.27) | collective-permute-done | bytes 327712 | tf_op jit(solution)/shard_map/ppermute | solution.py:468
  124.8 3.8 %collective-permute-done.32.ring_got = bf16[320,256]{1,0:T(8,128)(2,1)S(1)} collective-permute-done((bf16[320,256]{1,0:T(8,128)(2,1)S(1)}, bf16[320,256]{1,0:T(8,128)(2,1)S(1)}, u32[]{:S(2)}, u32[]{:S(2)}) %collective-permute-start.32) | collective-permute-done | bytes 163872 | tf_op jit(solution)/shard_map/ppermute | solution.py:468
  129.8 1.6 collective-permute-done.34.refs_4_
  131.5 5.3 %grad_context.1 = (bf16[512,320]{1,0:T(8,128)(2,1)S(1)}, bf16[512,320]{1,0:T(8,128)(2,1)S(1)}, bf16[512,1280]{1,0:T(8,128)(2,1)}, bf16[640,384]{1,0:T(8,128)(2,1...) custom-call(s32[3]{0:T(128)S(1)} %pad_add_fusion.refs_0_.s, ...), custom_call_target="tpu_custom_call" | custom-call | flops 1000000 | bytes 9469952 | tf_op jit(solution)/shard_map/grad_context/pallas_call | solution.py:30
  141.2 1.9 collective-permute-start.37
  143.1 5.5 %grad_scores.1 = (bf16[512,640]{1,0:T(8,128)(2,1)S(1)}, f32[8,320]{1,0:T(8,128)S(1)}) custom-call(s32[3]{0:T(128)S(1)} %pad_add_fusion.refs_0_.s, bf16[4,512,512]{2,1,0:T(8,128)(2,1)S(1)} %get-tuple-element.233.refs_2_.refs_6_.refs_1_, bf16[512,320]{1,0:T(8,128)(2,1)S(1)} %get-tuple-element.304.refs_2_, bf16[512,320]{1,0:T(8,128)(2,1)S(1)} %get-tuple-element.305.refs_3_, ...), custom_call_target="tpu_custom_call" | custom-call | flops 1000000 | bytes 4739072 | tf_op jit(solution)/shard_map/grad_scores/pallas_call | solution.py:30
  148.7 4.4 %collective-permute-done.37.refs_2_ = bf16[160,640]{1,0:T(8,128)(2,1)S(1)} collective-permute-done((bf16[160,640]{1,0:T(8,128)(2,1)S(1)}, bf16[160,640]{1,0:T(8,128)(2,1)S(1)}, u32[]{:S(2)}, u32[]{:S(2)}) %collective-permute-start.37) | collective-permute-done | bytes 204832 | tf_op jit(solution)/shard_map/ppermute | solution.py:468
  155.0 3.9 %grad_first.1 = (bf16[256,1280]{1,0:T(8,128)(2,1)S(1)}, f32[256,1280]{1,0:T(8,128)S(1)}, f32[8,1280]{1,0:T(8,128)S(1)}, bf16[672,384]{1,0:T(8,128)(2,1)S(1)}, bf...) custom-call(s32[3]{0:T(128)S(1)} %pad_add_fusion.refs_0_.s, ...), custom_call_target="tpu_custom_call" | custom-call | flops 1000000 | bytes 8474176 | tf_op jit(solution)/shard_map/grad_first/pallas_call | solution.py:30
  164.1 10.9 %collective-permute-done.45.ring_got = bf16[640,256]{1,0:T(8,128)(2,1)S(1)} collective-permute-done((bf16[640,256]{1,0:T(8,128)(2,1)S(1)}, bf16[640,256]{1,0:T(8,128)(2,1)S(1)}, u32[]{:S(2)}, u32[]{:S(2)}) %collective-permute-start.45) | collective-permute-done | bytes 327712 | tf_op jit(solution)/shard_map/ppermute | solution.py:468
  175.9 1.8 collective-permute-start.47
  180.7 4.0 %collective-permute-done.48.ring_got = bf16[320,256]{1,0:T(8,128)(2,1)S(1)} collective-permute-done((bf16[320,256]{1,0:T(8,128)(2,1)S(1)}, bf16[320,256]{1,0:T(8,128)(2,1)S(1)}, u32[]{:S(2)}, u32[]{:S(2)}) %collective-permute-start.48) | collective-permute-done | bytes 163872 | tf_op jit(solution)/shard_map/ppermute | solution.py:468
  186.9 1.9 output.1
  192.7 3.2 %collective-permute-done.51.two = f32[8,1280]{1,0:T(8,128)S(1)} collective-permute-done((f32[8,1280]{1,0:T(8,128)S(1)}, f32[8,1280]{1,0:T(8,128)S(1)}, u32[]{:S(2)}, u32[]{:S(2)}) %collective-permute-start.51) | collective-permute-done | bytes 40992 | tf_op jit(solution)/shard_map/ppermute | solution.py:468
  199.3 2.1 %last.1 = bf16[128,1280]{1,0:T(8,128)(2,1)} custom-call(s32[3]{0:T(128)S(1)} %pad_add_fusion.refs_0_.s, f32[128,1280]{1,0:T(8,128)S(1)} %get-tuple-element.351.refs_1_, bf16[128,1280]{1,0:T(8,128)(2,1)S(1)} %collective-permute-done.43.refs_2_, bf16[128,1280]{1,0:T(8,128)(2,1)S(1)} %get-tuple-element.250.x_own.refs_3_, ...), custom_call_target="tpu_custom_call" | custom-call | flops 1000000 | bytes 2334720 | tf_op jit(solution)/shard_map/last/pallas_call | solution.py:30
  (116 shorter events, 70.2 us)
Async XLA Ops:
  3.0 13.7 %collective-permute-start.1 = (bf16[160,640]{1,0:T(8,128)(2,1)S(1)}, bf16[160,640]{1,0:T(8,128)(2,1)S(1)}, u32[]{:S(2)}, u32[]{:S(2)}) collective-permute-start(bf16[160,640]{1,0:T(8,128)(2,1)S(1)} %pack_qk.1.refs_0_.refs_6_), channel_id=1, source_target_pairs={{0,16},{1,17},{2,18},{3,19},{4,20},{5,21},{6,22},{7,23},{8,24},{9,... | collective-permute-start | bytes 614408 | tf_op jit(solution)/shard_map/ppermute | solution.py:468
  7.1 9.8 %collective-permute-start = (bf16[160,640]{1,0:T(8,128)(2,1)S(1)}, bf16[160,640]{1,0:T(8,128)(2,1)S(1)}, u32[]{:S(2)}, u32[]{:S(2)}) collective-permute-start(bf16[160,640]{1,0:T(8,128)(2,1)S(1)} %pack_qk.1.refs_0_.refs_6_), channel_id=1, source_target_pairs={{0,8},{1,9},{2,10},{3,11},{4,12},{5,13},{6,14},{7,15},{8,0},{9,1},... | collective-permute-start | bytes 614408 | tf_op jit(solution)/shard_map/ppermute | solution.py:468
  17.4 17.7 %collective-permute-start.3 = (bf16[320,640]{1,0:T(8,128)(2,1)S(1)}, bf16[320,640]{1,0:T(8,128)(2,1)S(1)}, u32[]{:S(2)}, u32[]{:S(2)}) collective-permute-start(bf16[320,640]{1,0:T(8,128)(2,1)S(1)} %stack.19), channel_id=1, source_target_pairs={{0,4},{1,5},{2,6},{3,7},{4,0},{5,1},{6,2},{7,3},{8,12},{9,13},{10,... | collective-permute-start | bytes 1228808 | tf_op jit(solution)/shard_map/ppermute | solution.py:468
  19.1 16.0 %collective-permute-start.4 = (bf16[128,1280]{1,0:T(8,128)(2,1)S(1)}, bf16[128,1280]{1,0:T(8,128)(2,1)S(1)}, u32[]{:S(2)}, u32[]{:S(2)}) collective-permute-start(bf16[128,1280]{1,0:T(8,128)(2,1)S(1)} %get-tuple-element.213.refs_1_), channel_id=1, source_target_pairs={{0,2},{1,3},{2,0},{3,1},{4,6},{5,7},{6,4},{7,5},{8,10},{9,11},{10,... | collective-permute-start | bytes 983048 | tf_op jit(solution)/shard_map/ppermute | solution.py:468
  20.6 12.0 %collective-permute-start.2 = (bf16[160,640]{1,0:T(8,128)(2,1)S(1)}, bf16[160,640]{1,0:T(8,128)(2,1)S(1)}, u32[]{:S(2)}, u32[]{:S(2)}) collective-permute-start(bf16[160,640]{1,0:T(8,128)(2,1)S(1)} %collective-permute-done.1.refs_0_.refs_8_), channel_id=1, source_target_pairs={{0,8},{1,9},{2,10},{3,11},{4,12},{5,13},{6,14},{7,15},{8,0},{9,1},... | collective-permute-start | bytes 614408 | tf_op jit(solution)/shard_map/ppermute | solution.py:468
  22.0 11.2 %collective-permute-start.6 = (bf16[160,640]{1,0:T(8,128)(2,1)S(1)}, bf16[160,640]{1,0:T(8,128)(2,1)S(1)}, u32[]{:S(2)}, u32[]{:S(2)}) collective-permute-start(bf16[160,640]{1,0:T(8,128)(2,1)S(1)} %pack_vo.1.refs_0_.refs_4_), channel_id=1, source_target_pairs={{0,16},{1,17},{2,18},{3,19},{4,20},{5,21},{6,22},{7,23},{8,24},{9,... | collective-permute-start | bytes 614408 | tf_op jit(solution)/shard_map/ppermute | solution.py:468
  24.3 10.8 %collective-permute-start.5 = (bf16[160,640]{1,0:T(8,128)(2,1)S(1)}, bf16[160,640]{1,0:T(8,128)(2,1)S(1)}, u32[]{:S(2)}, u32[]{:S(2)}) collective-permute-start(bf16[160,640]{1,0:T(8,128)(2,1)S(1)} %pack_vo.1.refs_0_.refs_4_), channel_id=1, source_target_pairs={{0,8},{1,9},{2,10},{3,11},{4,12},{5,13},{6,14},{7,15},{8,0},{9,1},... | collective-permute-start | bytes 614408 | tf_op jit(solution)/shard_map/ppermute | solution.py:468
  35.1 9.6 %collective-permute-start.9 = (bf16[320,640]{1,0:T(8,128)(2,1)S(1)}, bf16[320,640]{1,0:T(8,128)(2,1)S(1)}, u32[]{:S(2)}, u32[]{:S(2)}) collective-permute-start(bf16[320,640]{1,0:T(8,128)(2,1)S(1)} %stack.18), channel_id=1, source_target_pairs={{0,4},{1,5},{2,6},{3,7},{4,0},{5,1},{6,2},{7,3},{8,12},{9,13},{10,... | collective-permute-start | bytes 1228808 | tf_op jit(solution)/shard_map/ppermute | solution.py:468
  44.7 14.8 %collective-permute-start.11 = (bf16[320,640]{1,0:T(8,128)(2,1)S(1)}, bf16[320,640]{1,0:T(8,128)(2,1)S(1)}, u32[]{:S(2)}, u32[]{:S(2)}) collective-permute-start(bf16[320,640]{1,0:T(8,128)(2,1)S(1)} %stack.20), channel_id=1, source_target_pairs={{0,4},{1,5},{2,6},{3,7},{4,0},{5,1},{6,2},{7,3},{8,12},{9,13},{10,... | collective-permute-start | bytes 1228808 | tf_op jit(solution)/shard_map/ppermute | solution.py:468
  45.2 14.3 %collective-permute-start.14 = (bf16[128,1280]{1,0:T(8,128)(2,1)S(1)}, bf16[128,1280]{1,0:T(8,128)(2,1)S(1)}, u32[]{:S(2)}, u32[]{:S(2)}) collective-permute-start(bf16[128,1280]{1,0:T(8,128)(2,1)S(1)} %get-tuple-element.253.refs_1_.grad), channel_id=1, source_target_pairs={{0,2},{1,3},{2,0},{3,1},{4,6},{5,7},{6,4},{7,5},{8,10},{9,11},{10,... | collective-permute-start | bytes 983048 | tf_op jit(solution)/shard_map/ppermute | solution.py:468
  45.8 13.7 %collective-permute-start.13 = (bf16[160,640]{1,0:T(8,128)(2,1)S(1)}, bf16[160,640]{1,0:T(8,128)(2,1)S(1)}, u32[]{:S(2)}, u32[]{:S(2)}) collective-permute-start(bf16[160,640]{1,0:T(8,128)(2,1)S(1)} %pack_hd.1.refs_0_.refs_5_), channel_id=1, source_target_pairs={{0,16},{1,17},{2,18},{3,19},{4,20},{5,21},{6,22},{7,23},{8,24},{9,... | collective-permute-start | bytes 614408 | tf_op jit(solution)/shard_map/ppermute | solution.py:468
  49.1 10.4 %collective-permute-start.12 = (bf16[160,640]{1,0:T(8,128)(2,1)S(1)}, bf16[160,640]{1,0:T(8,128)(2,1)S(1)}, u32[]{:S(2)}, u32[]{:S(2)}) collective-permute-start(bf16[160,640]{1,0:T(8,128)(2,1)S(1)} %pack_hd.1.refs_0_.refs_5_), channel_id=1, source_target_pairs={{0,8},{1,9},{2,10},{3,11},{4,12},{5,13},{6,14},{7,15},{8,0},{9,1},... | collective-permute-start | bytes 614408 | tf_op jit(solution)/shard_map/ppermute | solution.py:468
  51.6 13.2 %collective-permute-start.15 = (bf16[320,640]{1,0:T(8,128)(2,1)S(1)}, bf16[320,640]{1,0:T(8,128)(2,1)S(1)}, u32[]{:S(2)}, u32[]{:S(2)}) collective-permute-start(bf16[320,640]{1,0:T(8,128)(2,1)S(1)} %stack.21), channel_id=1, source_target_pairs={{0,4},{1,5},{2,6},{3,7},{4,0},{5,1},{6,2},{7,3},{8,12},{9,13},{10,... | collective-permute-start | bytes 1228808 | tf_op jit(solution)/shard_map/ppermute | solution.py:468
  60.1 13.7 %collective-permute-start.19 = (bf16[320,640]{1,0:T(8,128)(2,1)S(1)}, bf16[320,640]{1,0:T(8,128)(2,1)S(1)}, u32[]{:S(2)}, u32[]{:S(2)}) collective-permute-start(bf16[320,640]{1,0:T(8,128)(2,1)S(1)} %stack.22), channel_id=1, source_target_pairs={{0,4},{1,5},{2,6},{3,7},{4,0},{5,1},{6,2},{7,3},{8,12},{9,13},{10,... | collective-permute-start | bytes 1228808 | tf_op jit(solution)/shard_map/ppermute | solution.py:468
  74.4 11.9 %collective-permute-start.22 = (bf16[320,640]{1,0:T(8,128)(2,1)S(1)}, bf16[320,640]{1,0:T(8,128)(2,1)S(1)}, u32[]{:S(2)}, u32[]{:S(2)}) collective-permute-start(bf16[320,640]{1,0:T(8,128)(2,1)S(1)} %stack.23), channel_id=1, source_target_pairs={{0,4},{1,5},{2,6},{3,7},{4,0},{5,1},{6,2},{7,3},{8,12},{9,13},{10,... | collective-permute-start | bytes 1228808 | tf_op jit(solution)/shard_map/ppermute | solution.py:468
  76.7 9.9 %collective-permute-start.21 = (bf16[128,1280]{1,0:T(8,128)(2,1)S(1)}, bf16[128,1280]{1,0:T(8,128)(2,1)S(1)}, u32[]{:S(2)}, u32[]{:S(2)}) collective-permute-start(bf16[128,1280]{1,0:T(8,128)(2,1)S(1)} %get-tuple-element.246), channel_id=1, source_target_pairs={{0,2},{1,3},{2,0},{3,1},{4,6},{5,7},{6,4},{7,5},{8,10},{9,11},{10,... | collective-permute-start | bytes 983048 | tf_op jit(solution)/shard_map/ppermute | solution.py:468
  87.4 9.1 %collective-permute-start.23 = (bf16[128,1280]{1,0:T(8,128)(2,1)S(1)}, bf16[128,1280]{1,0:T(8,128)(2,1)S(1)}, u32[]{:S(2)}, u32[]{:S(2)}) collective-permute-start(bf16[128,1280]{1,0:T(8,128)(2,1)S(1)} %get-tuple-element.252.p0), channel_id=1, source_target_pairs={{0,2},{1,3},{2,0},{3,1},{4,6},{5,7},{6,4},{7,5},{8,10},{9,11},{10,... | collective-permute-start | bytes 983048 | tf_op jit(solution)/shard_map/ppermute | solution.py:468
  89.0 11.6 %collective-permute-start.24 = (bf16[128,1280]{1,0:T(8,128)(2,1)S(1)}, bf16[128,1280]{1,0:T(8,128)(2,1)S(1)}, u32[]{:S(2)}, u32[]{:S(2)}) collective-permute-start(bf16[128,1280]{1,0:T(8,128)(2,1)S(1)} %get-tuple-element.252.p0), channel_id=1, source_target_pairs={{0,1},{1,0},{2,3},{3,2},{4,5},{5,4},{6,7},{7,6},{8,9},{9,8},{10,11... | collective-permute-start | bytes 983048 | tf_op jit(solution)/shard_map/ppermute | solution.py:468
  106.5 13.2 %collective-permute-start.28 = (bf16[640,384]{1,0:T(8,128)(2,1)S(1)}, bf16[640,384]{1,0:T(8,128)(2,1)S(1)}, u32[]{:S(2)}, u32[]{:S(2)}) collective-permute-start(bf16[640,384]{1,0:T(8,128)(2,1)S(1)} %get-tuple-element.279), channel_id=1, source_target_pairs={{0,4},{1,5},{2,6},{3,7},{4,0},{5,1},{6,2},{7,3},{8,12},{9,13},{10,... | collective-permute-start | bytes 1474568 | tf_op jit(solution)/shard_map/ppermute | solution.py:468
  108.7 9.4 %collective-permute-start.27 = (bf16[128,1280]{1,0:T(8,128)(2,1)S(1)}, bf16[128,1280]{1,0:T(8,128)(2,1)S(1)}, u32[]{:S(2)}, u32[]{:S(2)}) collective-permute-start(bf16[128,1280]{1,0:T(8,128)(2,1)S(1)} %get-tuple-element.278), channel_id=1, source_target_pairs={{0,2},{1,3},{2,0},{3,1},{4,6},{5,7},{6,4},{7,5},{8,10},{9,11},{10,... | collective-permute-start | bytes 983048 | tf_op jit(solution)/shard_map/ppermute | solution.py:468
  110.3 9.1 %collective-permute-start.29 = (bf16[640,256]{1,0:T(8,128)(2,1)S(1)}, bf16[640,256]{1,0:T(8,128)(2,1)S(1)}, u32[]{:S(2)}, u32[]{:S(2)}) collective-permute-start(bf16[640,256]{1,0:T(8,128)(2,1)S(1)} %get-tuple-element.280), channel_id=1, source_target_pairs={{0,8},{1,9},{2,10},{3,11},{4,12},{5,13},{6,14},{7,15},{8,0},{9,1},... | collective-permute-start | bytes 983048 | tf_op jit(solution)/shard_map/ppermute | solution.py:468
  120.6 9.1 %collective-permute-start.30 = (bf16[128,1280]{1,0:T(8,128)(2,1)S(1)}, bf16[128,1280]{1,0:T(8,128)(2,1)S(1)}, u32[]{:S(2)}, u32[]{:S(2)}) collective-permute-start(bf16[128,1280]{1,0:T(8,128)(2,1)S(1)} %get-tuple-element.292.refs_1_), channel_id=1, source_target_pairs={{0,2},{1,3},{2,0},{3,1},{4,6},{5,7},{6,4},{7,5},{8,10},{9,11},{10,... | collective-permute-start | bytes 983048 | tf_op jit(solution)/shard_map/ppermute | solution.py:468
  136.8 16.3 %collective-permute-start.38 = (bf16[640,384]{1,0:T(8,128)(2,1)S(1)}, bf16[640,384]{1,0:T(8,128)(2,1)S(1)}, u32[]{:S(2)}, u32[]{:S(2)}) collective-permute-start(bf16[640,384]{1,0:T(8,128)(2,1)S(1)} %get-tuple-element.314), channel_id=1, source_target_pairs={{0,4},{1,5},{2,6},{3,7},{4,0},{5,1},{6,2},{7,3},{8,12},{9,13},{10,... | collective-permute-start | bytes 1474568 | tf_op jit(solution)/shard_map/ppermute | solution.py:468
  138.3 14.8 %collective-permute-start.39 = (bf16[640,256]{1,0:T(8,128)(2,1)S(1)}, bf16[640,256]{1,0:T(8,128)(2,1)S(1)}, u32[]{:S(2)}, u32[]{:S(2)}) collective-permute-start(bf16[640,256]{1,0:T(8,128)(2,1)S(1)} %get-tuple-element.315), channel_id=1, source_target_pairs={{0,8},{1,9},{2,10},{3,11},{4,12},{5,13},{6,14},{7,15},{8,0},{9,1},... | collective-permute-start | bytes 983048 | tf_op jit(solution)/shard_map/ppermute | solution.py:468
  139.6 13.5 %collective-permute-start.36 = (bf16[128,1280]{1,0:T(8,128)(2,1)S(1)}, bf16[128,1280]{1,0:T(8,128)(2,1)S(1)}, u32[]{:S(2)}, u32[]{:S(2)}) collective-permute-start(bf16[128,1280]{1,0:T(8,128)(2,1)S(1)} %get-tuple-element.312), channel_id=1, source_target_pairs={{0,2},{1,3},{2,0},{3,1},{4,6},{5,7},{6,4},{7,5},{8,10},{9,11},{10,... | collective-permute-start | bytes 983048 | tf_op jit(solution)/shard_map/ppermute | solution.py:468
  141.2 11.9 %collective-permute-start.37 = (bf16[160,640]{1,0:T(8,128)(2,1)S(1)}, bf16[160,640]{1,0:T(8,128)(2,1)S(1)}, u32[]{:S(2)}, u32[]{:S(2)}) collective-permute-start(bf16[160,640]{1,0:T(8,128)(2,1)S(1)} %get-tuple-element.313), channel_id=1, source_target_pairs={{0,16},{1,17},{2,18},{3,19},{4,20},{5,21},{6,22},{7,23},{8,24},{9,... | collective-permute-start | bytes 614408 | tf_op jit(solution)/shard_map/ppermute | solution.py:468
  160.1 14.9 %collective-permute-start.44 = (bf16[672,384]{1,0:T(8,128)(2,1)S(1)}, bf16[672,384]{1,0:T(8,128)(2,1)S(1)}, u32[]{:S(2)}, u32[]{:S(2)}) collective-permute-start(bf16[672,384]{1,0:T(8,128)(2,1)S(1)} %get-tuple-element.355), channel_id=1, source_target_pairs={{0,4},{1,5},{2,6},{3,7},{4,0},{5,1},{6,2},{7,3},{8,12},{9,13},{10,... | collective-permute-start | bytes 1548296 | tf_op jit(solution)/shard_map/ppermute | solution.py:468
  160.8 14.2 %collective-permute-start.45 = (bf16[640,256]{1,0:T(8,128)(2,1)S(1)}, bf16[640,256]{1,0:T(8,128)(2,1)S(1)}, u32[]{:S(2)}, u32[]{:S(2)}) collective-permute-start(bf16[640,256]{1,0:T(8,128)(2,1)S(1)} %get-tuple-element.356), channel_id=1, source_target_pairs={{0,8},{1,9},{2,10},{3,11},{4,12},{5,13},{6,14},{7,15},{8,0},{9,1},... | collective-permute-start | bytes 983048 | tf_op jit(solution)/shard_map/ppermute | solution.py:468
  163.0 12.1 %collective-permute-start.46 = (bf16[160,640]{1,0:T(8,128)(2,1)S(1)}, bf16[160,640]{1,0:T(8,128)(2,1)S(1)}, u32[]{:S(2)}, u32[]{:S(2)}) collective-permute-start(bf16[160,640]{1,0:T(8,128)(2,1)S(1)} %get-tuple-element.357), channel_id=1, source_target_pairs={{0,16},{1,17},{2,18},{3,19},{4,20},{5,21},{6,22},{7,23},{8,24},{9,... | collective-permute-start | bytes 614408 | tf_op jit(solution)/shard_map/ppermute | solution.py:468
  175.9 8.8 %collective-permute-start.47 = (bf16[352,384]{1,0:T(8,128)(2,1)S(1)}, bf16[352,384]{1,0:T(8,128)(2,1)S(1)}, u32[]{:S(2)}, u32[]{:S(2)}) collective-permute-start(bf16[352,384]{1,0:T(8,128)(2,1)S(1)} %get-tuple-element.363.refs_0_), channel_id=1, source_target_pairs={{0,8},{1,9},{2,10},{3,11},{4,12},{5,13},{6,14},{7,15},{8,0},{9,1},... | collective-permute-start | bytes 811016 | tf_op jit(solution)/shard_map/ppermute | solution.py:468
  178.4 11.8 %collective-permute-start.43 = (bf16[128,1280]{1,0:T(8,128)(2,1)S(1)}, bf16[128,1280]{1,0:T(8,128)(2,1)S(1)}, u32[]{:S(2)}, u32[]{:S(2)}) collective-permute-start(bf16[128,1280]{1,0:T(8,128)(2,1)S(1)} %get-tuple-element.344), channel_id=1, source_target_pairs={{0,2},{1,3},{2,0},{3,1},{4,6},{5,7},{6,4},{7,5},{8,10},{9,11},{10,... | collective-permute-start | bytes 983048 | tf_op jit(solution)/shard_map/ppermute | solution.py:468
  185.3 17.3 %collective-permute-start.49 = (bf16[160,640]{1,0:T(8,128)(2,1)S(1)}, bf16[160,640]{1,0:T(8,128)(2,1)S(1)}, u32[]{:S(2)}, u32[]{:S(2)}) collective-permute-start(bf16[160,640]{1,0:T(8,128)(2,1)S(1)} %get-tuple-element.370), channel_id=1, source_target_pairs={{0,16},{1,17},{2,18},{3,19},{4,20},{5,21},{6,22},{7,23},{8,24},{9,... | collective-permute-start | bytes 614408 | tf_op jit(solution)/shard_map/ppermute | solution.py:468
  (21 other events, 99.2 us)

commit v3 on v2

--- a/solution.py
+++ b/solution.py
@@ -670,7 +670,7 @@
         got, hd = tie(got, hd)
     n_hd = len(hd[0]), len(hd[0]) + len(hd[1])
     x_one, h_two_own = run("second_norm", second_norm_kernel, [rows_full, rows_low], keep, got, x_own, vectors)
-    h_two = links.gather_tensor(h_two_own)
+    h_two_chip = links.chip(h_two_own)
     grad_act, grad_all, w_hidden, w_down = run(
         "grad_act",
         bind(grad_act_kernel, n_hd, depth),
@@ -681,6 +681,8 @@
         remote=n_hd[1],
         scratch=term + sems,
     )
+    h_two_chip, grad_act = tie(h_two_chip, grad_act)
+    h_two = h_two_own, h_two_chip, links.core(h_two_own), links.core(h_two_chip)
     far, near, act, grad_pre, h_two_all = run(
         "hidden",
         hidden_kernel,
@@ -791,9 +793,6 @@
         grad_qk, mix_got = tie(grad_qk, mix_got)
     else:
         grad_qk, mix_got, part_hd, got_vo = tie(grad_qk, mix_got, part_hd, got_vo)
-        sums_vo = first_sum("vo", terms_vo, got_vo)
-        grad_qk, *sums_vo = tie(grad_qk, *sums_vo)
-        got_vo = second_send(sums_vo)
     terms_first = list(terms)
     if not wide:
         terms_first[0] = ((tall_sent + 32, cut), BF16)
@@ -821,27 +820,35 @@
         got = links.chip(send)
     else:
         got_qk = first_send(terms_qk)
-        far, got_vo = tie(far, got_vo)
-        sent_vo, zero_vo = second_sum("vo", sums_vo, got_vo)
-        send, keep, sent_vo = core_half(far, near, sent_vo)
+        far, *got_vo = tie(far, *got_vo)
+        sums_vo = first_sum("vo", terms_vo, got_vo)
+        send, keep, *sums_vo = core_half(far, near, *sums_vo)
+        got_vo = second_send(sums_vo)
         got = links.chip(send)
-        part_vo = links.along(sent_vo, 4)
         (output,) = run("output", bind(output_kernel, n_dp), [rows_low], mix_keep, mix_got, x_one, vectors)
         grad_hidden, grad_down = owned("hd", zero_hd, part_hd)
-        got, output, grad_hidden = tie(got, output, grad_hidden)
-        got_qk, part_vo = tie(got_qk, part_vo)
+        got_qk, got, output, grad_hidden = tie(got_qk, got, output, grad_hidden)
+        got_qk, got_vo = tie(got_qk, got_vo)
         sums_qk = first_sum("qk", terms_qk, got_qk, [sums])
         got_qk = second_send(sums_qk)
+        (grad_in,) = run("last", bind(last_kernel, n_dp), [rows_low], keep, got, x_own, grad_mid, vectors)
+        got_qk, grad_in = tie(got_qk, grad_in)
+        sent_vo, zero_vo = second_sum("vo", sums_vo, got_vo)
+        part_vo = links.along(sent_vo, 4)
         sent_qk, zero_qk, total = second_sum("qk", sums_qk, got_qk, True)
         far_qk = links.along(sent_qk, 4)
-        got, zero_vo, total = tie(got, zero_vo, total)
-    (grad_in,) = run("last", bind(last_kernel, n_dp), [rows_low], keep, got, x_own, grad_mid, vectors)
+        zero_vo, total = tie(zero_vo, total)
+    if wide:
+        (grad_in,) = run("last", bind(last_kernel, n_dp), [rows_low], keep, got, x_own, grad_mid, vectors)
     if wide:
         (output,) = run("output", bind(output_kernel, n_dp), [rows_low], mix_keep, mix_got, x_one, vectors)
     steps = links.steps()
     for step in steps[:-1]:
         total = exchange(total, step)
     moved = links.move(total, steps[-1])
+    if not wide:
+        grad_query, grad_key = owned("qk", zero_qk, far_qk)
+        moved, grad_query = tie(moved, grad_query)
     tall_vector = (tall, F32)
     *totals, total_scale = run(
         "total", total_kernel, [tall_vector] * 7 + [((1, head_size), F32)], total, moved
@@ -853,7 +860,6 @@
         grad_query, grad_key = links.scatter_wide(terms_qk[0])
     else:
         grad_output_v, grad_output_o = owned("vo", zero_vo, part_vo)
-        grad_query, grad_key = owned("qk", zero_qk, far_qk)
     return (
         output,
         grad_in,

time: 204 us -> 200 us (0.980)
  waiting for transfers between devices: 81.3 us -> 77.3 us
    ppermute x53, waiting for transfers between devices: 81.3 us -> 77.3 us  [move(): return lax.ppermute(value, AXES, pairs)]
  transfers between devices with their start and end apart: 53 -> 53, of which waited for: 25 -> 28; matrix products, arithmetic and copies ran while one was open for 0% -> 0% of each run, Pallas kernels for 28% -> 27%
where the time goes in v3:
time: 200 us; the launch traced here: 199 us
  waiting for transfers between devices  77.3 us (39%)
  Pallas kernels  66.3 us (33%)
  starting transfers between devices  53.4 us (27%)
    ppermute x53, waiting for transfers between devices, move(): return lax.ppermute(value, AXES, pairs)  77.3 us
    pallas_call x38, Pallas kernels, call(): pl.pallas_call(kernel, name=name, out_shape=outs, in_specs=[pl.BlockSpec(...  66.3 us
    ppermute x53, starting transfers between devices, move(): return lax.ppermute(value, AXES, pairs)  53.4 us
  transfers between devices with their start and end apart: 53, of which 28 were waited for; matrix products, arithmetic and copies ran while one was open for 0% of the time, Pallas kernels for 27%

profile of v3, /device:TPU:0, one launch (start us, length us, event | category | flops | bytes accessed | tf_op | source)
XLA Modules:
  0.0 199.5 jit_solution(7362574676888685041)
XLA Ops:
  3.0 4.1 %collective-permute-start.1 = (bf16[160,640]{1,0:T(8,128)(2,1)S(1)}, bf16[160,640]{1,0:T(8,128)(2,1)S(1)}, u32[]{:S(2)}, u32[]{:S(2)}) collective-permute-start(bf16[160,640]{1,0:T(8,128)(2,1)S(1)} %pack_qk.1.refs_0_.refs_6_), channel_id=1, source_target_pairs={{0,16},{1,17},{2,18},{3,19},{4,20},{5,21},{6,22},{7,23},{8,24},{9,... | collective-permute-start | bytes 614408 | tf_op jit(solution)/shard_map/ppermute | solution.py:468
  12.7 3.2 %prepare.1 = (bf16[128,1280]{1,0:T(8,128)(2,1)S(1)}, bf16[128,1280]{1,0:T(8,128)(2,1)S(1)}, bf16[128,1280]{1,0:T(8,128)(2,1)S(1)}, f32[8,1280]{1,0:T(8,128)S(1)}, f32[8,320]{1,0:T(8,128)S(1)}) custom-call(s32[3]{0:T(128)S(1)} %pad_add_fusion.refs_0_.s, f32[1,320]{1,0:T(1,128)S(1)} %broadcast_in_dim_tile.3.refs_1_, bf16[128,1280]{1,0:T(8,128)(2,1)} %refs_2_.1, ...), custom_call_target="tpu_custom_call" | custom-call | flops 1000000 | bytes 1726720 | tf_op jit(solution)/shard_map/prepare/pallas_call | solution.py:30
  22.0 2.3 %collective-permute-start.6 = (bf16[160,640]{1,0:T(8,128)(2,1)S(1)}, bf16[160,640]{1,0:T(8,128)(2,1)S(1)}, u32[]{:S(2)}, u32[]{:S(2)}) collective-permute-start(bf16[160,640]{1,0:T(8,128)(2,1)S(1)} %pack_vo.1.refs_0_.refs_4_), channel_id=1, source_target_pairs={{0,16},{1,17},{2,18},{3,19},{4,20},{5,21},{6,22},{7,23},{8,24},{9,... | collective-permute-start | bytes 614408 | tf_op jit(solution)/shard_map/ppermute | solution.py:468
  24.3 8.3 %collective-permute-done.2.refs_1_.refs_9_ = bf16[160,640]{1,0:T(8,128)(2,1)S(1)} collective-permute-done((bf16[160,640]{1,0:T(8,128)(2,1)S(1)}, bf16[160,640]{1,0:T(8,128)(2,1)S(1)}, u32[]{:S(2)}, u32[]{:S(2)}) %collective-permute-start.2) | collective-permute-done | bytes 204832 | tf_op jit(solution)/shard_map/ppermute | solution.py:468
  33.2 1.9 collective-permute-done.5.refs_1_.refs_5_
  38.1 5.0 %collective-permute-done.10.refs_1_.refs_7_ = bf16[160,640]{1,0:T(8,128)(2,1)S(1)} collective-permute-done((bf16[160,640]{1,0:T(8,128)(2,1)S(1)}, bf16[160,640]{1,0:T(8,128)(2,1)S(1)}, u32[]{:S(2)}, u32[]{:S(2)}) %collective-permute-start.10) | collective-permute-done | bytes 204832 | tf_op jit(solution)/shard_map/ppermute | solution.py:468
  45.8 3.3 %collective-permute-start.13 = (bf16[160,640]{1,0:T(8,128)(2,1)S(1)}, bf16[160,640]{1,0:T(8,128)(2,1)S(1)}, u32[]{:S(2)}, u32[]{:S(2)}) collective-permute-start(bf16[160,640]{1,0:T(8,128)(2,1)S(1)} %pack_hd.1.refs_0_.refs_5_), channel_id=1, source_target_pairs={{0,16},{1,17},{2,18},{3,19},{4,20},{5,21},{6,22},{7,23},{8,24},{9,... | collective-permute-start | bytes 614408 | tf_op jit(solution)/shard_map/ppermute | solution.py:468
  49.1 1.9 collective-permute-start.12
  53.2 6.3 %attend.1 = (f32[512,320]{1,0:T(8,128)S(1)}, bf16[512,320]{1,0:T(8,128)(2,1)S(1)}, bf16[512,320]{1,0:T(8,128)(2,1)S(1)}, bf16[512,1280]{1,0:T(8,128)(2,1)S(1)}, ...) custom-call(s32[3]{0:T(128)S(1)} %pad_add_fusion.refs_0_.s, ...), custom_call_target="tpu_custom_call" | custom-call | flops 1000000 | bytes 9316352 | tf_op jit(solution)/shard_map/attend/pallas_call | solution.py:30
  62.3 2.4 %collective-permute-done.15.refs_9_ = bf16[320,640]{1,0:T(8,128)(2,1)S(1)} collective-permute-done((bf16[320,640]{1,0:T(8,128)(2,1)S(1)}, bf16[320,640]{1,0:T(8,128)(2,1)S(1)}, u32[]{:S(2)}, u32[]{:S(2)}) %collective-permute-start.15) | collective-permute-done | bytes 409632 | tf_op jit(solution)/shard_map/ppermute | solution.py:468
  64.7 3.4 %collective-permute-done.18.refs_1_.refs_8_ = bf16[160,640]{1,0:T(8,128)(2,1)S(1)} collective-permute-done((bf16[160,640]{1,0:T(8,128)(2,1)S(1)}, bf16[160,640]{1,0:T(8,128)(2,1)S(1)}, u32[]{:S(2)}, u32[]{:S(2)}) %collective-permute-start.18) | collective-permute-done | bytes 204832 | tf_op jit(solution)/shard_map/ppermute | solution.py:468
  68.2 5.6 %context.1 = (bf16[512,320]{1,0:T(8,128)(2,1)S(1)}, bf16[512,320]{1,0:T(8,128)(2,1)S(1)}, bf16[256,1280]{1,0:T(8,128)(2,1)S(1)}, f32[256,1280]{1,0:T(8,128)S(1)}...) custom-call(s32[3]{0:T(128)S(1)} %pad_add_fusion.refs_0_.s, ...), custom_call_target="tpu_custom_call" | custom-call | flops 1000000 | bytes 9316352 | tf_op jit(solution)/shard_map/context/pallas_call | solution.py:30
  78.3 8.1 %collective-permute-done.22.refs_10_ = bf16[320,640]{1,0:T(8,128)(2,1)S(1)} collective-permute-done((bf16[320,640]{1,0:T(8,128)(2,1)S(1)}, bf16[320,640]{1,0:T(8,128)(2,1)S(1)}, u32[]{:S(2)}, u32[]{:S(2)}) %collective-permute-start.22) | collective-permute-done | bytes 409632 | tf_op jit(solution)/shard_map/ppermute | solution.py:468
  89.0 4.0 %grad_act.1 = (f32[512,320]{1,0:T(8,128)S(1)}, bf16[512,1280]{1,0:T(8,128)(2,1)S(1)}, bf16[1280,320]{1,0:T(8,128)(2,1)S(1)}, bf16[1280,320]{1,0:T(8,128)(2,1)S(1)}) custom-call(s32[3]{0:T(128)S(1)} %pad_add_fusion.refs_0_.s, bf16[128,1280]{1,0:T(8,128)(2,1)S(1)} %get-tuple-element.260.refs_1_.grad, bf16[128,1280]{1,0:T(8,128)(2,1)S(1)} %collective-permute-done.14.refs_2_, ...), custom_call_target="tpu_custom_call" | custom-call | flops 1000000 | bytes 6553600 | tf_op jit(solution)/shard_map/grad_act/pallas_call | solution.py:30
  93.0 3.6 %collective-permute-done.23.p1 = bf16[128,1280]{1,0:T(8,128)(2,1)S(1)} collective-permute-done((bf16[128,1280]{1,0:T(8,128)(2,1)S(1)}, bf16[128,1280]{1,0:T(8,128)(2,1)S(1)}, u32[]{:S(2)}, u32[]{:S(2)}) %collective-permute-start.23) | collective-permute-done | bytes 327712 | tf_op jit(solution)/shard_map/ppermute | solution.py:468
  98.2 2.3 %hidden.1 = (bf16[256,1280]{1,0:T(8,128)(2,1)S(1)}, f32[256,1280]{1,0:T(8,128)S(1)}, bf16[512,320]{1,0:T(8,128)(2,1)S(1)}, bf16[512,320]{1,0:T(8,128)(2,1)S(1)}, bf16[512,1280]{1,0:T(8,128)(2,1)S(1)}) custom-call(s32[3]{0:T(128)S(1)} %pad_add_fusion.refs_0_.s, bf16[128,1280]{1,0:T(8,128)(2,1)S(1)} %get-tuple-element.259.p0, ...), custom_call_target="tpu_custom_call" | custom-call | flops 1000000 | bytes 6727680 | tf_op jit(solution)/shard_map/hidden/pallas_call | solution.py:30
  100.7 3.0 %down.1 = (bf16[256,1280]{1,0:T(8,128)(2,1)S(1)}, f32[256,1280]{1,0:T(8,128)S(1)}, f32[1,320]{1,0:T(1,128)S(1)}, bf16[640,384]{1,0:T(8,128)(2,1)S(1)}, bf16[640,...) custom-call(s32[3]{0:T(128)S(1)} %pad_add_fusion.refs_0_.s, ...), custom_call_target="tpu_custom_call" | custom-call | flops 1000000 | bytes 7701760 | tf_op jit(solution)/shard_map/down/pallas_call | solution.py:30
  107.8 7.9 %collective-permute-done.27.got = bf16[128,1280]{1,0:T(8,128)(2,1)S(1)} collective-permute-done((bf16[128,1280]{1,0:T(8,128)(2,1)S(1)}, bf16[128,1280]{1,0:T(8,128)(2,1)S(1)}, u32[]{:S(2)}, u32[]{:S(2)}) %collective-permute-start.27) | collective-permute-done | bytes 327712 | tf_op jit(solution)/shard_map/ppermute | solution.py:468
  122.4 3.8 %collective-permute-done.32.ring_got = bf16[320,256]{1,0:T(8,128)(2,1)S(1)} collective-permute-done((bf16[320,256]{1,0:T(8,128)(2,1)S(1)}, bf16[320,256]{1,0:T(8,128)(2,1)S(1)}, u32[]{:S(2)}, u32[]{:S(2)}) %collective-permute-start.32) | collective-permute-done | bytes 163872 | tf_op jit(solution)/shard_map/ppermute | solution.py:468
  129.5 5.3 %grad_context.1 = (bf16[512,320]{1,0:T(8,128)(2,1)S(1)}, bf16[512,320]{1,0:T(8,128)(2,1)S(1)}, bf16[512,1280]{1,0:T(8,128)(2,1)}, bf16[640,384]{1,0:T(8,128)(2,1...) custom-call(s32[3]{0:T(128)S(1)} %pad_add_fusion.refs_0_.s, ...), custom_call_target="tpu_custom_call" | custom-call | flops 1000000 | bytes 9469952 | tf_op jit(solution)/shard_map/grad_context/pallas_call | solution.py:30
  139.2 1.9 collective-permute-start.37
  141.1 5.5 %grad_scores.1 = (bf16[512,640]{1,0:T(8,128)(2,1)S(1)}, f32[8,320]{1,0:T(8,128)S(1)}) custom-call(s32[3]{0:T(128)S(1)} %pad_add_fusion.refs_0_.s, bf16[4,512,512]{2,1,0:T(8,128)(2,1)S(1)} %get-tuple-element.240.refs_2_.refs_6_.refs_1_, bf16[512,320]{1,0:T(8,128)(2,1)S(1)} %get-tuple-element.313.refs_2_, bf16[512,320]{1,0:T(8,128)(2,1)S(1)} %get-tuple-element.314.refs_3_, ...), custom_call_target="tpu_custom_call" | custom-call | flops 1000000 | bytes 4739072 | tf_op jit(solution)/shard_map/grad_scores/pallas_call | solution.py:30
  146.6 4.4 %collective-permute-done.37.refs_2_ = bf16[160,640]{1,0:T(8,128)(2,1)S(1)} collective-permute-done((bf16[160,640]{1,0:T(8,128)(2,1)S(1)}, bf16[160,640]{1,0:T(8,128)(2,1)S(1)}, u32[]{:S(2)}, u32[]{:S(2)}) %collective-permute-start.37) | collective-permute-done | bytes 204832 | tf_op jit(solution)/shard_map/ppermute | solution.py:468
  151.1 3.9 %grad_first.1 = (bf16[256,1280]{1,0:T(8,128)(2,1)S(1)}, f32[256,1280]{1,0:T(8,128)S(1)}, f32[8,1280]{1,0:T(8,128)S(1)}, bf16[672,384]{1,0:T(8,128)(2,1)S(1)}, bf...) custom-call(s32[3]{0:T(128)S(1)} %pad_add_fusion.refs_0_.s, ...), custom_call_target="tpu_custom_call" | custom-call | flops 1000000 | bytes 8474176 | tf_op jit(solution)/shard_map/grad_first/pallas_call | solution.py:30
  161.5 1.8 output.1
  166.2 3.5 %collective-permute-done.40.pair_got = bf16[672,384]{1,0:T(8,128)(2,1)S(1)} collective-permute-done((bf16[672,384]{1,0:T(8,128)(2,1)S(1)}, bf16[672,384]{1,0:T(8,128)(2,1)S(1)}, u32[]{:S(2)}, u32[]{:S(2)}) %collective-permute-start.40) | collective-permute-done | bytes 516128 | tf_op jit(solution)/shard_map/ppermute | solution.py:468
  169.7 3.1 %collective-permute-done.45.ring_got = bf16[320,256]{1,0:T(8,128)(2,1)S(1)} collective-permute-done((bf16[320,256]{1,0:T(8,128)(2,1)S(1)}, bf16[320,256]{1,0:T(8,128)(2,1)S(1)}, u32[]{:S(2)}, u32[]{:S(2)}) %collective-permute-start.45) | collective-permute-done | bytes 163872 | tf_op jit(solution)/shard_map/ppermute | solution.py:468
  175.4 2.0 collective-permute-start.52
  177.4 2.1 %last.1 = bf16[128,1280]{1,0:T(8,128)(2,1)} custom-call(s32[3]{0:T(128)S(1)} %pad_add_fusion.refs_0_.s, f32[128,1280]{1,0:T(8,128)S(1)} %get-tuple-element.367.refs_1_, bf16[128,1280]{1,0:T(8,128)(2,1)S(1)} %collective-permute-done.43.refs_2_, bf16[128,1280]{1,0:T(8,128)(2,1)S(1)} %get-tuple-element.257.x_own.refs_3_, ...), custom_call_target="tpu_custom_call" | custom-call | flops 1000000 | bytes 2334720 | tf_op jit(solution)/shard_map/last/pallas_call | solution.py:30
  179.5 6.0 %collective-permute-done.46.pair_got = bf16[352,384]{1,0:T(8,128)(2,1)S(1)} collective-permute-done((bf16[352,384]{1,0:T(8,128)(2,1)S(1)}, bf16[352,384]{1,0:T(8,128)(2,1)S(1)}, u32[]{:S(2)}, u32[]{:S(2)}) %collective-permute-start.46) | collective-permute-done | bytes 270368 | tf_op jit(solution)/shard_map/ppermute | solution.py:468
  189.4 2.8 %collective-permute-done.49.two = f32[8,1280]{1,0:T(8,128)S(1)} collective-permute-done((f32[8,1280]{1,0:T(8,128)S(1)}, f32[8,1280]{1,0:T(8,128)S(1)}, u32[]{:S(2)}, u32[]{:S(2)}) %collective-permute-start.49) | collective-permute-done | bytes 40992 | tf_op jit(solution)/shard_map/ppermute | solution.py:468
  192.7 2.9 %collective-permute-start.50 = (f32[8,1280]{1,0:T(8,128)S(1)}, f32[8,1280]{1,0:T(8,128)S(1)}, u32[]{:S(2)}, u32[]{:S(2)}) collective-permute-start(f32[8,1280]{1,0:T(8,128)S(1)} %add.18.one), channel_id=1, source_target_pairs={{0,16},{1,17},{2,18},{3,19},{4,20},{5,21},{6,22},{7,23},{8,24},{9,... | collective-permute-start | bytes 122888 | tf_op jit(solution)/shard_map/ppermute | solution.py:468
  (116 shorter events, 72.3 us)
Async XLA Ops:
  3.0 13.7 %collective-permute-start.1 = (bf16[160,640]{1,0:T(8,128)(2,1)S(1)}, bf16[160,640]{1,0:T(8,128)(2,1)S(1)}, u32[]{:S(2)}, u32[]{:S(2)}) collective-permute-start(bf16[160,640]{1,0:T(8,128)(2,1)S(1)} %pack_qk.1.refs_0_.refs_6_), channel_id=1, source_target_pairs={{0,16},{1,17},{2,18},{3,19},{4,20},{5,21},{6,22},{7,23},{8,24},{9,... | collective-permute-start | bytes 614408 | tf_op jit(solution)/shard_map/ppermute | solution.py:468
  7.1 9.8 %collective-permute-start = (bf16[160,640]{1,0:T(8,128)(2,1)S(1)}, bf16[160,640]{1,0:T(8,128)(2,1)S(1)}, u32[]{:S(2)}, u32[]{:S(2)}) collective-permute-start(bf16[160,640]{1,0:T(8,128)(2,1)S(1)} %pack_qk.1.refs_0_.refs_6_), channel_id=1, source_target_pairs={{0,8},{1,9},{2,10},{3,11},{4,12},{5,13},{6,14},{7,15},{8,0},{9,1},... | collective-permute-start | bytes 614408 | tf_op jit(solution)/shard_map/ppermute | solution.py:468
  17.4 17.7 %collective-permute-start.3 = (bf16[320,640]{1,0:T(8,128)(2,1)S(1)}, bf16[320,640]{1,0:T(8,128)(2,1)S(1)}, u32[]{:S(2)}, u32[]{:S(2)}) collective-permute-start(bf16[320,640]{1,0:T(8,128)(2,1)S(1)} %stack.19), channel_id=1, source_target_pairs={{0,4},{1,5},{2,6},{3,7},{4,0},{5,1},{6,2},{7,3},{8,12},{9,13},{10,... | collective-permute-start | bytes 1228808 | tf_op jit(solution)/shard_map/ppermute | solution.py:468
  19.1 16.0 %collective-permute-start.4 = (bf16[128,1280]{1,0:T(8,128)(2,1)S(1)}, bf16[128,1280]{1,0:T(8,128)(2,1)S(1)}, u32[]{:S(2)}, u32[]{:S(2)}) collective-permute-start(bf16[128,1280]{1,0:T(8,128)(2,1)S(1)} %get-tuple-element.220.refs_1_), channel_id=1, source_target_pairs={{0,2},{1,3},{2,0},{3,1},{4,6},{5,7},{6,4},{7,5},{8,10},{9,11},{10,... | collective-permute-start | bytes 983048 | tf_op jit(solution)/shard_map/ppermute | solution.py:468
  20.6 12.0 %collective-permute-start.2 = (bf16[160,640]{1,0:T(8,128)(2,1)S(1)}, bf16[160,640]{1,0:T(8,128)(2,1)S(1)}, u32[]{:S(2)}, u32[]{:S(2)}) collective-permute-start(bf16[160,640]{1,0:T(8,128)(2,1)S(1)} %collective-permute-done.1.refs_0_.refs_8_), channel_id=1, source_target_pairs={{0,8},{1,9},{2,10},{3,11},{4,12},{5,13},{6,14},{7,15},{8,0},{9,1},... | collective-permute-start | bytes 614408 | tf_op jit(solution)/shard_map/ppermute | solution.py:468
  22.0 11.2 %collective-permute-start.6 = (bf16[160,640]{1,0:T(8,128)(2,1)S(1)}, bf16[160,640]{1,0:T(8,128)(2,1)S(1)}, u32[]{:S(2)}, u32[]{:S(2)}) collective-permute-start(bf16[160,640]{1,0:T(8,128)(2,1)S(1)} %pack_vo.1.refs_0_.refs_4_), channel_id=1, source_target_pairs={{0,16},{1,17},{2,18},{3,19},{4,20},{5,21},{6,22},{7,23},{8,24},{9,... | collective-permute-start | bytes 614408 | tf_op jit(solution)/shard_map/ppermute | solution.py:468
  24.3 10.8 %collective-permute-start.5 = (bf16[160,640]{1,0:T(8,128)(2,1)S(1)}, bf16[160,640]{1,0:T(8,128)(2,1)S(1)}, u32[]{:S(2)}, u32[]{:S(2)}) collective-permute-start(bf16[160,640]{1,0:T(8,128)(2,1)S(1)} %pack_vo.1.refs_0_.refs_4_), channel_id=1, source_target_pairs={{0,8},{1,9},{2,10},{3,11},{4,12},{5,13},{6,14},{7,15},{8,0},{9,1},... | collective-permute-start | bytes 614408 | tf_op jit(solution)/shard_map/ppermute | solution.py:468
  35.1 9.6 %collective-permute-start.9 = (bf16[320,640]{1,0:T(8,128)(2,1)S(1)}, bf16[320,640]{1,0:T(8,128)(2,1)S(1)}, u32[]{:S(2)}, u32[]{:S(2)}) collective-permute-start(bf16[320,640]{1,0:T(8,128)(2,1)S(1)} %stack.18), channel_id=1, source_target_pairs={{0,4},{1,5},{2,6},{3,7},{4,0},{5,1},{6,2},{7,3},{8,12},{9,13},{10,... | collective-permute-start | bytes 1228808 | tf_op jit(solution)/shard_map/ppermute | solution.py:468
  44.7 14.8 %collective-permute-start.11 = (bf16[320,640]{1,0:T(8,128)(2,1)S(1)}, bf16[320,640]{1,0:T(8,128)(2,1)S(1)}, u32[]{:S(2)}, u32[]{:S(2)}) collective-permute-start(bf16[320,640]{1,0:T(8,128)(2,1)S(1)} %stack.20), channel_id=1, source_target_pairs={{0,4},{1,5},{2,6},{3,7},{4,0},{5,1},{6,2},{7,3},{8,12},{9,13},{10,... | collective-permute-start | bytes 1228808 | tf_op jit(solution)/shard_map/ppermute | solution.py:468
  45.2 14.3 %collective-permute-start.14 = (bf16[128,1280]{1,0:T(8,128)(2,1)S(1)}, bf16[128,1280]{1,0:T(8,128)(2,1)S(1)}, u32[]{:S(2)}, u32[]{:S(2)}) collective-permute-start(bf16[128,1280]{1,0:T(8,128)(2,1)S(1)} %get-tuple-element.260.refs_1_.grad), channel_id=1, source_target_pairs={{0,2},{1,3},{2,0},{3,1},{4,6},{5,7},{6,4},{7,5},{8,10},{9,11},{10,... | collective-permute-start | bytes 983048 | tf_op jit(solution)/shard_map/ppermute | solution.py:468
  45.8 13.7 %collective-permute-start.13 = (bf16[160,640]{1,0:T(8,128)(2,1)S(1)}, bf16[160,640]{1,0:T(8,128)(2,1)S(1)}, u32[]{:S(2)}, u32[]{:S(2)}) collective-permute-start(bf16[160,640]{1,0:T(8,128)(2,1)S(1)} %pack_hd.1.refs_0_.refs_5_), channel_id=1, source_target_pairs={{0,16},{1,17},{2,18},{3,19},{4,20},{5,21},{6,22},{7,23},{8,24},{9,... | collective-permute-start | bytes 614408 | tf_op jit(solution)/shard_map/ppermute | solution.py:468
  49.1 10.4 %collective-permute-start.12 = (bf16[160,640]{1,0:T(8,128)(2,1)S(1)}, bf16[160,640]{1,0:T(8,128)(2,1)S(1)}, u32[]{:S(2)}, u32[]{:S(2)}) collective-permute-start(bf16[160,640]{1,0:T(8,128)(2,1)S(1)} %pack_hd.1.refs_0_.refs_5_), channel_id=1, source_target_pairs={{0,8},{1,9},{2,10},{3,11},{4,12},{5,13},{6,14},{7,15},{8,0},{9,1},... | collective-permute-start | bytes 614408 | tf_op jit(solution)/shard_map/ppermute | solution.py:468
  51.6 13.2 %collective-permute-start.15 = (bf16[320,640]{1,0:T(8,128)(2,1)S(1)}, bf16[320,640]{1,0:T(8,128)(2,1)S(1)}, u32[]{:S(2)}, u32[]{:S(2)}) collective-permute-start(bf16[320,640]{1,0:T(8,128)(2,1)S(1)} %stack.21), channel_id=1, source_target_pairs={{0,4},{1,5},{2,6},{3,7},{4,0},{5,1},{6,2},{7,3},{8,12},{9,13},{10,... | collective-permute-start | bytes 1228808 | tf_op jit(solution)/shard_map/ppermute | solution.py:468
  60.1 13.7 %collective-permute-start.19 = (bf16[320,640]{1,0:T(8,128)(2,1)S(1)}, bf16[320,640]{1,0:T(8,128)(2,1)S(1)}, u32[]{:S(2)}, u32[]{:S(2)}) collective-permute-start(bf16[320,640]{1,0:T(8,128)(2,1)S(1)} %stack.22), channel_id=1, source_target_pairs={{0,4},{1,5},{2,6},{3,7},{4,0},{5,1},{6,2},{7,3},{8,12},{9,13},{10,... | collective-permute-start | bytes 1228808 | tf_op jit(solution)/shard_map/ppermute | solution.py:468
  74.4 11.9 %collective-permute-start.22 = (bf16[320,640]{1,0:T(8,128)(2,1)S(1)}, bf16[320,640]{1,0:T(8,128)(2,1)S(1)}, u32[]{:S(2)}, u32[]{:S(2)}) collective-permute-start(bf16[320,640]{1,0:T(8,128)(2,1)S(1)} %stack.23), channel_id=1, source_target_pairs={{0,4},{1,5},{2,6},{3,7},{4,0},{5,1},{6,2},{7,3},{8,12},{9,13},{10,... | collective-permute-start | bytes 1228808 | tf_op jit(solution)/shard_map/ppermute | solution.py:468
  76.7 9.9 %collective-permute-start.21 = (bf16[128,1280]{1,0:T(8,128)(2,1)S(1)}, bf16[128,1280]{1,0:T(8,128)(2,1)S(1)}, u32[]{:S(2)}, u32[]{:S(2)}) collective-permute-start(bf16[128,1280]{1,0:T(8,128)(2,1)S(1)} %get-tuple-element.253), channel_id=1, source_target_pairs={{0,2},{1,3},{2,0},{3,1},{4,6},{5,7},{6,4},{7,5},{8,10},{9,11},{10,... | collective-permute-start | bytes 983048 | tf_op jit(solution)/shard_map/ppermute | solution.py:468
  103.7 13.6 %collective-permute-start.28 = (bf16[640,384]{1,0:T(8,128)(2,1)S(1)}, bf16[640,384]{1,0:T(8,128)(2,1)S(1)}, u32[]{:S(2)}, u32[]{:S(2)}) collective-permute-start(bf16[640,384]{1,0:T(8,128)(2,1)S(1)} %get-tuple-element.288), channel_id=1, source_target_pairs={{0,4},{1,5},{2,6},{3,7},{4,0},{5,1},{6,2},{7,3},{8,12},{9,13},{10,... | collective-permute-start | bytes 1474568 | tf_op jit(solution)/shard_map/ppermute | solution.py:468
  106.0 9.8 %collective-permute-start.27 = (bf16[128,1280]{1,0:T(8,128)(2,1)S(1)}, bf16[128,1280]{1,0:T(8,128)(2,1)S(1)}, u32[]{:S(2)}, u32[]{:S(2)}) collective-permute-start(bf16[128,1280]{1,0:T(8,128)(2,1)S(1)} %get-tuple-element.287), channel_id=1, source_target_pairs={{0,2},{1,3},{2,0},{3,1},{4,6},{5,7},{6,4},{7,5},{8,10},{9,11},{10,... | collective-permute-start | bytes 983048 | tf_op jit(solution)/shard_map/ppermute | solution.py:468
  107.5 9.4 %collective-permute-start.29 = (bf16[640,256]{1,0:T(8,128)(2,1)S(1)}, bf16[640,256]{1,0:T(8,128)(2,1)S(1)}, u32[]{:S(2)}, u32[]{:S(2)}) collective-permute-start(bf16[640,256]{1,0:T(8,128)(2,1)S(1)} %get-tuple-element.289), channel_id=1, source_target_pairs={{0,8},{1,9},{2,10},{3,11},{4,12},{5,13},{6,14},{7,15},{8,0},{9,1},... | collective-permute-start | bytes 983048 | tf_op jit(solution)/shard_map/ppermute | solution.py:468
  118.2 9.5 %collective-permute-start.30 = (bf16[128,1280]{1,0:T(8,128)(2,1)S(1)}, bf16[128,1280]{1,0:T(8,128)(2,1)S(1)}, u32[]{:S(2)}, u32[]{:S(2)}) collective-permute-start(bf16[128,1280]{1,0:T(8,128)(2,1)S(1)} %get-tuple-element.301.refs_1_), channel_id=1, source_target_pairs={{0,2},{1,3},{2,0},{3,1},{4,6},{5,7},{6,4},{7,5},{8,10},{9,11},{10,... | collective-permute-start | bytes 983048 | tf_op jit(solution)/shard_map/ppermute | solution.py:468
  134.7 16.3 %collective-permute-start.38 = (bf16[640,384]{1,0:T(8,128)(2,1)S(1)}, bf16[640,384]{1,0:T(8,128)(2,1)S(1)}, u32[]{:S(2)}, u32[]{:S(2)}) collective-permute-start(bf16[640,384]{1,0:T(8,128)(2,1)S(1)} %get-tuple-element.323), channel_id=1, source_target_pairs={{0,4},{1,5},{2,6},{3,7},{4,0},{5,1},{6,2},{7,3},{8,12},{9,13},{10,... | collective-permute-start | bytes 1474568 | tf_op jit(solution)/shard_map/ppermute | solution.py:468
  136.3 14.8 %collective-permute-start.39 = (bf16[640,256]{1,0:T(8,128)(2,1)S(1)}, bf16[640,256]{1,0:T(8,128)(2,1)S(1)}, u32[]{:S(2)}, u32[]{:S(2)}) collective-permute-start(bf16[640,256]{1,0:T(8,128)(2,1)S(1)} %get-tuple-element.324), channel_id=1, source_target_pairs={{0,8},{1,9},{2,10},{3,11},{4,12},{5,13},{6,14},{7,15},{8,0},{9,1},... | collective-permute-start | bytes 983048 | tf_op jit(solution)/shard_map/ppermute | solution.py:468
  137.3 13.8 %collective-permute-start.36 = (bf16[128,1280]{1,0:T(8,128)(2,1)S(1)}, bf16[128,1280]{1,0:T(8,128)(2,1)S(1)}, u32[]{:S(2)}, u32[]{:S(2)}) collective-permute-start(bf16[128,1280]{1,0:T(8,128)(2,1)S(1)} %get-tuple-element.321), channel_id=1, source_target_pairs={{0,2},{1,3},{2,0},{3,1},{4,6},{5,7},{6,4},{7,5},{8,10},{9,11},{10,... | collective-permute-start | bytes 983048 | tf_op jit(solution)/shard_map/ppermute | solution.py:468
  139.2 11.9 %collective-permute-start.37 = (bf16[160,640]{1,0:T(8,128)(2,1)S(1)}, bf16[160,640]{1,0:T(8,128)(2,1)S(1)}, u32[]{:S(2)}, u32[]{:S(2)}) collective-permute-start(bf16[160,640]{1,0:T(8,128)(2,1)S(1)} %get-tuple-element.322), channel_id=1, source_target_pairs={{0,16},{1,17},{2,18},{3,19},{4,20},{5,21},{6,22},{7,23},{8,24},{9,... | collective-permute-start | bytes 614408 | tf_op jit(solution)/shard_map/ppermute | solution.py:468
  155.1 14.6 %collective-permute-start.40 = (bf16[672,384]{1,0:T(8,128)(2,1)S(1)}, bf16[672,384]{1,0:T(8,128)(2,1)S(1)}, u32[]{:S(2)}, u32[]{:S(2)}) collective-permute-start(bf16[672,384]{1,0:T(8,128)(2,1)S(1)} %get-tuple-element.333), channel_id=1, source_target_pairs={{0,4},{1,5},{2,6},{3,7},{4,0},{5,1},{6,2},{7,3},{8,12},{9,13},{10,... | collective-permute-start | bytes 1548296 | tf_op jit(solution)/shard_map/ppermute | solution.py:468
  155.7 10.6 %collective-permute-start.41 = (bf16[640,256]{1,0:T(8,128)(2,1)S(1)}, bf16[640,256]{1,0:T(8,128)(2,1)S(1)}, u32[]{:S(2)}, u32[]{:S(2)}) collective-permute-start(bf16[640,256]{1,0:T(8,128)(2,1)S(1)} %get-tuple-element.334), channel_id=1, source_target_pairs={{0,8},{1,9},{2,10},{3,11},{4,12},{5,13},{6,14},{7,15},{8,0},{9,1},... | collective-permute-start | bytes 983048 | tf_op jit(solution)/shard_map/ppermute | solution.py:468
  157.8 11.9 %collective-permute-start.43 = (bf16[128,1280]{1,0:T(8,128)(2,1)S(1)}, bf16[128,1280]{1,0:T(8,128)(2,1)S(1)}, u32[]{:S(2)}, u32[]{:S(2)}) collective-permute-start(bf16[128,1280]{1,0:T(8,128)(2,1)S(1)} %get-tuple-element.349), channel_id=1, source_target_pairs={{0,2},{1,3},{2,0},{3,1},{4,6},{5,7},{6,4},{7,5},{8,10},{9,11},{10,... | collective-permute-start | bytes 983048 | tf_op jit(solution)/shard_map/ppermute | solution.py:468
  158.7 14.1 %collective-permute-start.44 = (bf16[320,384]{1,0:T(8,128)(2,1)S(1)}, bf16[320,384]{1,0:T(8,128)(2,1)S(1)}, u32[]{:S(2)}, u32[]{:S(2)}) collective-permute-start(bf16[320,384]{1,0:T(8,128)(2,1)S(1)} %get-tuple-element.359), channel_id=1, source_target_pairs={{0,8},{1,9},{2,10},{3,11},{4,12},{5,13},{6,14},{7,15},{8,0},{9,1},... | collective-permute-start | bytes 737288 | tf_op jit(solution)/shard_map/ppermute | solution.py:468
  160.0 12.8 %collective-permute-start.45 = (bf16[320,256]{1,0:T(8,128)(2,1)S(1)}, bf16[320,256]{1,0:T(8,128)(2,1)S(1)}, u32[]{:S(2)}, u32[]{:S(2)}) collective-permute-start(bf16[320,256]{1,0:T(8,128)(2,1)S(1)} %get-tuple-element.360), channel_id=1, source_target_pairs={{0,4},{1,5},{2,6},{3,7},{4,0},{5,1},{6,2},{7,3},{8,12},{9,13},{10,... | collective-permute-start | bytes 491528 | tf_op jit(solution)/shard_map/ppermute | solution.py:468
  173.6 11.9 %collective-permute-start.46 = (bf16[352,384]{1,0:T(8,128)(2,1)S(1)}, bf16[352,384]{1,0:T(8,128)(2,1)S(1)}, u32[]{:S(2)}, u32[]{:S(2)}) collective-permute-start(bf16[352,384]{1,0:T(8,128)(2,1)S(1)} %get-tuple-element.365.refs_0_), channel_id=1, source_target_pairs={{0,8},{1,9},{2,10},{3,11},{4,12},{5,13},{6,14},{7,15},{8,0},{9,1},... | collective-permute-start | bytes 811016 | tf_op jit(solution)/shard_map/ppermute | solution.py:468
  175.4 20.2 %collective-permute-start.52 = (bf16[160,640]{1,0:T(8,128)(2,1)S(1)}, bf16[160,640]{1,0:T(8,128)(2,1)S(1)}, u32[]{:S(2)}, u32[]{:S(2)}) collective-permute-start(bf16[160,640]{1,0:T(8,128)(2,1)S(1)} %get-tuple-element.388), channel_id=1, source_target_pairs={{0,16},{1,17},{2,18},{3,19},{4,20},{5,21},{6,22},{7,23},{8,24},{9,... | collective-permute-start | bytes 614408 | tf_op jit(solution)/shard_map/ppermute | solution.py:468
  186.1 10.8 %collective-permute-start.51 = (bf16[160,640]{1,0:T(8,128)(2,1)S(1)}, bf16[160,640]{1,0:T(8,128)(2,1)S(1)}, u32[]{:S(2)}, u32[]{:S(2)}) collective-permute-start(bf16[160,640]{1,0:T(8,128)(2,1)S(1)} %get-tuple-element.383), channel_id=1, source_target_pairs={{0,16},{1,17},{2,18},{3,19},{4,20},{5,21},{6,22},{7,23},{8,24},{9,... | collective-permute-start | bytes 614408 | tf_op jit(solution)/shard_map/ppermute | solution.py:468
  (21 other events, 102.3 us)

commit v4 on v3

--- a/solution.py
+++ b/solution.py
@@ -91,9 +91,11 @@
         copy.wait()
 
 
-def pack_kernel(s, first, second, out, one, two, sem):
-    load((first, second), (one, two), sem)
-    out[...] = pack(one[...].astype(F32), two[...].astype(F32)).astype(BF16)
+def pack_kernel(s, *refs):
+    sources, outs, loaded = refs[:6], refs[6:9], refs[9:15]
+    load(sources, loaded, refs[15])
+    for k, out in enumerate(outs):
+        out[...] = pack(loaded[2 * k][...].astype(F32), loaded[2 * k + 1][...].astype(F32)).astype(BF16)
 
 
 def row_of(ref):
@@ -562,15 +564,18 @@
     unit = SOFTPLUS_UNIT / jnp.sqrt(F32(head_size))
     scale_wide = jnp.tile(jax.nn.softplus(query_scale) * unit, heads)[None]
     slope = (jax.nn.sigmoid(query_scale) * unit)[None]
-    loads = [pltpu.VMEM((depth, local_width), BF16)] * 2 + [pltpu.SemaphoreType.DMA((2,))]
-
     def apart(value):
         return pltpu.with_memory_space_constraint(value, pltpu.HBM)
 
-    def pack_two(name, one, two):
-        return run("pack_" + name, pack_kernel, packed, apart(one), apart(two), remote=2, scratch=loads)[0]
-
-    own_qk = pack_two("qk", weight_query, weight_key)
+    weights = (weight_query, weight_key, weight_value, weight_output.T, weight_hidden, weight_down.T)
+    own_qk, own_vo, own_hd = run(
+        "pack",
+        pack_kernel,
+        packed * 3,
+        *(apart(w) for w in weights),
+        remote=6,
+        scratch=[pltpu.VMEM((depth, local_width), BF16)] * 6 + [pltpu.SemaphoreType.DMA((6,))],
+    )
     given = (gain_attention, gain_mixer, bias_output, bias_final, bias_query, bias_value, bias_hidden)
     scale_wide, slope = tie(scale_wide, slope)
     tall = (width // LANES, LANES)
@@ -585,8 +590,6 @@
         + [pltpu.VMEM(tall, F32)] * 7
         + [pltpu.SemaphoreType.DMA((9,))],
     )
-    own_vo = pack_two("vo", weight_value, weight_output.T)
-    own_hd = pack_two("hd", weight_hidden, weight_down.T)
 
     def stack(*blocks):
         rows = sum(block.shape[0] for block in blocks)
@@ -597,20 +600,21 @@
         h_one, grad_rows = links.gather_tensor(h_own), links.gather_tensor(grad_own)
     else:
         qk_one, qk_two = links.along(own_qk, 2), links.along(own_qk, 4)
-        h_own, own_vo, own_hd, qk_one, qk_two = tie(h_own, own_vo, own_hd, qk_one, qk_two)
+        hd_pair = links.pair(own_hd)
+        h_own, own_vo, own_hd, qk_one, qk_two, hd_pair = tie(h_own, own_vo, own_hd, qk_one, qk_two, hd_pair)
         h_chip = links.chip(h_own)
         qk_three = links.along(qk_two, 2)
         near_qk_pair = links.pair(stack(own_qk, qk_one))
-        vo_one, vo_two = links.along(own_vo, 2), links.along(own_vo, 4)
+        vo_two, vo_pair = links.along(own_vo, 4), links.pair(own_vo)
         far_stack = stack(qk_two, qk_three)
-        far_stack, near_qk_pair, h_chip, vo_one, vo_two = tie(far_stack, near_qk_pair, h_chip, vo_one, vo_two)
+        far_stack, near_qk_pair = tie(far_stack, near_qk_pair)
+        h_chip, vo_two, vo_pair, own_vo = tie(h_chip, vo_two, vo_pair, own_vo)
         h_one = h_own, h_chip, links.core(h_own), links.core(h_chip)
         far_qk_pair = links.pair(far_stack)
-        vo_three = links.along(vo_two, 2)
-        near_vo = stack(own_vo, vo_one)
+        vo_one, vo_three = links.along(own_vo, 2), links.along(vo_two, 2)
         qk = [own_qk, qk_one, qk_two, qk_three], [near_qk_pair, far_qk_pair]
-        h_one, qk, vo_three, near_vo = tie(h_one, qk, vo_three, near_vo)
-        near_vo_pair = links.pair(near_vo)
+        h_one, qk, vo_three, own_hd = tie(h_one, qk, vo_three, own_hd)
+        near_vo_pair = links.pair(vo_one)
         hd_one, hd_two = links.along(own_hd, 2), links.along(own_hd, 4)
         grad_chip = links.chip(grad_own)
     n_qk = len(qk[0]), len(qk[0]) + len(qk[1])
@@ -637,9 +641,9 @@
         far_vo_pair = links.pair(stack(vo_two, vo_three))
         hd_three = links.along(hd_two, 2)
         grad_rows = grad_own, grad_chip, links.core(grad_own), links.core(grad_chip)
-        vo = [own_vo, vo_one, vo_two, vo_three], [near_vo_pair, far_vo_pair]
-        turned, vo, grad_rows, hd_three = tie(turned, vo, grad_rows, hd_three)
-        near_hd_pair = links.pair(stack(own_hd, hd_one))
+        vo = [own_vo, vo_one, vo_two, vo_three], [vo_pair, near_vo_pair, far_vo_pair]
+        turned, vo, grad_rows = tie(turned, vo, grad_rows)
+        near_hd_pair = links.pair(hd_one)
     n_vo = len(vo[0]), len(vo[0]) + len(vo[1])
     v_low, context, far, near, w_value, w_output = run(
         "context",
@@ -662,11 +666,11 @@
         send, keep = core_half(far, near)
         got = links.chip(send)
     else:
-        far, near_hd_pair = tie(far, near_hd_pair)
+        far, near_hd_pair, hd_three = tie(far, near_hd_pair, hd_three)
         send, keep = core_half(far, near)
         got = links.chip(send)
         far_hd_pair = links.pair(stack(hd_two, hd_three))
-        hd = [own_hd, hd_one, hd_two, hd_three], [near_hd_pair, far_hd_pair]
+        hd = [own_hd, hd_one, hd_two, hd_three], [hd_pair, near_hd_pair, far_hd_pair]
         got, hd = tie(got, hd)
     n_hd = len(hd[0]), len(hd[0]) + len(hd[1])
     x_one, h_two_own = run("second_norm", second_norm_kernel, [rows_full, rows_low], keep, got, x_own, vectors)

time: 200 us -> 193 us (0.965)
  waiting for transfers between devices: 77.3 us -> 69.6 us
  starting transfers between devices: 53.4 us -> 59.1 us
  Pallas kernels: 66.3 us -> 62.1 us
    ppermute x53 -> x55, waiting for transfers between devices: 77.3 us -> 69.6 us  [move(): return lax.ppermute(value, AXES, pairs)]
    ppermute x53 -> x55, starting transfers between devices: 53.4 us -> 59.1 us  [move(): return lax.ppermute(value, AXES, pairs)]
    pallas_call x38 -> x34, Pallas kernels: 66.3 us -> 62.1 us  [call(): pl.pallas_call(kernel, name=name, out_shape=outs, in_specs=[pl.BlockSpec(...]
  transfers between devices with their start and end apart: 53 -> 55, of which waited for: 28 -> 27; matrix products, arithmetic and copies ran while one was open for 0% -> 0% of each run, Pallas kernels for 27% -> 26%
where the time goes in v4:
time: 193 us
  waiting for transfers between devices  69.6 us (36%)
  Pallas kernels  62.1 us (32%)
  starting transfers between devices  59.1 us (31%)
    ppermute x55, waiting for transfers between devices, move(): return lax.ppermute(value, AXES, pairs)  69.6 us
    pallas_call x34, Pallas kernels, call(): pl.pallas_call(kernel, name=name, out_shape=outs, in_specs=[pl.BlockSpec(...  62.1 us
    ppermute x55, starting transfers between devices, move(): return lax.ppermute(value, AXES, pairs)  59.1 us
  transfers between devices with their start and end apart: 55, of which 27 were waited for; matrix products, arithmetic and copies ran while one was open for 0% of the time, Pallas kernels for 26%

profile of v4, /device:TPU:0, one launch (start us, length us, event | category | flops | bytes accessed | tf_op | source)
XLA Modules:
  0.0 193.3 jit_solution(16372799898925745938)
XLA Ops:
  1.4 1.9 pack.1
  3.3 4.1 %collective-permute-start.1 = (bf16[160,640]{1,0:T(8,128)(2,1)S(1)}, bf16[160,640]{1,0:T(8,128)(2,1)S(1)}, u32[]{:S(2)}, u32[]{:S(2)}) collective-permute-start(bf16[160,640]{1,0:T(8,128)(2,1)S(1)} %get-tuple-element.235.refs_0_.refs_6_), channel_id=1, source_target_pairs={{0,16},{1,17},{2,18},{3,19},{4,20},{5,21},{6,22},{7,23},{8,24},{9,... | collective-permute-start | bytes 614408 | tf_op jit(solution)/shard_map/ppermute | solution.py:470
  11.3 3.2 %prepare.1 = (bf16[128,1280]{1,0:T(8,128)(2,1)S(1)}, bf16[128,1280]{1,0:T(8,128)(2,1)S(1)}, bf16[128,1280]{1,0:T(8,128)(2,1)S(1)}, f32[8,1280]{1,0:T(8,128)S(1)}, f32[8,320]{1,0:T(8,128)S(1)}) custom-call(s32[3]{0:T(128)S(1)} %pad_add_fusion.refs_0_.s, f32[1,320]{1,0:T(1,128)S(1)} %broadcast_in_dim_tile.3.refs_1_, bf16[128,1280]{1,0:T(8,128)(2,1)} %refs_2_.2, ...), custom_call_target="tpu_custom_call" | custom-call | flops 1000000 | bytes 1726720 | tf_op jit(solution)/shard_map/prepare/pallas_call | solution.py:30
  22.8 2.3 %collective-permute-start.4 = (bf16[160,640]{1,0:T(8,128)(2,1)S(1)}, bf16[160,640]{1,0:T(8,128)(2,1)S(1)}, u32[]{:S(2)}, u32[]{:S(2)}) collective-permute-start(bf16[160,640]{1,0:T(8,128)(2,1)S(1)} %get-tuple-element.252.refs_4_), channel_id=1, source_target_pairs={{0,16},{1,17},{2,18},{3,19},{4,20},{5,21},{6,22},{7,23},{8,24},{9,... | collective-permute-start | bytes 614408 | tf_op jit(solution)/shard_map/ppermute | solution.py:470
  25.1 5.3 %collective-permute-done.8.refs_1_.refs_9_ = bf16[160,640]{1,0:T(8,128)(2,1)S(1)} collective-permute-done((bf16[160,640]{1,0:T(8,128)(2,1)S(1)}, bf16[160,640]{1,0:T(8,128)(2,1)S(1)}, u32[]{:S(2)}, u32[]{:S(2)}) %collective-permute-start.8) | collective-permute-done | bytes 204832 | tf_op jit(solution)/shard_map/ppermute | solution.py:470
  36.9 4.9 %collective-permute-done.12.refs_5_ = bf16[160,640]{1,0:T(8,128)(2,1)S(1)} collective-permute-done((bf16[160,640]{1,0:T(8,128)(2,1)S(1)}, bf16[160,640]{1,0:T(8,128)(2,1)S(1)}, u32[]{:S(2)}, u32[]{:S(2)}) %collective-permute-start.12) | collective-permute-done | bytes 204832 | tf_op jit(solution)/shard_map/ppermute | solution.py:470
  43.1 2.6 %collective-permute-done.11.refs_1_.refs_7_ = bf16[160,640]{1,0:T(8,128)(2,1)S(1)} collective-permute-done((bf16[160,640]{1,0:T(8,128)(2,1)S(1)}, bf16[160,640]{1,0:T(8,128)(2,1)S(1)}, u32[]{:S(2)}, u32[]{:S(2)}) %collective-permute-start.11) | collective-permute-done | bytes 204832 | tf_op jit(solution)/shard_map/ppermute | solution.py:470
  45.8 1.8 collective-permute-start.15
  49.9 2.5 %collective-permute-start.17 = (bf16[320,640]{1,0:T(8,128)(2,1)S(1)}, bf16[320,640]{1,0:T(8,128)(2,1)S(1)}, u32[]{:S(2)}, u32[]{:S(2)}) collective-permute-start(bf16[320,640]{1,0:T(8,128)(2,1)S(1)} %stack.18), channel_id=1, source_target_pairs={{0,4},{1,5},{2,6},{3,7},{4,0},{5,1},{6,2},{7,3},{8,12},{9,13},{10,... | collective-permute-start | bytes 1228808 | tf_op jit(solution)/shard_map/ppermute | solution.py:470
  52.4 6.3 %attend.1 = (f32[512,320]{1,0:T(8,128)S(1)}, bf16[512,320]{1,0:T(8,128)(2,1)S(1)}, bf16[512,320]{1,0:T(8,128)(2,1)S(1)}, bf16[512,1280]{1,0:T(8,128)(2,1)S(1)}, ...) custom-call(s32[3]{0:T(128)S(1)} %pad_add_fusion.refs_0_.s, ...), custom_call_target="tpu_custom_call" | custom-call | flops 1000000 | bytes 9316352 | tf_op jit(solution)/shard_map/attend/pallas_call | solution.py:30
  61.3 5.6 %context.1 = (bf16[512,320]{1,0:T(8,128)(2,1)S(1)}, bf16[512,320]{1,0:T(8,128)(2,1)S(1)}, bf16[256,1280]{1,0:T(8,128)(2,1)S(1)}, f32[256,1280]{1,0:T(8,128)S(1)}...) custom-call(s32[3]{0:T(128)S(1)} %pad_add_fusion.refs_0_.s, ...), custom_call_target="tpu_custom_call" | custom-call | flops 1000000 | bytes 9316352 | tf_op jit(solution)/shard_map/context/pallas_call | solution.py:30
  71.5 8.1 %collective-permute-done.24.refs_11_ = bf16[320,640]{1,0:T(8,128)(2,1)S(1)} collective-permute-done((bf16[320,640]{1,0:T(8,128)(2,1)S(1)}, bf16[320,640]{1,0:T(8,128)(2,1)S(1)}, u32[]{:S(2)}, u32[]{:S(2)}) %collective-permute-start.24) | collective-permute-done | bytes 409632 | tf_op jit(solution)/shard_map/ppermute | solution.py:470
  82.2 4.0 %grad_act.1 = (f32[512,320]{1,0:T(8,128)S(1)}, bf16[512,1280]{1,0:T(8,128)(2,1)S(1)}, bf16[1280,320]{1,0:T(8,128)(2,1)S(1)}, bf16[1280,320]{1,0:T(8,128)(2,1)S(1)}) custom-call(s32[3]{0:T(128)S(1)} %pad_add_fusion.refs_0_.s, bf16[128,1280]{1,0:T(8,128)(2,1)S(1)} %get-tuple-element.273.refs_1_.grad, bf16[128,1280]{1,0:T(8,128)(2,1)S(1)} %collective-permute-done.16.refs_2_, ...), custom_call_target="tpu_custom_call" | custom-call | flops 1000000 | bytes 6553600 | tf_op jit(solution)/shard_map/grad_act/pallas_call | solution.py:30
  86.2 3.7 %collective-permute-done.25.p1 = bf16[128,1280]{1,0:T(8,128)(2,1)S(1)} collective-permute-done((bf16[128,1280]{1,0:T(8,128)(2,1)S(1)}, bf16[128,1280]{1,0:T(8,128)(2,1)S(1)}, u32[]{:S(2)}, u32[]{:S(2)}) %collective-permute-start.25) | collective-permute-done | bytes 327712 | tf_op jit(solution)/shard_map/ppermute | solution.py:470
  91.5 2.3 %hidden.1 = (bf16[256,1280]{1,0:T(8,128)(2,1)S(1)}, f32[256,1280]{1,0:T(8,128)S(1)}, bf16[512,320]{1,0:T(8,128)(2,1)S(1)}, bf16[512,320]{1,0:T(8,128)(2,1)S(1)}, bf16[512,1280]{1,0:T(8,128)(2,1)S(1)}) custom-call(s32[3]{0:T(128)S(1)} %pad_add_fusion.refs_0_.s, bf16[128,1280]{1,0:T(8,128)(2,1)S(1)} %get-tuple-element.272.p0, ...), custom_call_target="tpu_custom_call" | custom-call | flops 1000000 | bytes 6727680 | tf_op jit(solution)/shard_map/hidden/pallas_call | solution.py:30
  94.0 2.9 %down.1 = (bf16[256,1280]{1,0:T(8,128)(2,1)S(1)}, f32[256,1280]{1,0:T(8,128)S(1)}, f32[1,320]{1,0:T(1,128)S(1)}, bf16[640,384]{1,0:T(8,128)(2,1)S(1)}, bf16[640,...) custom-call(s32[3]{0:T(128)S(1)} %pad_add_fusion.refs_0_.s, ...), custom_call_target="tpu_custom_call" | custom-call | flops 1000000 | bytes 7701760 | tf_op jit(solution)/shard_map/down/pallas_call | solution.py:30
  101.2 7.6 %collective-permute-done.29.got = bf16[128,1280]{1,0:T(8,128)(2,1)S(1)} collective-permute-done((bf16[128,1280]{1,0:T(8,128)(2,1)S(1)}, bf16[128,1280]{1,0:T(8,128)(2,1)S(1)}, u32[]{:S(2)}, u32[]{:S(2)}) %collective-permute-start.29) | collective-permute-done | bytes 327712 | tf_op jit(solution)/shard_map/ppermute | solution.py:470
  115.8 4.7 %collective-permute-done.34.ring_got = bf16[320,256]{1,0:T(8,128)(2,1)S(1)} collective-permute-done((bf16[320,256]{1,0:T(8,128)(2,1)S(1)}, bf16[320,256]{1,0:T(8,128)(2,1)S(1)}, u32[]{:S(2)}, u32[]{:S(2)}) %collective-permute-start.34) | collective-permute-done | bytes 163872 | tf_op jit(solution)/shard_map/ppermute | solution.py:470
  122.8 5.3 %grad_context.1 = (bf16[512,320]{1,0:T(8,128)(2,1)S(1)}, bf16[512,320]{1,0:T(8,128)(2,1)S(1)}, bf16[512,1280]{1,0:T(8,128)(2,1)}, bf16[640,384]{1,0:T(8,128)(2,1...) custom-call(s32[3]{0:T(128)S(1)} %pad_add_fusion.refs_0_.s, ...), custom_call_target="tpu_custom_call" | custom-call | flops 1000000 | bytes 9469952 | tf_op jit(solution)/shard_map/grad_context/pallas_call | solution.py:30
  132.6 2.3 %collective-permute-start.39 = (bf16[160,640]{1,0:T(8,128)(2,1)S(1)}, bf16[160,640]{1,0:T(8,128)(2,1)S(1)}, u32[]{:S(2)}, u32[]{:S(2)}) collective-permute-start(bf16[160,640]{1,0:T(8,128)(2,1)S(1)} %get-tuple-element.336), channel_id=1, source_target_pairs={{0,16},{1,17},{2,18},{3,19},{4,20},{5,21},{6,22},{7,23},{8,24},{9,... | collective-permute-start | bytes 614408 | tf_op jit(solution)/shard_map/ppermute | solution.py:470
  134.9 5.5 %grad_scores.1 = (bf16[512,640]{1,0:T(8,128)(2,1)S(1)}, f32[8,320]{1,0:T(8,128)S(1)}) custom-call(s32[3]{0:T(128)S(1)} %pad_add_fusion.refs_0_.s, bf16[4,512,512]{2,1,0:T(8,128)(2,1)S(1)} %get-tuple-element.250.refs_2_.refs_6_.refs_1_, bf16[512,320]{1,0:T(8,128)(2,1)S(1)} %get-tuple-element.327.refs_2_, bf16[512,320]{1,0:T(8,128)(2,1)S(1)} %get-tuple-element.328.refs_3_, ...), custom_call_target="tpu_custom_call" | custom-call | flops 1000000 | bytes 4739072 | tf_op jit(solution)/shard_map/grad_scores/pallas_call | solution.py:30
  140.4 4.1 %collective-permute-done.39.refs_2_ = bf16[160,640]{1,0:T(8,128)(2,1)S(1)} collective-permute-done((bf16[160,640]{1,0:T(8,128)(2,1)S(1)}, bf16[160,640]{1,0:T(8,128)(2,1)S(1)}, u32[]{:S(2)}, u32[]{:S(2)}) %collective-permute-start.39) | collective-permute-done | bytes 204832 | tf_op jit(solution)/shard_map/ppermute | solution.py:470
  144.5 3.9 %grad_first.1 = (bf16[256,1280]{1,0:T(8,128)(2,1)S(1)}, f32[256,1280]{1,0:T(8,128)S(1)}, f32[8,1280]{1,0:T(8,128)S(1)}, bf16[672,384]{1,0:T(8,128)(2,1)S(1)}, bf...) custom-call(s32[3]{0:T(128)S(1)} %pad_add_fusion.refs_0_.s, ...), custom_call_target="tpu_custom_call" | custom-call | flops 1000000 | bytes 8474176 | tf_op jit(solution)/shard_map/grad_first/pallas_call | solution.py:30
  154.4 1.8 output.1
  157.6 3.0 %collective-permute-done.43.ring_got = bf16[640,256]{1,0:T(8,128)(2,1)S(1)} collective-permute-done((bf16[640,256]{1,0:T(8,128)(2,1)S(1)}, bf16[640,256]{1,0:T(8,128)(2,1)S(1)}, u32[]{:S(2)}, u32[]{:S(2)}) %collective-permute-start.43) | collective-permute-done | bytes 327712 | tf_op jit(solution)/shard_map/ppermute | solution.py:470
  160.6 2.6 %collective-permute-done.42.pair_got = bf16[672,384]{1,0:T(8,128)(2,1)S(1)} collective-permute-done((bf16[672,384]{1,0:T(8,128)(2,1)S(1)}, bf16[672,384]{1,0:T(8,128)(2,1)S(1)}, u32[]{:S(2)}, u32[]{:S(2)}) %collective-permute-start.42) | collective-permute-done | bytes 516128 | tf_op jit(solution)/shard_map/ppermute | solution.py:470
  163.1 3.1 %collective-permute-done.47.ring_got = bf16[320,256]{1,0:T(8,128)(2,1)S(1)} collective-permute-done((bf16[320,256]{1,0:T(8,128)(2,1)S(1)}, bf16[320,256]{1,0:T(8,128)(2,1)S(1)}, u32[]{:S(2)}, u32[]{:S(2)}) %collective-permute-start.47) | collective-permute-done | bytes 163872 | tf_op jit(solution)/shard_map/ppermute | solution.py:470
  169.7 2.4 %collective-permute-start.54 = (bf16[160,640]{1,0:T(8,128)(2,1)S(1)}, bf16[160,640]{1,0:T(8,128)(2,1)S(1)}, u32[]{:S(2)}, u32[]{:S(2)}) collective-permute-start(bf16[160,640]{1,0:T(8,128)(2,1)S(1)} %get-tuple-element.402), channel_id=1, source_target_pairs={{0,16},{1,17},{2,18},{3,19},{4,20},{5,21},{6,22},{7,23},{8,24},{9,... | collective-permute-start | bytes 614408 | tf_op jit(solution)/shard_map/ppermute | solution.py:470
  172.1 2.1 %last.1 = bf16[128,1280]{1,0:T(8,128)(2,1)} custom-call(s32[3]{0:T(128)S(1)} %pad_add_fusion.refs_0_.s, f32[128,1280]{1,0:T(8,128)S(1)} %get-tuple-element.381.refs_1_, bf16[128,1280]{1,0:T(8,128)(2,1)S(1)} %collective-permute-done.45.refs_2_, bf16[128,1280]{1,0:T(8,128)(2,1)S(1)} %get-tuple-element.270.x_own.refs_3_, ...), custom_call_target="tpu_custom_call" | custom-call | flops 1000000 | bytes 2334720 | tf_op jit(solution)/shard_map/last/pallas_call | solution.py:30
  174.2 4.3 %collective-permute-done.48.pair_got = bf16[352,384]{1,0:T(8,128)(2,1)S(1)} collective-permute-done((bf16[352,384]{1,0:T(8,128)(2,1)S(1)}, bf16[352,384]{1,0:T(8,128)(2,1)S(1)}, u32[]{:S(2)}, u32[]{:S(2)}) %collective-permute-start.48) | collective-permute-done | bytes 270368 | tf_op jit(solution)/shard_map/ppermute | solution.py:470
  182.1 3.0 %collective-permute-done.51.two = f32[8,1280]{1,0:T(8,128)S(1)} collective-permute-done((f32[8,1280]{1,0:T(8,128)S(1)}, f32[8,1280]{1,0:T(8,128)S(1)}, u32[]{:S(2)}, u32[]{:S(2)}) %collective-permute-start.51) | collective-permute-done | bytes 40992 | tf_op jit(solution)/shard_map/ppermute | solution.py:470
  185.6 2.9 %collective-permute-start.52 = (f32[8,1280]{1,0:T(8,128)S(1)}, f32[8,1280]{1,0:T(8,128)S(1)}, u32[]{:S(2)}, u32[]{:S(2)}) collective-permute-start(f32[8,1280]{1,0:T(8,128)S(1)} %add.18.one), channel_id=1, source_target_pairs={{0,16},{1,17},{2,18},{3,19},{4,20},{5,21},{6,22},{7,23},{8,24},{9,... | collective-permute-start | bytes 122888 | tf_op jit(solution)/shard_map/ppermute | solution.py:470
  (116 shorter events, 71.6 us)
Async XLA Ops:
  3.3 13.7 %collective-permute-start.1 = (bf16[160,640]{1,0:T(8,128)(2,1)S(1)}, bf16[160,640]{1,0:T(8,128)(2,1)S(1)}, u32[]{:S(2)}, u32[]{:S(2)}) collective-permute-start(bf16[160,640]{1,0:T(8,128)(2,1)S(1)} %get-tuple-element.235.refs_0_.refs_6_), channel_id=1, source_target_pairs={{0,16},{1,17},{2,18},{3,19},{4,20},{5,21},{6,22},{7,23},{8,24},{9,... | collective-permute-start | bytes 614408 | tf_op jit(solution)/shard_map/ppermute | solution.py:470
  7.4 9.8 %collective-permute-start = (bf16[160,640]{1,0:T(8,128)(2,1)S(1)}, bf16[160,640]{1,0:T(8,128)(2,1)S(1)}, u32[]{:S(2)}, u32[]{:S(2)}) collective-permute-start(bf16[160,640]{1,0:T(8,128)(2,1)S(1)} %get-tuple-element.235.refs_0_.refs_6_), channel_id=1, source_target_pairs={{0,8},{1,9},{2,10},{3,11},{4,12},{5,13},{6,14},{7,15},{8,0},{9,1},... | collective-permute-start | bytes 614408 | tf_op jit(solution)/shard_map/ppermute | solution.py:470
  17.8 13.3 %collective-permute-start.9 = (bf16[320,640]{1,0:T(8,128)(2,1)S(1)}, bf16[320,640]{1,0:T(8,128)(2,1)S(1)}, u32[]{:S(2)}, u32[]{:S(2)}) collective-permute-start(bf16[320,640]{1,0:T(8,128)(2,1)S(1)} %stack.17), channel_id=1, source_target_pairs={{0,4},{1,5},{2,6},{3,7},{4,0},{5,1},{6,2},{7,3},{8,12},{9,13},{10,... | collective-permute-start | bytes 1228808 | tf_op jit(solution)/shard_map/ppermute | solution.py:470
  19.4 14.5 %collective-permute-start.3 = (bf16[128,1280]{1,0:T(8,128)(2,1)S(1)}, bf16[128,1280]{1,0:T(8,128)(2,1)S(1)}, u32[]{:S(2)}, u32[]{:S(2)}) collective-permute-start(bf16[128,1280]{1,0:T(8,128)(2,1)S(1)} %get-tuple-element.230.refs_1_), channel_id=1, source_target_pairs={{0,2},{1,3},{2,0},{3,1},{4,6},{5,7},{6,4},{7,5},{8,10},{9,11},{10,... | collective-permute-start | bytes 983048 | tf_op jit(solution)/shard_map/ppermute | solution.py:470
  20.9 9.5 %collective-permute-start.8 = (bf16[160,640]{1,0:T(8,128)(2,1)S(1)}, bf16[160,640]{1,0:T(8,128)(2,1)S(1)}, u32[]{:S(2)}, u32[]{:S(2)}) collective-permute-start(bf16[160,640]{1,0:T(8,128)(2,1)S(1)} %collective-permute-done.1.refs_0_.refs_8_), channel_id=1, source_target_pairs={{0,8},{1,9},{2,10},{3,11},{4,12},{5,13},{6,14},{7,15},{8,0},{9,1},... | collective-permute-start | bytes 614408 | tf_op jit(solution)/shard_map/ppermute | solution.py:470
  22.3 10.3 %collective-permute-start.5 = (bf16[160,640]{1,0:T(8,128)(2,1)S(1)}, bf16[160,640]{1,0:T(8,128)(2,1)S(1)}, u32[]{:S(2)}, u32[]{:S(2)}) collective-permute-start(bf16[160,640]{1,0:T(8,128)(2,1)S(1)} %get-tuple-element.252.refs_4_), channel_id=1, source_target_pairs={{0,4},{1,5},{2,6},{3,7},{4,0},{5,1},{6,2},{7,3},{8,12},{9,13},{10,... | collective-permute-start | bytes 614408 | tf_op jit(solution)/shard_map/ppermute | solution.py:470
  22.8 11.0 %collective-permute-start.4 = (bf16[160,640]{1,0:T(8,128)(2,1)S(1)}, bf16[160,640]{1,0:T(8,128)(2,1)S(1)}, u32[]{:S(2)}, u32[]{:S(2)}) collective-permute-start(bf16[160,640]{1,0:T(8,128)(2,1)S(1)} %get-tuple-element.252.refs_4_), channel_id=1, source_target_pairs={{0,16},{1,17},{2,18},{3,19},{4,20},{5,21},{6,22},{7,23},{8,24},{9,... | collective-permute-start | bytes 614408 | tf_op jit(solution)/shard_map/ppermute | solution.py:470
  31.0 14.7 %collective-permute-start.10 = (bf16[320,640]{1,0:T(8,128)(2,1)S(1)}, bf16[320,640]{1,0:T(8,128)(2,1)S(1)}, u32[]{:S(2)}, u32[]{:S(2)}) collective-permute-start(bf16[320,640]{1,0:T(8,128)(2,1)S(1)} %stack.16), channel_id=1, source_target_pairs={{0,4},{1,5},{2,6},{3,7},{4,0},{5,1},{6,2},{7,3},{8,12},{9,13},{10,... | collective-permute-start | bytes 1228808 | tf_op jit(solution)/shard_map/ppermute | solution.py:470
  33.9 11.9 %collective-permute-start.7 = (bf16[128,1280]{1,0:T(8,128)(2,1)S(1)}, bf16[128,1280]{1,0:T(8,128)(2,1)S(1)}, u32[]{:S(2)}, u32[]{:S(2)}) collective-permute-start(bf16[128,1280]{1,0:T(8,128)(2,1)S(1)} %collective-permute-done.3.refs_2_), channel_id=1, source_target_pairs={{0,1},{1,0},{2,3},{3,2},{4,5},{5,4},{6,7},{7,6},{8,9},{9,8},{10,11... | collective-permute-start | bytes 983048 | tf_op jit(solution)/shard_map/ppermute | solution.py:470
  34.6 11.2 %collective-permute-start.11 = (bf16[160,640]{1,0:T(8,128)(2,1)S(1)}, bf16[160,640]{1,0:T(8,128)(2,1)S(1)}, u32[]{:S(2)}, u32[]{:S(2)}) collective-permute-start(bf16[160,640]{1,0:T(8,128)(2,1)S(1)} %collective-permute-done.4.refs_0_.refs_6_), channel_id=1, source_target_pairs={{0,8},{1,9},{2,10},{3,11},{4,12},{5,13},{6,14},{7,15},{8,0},{9,1},... | collective-permute-start | bytes 614408 | tf_op jit(solution)/shard_map/ppermute | solution.py:470
  35.9 22.8 %collective-permute-start.16 = (bf16[128,1280]{1,0:T(8,128)(2,1)S(1)}, bf16[128,1280]{1,0:T(8,128)(2,1)S(1)}, u32[]{:S(2)}, u32[]{:S(2)}) collective-permute-start(bf16[128,1280]{1,0:T(8,128)(2,1)S(1)} %get-tuple-element.273.refs_1_.grad), channel_id=1, source_target_pairs={{0,2},{1,3},{2,0},{3,1},{4,6},{5,7},{6,4},{7,5},{8,10},{9,11},{10,... | collective-permute-start | bytes 983048 | tf_op jit(solution)/shard_map/ppermute | solution.py:470
  41.8 17.0 %collective-permute-start.13 = (bf16[160,640]{1,0:T(8,128)(2,1)S(1)}, bf16[160,640]{1,0:T(8,128)(2,1)S(1)}, u32[]{:S(2)}, u32[]{:S(2)}) collective-permute-start(bf16[160,640]{1,0:T(8,128)(2,1)S(1)} %collective-permute-done.12.refs_5_), channel_id=1, source_target_pairs={{0,4},{1,5},{2,6},{3,7},{4,0},{5,1},{6,2},{7,3},{8,12},{9,13},{10,... | collective-permute-start | bytes 614408 | tf_op jit(solution)/shard_map/ppermute | solution.py:470
  45.8 13.0 %collective-permute-start.15 = (bf16[160,640]{1,0:T(8,128)(2,1)S(1)}, bf16[160,640]{1,0:T(8,128)(2,1)S(1)}, u32[]{:S(2)}, u32[]{:S(2)}) collective-permute-start(bf16[160,640]{1,0:T(8,128)(2,1)S(1)} %get-tuple-element.277.refs_5_), channel_id=1, source_target_pairs={{0,16},{1,17},{2,18},{3,19},{4,20},{5,21},{6,22},{7,23},{8,24},{9,... | collective-permute-start | bytes 614408 | tf_op jit(solution)/shard_map/ppermute | solution.py:470
  47.6 11.3 %collective-permute-start.14 = (bf16[160,640]{1,0:T(8,128)(2,1)S(1)}, bf16[160,640]{1,0:T(8,128)(2,1)S(1)}, u32[]{:S(2)}, u32[]{:S(2)}) collective-permute-start(bf16[160,640]{1,0:T(8,128)(2,1)S(1)} %get-tuple-element.277.refs_5_), channel_id=1, source_target_pairs={{0,8},{1,9},{2,10},{3,11},{4,12},{5,13},{6,14},{7,15},{8,0},{9,1},... | collective-permute-start | bytes 614408 | tf_op jit(solution)/shard_map/ppermute | solution.py:470
  49.9 11.4 %collective-permute-start.17 = (bf16[320,640]{1,0:T(8,128)(2,1)S(1)}, bf16[320,640]{1,0:T(8,128)(2,1)S(1)}, u32[]{:S(2)}, u32[]{:S(2)}) collective-permute-start(bf16[320,640]{1,0:T(8,128)(2,1)S(1)} %stack.18), channel_id=1, source_target_pairs={{0,4},{1,5},{2,6},{3,7},{4,0},{5,1},{6,2},{7,3},{8,12},{9,13},{10,... | collective-permute-start | bytes 1228808 | tf_op jit(solution)/shard_map/ppermute | solution.py:470
  67.7 11.9 %collective-permute-start.24 = (bf16[320,640]{1,0:T(8,128)(2,1)S(1)}, bf16[320,640]{1,0:T(8,128)(2,1)S(1)}, u32[]{:S(2)}, u32[]{:S(2)}) collective-permute-start(bf16[320,640]{1,0:T(8,128)(2,1)S(1)} %stack.19), channel_id=1, source_target_pairs={{0,4},{1,5},{2,6},{3,7},{4,0},{5,1},{6,2},{7,3},{8,12},{9,13},{10,... | collective-permute-start | bytes 1228808 | tf_op jit(solution)/shard_map/ppermute | solution.py:470
  69.9 9.9 %collective-permute-start.23 = (bf16[128,1280]{1,0:T(8,128)(2,1)S(1)}, bf16[128,1280]{1,0:T(8,128)(2,1)S(1)}, u32[]{:S(2)}, u32[]{:S(2)}) collective-permute-start(bf16[128,1280]{1,0:T(8,128)(2,1)S(1)} %get-tuple-element.265), channel_id=1, source_target_pairs={{0,2},{1,3},{2,0},{3,1},{4,6},{5,7},{6,4},{7,5},{8,10},{9,11},{10,... | collective-permute-start | bytes 983048 | tf_op jit(solution)/shard_map/ppermute | solution.py:470
  97.0 13.6 %collective-permute-start.30 = (bf16[640,384]{1,0:T(8,128)(2,1)S(1)}, bf16[640,384]{1,0:T(8,128)(2,1)S(1)}, u32[]{:S(2)}, u32[]{:S(2)}) collective-permute-start(bf16[640,384]{1,0:T(8,128)(2,1)S(1)} %get-tuple-element.302), channel_id=1, source_target_pairs={{0,4},{1,5},{2,6},{3,7},{4,0},{5,1},{6,2},{7,3},{8,12},{9,13},{10,... | collective-permute-start | bytes 1474568 | tf_op jit(solution)/shard_map/ppermute | solution.py:470
  99.1 9.8 %collective-permute-start.29 = (bf16[128,1280]{1,0:T(8,128)(2,1)S(1)}, bf16[128,1280]{1,0:T(8,128)(2,1)S(1)}, u32[]{:S(2)}, u32[]{:S(2)}) collective-permute-start(bf16[128,1280]{1,0:T(8,128)(2,1)S(1)} %get-tuple-element.301), channel_id=1, source_target_pairs={{0,2},{1,3},{2,0},{3,1},{4,6},{5,7},{6,4},{7,5},{8,10},{9,11},{10,... | collective-permute-start | bytes 983048 | tf_op jit(solution)/shard_map/ppermute | solution.py:470
  111.5 9.5 %collective-permute-start.32 = (bf16[128,1280]{1,0:T(8,128)(2,1)S(1)}, bf16[128,1280]{1,0:T(8,128)(2,1)S(1)}, u32[]{:S(2)}, u32[]{:S(2)}) collective-permute-start(bf16[128,1280]{1,0:T(8,128)(2,1)S(1)} %get-tuple-element.315.refs_1_), channel_id=1, source_target_pairs={{0,2},{1,3},{2,0},{3,1},{4,6},{5,7},{6,4},{7,5},{8,10},{9,11},{10,... | collective-permute-start | bytes 983048 | tf_op jit(solution)/shard_map/ppermute | solution.py:470
  128.0 16.5 %collective-permute-start.40 = (bf16[640,384]{1,0:T(8,128)(2,1)S(1)}, bf16[640,384]{1,0:T(8,128)(2,1)S(1)}, u32[]{:S(2)}, u32[]{:S(2)}) collective-permute-start(bf16[640,384]{1,0:T(8,128)(2,1)S(1)} %get-tuple-element.337), channel_id=1, source_target_pairs={{0,4},{1,5},{2,6},{3,7},{4,0},{5,1},{6,2},{7,3},{8,12},{9,13},{10,... | collective-permute-start | bytes 1474568 | tf_op jit(solution)/shard_map/ppermute | solution.py:470
  129.5 15.0 %collective-permute-start.41 = (bf16[640,256]{1,0:T(8,128)(2,1)S(1)}, bf16[640,256]{1,0:T(8,128)(2,1)S(1)}, u32[]{:S(2)}, u32[]{:S(2)}) collective-permute-start(bf16[640,256]{1,0:T(8,128)(2,1)S(1)} %get-tuple-element.338), channel_id=1, source_target_pairs={{0,8},{1,9},{2,10},{3,11},{4,12},{5,13},{6,14},{7,15},{8,0},{9,1},... | collective-permute-start | bytes 983048 | tf_op jit(solution)/shard_map/ppermute | solution.py:470
  130.7 13.8 %collective-permute-start.38 = (bf16[128,1280]{1,0:T(8,128)(2,1)S(1)}, bf16[128,1280]{1,0:T(8,128)(2,1)S(1)}, u32[]{:S(2)}, u32[]{:S(2)}) collective-permute-start(bf16[128,1280]{1,0:T(8,128)(2,1)S(1)} %get-tuple-element.335), channel_id=1, source_target_pairs={{0,2},{1,3},{2,0},{3,1},{4,6},{5,7},{6,4},{7,5},{8,10},{9,11},{10,... | collective-permute-start | bytes 983048 | tf_op jit(solution)/shard_map/ppermute | solution.py:470
  132.6 11.9 %collective-permute-start.39 = (bf16[160,640]{1,0:T(8,128)(2,1)S(1)}, bf16[160,640]{1,0:T(8,128)(2,1)S(1)}, u32[]{:S(2)}, u32[]{:S(2)}) collective-permute-start(bf16[160,640]{1,0:T(8,128)(2,1)S(1)} %get-tuple-element.336), channel_id=1, source_target_pairs={{0,16},{1,17},{2,18},{3,19},{4,20},{5,21},{6,22},{7,23},{8,24},{9,... | collective-permute-start | bytes 614408 | tf_op jit(solution)/shard_map/ppermute | solution.py:470
  148.5 14.6 %collective-permute-start.42 = (bf16[672,384]{1,0:T(8,128)(2,1)S(1)}, bf16[672,384]{1,0:T(8,128)(2,1)S(1)}, u32[]{:S(2)}, u32[]{:S(2)}) collective-permute-start(bf16[672,384]{1,0:T(8,128)(2,1)S(1)} %get-tuple-element.347), channel_id=1, source_target_pairs={{0,4},{1,5},{2,6},{3,7},{4,0},{5,1},{6,2},{7,3},{8,12},{9,13},{10,... | collective-permute-start | bytes 1548296 | tf_op jit(solution)/shard_map/ppermute | solution.py:470
  150.0 10.6 %collective-permute-start.43 = (bf16[640,256]{1,0:T(8,128)(2,1)S(1)}, bf16[640,256]{1,0:T(8,128)(2,1)S(1)}, u32[]{:S(2)}, u32[]{:S(2)}) collective-permute-start(bf16[640,256]{1,0:T(8,128)(2,1)S(1)} %get-tuple-element.348), channel_id=1, source_target_pairs={{0,8},{1,9},{2,10},{3,11},{4,12},{5,13},{6,14},{7,15},{8,0},{9,1},... | collective-permute-start | bytes 983048 | tf_op jit(solution)/shard_map/ppermute | solution.py:470
  152.0 11.1 %collective-permute-start.45 = (bf16[128,1280]{1,0:T(8,128)(2,1)S(1)}, bf16[128,1280]{1,0:T(8,128)(2,1)S(1)}, u32[]{:S(2)}, u32[]{:S(2)}) collective-permute-start(bf16[128,1280]{1,0:T(8,128)(2,1)S(1)} %get-tuple-element.363), channel_id=1, source_target_pairs={{0,2},{1,3},{2,0},{3,1},{4,6},{5,7},{6,4},{7,5},{8,10},{9,11},{10,... | collective-permute-start | bytes 983048 | tf_op jit(solution)/shard_map/ppermute | solution.py:470
  153.2 13.0 %collective-permute-start.46 = (bf16[320,384]{1,0:T(8,128)(2,1)S(1)}, bf16[320,384]{1,0:T(8,128)(2,1)S(1)}, u32[]{:S(2)}, u32[]{:S(2)}) collective-permute-start(bf16[320,384]{1,0:T(8,128)(2,1)S(1)} %get-tuple-element.373), channel_id=1, source_target_pairs={{0,8},{1,9},{2,10},{3,11},{4,12},{5,13},{6,14},{7,15},{8,0},{9,1},... | collective-permute-start | bytes 737288 | tf_op jit(solution)/shard_map/ppermute | solution.py:470
  153.6 12.6 %collective-permute-start.47 = (bf16[320,256]{1,0:T(8,128)(2,1)S(1)}, bf16[320,256]{1,0:T(8,128)(2,1)S(1)}, u32[]{:S(2)}, u32[]{:S(2)}) collective-permute-start(bf16[320,256]{1,0:T(8,128)(2,1)S(1)} %get-tuple-element.374), channel_id=1, source_target_pairs={{0,4},{1,5},{2,6},{3,7},{4,0},{5,1},{6,2},{7,3},{8,12},{9,13},{10,... | collective-permute-start | bytes 491528 | tf_op jit(solution)/shard_map/ppermute | solution.py:470
  167.0 11.4 %collective-permute-start.48 = (bf16[352,384]{1,0:T(8,128)(2,1)S(1)}, bf16[352,384]{1,0:T(8,128)(2,1)S(1)}, u32[]{:S(2)}, u32[]{:S(2)}) collective-permute-start(bf16[352,384]{1,0:T(8,128)(2,1)S(1)} %get-tuple-element.379.refs_0_), channel_id=1, source_target_pairs={{0,8},{1,9},{2,10},{3,11},{4,12},{5,13},{6,14},{7,15},{8,0},{9,1},... | collective-permute-start | bytes 811016 | tf_op jit(solution)/shard_map/ppermute | solution.py:470
  169.7 18.9 %collective-permute-start.54 = (bf16[160,640]{1,0:T(8,128)(2,1)S(1)}, bf16[160,640]{1,0:T(8,128)(2,1)S(1)}, u32[]{:S(2)}, u32[]{:S(2)}) collective-permute-start(bf16[160,640]{1,0:T(8,128)(2,1)S(1)} %get-tuple-element.402), channel_id=1, source_target_pairs={{0,16},{1,17},{2,18},{3,19},{4,20},{5,21},{6,22},{7,23},{8,24},{9,... | collective-permute-start | bytes 614408 | tf_op jit(solution)/shard_map/ppermute | solution.py:470
  179.1 11.6 %collective-permute-start.53 = (bf16[160,640]{1,0:T(8,128)(2,1)S(1)}, bf16[160,640]{1,0:T(8,128)(2,1)S(1)}, u32[]{:S(2)}, u32[]{:S(2)}) collective-permute-start(bf16[160,640]{1,0:T(8,128)(2,1)S(1)} %get-tuple-element.397), channel_id=1, source_target_pairs={{0,16},{1,17},{2,18},{3,19},{4,20},{5,21},{6,22},{7,23},{8,24},{9,... | collective-permute-start | bytes 614408 | tf_op jit(solution)/shard_map/ppermute | solution.py:470
  (23 other events, 120.6 us)

commit v5 on v4

--- a/solution.py
+++ b/solution.py
@@ -280,13 +280,13 @@
 
 def spread_terms(term, outs, depth):
     if len(outs) == 1:
-        outs[0][...] = term[...]
+        outs[0][...] = term
         return
     pair_sent, pair_kept, ring_sent, ring_kept = outs
     cut = pair_kept.shape[1]
 
     def copy(out, at, block, columns):
-        out[pl.ds(at * depth, depth)] = term[pl.ds(block * depth, depth), columns]
+        out[pl.ds(at * depth, depth)] = term[block * depth : (block + 1) * depth, columns]
 
     for at, j in enumerate(PAIR_FIRST):
         copy(pair_sent, at, 2 * j + 1, slice(0, cut))
@@ -297,17 +297,18 @@
         copy(ring_kept, at, 2 * k + m, slice(cut, None))
 
 
-def two_terms(left_one, right_one, left_two, right_two, term):
+def two_terms(left_one, right_one, left_two, right_two):
     first = dot(left_one[...], right_one[...], TN)
     second = dot(left_two[...], right_two[...], TN)
-    term[...] = pack(first, second).astype(BF16)
-
-
-def down_kernel(depth, s, h, g, act, grad_pre, w_down, far, near, b_hidden, *refs):
-    *outs, term = refs
-    two_terms(h, grad_pre, g, act, term)
-    spread_terms(term, outs, depth)
+    return pack(first, second).astype(BF16)
+
+
+def down_kernel(depth, s, h, g, act, grad_pre, b_hidden, *outs):
+    spread_terms(two_terms(h, grad_pre, g, act), outs, depth)
     b_hidden[...] = jnp.sum(grad_pre[...].astype(F32), axis=0, keepdims=True)
+
+
+def mixer_kernel(s, act, w_down, far, near):
     split_product(act, w_down, far, near)
 
 
@@ -330,45 +331,37 @@
 
 
 def grad_context_kernel(depth, head_size, s, p0, p1, p2, p3, w_output, turned, context, h, *refs):
-    grad_context, grad_value, gm, *outs, term = refs
+    grad_context, grad_value, gm, *outs = refs
     join((p0, p1, p2, p3), gm)
     grad_context[...] = dot(gm[...], w_output[...]).astype(BF16)
     grad_value[...] = mixed_heads(turned, grad_context[...], head_size, NN).astype(BF16)
-    two_terms(h, grad_value, gm, context, term)
-    spread_terms(term, outs, depth)
+    spread_terms(two_terms(h, grad_value, gm, context), outs, depth)
 
 
 def grad_scores_kernel(head_size, s, turned, grad_context, v_low, q_low, k_low, q_raw, biases, *refs):
-    grad_qk, sums, grad_q, grad_k, scores = refs
+    grad_qk, sums, scores = refs
     rows = q_low.shape[0]
-    grad_q[...] = jnp.zeros_like(grad_q)
-    grad_k[...] = jnp.zeros_like(grad_k)
-
-    def head(number, carry):
+    grad_q = grad_k = 0.0
+    for number in range(turned.shape[0]):
         grad_chance = dot(v_low[...], of_head(grad_context[...], number, head_size), NT)
         chance = turned[number].astype(F32)
         product = chance * grad_chance
         center = jnp.sum(product, axis=0, keepdims=True)
         scores[...] = (product - chance * center).astype(BF16)
-        grad_q[...] += dot(scores[...], of_head(k_low[...], number, head_size), TN)
-        grad_k[...] += dot(scores[...], of_head(q_low[...], number, head_size))
-        return carry
-
-    for number in range(turned.shape[0]):
-        head(number, 0)
-    low = grad_q[...].astype(BF16).astype(F32)
+        grad_q = grad_q + dot(scores[...], of_head(k_low[...], number, head_size), TN)
+        grad_k = grad_k + dot(scores[...], of_head(q_low[...], number, head_size))
+    low = grad_q.astype(BF16).astype(F32)
     sums[0:1] = jnp.sum(low * q_raw[...], axis=0, keepdims=True)
     low = (low * biases[7:8]).astype(BF16).astype(F32)
-    grad_qk[...] = pack(low, grad_k[...]).astype(BF16)
+    grad_qk[...] = pack(low, grad_k).astype(BF16)
     sums[1:2] = jnp.sum(low, axis=0, keepdims=True)
 
 
 def grad_first_kernel(
     n_dp, depth, s, grad_qk, w_qk, grad_value, w_value, h, sums_in, sums_q, b_hidden, slope, *refs
 ):
-    far, near, sums, *outs, term = refs
-    term[...] = dot(h[...], grad_qk[...], TN).astype(BF16)
-    spread_terms(term, outs, depth)
+    far, near, sums, *outs = refs
+    spread_terms(dot(h[...], grad_qk[...], TN).astype(BF16), outs, depth)
     mine, place = s[0], s[1]
     gained = split_product(grad_qk, w_qk, far, near, (grad_value, w_value), h) / sums_in[0:1]
     row = lax.broadcasted_iota(jnp.int32, sums.shape, 0)
@@ -701,19 +694,20 @@
     terms = [((width, both), BF16)]
     if not wide:
         terms = [((tall_sent, c), BF16) for c in (cut, cut, both - cut, both - cut)]
-    mix_far, mix_near, grad_b_hidden, *terms_hd = run(
+    grad_b_hidden, *terms_hd = run(
         "down",
         bind(down_kernel, depth),
-        [*split, ((1, local_width), F32), *terms],
+        [((1, local_width), F32), *terms],
         h_two_all,
         grad_all,
         act,
         grad_pre,
-        w_down,
-        scratch=term,
     )
     send, keep, terms_hd = core_half(far, near, terms_hd)
     got = links.chip(send)
+    act, keep = tie(act, keep)
+    mix_far, mix_near = run("mixer", mixer_kernel, split, act, w_down)
+    got, mix_far = tie(got, mix_far)
 
     def first_send(terms):
         return [links.pair(terms[0]), links.along(terms[2], 2)]
@@ -758,7 +752,10 @@
         grad_mid_chip, got_hd = tie(grad_mid_chip, got_hd)
         sent_hd, zero_hd = second_sum("hd", sums_hd, got_hd)
         grad_mid_rows = grad_mid_low, grad_mid_chip, links.core(grad_mid_low), links.core(grad_mid_chip)
-    grad_mid_rows, mix_far = tie(grad_mid_rows, mix_far)
+    if wide:
+        grad_mid_rows, mix_far = tie(grad_mid_rows, mix_far)
+    else:
+        grad_mid_rows, mix_far, sent_hd = tie(grad_mid_rows, mix_far, sent_hd)
     mix_send, mix_keep = core_half(mix_far, mix_near)
     mix_got = links.chip(mix_send)
     grad_context, grad_value, _, *terms_vo = run(
@@ -770,7 +767,6 @@
         turned,
         context,
         h_all,
-        scratch=term,
     )
     if not wide:
         got_vo = first_send(terms_vo)
@@ -787,11 +783,7 @@
         k_low,
         q_raw,
         biases,
-        scratch=[
-            pltpu.VMEM((all_rows, local_width), F32),
-            pltpu.VMEM((all_rows, local_width), F32),
-            pltpu.VMEM((all_rows, all_rows), BF16),
-        ],
+        scratch=[pltpu.VMEM((all_rows, all_rows), BF16)],
     )
     if wide:
         grad_qk, mix_got = tie(grad_qk, mix_got)
@@ -813,7 +805,6 @@
         sums_q,
         grad_b_hidden,
         slope,
-        scratch=term,
     )
     def exchange(value, step):
         return run("add", add_kernel, [vector], value, links.move(value, step))[0]

time: 193 us -> 192 us (level)
  waiting for transfers between devices: 69.6 us -> 66.8 us
    ppermute x55, waiting for transfers between devices: 69.6 us -> 66.8 us  [move(): return lax.ppermute(value, AXES, pairs)]
    pallas_call x34 -> x35, Pallas kernels: 62.1 us -> 62.3 us  [call(): pl.pallas_call(kernel, name=name, out_shape=outs, in_specs=[pl.BlockSpec(...]
  transfers between devices with their start and end apart: 55 -> 55, of which waited for: 27 -> 28; matrix products, arithmetic and copies ran while one was open for 0% -> 0% of each run, Pallas kernels for 26% -> 26%
where the time goes in v5:
time: 192 us
  waiting for transfers between devices  66.8 us (35%)
  Pallas kernels  62.3 us (32%)
  starting transfers between devices  60.7 us (32%)
    ppermute x55, waiting for transfers between devices, move(): return lax.ppermute(value, AXES, pairs)  66.8 us
    pallas_call x35, Pallas kernels, call(): pl.pallas_call(kernel, name=name, out_shape=outs, in_specs=[pl.BlockSpec(...  62.3 us
    ppermute x55, starting transfers between devices, move(): return lax.ppermute(value, AXES, pairs)  60.7 us
  transfers between devices with their start and end apart: 55, of which 28 were waited for; matrix products, arithmetic and copies ran while one was open for 0% of the time, Pallas kernels for 26%

profile of v5, /device:TPU:0, one launch (start us, length us, event | category | flops | bytes accessed | tf_op | source)
XLA Modules:
  0.0 192.2 jit_solution(66004549944004868)
XLA Ops:
  1.4 1.9 %pack.1 = (bf16[160,640]{1,0:T(8,128)(2,1)S(1)}, bf16[160,640]{1,0:T(8,128)(2,1)S(1)}, bf16[160,640]{1,0:T(8,128)(2,1)S(1)}) custom-call(s32[3]{0:T(128)S(1)} %pad_add_fusion.refs_0_.s, bf16[160,320]{1,0:T(8,128)(2,1)} %refs_0_.1, bf16[160,320]{1,0:T(8,128)(2,1)} %refs_1_.1, bf16[160,320]{1,0:T(8,128)(2,1)} %refs_2_.3, bf16[160,320]{1,0:T(8,128)(2,1)} %bitcast.23, ...), custom_call_target="tpu_custom_call" | custom-call | flops 1000000 | bytes 1228800 | tf_op jit(solution)/shard_map/pack/pallas_call | solution.py:30
  3.3 4.1 %collective-permute-start.1 = (bf16[160,640]{1,0:T(8,128)(2,1)S(1)}, bf16[160,640]{1,0:T(8,128)(2,1)S(1)}, u32[]{:S(2)}, u32[]{:S(2)}) collective-permute-start(bf16[160,640]{1,0:T(8,128)(2,1)S(1)} %get-tuple-element.240.refs_0_.refs_6_), channel_id=1, source_target_pairs={{0,16},{1,17},{2,18},{3,19},{4,20},{5,21},{6,22},{7,23},{8,24},{9,... | collective-permute-start | bytes 614408 | tf_op jit(solution)/shard_map/ppermute | solution.py:463
  11.3 3.2 %prepare.1 = (bf16[128,1280]{1,0:T(8,128)(2,1)S(1)}, bf16[128,1280]{1,0:T(8,128)(2,1)S(1)}, bf16[128,1280]{1,0:T(8,128)(2,1)S(1)}, f32[8,1280]{1,0:T(8,128)S(1)}, f32[8,320]{1,0:T(8,128)S(1)}) custom-call(s32[3]{0:T(128)S(1)} %pad_add_fusion.refs_0_.s, f32[1,320]{1,0:T(1,128)S(1)} %broadcast_in_dim_tile.3.refs_1_, bf16[128,1280]{1,0:T(8,128)(2,1)} %refs_2_.2, ...), custom_call_target="tpu_custom_call" | custom-call | flops 1000000 | bytes 1726720 | tf_op jit(solution)/shard_map/prepare/pallas_call | solution.py:30
  22.8 2.3 %collective-permute-start.4 = (bf16[160,640]{1,0:T(8,128)(2,1)S(1)}, bf16[160,640]{1,0:T(8,128)(2,1)S(1)}, u32[]{:S(2)}, u32[]{:S(2)}) collective-permute-start(bf16[160,640]{1,0:T(8,128)(2,1)S(1)} %get-tuple-element.257.refs_4_), channel_id=1, source_target_pairs={{0,16},{1,17},{2,18},{3,19},{4,20},{5,21},{6,22},{7,23},{8,24},{9,... | collective-permute-start | bytes 614408 | tf_op jit(solution)/shard_map/ppermute | solution.py:463
  25.1 5.3 %collective-permute-done.8.refs_1_.refs_9_ = bf16[160,640]{1,0:T(8,128)(2,1)S(1)} collective-permute-done((bf16[160,640]{1,0:T(8,128)(2,1)S(1)}, bf16[160,640]{1,0:T(8,128)(2,1)S(1)}, u32[]{:S(2)}, u32[]{:S(2)}) %collective-permute-start.8) | collective-permute-done | bytes 204832 | tf_op jit(solution)/shard_map/ppermute | solution.py:463
  36.9 4.9 %collective-permute-done.12.refs_5_ = bf16[160,640]{1,0:T(8,128)(2,1)S(1)} collective-permute-done((bf16[160,640]{1,0:T(8,128)(2,1)S(1)}, bf16[160,640]{1,0:T(8,128)(2,1)S(1)}, u32[]{:S(2)}, u32[]{:S(2)}) %collective-permute-start.12) | collective-permute-done | bytes 204832 | tf_op jit(solution)/shard_map/ppermute | solution.py:463
  43.1 2.6 %collective-permute-done.11.refs_1_.refs_7_ = bf16[160,640]{1,0:T(8,128)(2,1)S(1)} collective-permute-done((bf16[160,640]{1,0:T(8,128)(2,1)S(1)}, bf16[160,640]{1,0:T(8,128)(2,1)S(1)}, u32[]{:S(2)}, u32[]{:S(2)}) %collective-permute-start.11) | collective-permute-done | bytes 204832 | tf_op jit(solution)/shard_map/ppermute | solution.py:463
  49.9 2.5 %collective-permute-start.17 = (bf16[320,640]{1,0:T(8,128)(2,1)S(1)}, bf16[320,640]{1,0:T(8,128)(2,1)S(1)}, u32[]{:S(2)}, u32[]{:S(2)}) collective-permute-start(bf16[320,640]{1,0:T(8,128)(2,1)S(1)} %stack.18), channel_id=1, source_target_pairs={{0,4},{1,5},{2,6},{3,7},{4,0},{5,1},{6,2},{7,3},{8,12},{9,13},{10,... | collective-permute-start | bytes 1228808 | tf_op jit(solution)/shard_map/ppermute | solution.py:463
  52.4 6.3 %attend.1 = (f32[512,320]{1,0:T(8,128)S(1)}, bf16[512,320]{1,0:T(8,128)(2,1)S(1)}, bf16[512,320]{1,0:T(8,128)(2,1)S(1)}, bf16[512,1280]{1,0:T(8,128)(2,1)S(1)}, ...) custom-call(s32[3]{0:T(128)S(1)} %pad_add_fusion.refs_0_.s, ...), custom_call_target="tpu_custom_call" | custom-call | flops 1000000 | bytes 9316352 | tf_op jit(solution)/shard_map/attend/pallas_call | solution.py:30
  61.3 5.6 %context.1 = (bf16[512,320]{1,0:T(8,128)(2,1)S(1)}, bf16[512,320]{1,0:T(8,128)(2,1)S(1)}, bf16[256,1280]{1,0:T(8,128)(2,1)S(1)}, f32[256,1280]{1,0:T(8,128)S(1)}...) custom-call(s32[3]{0:T(128)S(1)} %pad_add_fusion.refs_0_.s, ...), custom_call_target="tpu_custom_call" | custom-call | flops 1000000 | bytes 9316352 | tf_op jit(solution)/shard_map/context/pallas_call | solution.py:30
  71.5 8.1 %collective-permute-done.24.refs_11_ = bf16[320,640]{1,0:T(8,128)(2,1)S(1)} collective-permute-done((bf16[320,640]{1,0:T(8,128)(2,1)S(1)}, bf16[320,640]{1,0:T(8,128)(2,1)S(1)}, u32[]{:S(2)}, u32[]{:S(2)}) %collective-permute-start.24) | collective-permute-done | bytes 409632 | tf_op jit(solution)/shard_map/ppermute | solution.py:463
  82.2 4.0 %grad_act.1 = (f32[512,320]{1,0:T(8,128)S(1)}, bf16[512,1280]{1,0:T(8,128)(2,1)S(1)}, bf16[1280,320]{1,0:T(8,128)(2,1)S(1)}, bf16[1280,320]{1,0:T(8,128)(2,1)S(1)}) custom-call(s32[3]{0:T(128)S(1)} %pad_add_fusion.refs_0_.s, bf16[128,1280]{1,0:T(8,128)(2,1)S(1)} %get-tuple-element.278.refs_1_.grad, bf16[128,1280]{1,0:T(8,128)(2,1)S(1)} %collective-permute-done.16.refs_2_, ...), custom_call_target="tpu_custom_call" | custom-call | flops 1000000 | bytes 6553600 | tf_op jit(solution)/shard_map/grad_act/pallas_call | solution.py:30
  86.1 3.7 %collective-permute-done.25.p1 = bf16[128,1280]{1,0:T(8,128)(2,1)S(1)} collective-permute-done((bf16[128,1280]{1,0:T(8,128)(2,1)S(1)}, bf16[128,1280]{1,0:T(8,128)(2,1)S(1)}, u32[]{:S(2)}, u32[]{:S(2)}) %collective-permute-start.25) | collective-permute-done | bytes 327712 | tf_op jit(solution)/shard_map/ppermute | solution.py:463
  91.5 2.3 %hidden.1 = (bf16[256,1280]{1,0:T(8,128)(2,1)S(1)}, f32[256,1280]{1,0:T(8,128)S(1)}, bf16[512,320]{1,0:T(8,128)(2,1)S(1)}, bf16[512,320]{1,0:T(8,128)(2,1)S(1)}, bf16[512,1280]{1,0:T(8,128)(2,1)S(1)}) custom-call(s32[3]{0:T(128)S(1)} %pad_add_fusion.refs_0_.s, bf16[128,1280]{1,0:T(8,128)(2,1)S(1)} %get-tuple-element.277.p0, ...), custom_call_target="tpu_custom_call" | custom-call | flops 1000000 | bytes 6727680 | tf_op jit(solution)/shard_map/hidden/pallas_call | solution.py:30
  94.0 2.2 %down.1 = (f32[1,320]{1,0:T(1,128)S(1)}, bf16[640,384]{1,0:T(8,128)(2,1)S(1)}, bf16[640,384]{1,0:T(8,128)(2,1)S(1)}, bf16[640,256]{1,0:T(8,128)(2,1)S(1)}, bf16[640,256]{1,0:T(8,128)(2,1)S(1)}) custom-call(s32[3]{0:T(128)S(1)} %pad_add_fusion.refs_0_.s, bf16[512,1280]{1,0:T(8,128)(2,1)S(1)} %get-tuple-element.296.refs_1_, ...), custom_call_target="tpu_custom_call" | custom-call | flops 1000000 | bytes 4916480 | tf_op jit(solution)/shard_map/down/pallas_call | solution.py:30
  101.9 6.2 %collective-permute-done.29.got = bf16[128,1280]{1,0:T(8,128)(2,1)S(1)} collective-permute-done((bf16[128,1280]{1,0:T(8,128)(2,1)S(1)}, bf16[128,1280]{1,0:T(8,128)(2,1)S(1)}, u32[]{:S(2)}, u32[]{:S(2)}) %collective-permute-start.29) | collective-permute-done | bytes 327712 | tf_op jit(solution)/shard_map/ppermute | solution.py:463
  115.0 4.7 %collective-permute-done.34.ring_got = bf16[320,256]{1,0:T(8,128)(2,1)S(1)} collective-permute-done((bf16[320,256]{1,0:T(8,128)(2,1)S(1)}, bf16[320,256]{1,0:T(8,128)(2,1)S(1)}, u32[]{:S(2)}, u32[]{:S(2)}) %collective-permute-start.34) | collective-permute-done | bytes 163872 | tf_op jit(solution)/shard_map/ppermute | solution.py:463
  122.0 5.1 %grad_context.1 = (bf16[512,320]{1,0:T(8,128)(2,1)S(1)}, bf16[512,320]{1,0:T(8,128)(2,1)S(1)}, bf16[512,1280]{1,0:T(8,128)(2,1)}, bf16[640,384]{1,0:T(8,128)(2,1...) custom-call(s32[3]{0:T(128)S(1)} %pad_add_fusion.refs_0_.s, ...), custom_call_target="tpu_custom_call" | custom-call | flops 1000000 | bytes 9469952 | tf_op jit(solution)/shard_map/grad_context/pallas_call | solution.py:30
  131.1 2.2 %collective-permute-start.39 = (bf16[160,640]{1,0:T(8,128)(2,1)S(1)}, bf16[160,640]{1,0:T(8,128)(2,1)S(1)}, u32[]{:S(2)}, u32[]{:S(2)}) collective-permute-start(bf16[160,640]{1,0:T(8,128)(2,1)S(1)} %get-tuple-element.346), channel_id=1, source_target_pairs={{0,16},{1,17},{2,18},{3,19},{4,20},{5,21},{6,22},{7,23},{8,24},{9,... | collective-permute-start | bytes 614408 | tf_op jit(solution)/shard_map/ppermute | solution.py:463
  133.3 5.3 %grad_scores.1 = (bf16[512,640]{1,0:T(8,128)(2,1)S(1)}, f32[8,320]{1,0:T(8,128)S(1)}) custom-call(s32[3]{0:T(128)S(1)} %pad_add_fusion.refs_0_.s, bf16[4,512,512]{2,1,0:T(8,128)(2,1)S(1)} %get-tuple-element.255.refs_2_.refs_6_.refs_1_, bf16[512,320]{1,0:T(8,128)(2,1)S(1)} %get-tuple-element.337.refs_2_, bf16[512,320]{1,0:T(8,128)(2,1)S(1)} %get-tuple-element.338.refs_3_, ...), custom_call_target="tpu_custom_call" | custom-call | flops 1000000 | bytes 4739072 | tf_op jit(solution)/shard_map/grad_scores/pallas_call | solution.py:30
  138.6 2.2 %collective-permute-done.39.refs_2_ = bf16[160,640]{1,0:T(8,128)(2,1)S(1)} collective-permute-done((bf16[160,640]{1,0:T(8,128)(2,1)S(1)}, bf16[160,640]{1,0:T(8,128)(2,1)S(1)}, u32[]{:S(2)}, u32[]{:S(2)}) %collective-permute-start.39) | collective-permute-done | bytes 204832 | tf_op jit(solution)/shard_map/ppermute | solution.py:463
  140.7 1.9 collective-permute-done.41.ring_got
  142.6 3.8 %grad_first.1 = (bf16[256,1280]{1,0:T(8,128)(2,1)S(1)}, f32[256,1280]{1,0:T(8,128)S(1)}, f32[8,1280]{1,0:T(8,128)S(1)}, bf16[672,384]{1,0:T(8,128)(2,1)S(1)}, bf...) custom-call(s32[3]{0:T(128)S(1)} %pad_add_fusion.refs_0_.s, ...), custom_call_target="tpu_custom_call" | custom-call | flops 1000000 | bytes 8474176 | tf_op jit(solution)/shard_map/grad_first/pallas_call | solution.py:30
  147.2 2.2 %collective-permute-start.43 = (bf16[640,256]{1,0:T(8,128)(2,1)S(1)}, bf16[640,256]{1,0:T(8,128)(2,1)S(1)}, u32[]{:S(2)}, u32[]{:S(2)}) collective-permute-start(bf16[640,256]{1,0:T(8,128)(2,1)S(1)} %get-tuple-element.358), channel_id=1, source_target_pairs={{0,8},{1,9},{2,10},{3,11},{4,12},{5,13},{6,14},{7,15},{8,0},{9,1},... | collective-permute-start | bytes 983048 | tf_op jit(solution)/shard_map/ppermute | solution.py:463
  153.4 1.8 output.1
  157.9 3.2 %collective-permute-done.42.pair_got = bf16[672,384]{1,0:T(8,128)(2,1)S(1)} collective-permute-done((bf16[672,384]{1,0:T(8,128)(2,1)S(1)}, bf16[672,384]{1,0:T(8,128)(2,1)S(1)}, u32[]{:S(2)}, u32[]{:S(2)}) %collective-permute-start.42) | collective-permute-done | bytes 516128 | tf_op jit(solution)/shard_map/ppermute | solution.py:463
  161.1 3.1 %collective-permute-done.47.ring_got = bf16[320,256]{1,0:T(8,128)(2,1)S(1)} collective-permute-done((bf16[320,256]{1,0:T(8,128)(2,1)S(1)}, bf16[320,256]{1,0:T(8,128)(2,1)S(1)}, u32[]{:S(2)}, u32[]{:S(2)}) %collective-permute-start.47) | collective-permute-done | bytes 163872 | tf_op jit(solution)/shard_map/ppermute | solution.py:463
  170.3 2.1 %last.1 = bf16[128,1280]{1,0:T(8,128)(2,1)} custom-call(s32[3]{0:T(128)S(1)} %pad_add_fusion.refs_0_.s, f32[128,1280]{1,0:T(8,128)S(1)} %get-tuple-element.391.refs_1_, bf16[128,1280]{1,0:T(8,128)(2,1)S(1)} %collective-permute-done.45.refs_2_, bf16[128,1280]{1,0:T(8,128)(2,1)S(1)} %get-tuple-element.275.x_own.refs_3_, ...), custom_call_target="tpu_custom_call" | custom-call | flops 1000000 | bytes 2334720 | tf_op jit(solution)/shard_map/last/pallas_call | solution.py:30
  172.4 3.7 %collective-permute-done.48.pair_got = bf16[352,384]{1,0:T(8,128)(2,1)S(1)} collective-permute-done((bf16[352,384]{1,0:T(8,128)(2,1)S(1)}, bf16[352,384]{1,0:T(8,128)(2,1)S(1)}, u32[]{:S(2)}, u32[]{:S(2)}) %collective-permute-start.48) | collective-permute-done | bytes 270368 | tf_op jit(solution)/shard_map/ppermute | solution.py:463
  180.8 2.7 %collective-permute-done.51.two = f32[8,1280]{1,0:T(8,128)S(1)} collective-permute-done((f32[8,1280]{1,0:T(8,128)S(1)}, f32[8,1280]{1,0:T(8,128)S(1)}, u32[]{:S(2)}, u32[]{:S(2)}) %collective-permute-start.51) | collective-permute-done | bytes 40992 | tf_op jit(solution)/shard_map/ppermute | solution.py:463
  184.0 2.2 %collective-permute-start.52 = (f32[8,1280]{1,0:T(8,128)S(1)}, f32[8,1280]{1,0:T(8,128)S(1)}, u32[]{:S(2)}, u32[]{:S(2)}) collective-permute-start(f32[8,1280]{1,0:T(8,128)S(1)} %add.18.one), channel_id=1, source_target_pairs={{0,16},{1,17},{2,18},{3,19},{4,20},{5,21},{6,22},{7,23},{8,24},{9,... | collective-permute-start | bytes 122888 | tf_op jit(solution)/shard_map/ppermute | solution.py:463
  187.6 2.1 %collective-permute-done.53.refs_2_ = bf16[160,640]{1,0:T(8,128)(2,1)S(1)} collective-permute-done((bf16[160,640]{1,0:T(8,128)(2,1)S(1)}, bf16[160,640]{1,0:T(8,128)(2,1)S(1)}, u32[]{:S(2)}, u32[]{:S(2)}) %collective-permute-start.53) | collective-permute-done | bytes 204832 | tf_op jit(solution)/shard_map/ppermute | solution.py:463
  (117 shorter events, 77.0 us)
Async XLA Ops:
  3.3 13.7 %collective-permute-start.1 = (bf16[160,640]{1,0:T(8,128)(2,1)S(1)}, bf16[160,640]{1,0:T(8,128)(2,1)S(1)}, u32[]{:S(2)}, u32[]{:S(2)}) collective-permute-start(bf16[160,640]{1,0:T(8,128)(2,1)S(1)} %get-tuple-element.240.refs_0_.refs_6_), channel_id=1, source_target_pairs={{0,16},{1,17},{2,18},{3,19},{4,20},{5,21},{6,22},{7,23},{8,24},{9,... | collective-permute-start | bytes 614408 | tf_op jit(solution)/shard_map/ppermute | solution.py:463
  7.4 9.8 %collective-permute-start = (bf16[160,640]{1,0:T(8,128)(2,1)S(1)}, bf16[160,640]{1,0:T(8,128)(2,1)S(1)}, u32[]{:S(2)}, u32[]{:S(2)}) collective-permute-start(bf16[160,640]{1,0:T(8,128)(2,1)S(1)} %get-tuple-element.240.refs_0_.refs_6_), channel_id=1, source_target_pairs={{0,8},{1,9},{2,10},{3,11},{4,12},{5,13},{6,14},{7,15},{8,0},{9,1},... | collective-permute-start | bytes 614408 | tf_op jit(solution)/shard_map/ppermute | solution.py:463
  17.8 13.3 %collective-permute-start.9 = (bf16[320,640]{1,0:T(8,128)(2,1)S(1)}, bf16[320,640]{1,0:T(8,128)(2,1)S(1)}, u32[]{:S(2)}, u32[]{:S(2)}) collective-permute-start(bf16[320,640]{1,0:T(8,128)(2,1)S(1)} %stack.17), channel_id=1, source_target_pairs={{0,4},{1,5},{2,6},{3,7},{4,0},{5,1},{6,2},{7,3},{8,12},{9,13},{10,... | collective-permute-start | bytes 1228808 | tf_op jit(solution)/shard_map/ppermute | solution.py:463
  19.4 14.5 %collective-permute-start.3 = (bf16[128,1280]{1,0:T(8,128)(2,1)S(1)}, bf16[128,1280]{1,0:T(8,128)(2,1)S(1)}, u32[]{:S(2)}, u32[]{:S(2)}) collective-permute-start(bf16[128,1280]{1,0:T(8,128)(2,1)S(1)} %get-tuple-element.235.refs_1_), channel_id=1, source_target_pairs={{0,2},{1,3},{2,0},{3,1},{4,6},{5,7},{6,4},{7,5},{8,10},{9,11},{10,... | collective-permute-start | bytes 983048 | tf_op jit(solution)/shard_map/ppermute | solution.py:463
  20.9 9.5 %collective-permute-start.8 = (bf16[160,640]{1,0:T(8,128)(2,1)S(1)}, bf16[160,640]{1,0:T(8,128)(2,1)S(1)}, u32[]{:S(2)}, u32[]{:S(2)}) collective-permute-start(bf16[160,640]{1,0:T(8,128)(2,1)S(1)} %collective-permute-done.1.refs_0_.refs_8_), channel_id=1, source_target_pairs={{0,8},{1,9},{2,10},{3,11},{4,12},{5,13},{6,14},{7,15},{8,0},{9,1},... | collective-permute-start | bytes 614408 | tf_op jit(solution)/shard_map/ppermute | solution.py:463
  22.3 10.3 %collective-permute-start.5 = (bf16[160,640]{1,0:T(8,128)(2,1)S(1)}, bf16[160,640]{1,0:T(8,128)(2,1)S(1)}, u32[]{:S(2)}, u32[]{:S(2)}) collective-permute-start(bf16[160,640]{1,0:T(8,128)(2,1)S(1)} %get-tuple-element.257.refs_4_), channel_id=1, source_target_pairs={{0,4},{1,5},{2,6},{3,7},{4,0},{5,1},{6,2},{7,3},{8,12},{9,13},{10,... | collective-permute-start | bytes 614408 | tf_op jit(solution)/shard_map/ppermute | solution.py:463
  22.8 11.0 %collective-permute-start.4 = (bf16[160,640]{1,0:T(8,128)(2,1)S(1)}, bf16[160,640]{1,0:T(8,128)(2,1)S(1)}, u32[]{:S(2)}, u32[]{:S(2)}) collective-permute-start(bf16[160,640]{1,0:T(8,128)(2,1)S(1)} %get-tuple-element.257.refs_4_), channel_id=1, source_target_pairs={{0,16},{1,17},{2,18},{3,19},{4,20},{5,21},{6,22},{7,23},{8,24},{9,... | collective-permute-start | bytes 614408 | tf_op jit(solution)/shard_map/ppermute | solution.py:463
  31.0 14.7 %collective-permute-start.10 = (bf16[320,640]{1,0:T(8,128)(2,1)S(1)}, bf16[320,640]{1,0:T(8,128)(2,1)S(1)}, u32[]{:S(2)}, u32[]{:S(2)}) collective-permute-start(bf16[320,640]{1,0:T(8,128)(2,1)S(1)} %stack.16), channel_id=1, source_target_pairs={{0,4},{1,5},{2,6},{3,7},{4,0},{5,1},{6,2},{7,3},{8,12},{9,13},{10,... | collective-permute-start | bytes 1228808 | tf_op jit(solution)/shard_map/ppermute | solution.py:463
  33.9 11.9 %collective-permute-start.7 = (bf16[128,1280]{1,0:T(8,128)(2,1)S(1)}, bf16[128,1280]{1,0:T(8,128)(2,1)S(1)}, u32[]{:S(2)}, u32[]{:S(2)}) collective-permute-start(bf16[128,1280]{1,0:T(8,128)(2,1)S(1)} %collective-permute-done.3.refs_2_), channel_id=1, source_target_pairs={{0,1},{1,0},{2,3},{3,2},{4,5},{5,4},{6,7},{7,6},{8,9},{9,8},{10,11... | collective-permute-start | bytes 983048 | tf_op jit(solution)/shard_map/ppermute | solution.py:463
  34.6 11.2 %collective-permute-start.11 = (bf16[160,640]{1,0:T(8,128)(2,1)S(1)}, bf16[160,640]{1,0:T(8,128)(2,1)S(1)}, u32[]{:S(2)}, u32[]{:S(2)}) collective-permute-start(bf16[160,640]{1,0:T(8,128)(2,1)S(1)} %collective-permute-done.4.refs_0_.refs_6_), channel_id=1, source_target_pairs={{0,8},{1,9},{2,10},{3,11},{4,12},{5,13},{6,14},{7,15},{8,0},{9,1},... | collective-permute-start | bytes 614408 | tf_op jit(solution)/shard_map/ppermute | solution.py:463
  35.9 22.8 %collective-permute-start.16 = (bf16[128,1280]{1,0:T(8,128)(2,1)S(1)}, bf16[128,1280]{1,0:T(8,128)(2,1)S(1)}, u32[]{:S(2)}, u32[]{:S(2)}) collective-permute-start(bf16[128,1280]{1,0:T(8,128)(2,1)S(1)} %get-tuple-element.278.refs_1_.grad), channel_id=1, source_target_pairs={{0,2},{1,3},{2,0},{3,1},{4,6},{5,7},{6,4},{7,5},{8,10},{9,11},{10,... | collective-permute-start | bytes 983048 | tf_op jit(solution)/shard_map/ppermute | solution.py:463
  41.8 17.0 %collective-permute-start.13 = (bf16[160,640]{1,0:T(8,128)(2,1)S(1)}, bf16[160,640]{1,0:T(8,128)(2,1)S(1)}, u32[]{:S(2)}, u32[]{:S(2)}) collective-permute-start(bf16[160,640]{1,0:T(8,128)(2,1)S(1)} %collective-permute-done.12.refs_5_), channel_id=1, source_target_pairs={{0,4},{1,5},{2,6},{3,7},{4,0},{5,1},{6,2},{7,3},{8,12},{9,13},{10,... | collective-permute-start | bytes 614408 | tf_op jit(solution)/shard_map/ppermute | solution.py:463
  45.8 13.0 %collective-permute-start.15 = (bf16[160,640]{1,0:T(8,128)(2,1)S(1)}, bf16[160,640]{1,0:T(8,128)(2,1)S(1)}, u32[]{:S(2)}, u32[]{:S(2)}) collective-permute-start(bf16[160,640]{1,0:T(8,128)(2,1)S(1)} %get-tuple-element.282.refs_5_), channel_id=1, source_target_pairs={{0,16},{1,17},{2,18},{3,19},{4,20},{5,21},{6,22},{7,23},{8,24},{9,... | collective-permute-start | bytes 614408 | tf_op jit(solution)/shard_map/ppermute | solution.py:463
  47.6 11.3 %collective-permute-start.14 = (bf16[160,640]{1,0:T(8,128)(2,1)S(1)}, bf16[160,640]{1,0:T(8,128)(2,1)S(1)}, u32[]{:S(2)}, u32[]{:S(2)}) collective-permute-start(bf16[160,640]{1,0:T(8,128)(2,1)S(1)} %get-tuple-element.282.refs_5_), channel_id=1, source_target_pairs={{0,8},{1,9},{2,10},{3,11},{4,12},{5,13},{6,14},{7,15},{8,0},{9,1},... | collective-permute-start | bytes 614408 | tf_op jit(solution)/shard_map/ppermute | solution.py:463
  49.9 11.4 %collective-permute-start.17 = (bf16[320,640]{1,0:T(8,128)(2,1)S(1)}, bf16[320,640]{1,0:T(8,128)(2,1)S(1)}, u32[]{:S(2)}, u32[]{:S(2)}) collective-permute-start(bf16[320,640]{1,0:T(8,128)(2,1)S(1)} %stack.18), channel_id=1, source_target_pairs={{0,4},{1,5},{2,6},{3,7},{4,0},{5,1},{6,2},{7,3},{8,12},{9,13},{10,... | collective-permute-start | bytes 1228808 | tf_op jit(solution)/shard_map/ppermute | solution.py:463
  67.7 11.9 %collective-permute-start.24 = (bf16[320,640]{1,0:T(8,128)(2,1)S(1)}, bf16[320,640]{1,0:T(8,128)(2,1)S(1)}, u32[]{:S(2)}, u32[]{:S(2)}) collective-permute-start(bf16[320,640]{1,0:T(8,128)(2,1)S(1)} %stack.19), channel_id=1, source_target_pairs={{0,4},{1,5},{2,6},{3,7},{4,0},{5,1},{6,2},{7,3},{8,12},{9,13},{10,... | collective-permute-start | bytes 1228808 | tf_op jit(solution)/shard_map/ppermute | solution.py:463
  69.9 9.9 %collective-permute-start.23 = (bf16[128,1280]{1,0:T(8,128)(2,1)S(1)}, bf16[128,1280]{1,0:T(8,128)(2,1)S(1)}, u32[]{:S(2)}, u32[]{:S(2)}) collective-permute-start(bf16[128,1280]{1,0:T(8,128)(2,1)S(1)} %get-tuple-element.270), channel_id=1, source_target_pairs={{0,2},{1,3},{2,0},{3,1},{4,6},{5,7},{6,4},{7,5},{8,10},{9,11},{10,... | collective-permute-start | bytes 983048 | tf_op jit(solution)/shard_map/ppermute | solution.py:463
  96.2 13.5 %collective-permute-start.30 = (bf16[640,384]{1,0:T(8,128)(2,1)S(1)}, bf16[640,384]{1,0:T(8,128)(2,1)S(1)}, u32[]{:S(2)}, u32[]{:S(2)}) collective-permute-start(bf16[640,384]{1,0:T(8,128)(2,1)S(1)} %get-tuple-element.311), channel_id=1, source_target_pairs={{0,4},{1,5},{2,6},{3,7},{4,0},{5,1},{6,2},{7,3},{8,12},{9,13},{10,... | collective-permute-start | bytes 1474568 | tf_op jit(solution)/shard_map/ppermute | solution.py:463
  98.4 9.8 %collective-permute-start.29 = (bf16[128,1280]{1,0:T(8,128)(2,1)S(1)}, bf16[128,1280]{1,0:T(8,128)(2,1)S(1)}, u32[]{:S(2)}, u32[]{:S(2)}) collective-permute-start(bf16[128,1280]{1,0:T(8,128)(2,1)S(1)} %get-tuple-element.306), channel_id=1, source_target_pairs={{0,2},{1,3},{2,0},{3,1},{4,6},{5,7},{6,4},{7,5},{8,10},{9,11},{10,... | collective-permute-start | bytes 983048 | tf_op jit(solution)/shard_map/ppermute | solution.py:463
  110.7 9.5 %collective-permute-start.32 = (bf16[128,1280]{1,0:T(8,128)(2,1)S(1)}, bf16[128,1280]{1,0:T(8,128)(2,1)S(1)}, u32[]{:S(2)}, u32[]{:S(2)}) collective-permute-start(bf16[128,1280]{1,0:T(8,128)(2,1)S(1)} %get-tuple-element.329.refs_1_), channel_id=1, source_target_pairs={{0,2},{1,3},{2,0},{3,1},{4,6},{5,7},{6,4},{7,5},{8,10},{9,11},{10,... | collective-permute-start | bytes 983048 | tf_op jit(solution)/shard_map/ppermute | solution.py:463
  127.1 15.5 %collective-permute-start.40 = (bf16[640,384]{1,0:T(8,128)(2,1)S(1)}, bf16[640,384]{1,0:T(8,128)(2,1)S(1)}, u32[]{:S(2)}, u32[]{:S(2)}) collective-permute-start(bf16[640,384]{1,0:T(8,128)(2,1)S(1)} %get-tuple-element.347), channel_id=1, source_target_pairs={{0,4},{1,5},{2,6},{3,7},{4,0},{5,1},{6,2},{7,3},{8,12},{9,13},{10,... | collective-permute-start | bytes 1474568 | tf_op jit(solution)/shard_map/ppermute | solution.py:463
  128.5 14.1 %collective-permute-start.41 = (bf16[640,256]{1,0:T(8,128)(2,1)S(1)}, bf16[640,256]{1,0:T(8,128)(2,1)S(1)}, u32[]{:S(2)}, u32[]{:S(2)}) collective-permute-start(bf16[640,256]{1,0:T(8,128)(2,1)S(1)} %get-tuple-element.348), channel_id=1, source_target_pairs={{0,8},{1,9},{2,10},{3,11},{4,12},{5,13},{6,14},{7,15},{8,0},{9,1},... | collective-permute-start | bytes 983048 | tf_op jit(solution)/shard_map/ppermute | solution.py:463
  129.8 12.9 %collective-permute-start.38 = (bf16[128,1280]{1,0:T(8,128)(2,1)S(1)}, bf16[128,1280]{1,0:T(8,128)(2,1)S(1)}, u32[]{:S(2)}, u32[]{:S(2)}) collective-permute-start(bf16[128,1280]{1,0:T(8,128)(2,1)S(1)} %get-tuple-element.345), channel_id=1, source_target_pairs={{0,2},{1,3},{2,0},{3,1},{4,6},{5,7},{6,4},{7,5},{8,10},{9,11},{10,... | collective-permute-start | bytes 983048 | tf_op jit(solution)/shard_map/ppermute | solution.py:463
  131.1 9.7 %collective-permute-start.39 = (bf16[160,640]{1,0:T(8,128)(2,1)S(1)}, bf16[160,640]{1,0:T(8,128)(2,1)S(1)}, u32[]{:S(2)}, u32[]{:S(2)}) collective-permute-start(bf16[160,640]{1,0:T(8,128)(2,1)S(1)} %get-tuple-element.346), channel_id=1, source_target_pairs={{0,16},{1,17},{2,18},{3,19},{4,20},{5,21},{6,22},{7,23},{8,24},{9,... | collective-permute-start | bytes 614408 | tf_op jit(solution)/shard_map/ppermute | solution.py:463
  146.5 14.6 %collective-permute-start.42 = (bf16[672,384]{1,0:T(8,128)(2,1)S(1)}, bf16[672,384]{1,0:T(8,128)(2,1)S(1)}, u32[]{:S(2)}, u32[]{:S(2)}) collective-permute-start(bf16[672,384]{1,0:T(8,128)(2,1)S(1)} %get-tuple-element.357), channel_id=1, source_target_pairs={{0,4},{1,5},{2,6},{3,7},{4,0},{5,1},{6,2},{7,3},{8,12},{9,13},{10,... | collective-permute-start | bytes 1548296 | tf_op jit(solution)/shard_map/ppermute | solution.py:463
  147.2 10.7 %collective-permute-start.43 = (bf16[640,256]{1,0:T(8,128)(2,1)S(1)}, bf16[640,256]{1,0:T(8,128)(2,1)S(1)}, u32[]{:S(2)}, u32[]{:S(2)}) collective-permute-start(bf16[640,256]{1,0:T(8,128)(2,1)S(1)} %get-tuple-element.358), channel_id=1, source_target_pairs={{0,8},{1,9},{2,10},{3,11},{4,12},{5,13},{6,14},{7,15},{8,0},{9,1},... | collective-permute-start | bytes 983048 | tf_op jit(solution)/shard_map/ppermute | solution.py:463
  150.8 10.3 %collective-permute-start.45 = (bf16[128,1280]{1,0:T(8,128)(2,1)S(1)}, bf16[128,1280]{1,0:T(8,128)(2,1)S(1)}, u32[]{:S(2)}, u32[]{:S(2)}) collective-permute-start(bf16[128,1280]{1,0:T(8,128)(2,1)S(1)} %get-tuple-element.373), channel_id=1, source_target_pairs={{0,2},{1,3},{2,0},{3,1},{4,6},{5,7},{6,4},{7,5},{8,10},{9,11},{10,... | collective-permute-start | bytes 983048 | tf_op jit(solution)/shard_map/ppermute | solution.py:463
  152.1 12.0 %collective-permute-start.46 = (bf16[320,384]{1,0:T(8,128)(2,1)S(1)}, bf16[320,384]{1,0:T(8,128)(2,1)S(1)}, u32[]{:S(2)}, u32[]{:S(2)}) collective-permute-start(bf16[320,384]{1,0:T(8,128)(2,1)S(1)} %get-tuple-element.383), channel_id=1, source_target_pairs={{0,8},{1,9},{2,10},{3,11},{4,12},{5,13},{6,14},{7,15},{8,0},{9,1},... | collective-permute-start | bytes 737288 | tf_op jit(solution)/shard_map/ppermute | solution.py:463
  152.1 12.0 %collective-permute-start.47 = (bf16[320,256]{1,0:T(8,128)(2,1)S(1)}, bf16[320,256]{1,0:T(8,128)(2,1)S(1)}, u32[]{:S(2)}, u32[]{:S(2)}) collective-permute-start(bf16[320,256]{1,0:T(8,128)(2,1)S(1)} %get-tuple-element.384), channel_id=1, source_target_pairs={{0,4},{1,5},{2,6},{3,7},{4,0},{5,1},{6,2},{7,3},{8,12},{9,13},{10,... | collective-permute-start | bytes 491528 | tf_op jit(solution)/shard_map/ppermute | solution.py:463
  165.0 11.1 %collective-permute-start.48 = (bf16[352,384]{1,0:T(8,128)(2,1)S(1)}, bf16[352,384]{1,0:T(8,128)(2,1)S(1)}, u32[]{:S(2)}, u32[]{:S(2)}) collective-permute-start(bf16[352,384]{1,0:T(8,128)(2,1)S(1)} %get-tuple-element.389.refs_0_), channel_id=1, source_target_pairs={{0,8},{1,9},{2,10},{3,11},{4,12},{5,13},{6,14},{7,15},{8,0},{9,1},... | collective-permute-start | bytes 811016 | tf_op jit(solution)/shard_map/ppermute | solution.py:463
  168.5 17.7 %collective-permute-start.54 = (bf16[160,640]{1,0:T(8,128)(2,1)S(1)}, bf16[160,640]{1,0:T(8,128)(2,1)S(1)}, u32[]{:S(2)}, u32[]{:S(2)}) collective-permute-start(bf16[160,640]{1,0:T(8,128)(2,1)S(1)} %get-tuple-element.412), channel_id=1, source_target_pairs={{0,16},{1,17},{2,18},{3,19},{4,20},{5,21},{6,22},{7,23},{8,24},{9,... | collective-permute-start | bytes 614408 | tf_op jit(solution)/shard_map/ppermute | solution.py:463
  176.8 12.9 %collective-permute-start.53 = (bf16[160,640]{1,0:T(8,128)(2,1)S(1)}, bf16[160,640]{1,0:T(8,128)(2,1)S(1)}, u32[]{:S(2)}, u32[]{:S(2)}) collective-permute-start(bf16[160,640]{1,0:T(8,128)(2,1)S(1)} %get-tuple-element.407), channel_id=1, source_target_pairs={{0,16},{1,17},{2,18},{3,19},{4,20},{5,21},{6,22},{7,23},{8,24},{9,... | collective-permute-start | bytes 614408 | tf_op jit(solution)/shard_map/ppermute | solution.py:463
  (23 other events, 121.1 us)

commit v6 on v5

--- a/solution.py
+++ b/solution.py
@@ -788,7 +788,7 @@
     if wide:
         grad_qk, mix_got = tie(grad_qk, mix_got)
     else:
-        grad_qk, mix_got, part_hd, got_vo = tie(grad_qk, mix_got, part_hd, got_vo)
+        grad_qk, mix_got, got_vo = tie(grad_qk, mix_got, got_vo)
     terms_first = list(terms)
     if not wide:
         terms_first[0] = ((tall_sent + 32, cut), BF16)
@@ -815,7 +815,7 @@
         got = links.chip(send)
     else:
         got_qk = first_send(terms_qk)
-        far, *got_vo = tie(far, *got_vo)
+        far, part_hd, *got_vo = tie(far, part_hd, *got_vo)
         sums_vo = first_sum("vo", terms_vo, got_vo)
         send, keep, *sums_vo = core_half(far, near, *sums_vo)
         got_vo = second_send(sums_vo)

time: 192 us -> 191 us (level)
  transfers between devices with their start and end apart: 55 -> 55, of which waited for: 28 -> 27; matrix products, arithmetic and copies ran while one was open for 0% -> 0% of each run, Pallas kernels for 26% -> 28%
where the time goes in v6:
time: 191 us
  waiting for transfers between devices  66.7 us (35%)
  Pallas kernels  62.3 us (33%)
  starting transfers between devices  59.5 us (31%)
    ppermute x55, waiting for transfers between devices, move(): return lax.ppermute(value, AXES, pairs)  66.7 us
    pallas_call x35, Pallas kernels, call(): pl.pallas_call(kernel, name=name, out_shape=outs, in_specs=[pl.BlockSpec(...  62.3 us
    ppermute x55, starting transfers between devices, move(): return lax.ppermute(value, AXES, pairs)  59.5 us
  transfers between devices with their start and end apart: 55, of which 27 were waited for; matrix products, arithmetic and copies ran while one was open for 0% of the time, Pallas kernels for 28%

profile of v6, /device:TPU:0, one launch (start us, length us, event | category | flops | bytes accessed | tf_op | source)
XLA Modules:
  0.0 190.9 jit_solution(3877433579705987933)
XLA Ops:
  1.4 1.9 %pack.1 = (bf16[160,640]{1,0:T(8,128)(2,1)S(1)}, bf16[160,640]{1,0:T(8,128)(2,1)S(1)}, bf16[160,640]{1,0:T(8,128)(2,1)S(1)}) custom-call(s32[3]{0:T(128)S(1)} %pad_add_fusion.refs_0_.s, bf16[160,320]{1,0:T(8,128)(2,1)} %refs_0_.1, bf16[160,320]{1,0:T(8,128)(2,1)} %refs_1_.1, bf16[160,320]{1,0:T(8,128)(2,1)} %refs_2_.3, bf16[160,320]{1,0:T(8,128)(2,1)} %bitcast.23, ...), custom_call_target="tpu_custom_call" | custom-call | flops 1000000 | bytes 1228800 | tf_op jit(solution)/shard_map/pack/pallas_call | solution.py:30
  3.3 4.1 %collective-permute-start.1 = (bf16[160,640]{1,0:T(8,128)(2,1)S(1)}, bf16[160,640]{1,0:T(8,128)(2,1)S(1)}, u32[]{:S(2)}, u32[]{:S(2)}) collective-permute-start(bf16[160,640]{1,0:T(8,128)(2,1)S(1)} %get-tuple-element.240.refs_0_.refs_6_), channel_id=1, source_target_pairs={{0,16},{1,17},{2,18},{3,19},{4,20},{5,21},{6,22},{7,23},{8,24},{9,... | collective-permute-start | bytes 614408 | tf_op jit(solution)/shard_map/ppermute | solution.py:463
  11.3 3.2 %prepare.1 = (bf16[128,1280]{1,0:T(8,128)(2,1)S(1)}, bf16[128,1280]{1,0:T(8,128)(2,1)S(1)}, bf16[128,1280]{1,0:T(8,128)(2,1)S(1)}, f32[8,1280]{1,0:T(8,128)S(1)}, f32[8,320]{1,0:T(8,128)S(1)}) custom-call(s32[3]{0:T(128)S(1)} %pad_add_fusion.refs_0_.s, f32[1,320]{1,0:T(1,128)S(1)} %broadcast_in_dim_tile.3.refs_1_, bf16[128,1280]{1,0:T(8,128)(2,1)} %refs_2_.2, ...), custom_call_target="tpu_custom_call" | custom-call | flops 1000000 | bytes 1726720 | tf_op jit(solution)/shard_map/prepare/pallas_call | solution.py:30
  22.8 2.3 %collective-permute-start.4 = (bf16[160,640]{1,0:T(8,128)(2,1)S(1)}, bf16[160,640]{1,0:T(8,128)(2,1)S(1)}, u32[]{:S(2)}, u32[]{:S(2)}) collective-permute-start(bf16[160,640]{1,0:T(8,128)(2,1)S(1)} %get-tuple-element.257.refs_4_), channel_id=1, source_target_pairs={{0,16},{1,17},{2,18},{3,19},{4,20},{5,21},{6,22},{7,23},{8,24},{9,... | collective-permute-start | bytes 614408 | tf_op jit(solution)/shard_map/ppermute | solution.py:463
  25.1 5.3 %collective-permute-done.8.refs_1_.refs_9_ = bf16[160,640]{1,0:T(8,128)(2,1)S(1)} collective-permute-done((bf16[160,640]{1,0:T(8,128)(2,1)S(1)}, bf16[160,640]{1,0:T(8,128)(2,1)S(1)}, u32[]{:S(2)}, u32[]{:S(2)}) %collective-permute-start.8) | collective-permute-done | bytes 204832 | tf_op jit(solution)/shard_map/ppermute | solution.py:463
  36.9 4.9 %collective-permute-done.12.refs_5_ = bf16[160,640]{1,0:T(8,128)(2,1)S(1)} collective-permute-done((bf16[160,640]{1,0:T(8,128)(2,1)S(1)}, bf16[160,640]{1,0:T(8,128)(2,1)S(1)}, u32[]{:S(2)}, u32[]{:S(2)}) %collective-permute-start.12) | collective-permute-done | bytes 204832 | tf_op jit(solution)/shard_map/ppermute | solution.py:463
  43.1 2.6 %collective-permute-done.11.refs_1_.refs_7_ = bf16[160,640]{1,0:T(8,128)(2,1)S(1)} collective-permute-done((bf16[160,640]{1,0:T(8,128)(2,1)S(1)}, bf16[160,640]{1,0:T(8,128)(2,1)S(1)}, u32[]{:S(2)}, u32[]{:S(2)}) %collective-permute-start.11) | collective-permute-done | bytes 204832 | tf_op jit(solution)/shard_map/ppermute | solution.py:463
  45.8 1.8 collective-permute-start.15
  47.6 1.7 collective-permute-start.14
  49.9 2.5 %collective-permute-start.17 = (bf16[320,640]{1,0:T(8,128)(2,1)S(1)}, bf16[320,640]{1,0:T(8,128)(2,1)S(1)}, u32[]{:S(2)}, u32[]{:S(2)}) collective-permute-start(bf16[320,640]{1,0:T(8,128)(2,1)S(1)} %stack.18), channel_id=1, source_target_pairs={{0,4},{1,5},{2,6},{3,7},{4,0},{5,1},{6,2},{7,3},{8,12},{9,13},{10,... | collective-permute-start | bytes 1228808 | tf_op jit(solution)/shard_map/ppermute | solution.py:463
  52.4 6.3 %attend.1 = (f32[512,320]{1,0:T(8,128)S(1)}, bf16[512,320]{1,0:T(8,128)(2,1)S(1)}, bf16[512,320]{1,0:T(8,128)(2,1)S(1)}, bf16[512,1280]{1,0:T(8,128)(2,1)S(1)}, ...) custom-call(s32[3]{0:T(128)S(1)} %pad_add_fusion.refs_0_.s, ...), custom_call_target="tpu_custom_call" | custom-call | flops 1000000 | bytes 9316352 | tf_op jit(solution)/shard_map/attend/pallas_call | solution.py:30
  61.3 5.6 %context.1 = (bf16[512,320]{1,0:T(8,128)(2,1)S(1)}, bf16[512,320]{1,0:T(8,128)(2,1)S(1)}, bf16[256,1280]{1,0:T(8,128)(2,1)S(1)}, f32[256,1280]{1,0:T(8,128)S(1)}...) custom-call(s32[3]{0:T(128)S(1)} %pad_add_fusion.refs_0_.s, ...), custom_call_target="tpu_custom_call" | custom-call | flops 1000000 | bytes 9316352 | tf_op jit(solution)/shard_map/context/pallas_call | solution.py:30
  71.5 8.1 %collective-permute-done.24.refs_11_ = bf16[320,640]{1,0:T(8,128)(2,1)S(1)} collective-permute-done((bf16[320,640]{1,0:T(8,128)(2,1)S(1)}, bf16[320,640]{1,0:T(8,128)(2,1)S(1)}, u32[]{:S(2)}, u32[]{:S(2)}) %collective-permute-start.24) | collective-permute-done | bytes 409632 | tf_op jit(solution)/shard_map/ppermute | solution.py:463
  82.2 4.0 %grad_act.1 = (f32[512,320]{1,0:T(8,128)S(1)}, bf16[512,1280]{1,0:T(8,128)(2,1)S(1)}, bf16[1280,320]{1,0:T(8,128)(2,1)S(1)}, bf16[1280,320]{1,0:T(8,128)(2,1)S(1)}) custom-call(s32[3]{0:T(128)S(1)} %pad_add_fusion.refs_0_.s, bf16[128,1280]{1,0:T(8,128)(2,1)S(1)} %get-tuple-element.278.refs_1_.grad, bf16[128,1280]{1,0:T(8,128)(2,1)S(1)} %collective-permute-done.16.refs_2_, ...), custom_call_target="tpu_custom_call" | custom-call | flops 1000000 | bytes 6553600 | tf_op jit(solution)/shard_map/grad_act/pallas_call | solution.py:30
  86.1 3.7 %collective-permute-done.25.p1 = bf16[128,1280]{1,0:T(8,128)(2,1)S(1)} collective-permute-done((bf16[128,1280]{1,0:T(8,128)(2,1)S(1)}, bf16[128,1280]{1,0:T(8,128)(2,1)S(1)}, u32[]{:S(2)}, u32[]{:S(2)}) %collective-permute-start.25) | collective-permute-done | bytes 327712 | tf_op jit(solution)/shard_map/ppermute | solution.py:463
  91.5 2.3 %hidden.1 = (bf16[256,1280]{1,0:T(8,128)(2,1)S(1)}, f32[256,1280]{1,0:T(8,128)S(1)}, bf16[512,320]{1,0:T(8,128)(2,1)S(1)}, bf16[512,320]{1,0:T(8,128)(2,1)S(1)}, bf16[512,1280]{1,0:T(8,128)(2,1)S(1)}) custom-call(s32[3]{0:T(128)S(1)} %pad_add_fusion.refs_0_.s, bf16[128,1280]{1,0:T(8,128)(2,1)S(1)} %get-tuple-element.277.p0, ...), custom_call_target="tpu_custom_call" | custom-call | flops 1000000 | bytes 6727680 | tf_op jit(solution)/shard_map/hidden/pallas_call | solution.py:30
  94.0 2.2 %down.1 = (f32[1,320]{1,0:T(1,128)S(1)}, bf16[640,384]{1,0:T(8,128)(2,1)S(1)}, bf16[640,384]{1,0:T(8,128)(2,1)S(1)}, bf16[640,256]{1,0:T(8,128)(2,1)S(1)}, bf16[640,256]{1,0:T(8,128)(2,1)S(1)}) custom-call(s32[3]{0:T(128)S(1)} %pad_add_fusion.refs_0_.s, bf16[512,1280]{1,0:T(8,128)(2,1)S(1)} %get-tuple-element.296.refs_1_, ...), custom_call_target="tpu_custom_call" | custom-call | flops 1000000 | bytes 4916480 | tf_op jit(solution)/shard_map/down/pallas_call | solution.py:30
  101.9 6.2 %collective-permute-done.29.got = bf16[128,1280]{1,0:T(8,128)(2,1)S(1)} collective-permute-done((bf16[128,1280]{1,0:T(8,128)(2,1)S(1)}, bf16[128,1280]{1,0:T(8,128)(2,1)S(1)}, u32[]{:S(2)}, u32[]{:S(2)}) %collective-permute-start.29) | collective-permute-done | bytes 327712 | tf_op jit(solution)/shard_map/ppermute | solution.py:463
  115.0 4.7 %collective-permute-done.34.ring_got = bf16[320,256]{1,0:T(8,128)(2,1)S(1)} collective-permute-done((bf16[320,256]{1,0:T(8,128)(2,1)S(1)}, bf16[320,256]{1,0:T(8,128)(2,1)S(1)}, u32[]{:S(2)}, u32[]{:S(2)}) %collective-permute-start.34) | collective-permute-done | bytes 163872 | tf_op jit(solution)/shard_map/ppermute | solution.py:463
  122.0 5.1 %grad_context.1 = (bf16[512,320]{1,0:T(8,128)(2,1)S(1)}, bf16[512,320]{1,0:T(8,128)(2,1)S(1)}, bf16[512,1280]{1,0:T(8,128)(2,1)}, bf16[640,384]{1,0:T(8,128)(2,1...) custom-call(s32[3]{0:T(128)S(1)} %pad_add_fusion.refs_0_.s, ...), custom_call_target="tpu_custom_call" | custom-call | flops 1000000 | bytes 9469952 | tf_op jit(solution)/shard_map/grad_context/pallas_call | solution.py:30
  131.1 2.2 %collective-permute-start.43 = (bf16[160,640]{1,0:T(8,128)(2,1)S(1)}, bf16[160,640]{1,0:T(8,128)(2,1)S(1)}, u32[]{:S(2)}, u32[]{:S(2)}) collective-permute-start(bf16[160,640]{1,0:T(8,128)(2,1)S(1)} %get-tuple-element.360), channel_id=1, source_target_pairs={{0,16},{1,17},{2,18},{3,19},{4,20},{5,21},{6,22},{7,23},{8,24},{9,... | collective-permute-start | bytes 614408 | tf_op jit(solution)/shard_map/ppermute | solution.py:463
  133.3 5.3 %grad_scores.1 = (bf16[512,640]{1,0:T(8,128)(2,1)S(1)}, f32[8,320]{1,0:T(8,128)S(1)}) custom-call(s32[3]{0:T(128)S(1)} %pad_add_fusion.refs_0_.s, bf16[4,512,512]{2,1,0:T(8,128)(2,1)S(1)} %get-tuple-element.255.refs_2_.refs_6_.refs_1_, bf16[512,320]{1,0:T(8,128)(2,1)S(1)} %get-tuple-element.337.refs_2_, bf16[512,320]{1,0:T(8,128)(2,1)S(1)} %get-tuple-element.338.refs_3_, ...), custom_call_target="tpu_custom_call" | custom-call | flops 1000000 | bytes 4739072 | tf_op jit(solution)/shard_map/grad_scores/pallas_call | solution.py:30
  138.6 4.0 %collective-permute-done.40.ring_got = bf16[640,256]{1,0:T(8,128)(2,1)S(1)} collective-permute-done((bf16[640,256]{1,0:T(8,128)(2,1)S(1)}, bf16[640,256]{1,0:T(8,128)(2,1)S(1)}, u32[]{:S(2)}, u32[]{:S(2)}) %collective-permute-start.40) | collective-permute-done | bytes 327712 | tf_op jit(solution)/shard_map/ppermute | solution.py:463
  142.6 3.8 %grad_first.1 = (bf16[256,1280]{1,0:T(8,128)(2,1)S(1)}, f32[256,1280]{1,0:T(8,128)S(1)}, f32[8,1280]{1,0:T(8,128)S(1)}, bf16[672,384]{1,0:T(8,128)(2,1)S(1)}, bf...) custom-call(s32[3]{0:T(128)S(1)} %pad_add_fusion.refs_0_.s, ...), custom_call_target="tpu_custom_call" | custom-call | flops 1000000 | bytes 8474176 | tf_op jit(solution)/shard_map/grad_first/pallas_call | solution.py:30
  153.4 1.8 output.1
  157.7 3.4 %collective-permute-done.41.pair_got = bf16[672,384]{1,0:T(8,128)(2,1)S(1)} collective-permute-done((bf16[672,384]{1,0:T(8,128)(2,1)S(1)}, bf16[672,384]{1,0:T(8,128)(2,1)S(1)}, u32[]{:S(2)}, u32[]{:S(2)}) %collective-permute-start.41) | collective-permute-done | bytes 516128 | tf_op jit(solution)/shard_map/ppermute | solution.py:463
  161.1 3.1 %collective-permute-done.47.ring_got = bf16[320,256]{1,0:T(8,128)(2,1)S(1)} collective-permute-done((bf16[320,256]{1,0:T(8,128)(2,1)S(1)}, bf16[320,256]{1,0:T(8,128)(2,1)S(1)}, u32[]{:S(2)}, u32[]{:S(2)}) %collective-permute-start.47) | collective-permute-done | bytes 163872 | tf_op jit(solution)/shard_map/ppermute | solution.py:463
  166.4 3.6 %collective-permute-start.54 = (bf16[160,640]{1,0:T(8,128)(2,1)S(1)}, bf16[160,640]{1,0:T(8,128)(2,1)S(1)}, u32[]{:S(2)}, u32[]{:S(2)}) collective-permute-start(bf16[160,640]{1,0:T(8,128)(2,1)S(1)} %get-tuple-element.412), channel_id=1, source_target_pairs={{0,16},{1,17},{2,18},{3,19},{4,20},{5,21},{6,22},{7,23},{8,24},{9,... | collective-permute-start | bytes 614408 | tf_op jit(solution)/shard_map/ppermute | solution.py:463
  170.0 2.1 %last.1 = bf16[128,1280]{1,0:T(8,128)(2,1)} custom-call(s32[3]{0:T(128)S(1)} %pad_add_fusion.refs_0_.s, f32[128,1280]{1,0:T(8,128)S(1)} %get-tuple-element.391.refs_1_, bf16[128,1280]{1,0:T(8,128)(2,1)S(1)} %collective-permute-done.45.refs_2_, bf16[128,1280]{1,0:T(8,128)(2,1)S(1)} %get-tuple-element.275.x_own.refs_3_, ...), custom_call_target="tpu_custom_call" | custom-call | flops 1000000 | bytes 2334720 | tf_op jit(solution)/shard_map/last/pallas_call | solution.py:30
  172.1 4.8 %collective-permute-done.48.pair_got = bf16[352,384]{1,0:T(8,128)(2,1)S(1)} collective-permute-done((bf16[352,384]{1,0:T(8,128)(2,1)S(1)}, bf16[352,384]{1,0:T(8,128)(2,1)S(1)}, u32[]{:S(2)}, u32[]{:S(2)}) %collective-permute-start.48) | collective-permute-done | bytes 270368 | tf_op jit(solution)/shard_map/ppermute | solution.py:463
  180.7 2.8 %collective-permute-done.51.two = f32[8,1280]{1,0:T(8,128)S(1)} collective-permute-done((f32[8,1280]{1,0:T(8,128)S(1)}, f32[8,1280]{1,0:T(8,128)S(1)}, u32[]{:S(2)}, u32[]{:S(2)}) %collective-permute-start.51) | collective-permute-done | bytes 40992 | tf_op jit(solution)/shard_map/ppermute | solution.py:463
  184.1 2.9 %collective-permute-start.52 = (f32[8,1280]{1,0:T(8,128)S(1)}, f32[8,1280]{1,0:T(8,128)S(1)}, u32[]{:S(2)}, u32[]{:S(2)}) collective-permute-start(f32[8,1280]{1,0:T(8,128)S(1)} %add.18.one), channel_id=1, source_target_pairs={{0,16},{1,17},{2,18},{3,19},{4,20},{5,21},{6,22},{7,23},{8,24},{9,... | collective-permute-start | bytes 122888 | tf_op jit(solution)/shard_map/ppermute | solution.py:463
  (117 shorter events, 70.8 us)
Async XLA Ops:
  3.3 13.7 %collective-permute-start.1 = (bf16[160,640]{1,0:T(8,128)(2,1)S(1)}, bf16[160,640]{1,0:T(8,128)(2,1)S(1)}, u32[]{:S(2)}, u32[]{:S(2)}) collective-permute-start(bf16[160,640]{1,0:T(8,128)(2,1)S(1)} %get-tuple-element.240.refs_0_.refs_6_), channel_id=1, source_target_pairs={{0,16},{1,17},{2,18},{3,19},{4,20},{5,21},{6,22},{7,23},{8,24},{9,... | collective-permute-start | bytes 614408 | tf_op jit(solution)/shard_map/ppermute | solution.py:463
  7.4 9.8 %collective-permute-start = (bf16[160,640]{1,0:T(8,128)(2,1)S(1)}, bf16[160,640]{1,0:T(8,128)(2,1)S(1)}, u32[]{:S(2)}, u32[]{:S(2)}) collective-permute-start(bf16[160,640]{1,0:T(8,128)(2,1)S(1)} %get-tuple-element.240.refs_0_.refs_6_), channel_id=1, source_target_pairs={{0,8},{1,9},{2,10},{3,11},{4,12},{5,13},{6,14},{7,15},{8,0},{9,1},... | collective-permute-start | bytes 614408 | tf_op jit(solution)/shard_map/ppermute | solution.py:463
  17.8 13.3 %collective-permute-start.9 = (bf16[320,640]{1,0:T(8,128)(2,1)S(1)}, bf16[320,640]{1,0:T(8,128)(2,1)S(1)}, u32[]{:S(2)}, u32[]{:S(2)}) collective-permute-start(bf16[320,640]{1,0:T(8,128)(2,1)S(1)} %stack.17), channel_id=1, source_target_pairs={{0,4},{1,5},{2,6},{3,7},{4,0},{5,1},{6,2},{7,3},{8,12},{9,13},{10,... | collective-permute-start | bytes 1228808 | tf_op jit(solution)/shard_map/ppermute | solution.py:463
  19.4 14.5 %collective-permute-start.3 = (bf16[128,1280]{1,0:T(8,128)(2,1)S(1)}, bf16[128,1280]{1,0:T(8,128)(2,1)S(1)}, u32[]{:S(2)}, u32[]{:S(2)}) collective-permute-start(bf16[128,1280]{1,0:T(8,128)(2,1)S(1)} %get-tuple-element.235.refs_1_), channel_id=1, source_target_pairs={{0,2},{1,3},{2,0},{3,1},{4,6},{5,7},{6,4},{7,5},{8,10},{9,11},{10,... | collective-permute-start | bytes 983048 | tf_op jit(solution)/shard_map/ppermute | solution.py:463
  20.9 9.5 %collective-permute-start.8 = (bf16[160,640]{1,0:T(8,128)(2,1)S(1)}, bf16[160,640]{1,0:T(8,128)(2,1)S(1)}, u32[]{:S(2)}, u32[]{:S(2)}) collective-permute-start(bf16[160,640]{1,0:T(8,128)(2,1)S(1)} %collective-permute-done.1.refs_0_.refs_8_), channel_id=1, source_target_pairs={{0,8},{1,9},{2,10},{3,11},{4,12},{5,13},{6,14},{7,15},{8,0},{9,1},... | collective-permute-start | bytes 614408 | tf_op jit(solution)/shard_map/ppermute | solution.py:463
  22.3 10.3 %collective-permute-start.5 = (bf16[160,640]{1,0:T(8,128)(2,1)S(1)}, bf16[160,640]{1,0:T(8,128)(2,1)S(1)}, u32[]{:S(2)}, u32[]{:S(2)}) collective-permute-start(bf16[160,640]{1,0:T(8,128)(2,1)S(1)} %get-tuple-element.257.refs_4_), channel_id=1, source_target_pairs={{0,4},{1,5},{2,6},{3,7},{4,0},{5,1},{6,2},{7,3},{8,12},{9,13},{10,... | collective-permute-start | bytes 614408 | tf_op jit(solution)/shard_map/ppermute | solution.py:463
  22.8 11.0 %collective-permute-start.4 = (bf16[160,640]{1,0:T(8,128)(2,1)S(1)}, bf16[160,640]{1,0:T(8,128)(2,1)S(1)}, u32[]{:S(2)}, u32[]{:S(2)}) collective-permute-start(bf16[160,640]{1,0:T(8,128)(2,1)S(1)} %get-tuple-element.257.refs_4_), channel_id=1, source_target_pairs={{0,16},{1,17},{2,18},{3,19},{4,20},{5,21},{6,22},{7,23},{8,24},{9,... | collective-permute-start | bytes 614408 | tf_op jit(solution)/shard_map/ppermute | solution.py:463
  31.0 14.7 %collective-permute-start.10 = (bf16[320,640]{1,0:T(8,128)(2,1)S(1)}, bf16[320,640]{1,0:T(8,128)(2,1)S(1)}, u32[]{:S(2)}, u32[]{:S(2)}) collective-permute-start(bf16[320,640]{1,0:T(8,128)(2,1)S(1)} %stack.16), channel_id=1, source_target_pairs={{0,4},{1,5},{2,6},{3,7},{4,0},{5,1},{6,2},{7,3},{8,12},{9,13},{10,... | collective-permute-start | bytes 1228808 | tf_op jit(solution)/shard_map/ppermute | solution.py:463
  33.9 11.9 %collective-permute-start.7 = (bf16[128,1280]{1,0:T(8,128)(2,1)S(1)}, bf16[128,1280]{1,0:T(8,128)(2,1)S(1)}, u32[]{:S(2)}, u32[]{:S(2)}) collective-permute-start(bf16[128,1280]{1,0:T(8,128)(2,1)S(1)} %collective-permute-done.3.refs_2_), channel_id=1, source_target_pairs={{0,1},{1,0},{2,3},{3,2},{4,5},{5,4},{6,7},{7,6},{8,9},{9,8},{10,11... | collective-permute-start | bytes 983048 | tf_op jit(solution)/shard_map/ppermute | solution.py:463
  34.6 11.2 %collective-permute-start.11 = (bf16[160,640]{1,0:T(8,128)(2,1)S(1)}, bf16[160,640]{1,0:T(8,128)(2,1)S(1)}, u32[]{:S(2)}, u32[]{:S(2)}) collective-permute-start(bf16[160,640]{1,0:T(8,128)(2,1)S(1)} %collective-permute-done.4.refs_0_.refs_6_), channel_id=1, source_target_pairs={{0,8},{1,9},{2,10},{3,11},{4,12},{5,13},{6,14},{7,15},{8,0},{9,1},... | collective-permute-start | bytes 614408 | tf_op jit(solution)/shard_map/ppermute | solution.py:463
  35.9 22.8 %collective-permute-start.16 = (bf16[128,1280]{1,0:T(8,128)(2,1)S(1)}, bf16[128,1280]{1,0:T(8,128)(2,1)S(1)}, u32[]{:S(2)}, u32[]{:S(2)}) collective-permute-start(bf16[128,1280]{1,0:T(8,128)(2,1)S(1)} %get-tuple-element.278.refs_1_.grad), channel_id=1, source_target_pairs={{0,2},{1,3},{2,0},{3,1},{4,6},{5,7},{6,4},{7,5},{8,10},{9,11},{10,... | collective-permute-start | bytes 983048 | tf_op jit(solution)/shard_map/ppermute | solution.py:463
  41.8 17.0 %collective-permute-start.13 = (bf16[160,640]{1,0:T(8,128)(2,1)S(1)}, bf16[160,640]{1,0:T(8,128)(2,1)S(1)}, u32[]{:S(2)}, u32[]{:S(2)}) collective-permute-start(bf16[160,640]{1,0:T(8,128)(2,1)S(1)} %collective-permute-done.12.refs_5_), channel_id=1, source_target_pairs={{0,4},{1,5},{2,6},{3,7},{4,0},{5,1},{6,2},{7,3},{8,12},{9,13},{10,... | collective-permute-start | bytes 614408 | tf_op jit(solution)/shard_map/ppermute | solution.py:463
  45.8 13.0 %collective-permute-start.15 = (bf16[160,640]{1,0:T(8,128)(2,1)S(1)}, bf16[160,640]{1,0:T(8,128)(2,1)S(1)}, u32[]{:S(2)}, u32[]{:S(2)}) collective-permute-start(bf16[160,640]{1,0:T(8,128)(2,1)S(1)} %get-tuple-element.282.refs_5_), channel_id=1, source_target_pairs={{0,16},{1,17},{2,18},{3,19},{4,20},{5,21},{6,22},{7,23},{8,24},{9,... | collective-permute-start | bytes 614408 | tf_op jit(solution)/shard_map/ppermute | solution.py:463
  47.6 11.3 %collective-permute-start.14 = (bf16[160,640]{1,0:T(8,128)(2,1)S(1)}, bf16[160,640]{1,0:T(8,128)(2,1)S(1)}, u32[]{:S(2)}, u32[]{:S(2)}) collective-permute-start(bf16[160,640]{1,0:T(8,128)(2,1)S(1)} %get-tuple-element.282.refs_5_), channel_id=1, source_target_pairs={{0,8},{1,9},{2,10},{3,11},{4,12},{5,13},{6,14},{7,15},{8,0},{9,1},... | collective-permute-start | bytes 614408 | tf_op jit(solution)/shard_map/ppermute | solution.py:463
  49.9 11.4 %collective-permute-start.17 = (bf16[320,640]{1,0:T(8,128)(2,1)S(1)}, bf16[320,640]{1,0:T(8,128)(2,1)S(1)}, u32[]{:S(2)}, u32[]{:S(2)}) collective-permute-start(bf16[320,640]{1,0:T(8,128)(2,1)S(1)} %stack.18), channel_id=1, source_target_pairs={{0,4},{1,5},{2,6},{3,7},{4,0},{5,1},{6,2},{7,3},{8,12},{9,13},{10,... | collective-permute-start | bytes 1228808 | tf_op jit(solution)/shard_map/ppermute | solution.py:463
  67.7 11.9 %collective-permute-start.24 = (bf16[320,640]{1,0:T(8,128)(2,1)S(1)}, bf16[320,640]{1,0:T(8,128)(2,1)S(1)}, u32[]{:S(2)}, u32[]{:S(2)}) collective-permute-start(bf16[320,640]{1,0:T(8,128)(2,1)S(1)} %stack.19), channel_id=1, source_target_pairs={{0,4},{1,5},{2,6},{3,7},{4,0},{5,1},{6,2},{7,3},{8,12},{9,13},{10,... | collective-permute-start | bytes 1228808 | tf_op jit(solution)/shard_map/ppermute | solution.py:463
  69.9 9.9 %collective-permute-start.23 = (bf16[128,1280]{1,0:T(8,128)(2,1)S(1)}, bf16[128,1280]{1,0:T(8,128)(2,1)S(1)}, u32[]{:S(2)}, u32[]{:S(2)}) collective-permute-start(bf16[128,1280]{1,0:T(8,128)(2,1)S(1)} %get-tuple-element.270), channel_id=1, source_target_pairs={{0,2},{1,3},{2,0},{3,1},{4,6},{5,7},{6,4},{7,5},{8,10},{9,11},{10,... | collective-permute-start | bytes 983048 | tf_op jit(solution)/shard_map/ppermute | solution.py:463
  96.2 13.5 %collective-permute-start.30 = (bf16[640,384]{1,0:T(8,128)(2,1)S(1)}, bf16[640,384]{1,0:T(8,128)(2,1)S(1)}, u32[]{:S(2)}, u32[]{:S(2)}) collective-permute-start(bf16[640,384]{1,0:T(8,128)(2,1)S(1)} %get-tuple-element.311), channel_id=1, source_target_pairs={{0,4},{1,5},{2,6},{3,7},{4,0},{5,1},{6,2},{7,3},{8,12},{9,13},{10,... | collective-permute-start | bytes 1474568 | tf_op jit(solution)/shard_map/ppermute | solution.py:463
  98.4 9.8 %collective-permute-start.29 = (bf16[128,1280]{1,0:T(8,128)(2,1)S(1)}, bf16[128,1280]{1,0:T(8,128)(2,1)S(1)}, u32[]{:S(2)}, u32[]{:S(2)}) collective-permute-start(bf16[128,1280]{1,0:T(8,128)(2,1)S(1)} %get-tuple-element.306), channel_id=1, source_target_pairs={{0,2},{1,3},{2,0},{3,1},{4,6},{5,7},{6,4},{7,5},{8,10},{9,11},{10,... | collective-permute-start | bytes 983048 | tf_op jit(solution)/shard_map/ppermute | solution.py:463
  110.7 9.5 %collective-permute-start.32 = (bf16[128,1280]{1,0:T(8,128)(2,1)S(1)}, bf16[128,1280]{1,0:T(8,128)(2,1)S(1)}, u32[]{:S(2)}, u32[]{:S(2)}) collective-permute-start(bf16[128,1280]{1,0:T(8,128)(2,1)S(1)} %get-tuple-element.329.refs_1_), channel_id=1, source_target_pairs={{0,2},{1,3},{2,0},{3,1},{4,6},{5,7},{6,4},{7,5},{8,10},{9,11},{10,... | collective-permute-start | bytes 983048 | tf_op jit(solution)/shard_map/ppermute | solution.py:463
  127.1 15.5 %collective-permute-start.39 = (bf16[640,384]{1,0:T(8,128)(2,1)S(1)}, bf16[640,384]{1,0:T(8,128)(2,1)S(1)}, u32[]{:S(2)}, u32[]{:S(2)}) collective-permute-start(bf16[640,384]{1,0:T(8,128)(2,1)S(1)} %get-tuple-element.346), channel_id=1, source_target_pairs={{0,4},{1,5},{2,6},{3,7},{4,0},{5,1},{6,2},{7,3},{8,12},{9,13},{10,... | collective-permute-start | bytes 1474568 | tf_op jit(solution)/shard_map/ppermute | solution.py:463
  128.5 14.1 %collective-permute-start.40 = (bf16[640,256]{1,0:T(8,128)(2,1)S(1)}, bf16[640,256]{1,0:T(8,128)(2,1)S(1)}, u32[]{:S(2)}, u32[]{:S(2)}) collective-permute-start(bf16[640,256]{1,0:T(8,128)(2,1)S(1)} %get-tuple-element.347), channel_id=1, source_target_pairs={{0,8},{1,9},{2,10},{3,11},{4,12},{5,13},{6,14},{7,15},{8,0},{9,1},... | collective-permute-start | bytes 983048 | tf_op jit(solution)/shard_map/ppermute | solution.py:463
  129.8 12.9 %collective-permute-start.38 = (bf16[128,1280]{1,0:T(8,128)(2,1)S(1)}, bf16[128,1280]{1,0:T(8,128)(2,1)S(1)}, u32[]{:S(2)}, u32[]{:S(2)}) collective-permute-start(bf16[128,1280]{1,0:T(8,128)(2,1)S(1)} %get-tuple-element.345), channel_id=1, source_target_pairs={{0,2},{1,3},{2,0},{3,1},{4,6},{5,7},{6,4},{7,5},{8,10},{9,11},{10,... | collective-permute-start | bytes 983048 | tf_op jit(solution)/shard_map/ppermute | solution.py:463
  131.1 15.3 %collective-permute-start.43 = (bf16[160,640]{1,0:T(8,128)(2,1)S(1)}, bf16[160,640]{1,0:T(8,128)(2,1)S(1)}, u32[]{:S(2)}, u32[]{:S(2)}) collective-permute-start(bf16[160,640]{1,0:T(8,128)(2,1)S(1)} %get-tuple-element.360), channel_id=1, source_target_pairs={{0,16},{1,17},{2,18},{3,19},{4,20},{5,21},{6,22},{7,23},{8,24},{9,... | collective-permute-start | bytes 614408 | tf_op jit(solution)/shard_map/ppermute | solution.py:463
  146.5 14.6 %collective-permute-start.41 = (bf16[672,384]{1,0:T(8,128)(2,1)S(1)}, bf16[672,384]{1,0:T(8,128)(2,1)S(1)}, u32[]{:S(2)}, u32[]{:S(2)}) collective-permute-start(bf16[672,384]{1,0:T(8,128)(2,1)S(1)} %get-tuple-element.356), channel_id=1, source_target_pairs={{0,4},{1,5},{2,6},{3,7},{4,0},{5,1},{6,2},{7,3},{8,12},{9,13},{10,... | collective-permute-start | bytes 1548296 | tf_op jit(solution)/shard_map/ppermute | solution.py:463
  147.2 10.6 %collective-permute-start.42 = (bf16[640,256]{1,0:T(8,128)(2,1)S(1)}, bf16[640,256]{1,0:T(8,128)(2,1)S(1)}, u32[]{:S(2)}, u32[]{:S(2)}) collective-permute-start(bf16[640,256]{1,0:T(8,128)(2,1)S(1)} %get-tuple-element.357), channel_id=1, source_target_pairs={{0,8},{1,9},{2,10},{3,11},{4,12},{5,13},{6,14},{7,15},{8,0},{9,1},... | collective-permute-start | bytes 983048 | tf_op jit(solution)/shard_map/ppermute | solution.py:463
  149.3 11.8 %collective-permute-start.45 = (bf16[128,1280]{1,0:T(8,128)(2,1)S(1)}, bf16[128,1280]{1,0:T(8,128)(2,1)S(1)}, u32[]{:S(2)}, u32[]{:S(2)}) collective-permute-start(bf16[128,1280]{1,0:T(8,128)(2,1)S(1)} %get-tuple-element.373), channel_id=1, source_target_pairs={{0,2},{1,3},{2,0},{3,1},{4,6},{5,7},{6,4},{7,5},{8,10},{9,11},{10,... | collective-permute-start | bytes 983048 | tf_op jit(solution)/shard_map/ppermute | solution.py:463
  150.6 13.6 %collective-permute-start.46 = (bf16[320,384]{1,0:T(8,128)(2,1)S(1)}, bf16[320,384]{1,0:T(8,128)(2,1)S(1)}, u32[]{:S(2)}, u32[]{:S(2)}) collective-permute-start(bf16[320,384]{1,0:T(8,128)(2,1)S(1)} %get-tuple-element.383), channel_id=1, source_target_pairs={{0,8},{1,9},{2,10},{3,11},{4,12},{5,13},{6,14},{7,15},{8,0},{9,1},... | collective-permute-start | bytes 737288 | tf_op jit(solution)/shard_map/ppermute | solution.py:463
  151.9 12.2 %collective-permute-start.47 = (bf16[320,256]{1,0:T(8,128)(2,1)S(1)}, bf16[320,256]{1,0:T(8,128)(2,1)S(1)}, u32[]{:S(2)}, u32[]{:S(2)}) collective-permute-start(bf16[320,256]{1,0:T(8,128)(2,1)S(1)} %get-tuple-element.384), channel_id=1, source_target_pairs={{0,4},{1,5},{2,6},{3,7},{4,0},{5,1},{6,2},{7,3},{8,12},{9,13},{10,... | collective-permute-start | bytes 491528 | tf_op jit(solution)/shard_map/ppermute | solution.py:463
  165.0 11.9 %collective-permute-start.48 = (bf16[352,384]{1,0:T(8,128)(2,1)S(1)}, bf16[352,384]{1,0:T(8,128)(2,1)S(1)}, u32[]{:S(2)}, u32[]{:S(2)}) collective-permute-start(bf16[352,384]{1,0:T(8,128)(2,1)S(1)} %get-tuple-element.389.refs_0_), channel_id=1, source_target_pairs={{0,8},{1,9},{2,10},{3,11},{4,12},{5,13},{6,14},{7,15},{8,0},{9,1},... | collective-permute-start | bytes 811016 | tf_op jit(solution)/shard_map/ppermute | solution.py:463
  166.4 20.6 %collective-permute-start.54 = (bf16[160,640]{1,0:T(8,128)(2,1)S(1)}, bf16[160,640]{1,0:T(8,128)(2,1)S(1)}, u32[]{:S(2)}, u32[]{:S(2)}) collective-permute-start(bf16[160,640]{1,0:T(8,128)(2,1)S(1)} %get-tuple-element.412), channel_id=1, source_target_pairs={{0,16},{1,17},{2,18},{3,19},{4,20},{5,21},{6,22},{7,23},{8,24},{9,... | collective-permute-start | bytes 614408 | tf_op jit(solution)/shard_map/ppermute | solution.py:463
  177.5 10.8 %collective-permute-start.53 = (bf16[160,640]{1,0:T(8,128)(2,1)S(1)}, bf16[160,640]{1,0:T(8,128)(2,1)S(1)}, u32[]{:S(2)}, u32[]{:S(2)}) collective-permute-start(bf16[160,640]{1,0:T(8,128)(2,1)S(1)} %get-tuple-element.407), channel_id=1, source_target_pairs={{0,16},{1,17},{2,18},{3,19},{4,20},{5,21},{6,22},{7,23},{8,24},{9,... | collective-permute-start | bytes 614408 | tf_op jit(solution)/shard_map/ppermute | solution.py:463
  (23 other events, 119.2 us)

commit v7 on v6

--- a/solution.py
+++ b/solution.py
@@ -382,43 +382,44 @@
         total = total + scale[:, number * head_size : (number + 1) * head_size]
     sums[3:4, :head_size] = total * slope[...]
     if len(outs) > 1:
-        outs[0][pl.ds(4 * depth, 32)] = fold(sums[...], outs[0].shape[1])
+        outs[2][pl.ds(4 * depth, 48)] = fold(sums[...], outs[2].shape[1])
 
 
 def fold(vectors, width):
-    part = vectors.shape[1] // 4
-    rows = jnp.concatenate([vectors[:, k * part : (k + 1) * part] for k in range(4)], axis=0)
-    return jnp.concatenate([rows, jnp.zeros((32, width - part), F32)], axis=1).astype(BF16)
-
-
-def unfold(rows, part):
-    return jnp.concatenate([rows[8 * k : 8 * k + 8, :part] for k in range(4)], axis=1)
+    count = vectors.shape[1] // width
+    rows = [vectors[:, k * width : (k + 1) * width] for k in range(count)]
+    return jnp.concatenate(rows + [jnp.zeros((48 - 8 * count, width), F32)], axis=0).astype(BF16)
+
+
+def unfold(rows, count):
+    return jnp.concatenate([rows[8 * k : 8 * k + 8] for k in range(count)], axis=1)
 
 
 def first_sum_kernel(s, pair_kept, pair_got, ring_kept, ring_got, *refs):
     *given, pair_out, pair_mid, ring_out, ring_mid = refs
     half = pair_mid.shape[0]
-    value = pair_kept[...].astype(F32) + pair_got[pl.ds(0, 2 * half)].astype(F32)
-    pair_out[pl.ds(0, half)] = value[:half].astype(BF16)
+    value = pair_kept[...].astype(F32) + pair_got[...].astype(F32)
+    pair_out[...] = value[:half].astype(BF16)
     pair_mid[...] = value[half:]
-    value = ring_kept[...].astype(F32) + ring_got[...].astype(F32)
-    ring_out[...] = value[:half].astype(BF16)
+    value = ring_kept[...].astype(F32) + ring_got[pl.ds(0, 2 * half)].astype(F32)
+    ring_out[pl.ds(0, half)] = value[:half].astype(BF16)
     ring_mid[...] = value[half:]
     if given:
-        low = fold(given[0][...], pair_out.shape[1]).astype(F32) + pair_got[pl.ds(2 * half, 32)].astype(F32)
-        pair_out[pl.ds(half, 32)] = low.astype(BF16)
+        low = fold(given[0][...], ring_out.shape[1]).astype(F32) + ring_got[pl.ds(2 * half, 48)].astype(F32)
+        ring_out[pl.ds(half, 48)] = low.astype(BF16)
 
 
 def second_sum_kernel(s, pair_mid, pair_got, ring_mid, ring_got, *refs):
     half, depth, cut = pair_mid.shape[0], pair_mid.shape[0] // 2, pair_mid.shape[1]
     given, out, zero = refs[: len(refs) // 3], refs[len(refs) // 3], refs[len(refs) // 3 + 1]
-    pair = pair_mid[...] + pair_got[pl.ds(0, half)].astype(F32)
-    ring = ring_mid[...] + ring_got[...].astype(F32)
+    pair = pair_mid[...] + pair_got[...].astype(F32)
+    ring = ring_mid[...] + ring_got[pl.ds(0, half)].astype(F32)
     out[:, :cut], out[:, cut:] = pair[:depth].astype(BF16), ring[:depth].astype(BF16)
     zero[:, :cut], zero[:, cut:] = pair[depth:], ring[depth:]
     if given:
-        at, vectors = pl.ds(half, 32), refs[-1]
-        vectors[...] = unfold(given[0][at].astype(F32) + pair_got[at].astype(F32), vectors.shape[1] // 4)
+        at, vectors = pl.ds(half, 48), refs[-1]
+        total = given[0][at].astype(F32) + ring_got[at].astype(F32)
+        vectors[...] = unfold(total, vectors.shape[1] // ring.shape[1])
 
 
 def total_kernel(s, one, two, *outs):
@@ -714,8 +715,8 @@
 
     def first_sum(name, terms, got, given=()):
         rows = tall_sent // 2
-        extra = 32 if given else 0
-        outs = [((rows + extra, cut), BF16), ((rows, cut), F32), ((rows, both - cut), BF16), ((rows, both - cut), F32)]
+        extra, rest = 48 if given else 0, both - cut
+        outs = [((rows, cut), BF16), ((rows, cut), F32), ((rows + extra, rest), BF16), ((rows, rest), F32)]
         return run("first_" + name, first_sum_kernel, outs, terms[1], got[0], terms[3], got[1], *given)
 
     def second_send(sums):
@@ -723,7 +724,7 @@
 
     def second_sum(name, sums, got, given=False):
         outs = packed + [((depth, both), F32)] + ([vector] if given else [])
-        more = sums[:1] if given else []
+        more = sums[2:3] if given else []
         return run("second_" + name, second_sum_kernel, outs, sums[1], got[0], sums[3], got[1], *more)
 
     def owned(name, *parts):
@@ -791,7 +792,7 @@
         grad_qk, mix_got, got_vo = tie(grad_qk, mix_got, got_vo)
     terms_first = list(terms)
     if not wide:
-        terms_first[0] = ((tall_sent + 32, cut), BF16)
+        terms_first[2] = ((tall_sent + 48, both - cut), BF16)
     far, near, sums, *terms_qk = run(
         "grad_first",
         bind(grad_first_kernel, n_dp, depth),

time: 191 us -> 191 us (level)
  transfers between devices with their start and end apart: 55 -> 55, of which waited for: 27 -> 28; matrix products, arithmetic and copies ran while one was open for 0% -> 0% of each run, Pallas kernels for 28% -> 28%
where the time goes in v7:
time: 191 us; the launch traced here: 190 us
  waiting for transfers between devices  66.3 us (35%)
  Pallas kernels  62.1 us (33%)
  starting transfers between devices  59.5 us (31%)
    ppermute x55, waiting for transfers between devices, move(): return lax.ppermute(value, AXES, pairs)  66.3 us
    pallas_call x35, Pallas kernels, call(): pl.pallas_call(kernel, name=name, out_shape=outs, in_specs=[pl.BlockSpec(...  62.1 us
    ppermute x55, starting transfers between devices, move(): return lax.ppermute(value, AXES, pairs)  59.5 us
  transfers between devices with their start and end apart: 55, of which 28 were waited for; matrix products, arithmetic and copies ran while one was open for 0% of the time, Pallas kernels for 28%

profile of v7, /device:TPU:0, one launch (start us, length us, event | category | flops | bytes accessed | tf_op | source)
XLA Modules:
  0.0 190.3 jit_solution(909157763017000167)
XLA Ops:
  1.4 1.9 %pack.1 = (bf16[160,640]{1,0:T(8,128)(2,1)S(1)}, bf16[160,640]{1,0:T(8,128)(2,1)S(1)}, bf16[160,640]{1,0:T(8,128)(2,1)S(1)}) custom-call(s32[3]{0:T(128)S(1)} %pad_add_fusion.refs_0_.s, bf16[160,320]{1,0:T(8,128)(2,1)} %refs_0_.1, bf16[160,320]{1,0:T(8,128)(2,1)} %refs_1_.1, bf16[160,320]{1,0:T(8,128)(2,1)} %refs_2_.3, bf16[160,320]{1,0:T(8,128)(2,1)} %bitcast.23, ...), custom_call_target="tpu_custom_call" | custom-call | flops 1000000 | bytes 1228800 | tf_op jit(solution)/shard_map/pack/pallas_call | solution.py:30
  3.3 4.1 %collective-permute-start.1 = (bf16[160,640]{1,0:T(8,128)(2,1)S(1)}, bf16[160,640]{1,0:T(8,128)(2,1)S(1)}, u32[]{:S(2)}, u32[]{:S(2)}) collective-permute-start(bf16[160,640]{1,0:T(8,128)(2,1)S(1)} %get-tuple-element.240.refs_0_.refs_6_), channel_id=1, source_target_pairs={{0,16},{1,17},{2,18},{3,19},{4,20},{5,21},{6,22},{7,23},{8,24},{9,... | collective-permute-start | bytes 614408 | tf_op jit(solution)/shard_map/ppermute | solution.py:464
  11.3 3.2 %prepare.1 = (bf16[128,1280]{1,0:T(8,128)(2,1)S(1)}, bf16[128,1280]{1,0:T(8,128)(2,1)S(1)}, bf16[128,1280]{1,0:T(8,128)(2,1)S(1)}, f32[8,1280]{1,0:T(8,128)S(1)}, f32[8,320]{1,0:T(8,128)S(1)}) custom-call(s32[3]{0:T(128)S(1)} %pad_add_fusion.refs_0_.s, f32[1,320]{1,0:T(1,128)S(1)} %broadcast_in_dim_tile.3.refs_1_, bf16[128,1280]{1,0:T(8,128)(2,1)} %refs_2_.2, ...), custom_call_target="tpu_custom_call" | custom-call | flops 1000000 | bytes 1726720 | tf_op jit(solution)/shard_map/prepare/pallas_call | solution.py:30
  22.8 2.3 %collective-permute-start.4 = (bf16[160,640]{1,0:T(8,128)(2,1)S(1)}, bf16[160,640]{1,0:T(8,128)(2,1)S(1)}, u32[]{:S(2)}, u32[]{:S(2)}) collective-permute-start(bf16[160,640]{1,0:T(8,128)(2,1)S(1)} %get-tuple-element.257.refs_4_), channel_id=1, source_target_pairs={{0,16},{1,17},{2,18},{3,19},{4,20},{5,21},{6,22},{7,23},{8,24},{9,... | collective-permute-start | bytes 614408 | tf_op jit(solution)/shard_map/ppermute | solution.py:464
  25.1 5.3 %collective-permute-done.8.refs_1_.refs_9_ = bf16[160,640]{1,0:T(8,128)(2,1)S(1)} collective-permute-done((bf16[160,640]{1,0:T(8,128)(2,1)S(1)}, bf16[160,640]{1,0:T(8,128)(2,1)S(1)}, u32[]{:S(2)}, u32[]{:S(2)}) %collective-permute-start.8) | collective-permute-done | bytes 204832 | tf_op jit(solution)/shard_map/ppermute | solution.py:464
  36.9 4.9 %collective-permute-done.12.refs_5_ = bf16[160,640]{1,0:T(8,128)(2,1)S(1)} collective-permute-done((bf16[160,640]{1,0:T(8,128)(2,1)S(1)}, bf16[160,640]{1,0:T(8,128)(2,1)S(1)}, u32[]{:S(2)}, u32[]{:S(2)}) %collective-permute-start.12) | collective-permute-done | bytes 204832 | tf_op jit(solution)/shard_map/ppermute | solution.py:464
  43.1 2.6 %collective-permute-done.11.refs_1_.refs_7_ = bf16[160,640]{1,0:T(8,128)(2,1)S(1)} collective-permute-done((bf16[160,640]{1,0:T(8,128)(2,1)S(1)}, bf16[160,640]{1,0:T(8,128)(2,1)S(1)}, u32[]{:S(2)}, u32[]{:S(2)}) %collective-permute-start.11) | collective-permute-done | bytes 204832 | tf_op jit(solution)/shard_map/ppermute | solution.py:464
  45.8 1.8 collective-permute-start.15
  47.6 1.7 collective-permute-start.14
  49.9 2.5 %collective-permute-start.17 = (bf16[320,640]{1,0:T(8,128)(2,1)S(1)}, bf16[320,640]{1,0:T(8,128)(2,1)S(1)}, u32[]{:S(2)}, u32[]{:S(2)}) collective-permute-start(bf16[320,640]{1,0:T(8,128)(2,1)S(1)} %stack.18), channel_id=1, source_target_pairs={{0,4},{1,5},{2,6},{3,7},{4,0},{5,1},{6,2},{7,3},{8,12},{9,13},{10,... | collective-permute-start | bytes 1228808 | tf_op jit(solution)/shard_map/ppermute | solution.py:464
  52.4 6.3 %attend.1 = (f32[512,320]{1,0:T(8,128)S(1)}, bf16[512,320]{1,0:T(8,128)(2,1)S(1)}, bf16[512,320]{1,0:T(8,128)(2,1)S(1)}, bf16[512,1280]{1,0:T(8,128)(2,1)S(1)}, ...) custom-call(s32[3]{0:T(128)S(1)} %pad_add_fusion.refs_0_.s, ...), custom_call_target="tpu_custom_call" | custom-call | flops 1000000 | bytes 9316352 | tf_op jit(solution)/shard_map/attend/pallas_call | solution.py:30
  61.3 5.6 %context.1 = (bf16[512,320]{1,0:T(8,128)(2,1)S(1)}, bf16[512,320]{1,0:T(8,128)(2,1)S(1)}, bf16[256,1280]{1,0:T(8,128)(2,1)S(1)}, f32[256,1280]{1,0:T(8,128)S(1)}...) custom-call(s32[3]{0:T(128)S(1)} %pad_add_fusion.refs_0_.s, ...), custom_call_target="tpu_custom_call" | custom-call | flops 1000000 | bytes 9316352 | tf_op jit(solution)/shard_map/context/pallas_call | solution.py:30
  71.5 8.1 %collective-permute-done.24.refs_11_ = bf16[320,640]{1,0:T(8,128)(2,1)S(1)} collective-permute-done((bf16[320,640]{1,0:T(8,128)(2,1)S(1)}, bf16[320,640]{1,0:T(8,128)(2,1)S(1)}, u32[]{:S(2)}, u32[]{:S(2)}) %collective-permute-start.24) | collective-permute-done | bytes 409632 | tf_op jit(solution)/shard_map/ppermute | solution.py:464
  82.2 4.0 %grad_act.1 = (f32[512,320]{1,0:T(8,128)S(1)}, bf16[512,1280]{1,0:T(8,128)(2,1)S(1)}, bf16[1280,320]{1,0:T(8,128)(2,1)S(1)}, bf16[1280,320]{1,0:T(8,128)(2,1)S(1)}) custom-call(s32[3]{0:T(128)S(1)} %pad_add_fusion.refs_0_.s, bf16[128,1280]{1,0:T(8,128)(2,1)S(1)} %get-tuple-element.278.refs_1_.grad, bf16[128,1280]{1,0:T(8,128)(2,1)S(1)} %collective-permute-done.16.refs_2_, ...), custom_call_target="tpu_custom_call" | custom-call | flops 1000000 | bytes 6553600 | tf_op jit(solution)/shard_map/grad_act/pallas_call | solution.py:30
  86.1 3.7 %collective-permute-done.25.p1 = bf16[128,1280]{1,0:T(8,128)(2,1)S(1)} collective-permute-done((bf16[128,1280]{1,0:T(8,128)(2,1)S(1)}, bf16[128,1280]{1,0:T(8,128)(2,1)S(1)}, u32[]{:S(2)}, u32[]{:S(2)}) %collective-permute-start.25) | collective-permute-done | bytes 327712 | tf_op jit(solution)/shard_map/ppermute | solution.py:464
  91.5 2.3 %hidden.1 = (bf16[256,1280]{1,0:T(8,128)(2,1)S(1)}, f32[256,1280]{1,0:T(8,128)S(1)}, bf16[512,320]{1,0:T(8,128)(2,1)S(1)}, bf16[512,320]{1,0:T(8,128)(2,1)S(1)}, bf16[512,1280]{1,0:T(8,128)(2,1)S(1)}) custom-call(s32[3]{0:T(128)S(1)} %pad_add_fusion.refs_0_.s, bf16[128,1280]{1,0:T(8,128)(2,1)S(1)} %get-tuple-element.277.p0, ...), custom_call_target="tpu_custom_call" | custom-call | flops 1000000 | bytes 6727680 | tf_op jit(solution)/shard_map/hidden/pallas_call | solution.py:30
  94.0 2.2 %down.1 = (f32[1,320]{1,0:T(1,128)S(1)}, bf16[640,384]{1,0:T(8,128)(2,1)S(1)}, bf16[640,384]{1,0:T(8,128)(2,1)S(1)}, bf16[640,256]{1,0:T(8,128)(2,1)S(1)}, bf16[640,256]{1,0:T(8,128)(2,1)S(1)}) custom-call(s32[3]{0:T(128)S(1)} %pad_add_fusion.refs_0_.s, bf16[512,1280]{1,0:T(8,128)(2,1)S(1)} %get-tuple-element.296.refs_1_, ...), custom_call_target="tpu_custom_call" | custom-call | flops 1000000 | bytes 4916480 | tf_op jit(solution)/shard_map/down/pallas_call | solution.py:30
  101.9 6.2 %collective-permute-done.29.got = bf16[128,1280]{1,0:T(8,128)(2,1)S(1)} collective-permute-done((bf16[128,1280]{1,0:T(8,128)(2,1)S(1)}, bf16[128,1280]{1,0:T(8,128)(2,1)S(1)}, u32[]{:S(2)}, u32[]{:S(2)}) %collective-permute-start.29) | collective-permute-done | bytes 327712 | tf_op jit(solution)/shard_map/ppermute | solution.py:464
  115.0 4.7 %collective-permute-done.34.ring_got = bf16[320,256]{1,0:T(8,128)(2,1)S(1)} collective-permute-done((bf16[320,256]{1,0:T(8,128)(2,1)S(1)}, bf16[320,256]{1,0:T(8,128)(2,1)S(1)}, u32[]{:S(2)}, u32[]{:S(2)}) %collective-permute-start.34) | collective-permute-done | bytes 163872 | tf_op jit(solution)/shard_map/ppermute | solution.py:464
  122.0 5.1 %grad_context.1 = (bf16[512,320]{1,0:T(8,128)(2,1)S(1)}, bf16[512,320]{1,0:T(8,128)(2,1)S(1)}, bf16[512,1280]{1,0:T(8,128)(2,1)}, bf16[640,384]{1,0:T(8,128)(2,1...) custom-call(s32[3]{0:T(128)S(1)} %pad_add_fusion.refs_0_.s, ...), custom_call_target="tpu_custom_call" | custom-call | flops 1000000 | bytes 9469952 | tf_op jit(solution)/shard_map/grad_context/pallas_call | solution.py:30
  131.1 2.2 %collective-permute-start.43 = (bf16[160,640]{1,0:T(8,128)(2,1)S(1)}, bf16[160,640]{1,0:T(8,128)(2,1)S(1)}, u32[]{:S(2)}, u32[]{:S(2)}) collective-permute-start(bf16[160,640]{1,0:T(8,128)(2,1)S(1)} %get-tuple-element.360), channel_id=1, source_target_pairs={{0,16},{1,17},{2,18},{3,19},{4,20},{5,21},{6,22},{7,23},{8,24},{9,... | collective-permute-start | bytes 614408 | tf_op jit(solution)/shard_map/ppermute | solution.py:464
  133.3 5.3 %grad_scores.1 = (bf16[512,640]{1,0:T(8,128)(2,1)S(1)}, f32[8,320]{1,0:T(8,128)S(1)}) custom-call(s32[3]{0:T(128)S(1)} %pad_add_fusion.refs_0_.s, bf16[4,512,512]{2,1,0:T(8,128)(2,1)S(1)} %get-tuple-element.255.refs_2_.refs_6_.refs_1_, bf16[512,320]{1,0:T(8,128)(2,1)S(1)} %get-tuple-element.337.refs_2_, bf16[512,320]{1,0:T(8,128)(2,1)S(1)} %get-tuple-element.338.refs_3_, ...), custom_call_target="tpu_custom_call" | custom-call | flops 1000000 | bytes 4739072 | tf_op jit(solution)/shard_map/grad_scores/pallas_call | solution.py:30
  138.6 4.0 %collective-permute-done.40.ring_got = bf16[640,256]{1,0:T(8,128)(2,1)S(1)} collective-permute-done((bf16[640,256]{1,0:T(8,128)(2,1)S(1)}, bf16[640,256]{1,0:T(8,128)(2,1)S(1)}, u32[]{:S(2)}, u32[]{:S(2)}) %collective-permute-start.40) | collective-permute-done | bytes 327712 | tf_op jit(solution)/shard_map/ppermute | solution.py:464
  142.6 3.8 %grad_first.1 = (bf16[256,1280]{1,0:T(8,128)(2,1)S(1)}, f32[256,1280]{1,0:T(8,128)S(1)}, f32[8,1280]{1,0:T(8,128)S(1)}, bf16[640,384]{1,0:T(8,128)(2,1)S(1)}, bf...) custom-call(s32[3]{0:T(128)S(1)} %pad_add_fusion.refs_0_.s, ...), custom_call_target="tpu_custom_call" | custom-call | flops 1000000 | bytes 8474176 | tf_op jit(solution)/shard_map/grad_first/pallas_call | solution.py:30
  153.4 1.8 output.1
  158.2 2.3 %collective-permute-done.41.pair_got = bf16[640,384]{1,0:T(8,128)(2,1)S(1)} collective-permute-done((bf16[640,384]{1,0:T(8,128)(2,1)S(1)}, bf16[640,384]{1,0:T(8,128)(2,1)S(1)}, u32[]{:S(2)}, u32[]{:S(2)}) %collective-permute-start.41) | collective-permute-done | bytes 491552 | tf_op jit(solution)/shard_map/ppermute | solution.py:464
  160.6 3.1 %collective-permute-done.47.ring_got = bf16[320,256]{1,0:T(8,128)(2,1)S(1)} collective-permute-done((bf16[320,256]{1,0:T(8,128)(2,1)S(1)}, bf16[320,256]{1,0:T(8,128)(2,1)S(1)}, u32[]{:S(2)}, u32[]{:S(2)}) %collective-permute-start.47) | collective-permute-done | bytes 163872 | tf_op jit(solution)/shard_map/ppermute | solution.py:464
  165.9 3.5 %collective-permute-start.54 = (bf16[160,640]{1,0:T(8,128)(2,1)S(1)}, bf16[160,640]{1,0:T(8,128)(2,1)S(1)}, u32[]{:S(2)}, u32[]{:S(2)}) collective-permute-start(bf16[160,640]{1,0:T(8,128)(2,1)S(1)} %get-tuple-element.412), channel_id=1, source_target_pairs={{0,16},{1,17},{2,18},{3,19},{4,20},{5,21},{6,22},{7,23},{8,24},{9,... | collective-permute-start | bytes 614408 | tf_op jit(solution)/shard_map/ppermute | solution.py:464
  169.4 2.1 %last.1 = bf16[128,1280]{1,0:T(8,128)(2,1)} custom-call(s32[3]{0:T(128)S(1)} %pad_add_fusion.refs_0_.s, f32[128,1280]{1,0:T(8,128)S(1)} %get-tuple-element.391.refs_1_, bf16[128,1280]{1,0:T(8,128)(2,1)S(1)} %collective-permute-done.45.refs_2_, bf16[128,1280]{1,0:T(8,128)(2,1)S(1)} %get-tuple-element.275.x_own.refs_3_, ...), custom_call_target="tpu_custom_call" | custom-call | flops 1000000 | bytes 2334720 | tf_op jit(solution)/shard_map/last/pallas_call | solution.py:30
  171.5 3.7 %collective-permute-done.48.pair_got = bf16[320,384]{1,0:T(8,128)(2,1)S(1)} collective-permute-done((bf16[320,384]{1,0:T(8,128)(2,1)S(1)}, bf16[320,384]{1,0:T(8,128)(2,1)S(1)}, u32[]{:S(2)}, u32[]{:S(2)}) %collective-permute-start.48) | collective-permute-done | bytes 245792 | tf_op jit(solution)/shard_map/ppermute | solution.py:464
  178.9 2.8 %collective-permute-done.51.two = f32[8,1280]{1,0:T(8,128)S(1)} collective-permute-done((f32[8,1280]{1,0:T(8,128)S(1)}, f32[8,1280]{1,0:T(8,128)S(1)}, u32[]{:S(2)}, u32[]{:S(2)}) %collective-permute-start.51) | collective-permute-done | bytes 40992 | tf_op jit(solution)/shard_map/ppermute | solution.py:464
  182.3 2.9 %collective-permute-start.52 = (f32[8,1280]{1,0:T(8,128)S(1)}, f32[8,1280]{1,0:T(8,128)S(1)}, u32[]{:S(2)}, u32[]{:S(2)}) collective-permute-start(f32[8,1280]{1,0:T(8,128)S(1)} %add.18.one), channel_id=1, source_target_pairs={{0,16},{1,17},{2,18},{3,19},{4,20},{5,21},{6,22},{7,23},{8,24},{9,... | collective-permute-start | bytes 122888 | tf_op jit(solution)/shard_map/ppermute | solution.py:464
  (117 shorter events, 72.5 us)
Async XLA Ops:
  3.3 13.7 %collective-permute-start.1 = (bf16[160,640]{1,0:T(8,128)(2,1)S(1)}, bf16[160,640]{1,0:T(8,128)(2,1)S(1)}, u32[]{:S(2)}, u32[]{:S(2)}) collective-permute-start(bf16[160,640]{1,0:T(8,128)(2,1)S(1)} %get-tuple-element.240.refs_0_.refs_6_), channel_id=1, source_target_pairs={{0,16},{1,17},{2,18},{3,19},{4,20},{5,21},{6,22},{7,23},{8,24},{9,... | collective-permute-start | bytes 614408 | tf_op jit(solution)/shard_map/ppermute | solution.py:464
  7.4 9.8 %collective-permute-start = (bf16[160,640]{1,0:T(8,128)(2,1)S(1)}, bf16[160,640]{1,0:T(8,128)(2,1)S(1)}, u32[]{:S(2)}, u32[]{:S(2)}) collective-permute-start(bf16[160,640]{1,0:T(8,128)(2,1)S(1)} %get-tuple-element.240.refs_0_.refs_6_), channel_id=1, source_target_pairs={{0,8},{1,9},{2,10},{3,11},{4,12},{5,13},{6,14},{7,15},{8,0},{9,1},... | collective-permute-start | bytes 614408 | tf_op jit(solution)/shard_map/ppermute | solution.py:464
  17.8 13.3 %collective-permute-start.9 = (bf16[320,640]{1,0:T(8,128)(2,1)S(1)}, bf16[320,640]{1,0:T(8,128)(2,1)S(1)}, u32[]{:S(2)}, u32[]{:S(2)}) collective-permute-start(bf16[320,640]{1,0:T(8,128)(2,1)S(1)} %stack.17), channel_id=1, source_target_pairs={{0,4},{1,5},{2,6},{3,7},{4,0},{5,1},{6,2},{7,3},{8,12},{9,13},{10,... | collective-permute-start | bytes 1228808 | tf_op jit(solution)/shard_map/ppermute | solution.py:464
  19.4 14.5 %collective-permute-start.3 = (bf16[128,1280]{1,0:T(8,128)(2,1)S(1)}, bf16[128,1280]{1,0:T(8,128)(2,1)S(1)}, u32[]{:S(2)}, u32[]{:S(2)}) collective-permute-start(bf16[128,1280]{1,0:T(8,128)(2,1)S(1)} %get-tuple-element.235.refs_1_), channel_id=1, source_target_pairs={{0,2},{1,3},{2,0},{3,1},{4,6},{5,7},{6,4},{7,5},{8,10},{9,11},{10,... | collective-permute-start | bytes 983048 | tf_op jit(solution)/shard_map/ppermute | solution.py:464
  20.9 9.5 %collective-permute-start.8 = (bf16[160,640]{1,0:T(8,128)(2,1)S(1)}, bf16[160,640]{1,0:T(8,128)(2,1)S(1)}, u32[]{:S(2)}, u32[]{:S(2)}) collective-permute-start(bf16[160,640]{1,0:T(8,128)(2,1)S(1)} %collective-permute-done.1.refs_0_.refs_8_), channel_id=1, source_target_pairs={{0,8},{1,9},{2,10},{3,11},{4,12},{5,13},{6,14},{7,15},{8,0},{9,1},... | collective-permute-start | bytes 614408 | tf_op jit(solution)/shard_map/ppermute | solution.py:464
  22.3 10.3 %collective-permute-start.5 = (bf16[160,640]{1,0:T(8,128)(2,1)S(1)}, bf16[160,640]{1,0:T(8,128)(2,1)S(1)}, u32[]{:S(2)}, u32[]{:S(2)}) collective-permute-start(bf16[160,640]{1,0:T(8,128)(2,1)S(1)} %get-tuple-element.257.refs_4_), channel_id=1, source_target_pairs={{0,4},{1,5},{2,6},{3,7},{4,0},{5,1},{6,2},{7,3},{8,12},{9,13},{10,... | collective-permute-start | bytes 614408 | tf_op jit(solution)/shard_map/ppermute | solution.py:464
  22.8 11.0 %collective-permute-start.4 = (bf16[160,640]{1,0:T(8,128)(2,1)S(1)}, bf16[160,640]{1,0:T(8,128)(2,1)S(1)}, u32[]{:S(2)}, u32[]{:S(2)}) collective-permute-start(bf16[160,640]{1,0:T(8,128)(2,1)S(1)} %get-tuple-element.257.refs_4_), channel_id=1, source_target_pairs={{0,16},{1,17},{2,18},{3,19},{4,20},{5,21},{6,22},{7,23},{8,24},{9,... | collective-permute-start | bytes 614408 | tf_op jit(solution)/shard_map/ppermute | solution.py:464
  31.0 14.7 %collective-permute-start.10 = (bf16[320,640]{1,0:T(8,128)(2,1)S(1)}, bf16[320,640]{1,0:T(8,128)(2,1)S(1)}, u32[]{:S(2)}, u32[]{:S(2)}) collective-permute-start(bf16[320,640]{1,0:T(8,128)(2,1)S(1)} %stack.16), channel_id=1, source_target_pairs={{0,4},{1,5},{2,6},{3,7},{4,0},{5,1},{6,2},{7,3},{8,12},{9,13},{10,... | collective-permute-start | bytes 1228808 | tf_op jit(solution)/shard_map/ppermute | solution.py:464
  33.9 11.9 %collective-permute-start.7 = (bf16[128,1280]{1,0:T(8,128)(2,1)S(1)}, bf16[128,1280]{1,0:T(8,128)(2,1)S(1)}, u32[]{:S(2)}, u32[]{:S(2)}) collective-permute-start(bf16[128,1280]{1,0:T(8,128)(2,1)S(1)} %collective-permute-done.3.refs_2_), channel_id=1, source_target_pairs={{0,1},{1,0},{2,3},{3,2},{4,5},{5,4},{6,7},{7,6},{8,9},{9,8},{10,11... | collective-permute-start | bytes 983048 | tf_op jit(solution)/shard_map/ppermute | solution.py:464
  34.6 11.2 %collective-permute-start.11 = (bf16[160,640]{1,0:T(8,128)(2,1)S(1)}, bf16[160,640]{1,0:T(8,128)(2,1)S(1)}, u32[]{:S(2)}, u32[]{:S(2)}) collective-permute-start(bf16[160,640]{1,0:T(8,128)(2,1)S(1)} %collective-permute-done.4.refs_0_.refs_6_), channel_id=1, source_target_pairs={{0,8},{1,9},{2,10},{3,11},{4,12},{5,13},{6,14},{7,15},{8,0},{9,1},... | collective-permute-start | bytes 614408 | tf_op jit(solution)/shard_map/ppermute | solution.py:464
  35.9 22.8 %collective-permute-start.16 = (bf16[128,1280]{1,0:T(8,128)(2,1)S(1)}, bf16[128,1280]{1,0:T(8,128)(2,1)S(1)}, u32[]{:S(2)}, u32[]{:S(2)}) collective-permute-start(bf16[128,1280]{1,0:T(8,128)(2,1)S(1)} %get-tuple-element.278.refs_1_.grad), channel_id=1, source_target_pairs={{0,2},{1,3},{2,0},{3,1},{4,6},{5,7},{6,4},{7,5},{8,10},{9,11},{10,... | collective-permute-start | bytes 983048 | tf_op jit(solution)/shard_map/ppermute | solution.py:464
  41.8 17.0 %collective-permute-start.13 = (bf16[160,640]{1,0:T(8,128)(2,1)S(1)}, bf16[160,640]{1,0:T(8,128)(2,1)S(1)}, u32[]{:S(2)}, u32[]{:S(2)}) collective-permute-start(bf16[160,640]{1,0:T(8,128)(2,1)S(1)} %collective-permute-done.12.refs_5_), channel_id=1, source_target_pairs={{0,4},{1,5},{2,6},{3,7},{4,0},{5,1},{6,2},{7,3},{8,12},{9,13},{10,... | collective-permute-start | bytes 614408 | tf_op jit(solution)/shard_map/ppermute | solution.py:464
  45.8 13.0 %collective-permute-start.15 = (bf16[160,640]{1,0:T(8,128)(2,1)S(1)}, bf16[160,640]{1,0:T(8,128)(2,1)S(1)}, u32[]{:S(2)}, u32[]{:S(2)}) collective-permute-start(bf16[160,640]{1,0:T(8,128)(2,1)S(1)} %get-tuple-element.282.refs_5_), channel_id=1, source_target_pairs={{0,16},{1,17},{2,18},{3,19},{4,20},{5,21},{6,22},{7,23},{8,24},{9,... | collective-permute-start | bytes 614408 | tf_op jit(solution)/shard_map/ppermute | solution.py:464
  47.6 11.3 %collective-permute-start.14 = (bf16[160,640]{1,0:T(8,128)(2,1)S(1)}, bf16[160,640]{1,0:T(8,128)(2,1)S(1)}, u32[]{:S(2)}, u32[]{:S(2)}) collective-permute-start(bf16[160,640]{1,0:T(8,128)(2,1)S(1)} %get-tuple-element.282.refs_5_), channel_id=1, source_target_pairs={{0,8},{1,9},{2,10},{3,11},{4,12},{5,13},{6,14},{7,15},{8,0},{9,1},... | collective-permute-start | bytes 614408 | tf_op jit(solution)/shard_map/ppermute | solution.py:464
  49.9 11.4 %collective-permute-start.17 = (bf16[320,640]{1,0:T(8,128)(2,1)S(1)}, bf16[320,640]{1,0:T(8,128)(2,1)S(1)}, u32[]{:S(2)}, u32[]{:S(2)}) collective-permute-start(bf16[320,640]{1,0:T(8,128)(2,1)S(1)} %stack.18), channel_id=1, source_target_pairs={{0,4},{1,5},{2,6},{3,7},{4,0},{5,1},{6,2},{7,3},{8,12},{9,13},{10,... | collective-permute-start | bytes 1228808 | tf_op jit(solution)/shard_map/ppermute | solution.py:464
  67.7 11.9 %collective-permute-start.24 = (bf16[320,640]{1,0:T(8,128)(2,1)S(1)}, bf16[320,640]{1,0:T(8,128)(2,1)S(1)}, u32[]{:S(2)}, u32[]{:S(2)}) collective-permute-start(bf16[320,640]{1,0:T(8,128)(2,1)S(1)} %stack.19), channel_id=1, source_target_pairs={{0,4},{1,5},{2,6},{3,7},{4,0},{5,1},{6,2},{7,3},{8,12},{9,13},{10,... | collective-permute-start | bytes 1228808 | tf_op jit(solution)/shard_map/ppermute | solution.py:464
  69.9 9.9 %collective-permute-start.23 = (bf16[128,1280]{1,0:T(8,128)(2,1)S(1)}, bf16[128,1280]{1,0:T(8,128)(2,1)S(1)}, u32[]{:S(2)}, u32[]{:S(2)}) collective-permute-start(bf16[128,1280]{1,0:T(8,128)(2,1)S(1)} %get-tuple-element.270), channel_id=1, source_target_pairs={{0,2},{1,3},{2,0},{3,1},{4,6},{5,7},{6,4},{7,5},{8,10},{9,11},{10,... | collective-permute-start | bytes 983048 | tf_op jit(solution)/shard_map/ppermute | solution.py:464
  96.2 13.5 %collective-permute-start.30 = (bf16[640,384]{1,0:T(8,128)(2,1)S(1)}, bf16[640,384]{1,0:T(8,128)(2,1)S(1)}, u32[]{:S(2)}, u32[]{:S(2)}) collective-permute-start(bf16[640,384]{1,0:T(8,128)(2,1)S(1)} %get-tuple-element.311), channel_id=1, source_target_pairs={{0,4},{1,5},{2,6},{3,7},{4,0},{5,1},{6,2},{7,3},{8,12},{9,13},{10,... | collective-permute-start | bytes 1474568 | tf_op jit(solution)/shard_map/ppermute | solution.py:464
  98.4 9.8 %collective-permute-start.29 = (bf16[128,1280]{1,0:T(8,128)(2,1)S(1)}, bf16[128,1280]{1,0:T(8,128)(2,1)S(1)}, u32[]{:S(2)}, u32[]{:S(2)}) collective-permute-start(bf16[128,1280]{1,0:T(8,128)(2,1)S(1)} %get-tuple-element.306), channel_id=1, source_target_pairs={{0,2},{1,3},{2,0},{3,1},{4,6},{5,7},{6,4},{7,5},{8,10},{9,11},{10,... | collective-permute-start | bytes 983048 | tf_op jit(solution)/shard_map/ppermute | solution.py:464
  110.7 9.5 %collective-permute-start.32 = (bf16[128,1280]{1,0:T(8,128)(2,1)S(1)}, bf16[128,1280]{1,0:T(8,128)(2,1)S(1)}, u32[]{:S(2)}, u32[]{:S(2)}) collective-permute-start(bf16[128,1280]{1,0:T(8,128)(2,1)S(1)} %get-tuple-element.329.refs_1_), channel_id=1, source_target_pairs={{0,2},{1,3},{2,0},{3,1},{4,6},{5,7},{6,4},{7,5},{8,10},{9,11},{10,... | collective-permute-start | bytes 983048 | tf_op jit(solution)/shard_map/ppermute | solution.py:464
  127.1 15.5 %collective-permute-start.39 = (bf16[640,384]{1,0:T(8,128)(2,1)S(1)}, bf16[640,384]{1,0:T(8,128)(2,1)S(1)}, u32[]{:S(2)}, u32[]{:S(2)}) collective-permute-start(bf16[640,384]{1,0:T(8,128)(2,1)S(1)} %get-tuple-element.346), channel_id=1, source_target_pairs={{0,4},{1,5},{2,6},{3,7},{4,0},{5,1},{6,2},{7,3},{8,12},{9,13},{10,... | collective-permute-start | bytes 1474568 | tf_op jit(solution)/shard_map/ppermute | solution.py:464
  128.5 14.1 %collective-permute-start.40 = (bf16[640,256]{1,0:T(8,128)(2,1)S(1)}, bf16[640,256]{1,0:T(8,128)(2,1)S(1)}, u32[]{:S(2)}, u32[]{:S(2)}) collective-permute-start(bf16[640,256]{1,0:T(8,128)(2,1)S(1)} %get-tuple-element.347), channel_id=1, source_target_pairs={{0,8},{1,9},{2,10},{3,11},{4,12},{5,13},{6,14},{7,15},{8,0},{9,1},... | collective-permute-start | bytes 983048 | tf_op jit(solution)/shard_map/ppermute | solution.py:464
  129.8 12.9 %collective-permute-start.38 = (bf16[128,1280]{1,0:T(8,128)(2,1)S(1)}, bf16[128,1280]{1,0:T(8,128)(2,1)S(1)}, u32[]{:S(2)}, u32[]{:S(2)}) collective-permute-start(bf16[128,1280]{1,0:T(8,128)(2,1)S(1)} %get-tuple-element.345), channel_id=1, source_target_pairs={{0,2},{1,3},{2,0},{3,1},{4,6},{5,7},{6,4},{7,5},{8,10},{9,11},{10,... | collective-permute-start | bytes 983048 | tf_op jit(solution)/shard_map/ppermute | solution.py:464
  131.1 15.3 %collective-permute-start.43 = (bf16[160,640]{1,0:T(8,128)(2,1)S(1)}, bf16[160,640]{1,0:T(8,128)(2,1)S(1)}, u32[]{:S(2)}, u32[]{:S(2)}) collective-permute-start(bf16[160,640]{1,0:T(8,128)(2,1)S(1)} %get-tuple-element.360), channel_id=1, source_target_pairs={{0,16},{1,17},{2,18},{3,19},{4,20},{5,21},{6,22},{7,23},{8,24},{9,... | collective-permute-start | bytes 614408 | tf_op jit(solution)/shard_map/ppermute | solution.py:464
  146.5 14.1 %collective-permute-start.41 = (bf16[640,384]{1,0:T(8,128)(2,1)S(1)}, bf16[640,384]{1,0:T(8,128)(2,1)S(1)}, u32[]{:S(2)}, u32[]{:S(2)}) collective-permute-start(bf16[640,384]{1,0:T(8,128)(2,1)S(1)} %get-tuple-element.356), channel_id=1, source_target_pairs={{0,4},{1,5},{2,6},{3,7},{4,0},{5,1},{6,2},{7,3},{8,12},{9,13},{10,... | collective-permute-start | bytes 1474568 | tf_op jit(solution)/shard_map/ppermute | solution.py:464
  147.2 11.1 %collective-permute-start.42 = (bf16[688,256]{1,0:T(8,128)(2,1)S(1)}, bf16[688,256]{1,0:T(8,128)(2,1)S(1)}, u32[]{:S(2)}, u32[]{:S(2)}) collective-permute-start(bf16[688,256]{1,0:T(8,128)(2,1)S(1)} %get-tuple-element.357), channel_id=1, source_target_pairs={{0,8},{1,9},{2,10},{3,11},{4,12},{5,13},{6,14},{7,15},{8,0},{9,1},... | collective-permute-start | bytes 1056776 | tf_op jit(solution)/shard_map/ppermute | solution.py:464
  149.3 11.3 %collective-permute-start.45 = (bf16[128,1280]{1,0:T(8,128)(2,1)S(1)}, bf16[128,1280]{1,0:T(8,128)(2,1)S(1)}, u32[]{:S(2)}, u32[]{:S(2)}) collective-permute-start(bf16[128,1280]{1,0:T(8,128)(2,1)S(1)} %get-tuple-element.373), channel_id=1, source_target_pairs={{0,2},{1,3},{2,0},{3,1},{4,6},{5,7},{6,4},{7,5},{8,10},{9,11},{10,... | collective-permute-start | bytes 983048 | tf_op jit(solution)/shard_map/ppermute | solution.py:464
  150.6 13.1 %collective-permute-start.46 = (bf16[320,384]{1,0:T(8,128)(2,1)S(1)}, bf16[320,384]{1,0:T(8,128)(2,1)S(1)}, u32[]{:S(2)}, u32[]{:S(2)}) collective-permute-start(bf16[320,384]{1,0:T(8,128)(2,1)S(1)} %get-tuple-element.383), channel_id=1, source_target_pairs={{0,8},{1,9},{2,10},{3,11},{4,12},{5,13},{6,14},{7,15},{8,0},{9,1},... | collective-permute-start | bytes 737288 | tf_op jit(solution)/shard_map/ppermute | solution.py:464
  151.9 11.7 %collective-permute-start.47 = (bf16[320,256]{1,0:T(8,128)(2,1)S(1)}, bf16[320,256]{1,0:T(8,128)(2,1)S(1)}, u32[]{:S(2)}, u32[]{:S(2)}) collective-permute-start(bf16[320,256]{1,0:T(8,128)(2,1)S(1)} %get-tuple-element.384), channel_id=1, source_target_pairs={{0,4},{1,5},{2,6},{3,7},{4,0},{5,1},{6,2},{7,3},{8,12},{9,13},{10,... | collective-permute-start | bytes 491528 | tf_op jit(solution)/shard_map/ppermute | solution.py:464
  164.4 10.8 %collective-permute-start.48 = (bf16[320,384]{1,0:T(8,128)(2,1)S(1)}, bf16[320,384]{1,0:T(8,128)(2,1)S(1)}, u32[]{:S(2)}, u32[]{:S(2)}) collective-permute-start(bf16[320,384]{1,0:T(8,128)(2,1)S(1)} %get-tuple-element.389), channel_id=1, source_target_pairs={{0,8},{1,9},{2,10},{3,11},{4,12},{5,13},{6,14},{7,15},{8,0},{9,1},... | collective-permute-start | bytes 737288 | tf_op jit(solution)/shard_map/ppermute | solution.py:464
  165.9 19.4 %collective-permute-start.54 = (bf16[160,640]{1,0:T(8,128)(2,1)S(1)}, bf16[160,640]{1,0:T(8,128)(2,1)S(1)}, u32[]{:S(2)}, u32[]{:S(2)}) collective-permute-start(bf16[160,640]{1,0:T(8,128)(2,1)S(1)} %get-tuple-element.412), channel_id=1, source_target_pairs={{0,16},{1,17},{2,18},{3,19},{4,20},{5,21},{6,22},{7,23},{8,24},{9,... | collective-permute-start | bytes 614408 | tf_op jit(solution)/shard_map/ppermute | solution.py:464
  175.8 12.0 %collective-permute-start.53 = (bf16[160,640]{1,0:T(8,128)(2,1)S(1)}, bf16[160,640]{1,0:T(8,128)(2,1)S(1)}, u32[]{:S(2)}, u32[]{:S(2)}) collective-permute-start(bf16[160,640]{1,0:T(8,128)(2,1)S(1)} %get-tuple-element.407), channel_id=1, source_target_pairs={{0,16},{1,17},{2,18},{3,19},{4,20},{5,21},{6,22},{7,23},{8,24},{9,... | collective-permute-start | bytes 614408 | tf_op jit(solution)/shard_map/ppermute | solution.py:464
  (23 other events, 120.4 us)
